TPU v7x, 512 devices: a whole 4x4x16 slice. The times are simulated.
512 devices in a mesh: tile: 128 (over z_lo, y, x, core), head: 4 (over z_hi).
Axes of the slice: x: 4, y: 4, z: 16 (z_hi: 4, z_lo: 4; z = z_hi * 4 + z_lo), core: 2. Of those that a mesh axis runs over, the one named last changes fastest.
Arguments:
- self_query: bfloat16 [16384, 5120], P('tile', 'head')
- self_key: bfloat16 [16384, 5120], P('tile', 'head')
- self_value: bfloat16 [16384, 5120], P('tile', 'head'), may hold values from -6 to 6
- cross_query: bfloat16 [16384, 5120], P('tile', 'head')
- text_key: bfloat16 [32768, 5120], P('tile', 'head'), as said below
- text_value: bfloat16 [32768, 5120], P('tile', 'head'), as said below
- query_gain: float32 [5120], P('head'), may hold values from 0.5 to 1.5
- key_gain: float32 [5120], P('head'), may hold values from 0.5 to 1.5
- cross_gain: float32 [5120], P('head'), may hold values from 0.5 to 1.5
- text_gain: float32 [5120], P('head'), may hold values from 0.5 to 1.5
- tile_item: int32 [128], replicated, may hold values from 0 to 63, as said below
- row_count: int32 [128], replicated, may hold values from 32 to 128, as said below
- text_len: int32 [128], replicated, may hold values from 2 to 256, as said below
Outputs:
- attended: bfloat16 [16384, 5120], P('tile', 'head')
Inputs may be any that keep to these rules, and one draw needn't show every extreme that they name: `tile_item`: never falling and 0 on the first tile; every item holds 1 to 7 consecutive tiles, some item holds exactly 7, and there are 64 items. `row_count`: some tile holds exactly 128. `text_len`: entries past the last item are not used; some item has exactly 256. `text_key`: tiles of one item hold the same text rows. `text_value`: tiles of one item hold the same text rows.
All inputs are finite; a program needn't handle non-finite values.
Results may differ from a plain program's by a relative error of at most 0.0015.
The roundings to bfloat16 on the way count: a program that leaves them out, or rounds other values in their place, can miss the bound.
Values may be sent and summed in bfloat16 or wider, within the bound.
No kernel may reach another device: no remote copies, remote signals or barrier semaphores. Data moves between devices by JAX's collectives and lax.ppermute only.
A program may use at most 64 MiB of HBM per device.

v0:
```python
import math

import jax
import jax.numpy as jnp
from jax import lax
from jax.sharding import PartitionSpec as P

D = 5120
HD = 128
HGT = 30
WID = 52


EPSILON = 1e-06


def shifted(value, axis, by):
    peers = lax.axis_size(axis)
    pairs = [(i, i + by) for i in range(peers) if 0 <= i + by < peers]
    return lax.ppermute(value, axis, pairs)


def frequencies(amount, dimension):
    return 1.0 / 10000.0 ** (jnp.arange(amount, dtype=jnp.float32) * 2.0 / dimension)


def rope_angles(positions):
    spatial = HD // 6
    temporal = HD // 2 - 2 * spatial
    frame = (positions // (HGT * WID)).astype(jnp.float32)
    height = (positions // WID % HGT).astype(jnp.float32)
    across = (positions % WID).astype(jnp.float32)
    return jnp.concatenate(
        [
            frame[:, None] * frequencies(temporal, 2 * temporal)[None, :],
            height[:, None] * frequencies(spatial, 2 * spatial)[None, :],
            across[:, None] * frequencies(spatial, 2 * spatial)[None, :],
        ],
        axis=1,
    )


def pair_partner(matrix):
    index = jnp.arange(matrix.shape[-1])
    return jnp.where(index % 2 == 0, -jnp.roll(matrix, -1, axis=-1), jnp.roll(matrix, 1, axis=-1))


def rotate(matrix, angle):
    cosine = jnp.repeat(jnp.cos(angle), 2, axis=1)
    sine = jnp.repeat(jnp.sin(angle), 2, axis=1)
    shaped = matrix.reshape(matrix.shape[0], matrix.shape[1] // HD, HD)
    turned = shaped * cosine[:, None, :] + pair_partner(shaped) * sine[:, None, :]
    return turned.reshape(matrix.shape)


def scaled_rows(values, mean_square, gain):
    return values * lax.rsqrt(mean_square[:, None] + EPSILON) * gain[None, :]


def attend_head(query, key_rows, value_rows, live):
    scale = 1.0 / math.sqrt(HD)
    scores = (
        lax.dot_general(
            query, key_rows, (((1,), (1,)), ((), ())), preferred_element_type=jnp.float32
        )
        * scale
    )
    scores = jnp.where(live[None, :], scores, -1e30)
    highest = jnp.max(scores, axis=1, keepdims=True)
    weights = jnp.exp(scores - highest)
    total = jnp.sum(weights, axis=1, keepdims=True)
    mixed = jnp.dot(weights.astype(jnp.bfloat16), value_rows, preferred_element_type=jnp.float32)
    return mixed / total


def per_device(
    self_query,
    self_key,
    self_value,
    cross_query,
    text_key,
    text_value,
    query_gain,
    key_gain,
    cross_gain,
    text_gain,
    tile_item,
    row_count,
    text_len,
):
    row_total = self_query.shape[0]
    text_total = text_key.shape[0]
    head_total = self_query.shape[1] // HD
    tile_here = lax.axis_index("tile")
    tile_total = lax.axis_size("tile")
    span = min(7, tile_total // 2)
    item_here = tile_item[tile_here]
    first_tile = jnp.sum((tile_item < item_here).astype(jnp.int32))
    positions = (tile_here - first_tile) * row_total + jnp.arange(row_total, dtype=jnp.int32)
    angle = rope_angles(positions)
    query_float = self_query.astype(jnp.float32)
    key_float = self_key.astype(jnp.float32)
    cross_float = cross_query.astype(jnp.float32)
    text_float = text_key.astype(jnp.float32)
    query_sq, key_sq, cross_sq, text_sq = lax.psum(
        (
            jnp.sum(query_float * query_float, axis=1),
            jnp.sum(key_float * key_float, axis=1),
            jnp.sum(cross_float * cross_float, axis=1),
            jnp.sum(text_float * text_float, axis=1),
        ),
        "head",
    )
    queries = rotate(scaled_rows(query_float, query_sq / D, query_gain), angle).astype(jnp.bfloat16)
    rotated_keys = rotate(scaled_rows(key_float, key_sq / D, key_gain), angle).astype(jnp.bfloat16)
    cross = scaled_rows(cross_float, cross_sq / D, cross_gain).astype(jnp.bfloat16)
    texts = scaled_rows(text_float, text_sq / D, text_gain).astype(jnp.bfloat16)

    def live_rows(source):
        inside = (source >= 0) & (source < tile_total)
        clipped = jnp.clip(source, 0, tile_total - 1)
        same_item = inside & (tile_item[clipped] == item_here)
        return same_item & (jnp.arange(row_total, dtype=jnp.int32) < row_count[clipped])

    key_parts = [rotated_keys]
    value_parts = [self_value]
    live_parts = [live_rows(tile_here)]
    for distance in range(1, span):
        for offset in (distance, -distance):
            moved_keys, moved_values = shifted((rotated_keys, self_value), "tile", offset)
            key_parts.append(moved_keys)
            value_parts.append(moved_values)
            live_parts.append(live_rows(tile_here - offset))
    keys_all = jnp.concatenate(key_parts, axis=0)
    values_all = jnp.concatenate(value_parts, axis=0)
    live_all = jnp.concatenate(live_parts, axis=0)
    text_live = jnp.arange(text_total, dtype=jnp.int32) < text_len[item_here]

    def per_head(head_index):
        first_column = head_index * HD

        def columns(matrix):
            return lax.dynamic_slice_in_dim(matrix, first_column, HD, 1)

        local_part = attend_head(columns(queries), columns(keys_all), columns(values_all), live_all)
        text_part = attend_head(columns(cross), columns(texts), columns(text_value), text_live)
        return (local_part + text_part).astype(jnp.bfloat16)

    head_outputs = lax.map(per_head, jnp.arange(head_total, dtype=jnp.int32))
    return jnp.moveaxis(head_outputs, 0, 1).reshape(row_total, head_total * HD)


def solution(mesh):
    in_specs = (
        P("tile", "head"),
        P("tile", "head"),
        P("tile", "head"),
        P("tile", "head"),
        P("tile", "head"),
        P("tile", "head"),
        P("head"),
        P("head"),
        P("head"),
        P("head"),
        P(),
        P(),
        P(),
    )
    out_specs = P("tile", "head")
    return jax.shard_map(
        per_device, mesh=mesh, in_specs=in_specs, out_specs=out_specs, check_vma=False
    )
```

profile of v0, /device:TPU:58, one launch (start us, length us, event | category | flops | bytes accessed | tf_op | source)
XLA Modules:
  0.0 284.6 jit_solution(17567701368617881039)
XLA Ops:
  5.2 20.4 %all-reduce = (f32[128]{0:T(128)S(1)}, f32[128]{0:T(128)S(1)}, f32[128]{0:T(128)S(1)}, f32[256]{0:T(256)S(1)}) all-reduce(f32[128]{0:T(128)S(1)} %fusion.28, f32[128]{0:T(128)S(1)} %fusion.30, f32[128]{0:T(128)S(1)} %fusion.32, f32[256]{0:T(256)S(1)} %fusion.25), channel_id=1, replica_groups=mesh['tile'=128,'head'=4] {'head'}, use_global_device_ids=true, to_apply=%region_1.2 | all-reduce | flops 640 | bytes 5120 | tf_op jit(solution)/shard_map/psum | solution.py:105
  33.2 3.6 %collective-permute-start.1 = (bf16[128,1280]{0,1:T(8,128)(2,1)S(1)}, bf16[128,1280]{0,1:T(8,128)(2,1)}, u32[]{:S(2)}, u32[]{:S(2)}) collective-permute-start(bf16[128,1280]{0,1:T(8,128)(2,1)S(1)} %get-tuple-element.137), channel_id=1, source_target_pairs={{4,0},{8,4},{12,8},{16,12},{20,16},{24,20},{28,24},{32,28},{36,32}... | collective-permute-start | bytes 983048 | tf_op jit(solution)/shard_map/ppermute | solution.py:20
  36.8 3.4 %collective-permute-start.2 = (bf16[128,1280]{0,1:T(8,128)(2,1)S(1)}, bf16[128,1280]{0,1:T(8,128)(2,1)}, u32[]{:S(2)}, u32[]{:S(2)}) collective-permute-start(bf16[128,1280]{0,1:T(8,128)(2,1)S(1)} %get-tuple-element.137), channel_id=1, source_target_pairs={{0,8},{4,12},{8,16},{12,20},{16,24},{20,28},{24,32},{28,36},{32,40... | collective-permute-start | bytes 983048 | tf_op jit(solution)/shard_map/ppermute | solution.py:20
  40.2 3.1 %collective-permute-start.3 = (bf16[128,1280]{0,1:T(8,128)(2,1)S(1)}, bf16[128,1280]{0,1:T(8,128)(2,1)}, u32[]{:S(2)}, u32[]{:S(2)}) collective-permute-start(bf16[128,1280]{0,1:T(8,128)(2,1)S(1)} %get-tuple-element.137), channel_id=1, source_target_pairs={{8,0},{12,4},{16,8},{20,12},{24,16},{28,20},{32,24},{36,28},{40,32... | collective-permute-start | bytes 983048 | tf_op jit(solution)/shard_map/ppermute | solution.py:20
  77.1 6.3 %collective-permute-start.5 = (bf16[128,1280]{0,1:T(8,128)(2,1)S(1)}, bf16[128,1280]{0,1:T(8,128)(2,1)S(1)}, u32[]{:S(2)}, u32[]{:S(2)}) collective-permute-start(bf16[128,1280]{0,1:T(8,128)(2,1)S(1)} %get-tuple-element.137), channel_id=1, source_target_pairs={{12,0},{16,4},{20,8},{24,12},{28,16},{32,20},{36,24},{40,28},{44,3... | collective-permute-start | bytes 983048 | tf_op jit(solution)/shard_map/ppermute | solution.py:20
  85.3 5.3 %collective-permute-start.6 = (bf16[128,1280]{0,1:T(8,128)(2,1)S(1)}, bf16[128,1280]{0,1:T(8,128)(2,1)S(1)}, u32[]{:S(2)}, u32[]{:S(2)}) collective-permute-start(bf16[128,1280]{0,1:T(8,128)(2,1)S(1)} %get-tuple-element.137), channel_id=1, source_target_pairs={{0,16},{4,20},{8,24},{12,28},{16,32},{20,36},{24,40},{28,44},{32,4... | collective-permute-start | bytes 983048 | tf_op jit(solution)/shard_map/ppermute | solution.py:20
  92.3 2.9 %collective-permute-start.7 = (bf16[128,1280]{0,1:T(8,128)(2,1)S(1)}, bf16[128,1280]{0,1:T(8,128)(2,1)S(1)}, u32[]{:S(2)}, u32[]{:S(2)}) collective-permute-start(bf16[128,1280]{0,1:T(8,128)(2,1)S(1)} %get-tuple-element.137), channel_id=1, source_target_pairs={{16,0},{20,4},{24,8},{28,12},{32,16},{36,20},{40,24},{44,28},{48,3... | collective-permute-start | bytes 983048 | tf_op jit(solution)/shard_map/ppermute | solution.py:20
  97.0 4.8 %collective-permute-start.8 = (bf16[128,1280]{0,1:T(8,128)(2,1)S(1)}, bf16[128,1280]{0,1:T(8,128)(2,1)S(1)}, u32[]{:S(2)}, u32[]{:S(2)}) collective-permute-start(bf16[128,1280]{0,1:T(8,128)(2,1)S(1)} %get-tuple-element.137), channel_id=1, source_target_pairs={{0,20},{4,24},{8,28},{12,32},{16,36},{20,40},{24,44},{28,48},{32,5... | collective-permute-start | bytes 983048 | tf_op jit(solution)/shard_map/ppermute | solution.py:20
  107.3 13.6 %collective-permute-done.5 = bf16[128,1280]{0,1:T(8,128)(2,1)S(1)} collective-permute-done((bf16[128,1280]{0,1:T(8,128)(2,1)S(1)}, bf16[128,1280]{0,1:T(8,128)(2,1)S(1)}, u32[]{:S(2)}, u32[]{:S(2)}) %collective-permute-start.5) | collective-permute-done | bytes 327712 | tf_op jit(solution)/shard_map/ppermute | solution.py:20
  120.9 2.9 %collective-permute-start.10 = (bf16[128,1280]{0,1:T(8,128)(2,1)S(1)}, bf16[128,1280]{0,1:T(8,128)(2,1)S(1)}, u32[]{:S(2)}, u32[]{:S(2)}) collective-permute-start(bf16[128,1280]{0,1:T(8,128)(2,1)S(1)} %get-tuple-element.137), channel_id=1, source_target_pairs={{0,24},{4,28},{8,32},{12,36},{16,40},{20,44},{24,48},{28,52},{32,5... | collective-permute-start | bytes 983048 | tf_op jit(solution)/shard_map/ppermute | solution.py:20
  124.6 3.9 %collective-permute-start.11 = (bf16[128,1280]{0,1:T(8,128)(2,1)S(1)}, bf16[128,1280]{0,1:T(8,128)(2,1)S(1)}, u32[]{:S(2)}, u32[]{:S(2)}) collective-permute-start(bf16[128,1280]{0,1:T(8,128)(2,1)S(1)} %get-tuple-element.137), channel_id=1, source_target_pairs={{24,0},{28,4},{32,8},{36,12},{40,16},{44,20},{48,24},{52,28},{56,3... | collective-permute-start | bytes 983048 | tf_op jit(solution)/shard_map/ppermute | solution.py:20
  131.9 3.6 %collective-permute-start.13 = (bf16[128,1280]{1,0:T(8,128)(2,1)S(1)}, bf16[128,1280]{1,0:T(8,128)(2,1)S(1)}, u32[]{:S(2)}, u32[]{:S(2)}) collective-permute-start(bf16[128,1280]{1,0:T(8,128)(2,1)S(1)} %copy-done.4), channel_id=1, source_target_pairs={{4,0},{8,4},{12,8},{16,12},{20,16},{24,20},{28,24},{32,28},{36,32}... | collective-permute-start | bytes 983048 | tf_op jit(solution)/shard_map/ppermute | solution.py:20
  139.1 3.9 %collective-permute-start.15 = (bf16[128,1280]{1,0:T(8,128)(2,1)S(1)}, bf16[128,1280]{1,0:T(8,128)(2,1)S(1)}, u32[]{:S(2)}, u32[]{:S(2)}) collective-permute-start(bf16[128,1280]{1,0:T(8,128)(2,1)S(1)} %copy-done.4), channel_id=1, source_target_pairs={{8,0},{12,4},{16,8},{20,12},{24,16},{28,20},{32,24},{36,28},{40,32... | collective-permute-start | bytes 983048 | tf_op jit(solution)/shard_map/ppermute | solution.py:20
  143.8 3.3 %collective-permute-start.16 = (bf16[128,1280]{1,0:T(8,128)(2,1)S(1)}, bf16[128,1280]{1,0:T(8,128)(2,1)S(1)}, u32[]{:S(2)}, u32[]{:S(2)}) collective-permute-start(bf16[128,1280]{1,0:T(8,128)(2,1)S(1)} %copy-done.4), channel_id=1, source_target_pairs={{0,12},{4,16},{8,20},{12,24},{16,28},{20,32},{24,36},{28,40},{32,4... | collective-permute-start | bytes 983048 | tf_op jit(solution)/shard_map/ppermute | solution.py:20
  147.8 4.7 %collective-permute-start.17 = (bf16[128,1280]{1,0:T(8,128)(2,1)S(1)}, bf16[128,1280]{1,0:T(8,128)(2,1)S(1)}, u32[]{:S(2)}, u32[]{:S(2)}) collective-permute-start(bf16[128,1280]{1,0:T(8,128)(2,1)S(1)} %copy-done.4), channel_id=1, source_target_pairs={{12,0},{16,4},{20,8},{24,12},{28,16},{32,20},{36,24},{40,28},{44,3... | collective-permute-start | bytes 983048 | tf_op jit(solution)/shard_map/ppermute | solution.py:20
  152.6 8.4 %collective-permute-start.18 = (bf16[128,1280]{1,0:T(8,128)(2,1)S(1)}, bf16[128,1280]{1,0:T(8,128)(2,1)S(1)}, u32[]{:S(2)}, u32[]{:S(2)}) collective-permute-start(bf16[128,1280]{1,0:T(8,128)(2,1)S(1)} %copy-done.4), channel_id=1, source_target_pairs={{0,16},{4,20},{8,24},{12,28},{16,32},{20,36},{24,40},{28,44},{32,4... | collective-permute-start | bytes 983048 | tf_op jit(solution)/shard_map/ppermute | solution.py:20
  162.9 5.8 %collective-permute-start.20 = (bf16[128,1280]{1,0:T(8,128)(2,1)S(1)}, bf16[128,1280]{1,0:T(8,128)(2,1)S(1)}, u32[]{:S(2)}, u32[]{:S(2)}) collective-permute-start(bf16[128,1280]{1,0:T(8,128)(2,1)S(1)} %copy-done.4), channel_id=1, source_target_pairs={{0,20},{4,24},{8,28},{12,32},{16,36},{20,40},{24,44},{28,48},{32,5... | collective-permute-start | bytes 983048 | tf_op jit(solution)/shard_map/ppermute | solution.py:20
  168.8 3.8 %collective-permute-done.16 = bf16[128,1280]{1,0:T(8,128)(2,1)S(1)} collective-permute-done((bf16[128,1280]{1,0:T(8,128)(2,1)S(1)}, bf16[128,1280]{1,0:T(8,128)(2,1)S(1)}, u32[]{:S(2)}, u32[]{:S(2)}) %collective-permute-start.16) | collective-permute-done | bytes 327712 | tf_op jit(solution)/shard_map/ppermute | solution.py:20
  174.5 26.1 %collective-permute-done.17 = bf16[128,1280]{1,0:T(8,128)(2,1)S(1)} collective-permute-done((bf16[128,1280]{1,0:T(8,128)(2,1)S(1)}, bf16[128,1280]{1,0:T(8,128)(2,1)S(1)}, u32[]{:S(2)}, u32[]{:S(2)}) %collective-permute-start.17) | collective-permute-done | bytes 327712 | tf_op jit(solution)/shard_map/ppermute | solution.py:20
  202.6 4.8 %collective-permute-start.23 = (bf16[128,1280]{1,0:T(8,128)(2,1)S(1)}, bf16[128,1280]{1,0:T(8,128)(2,1)S(1)}, u32[]{:S(2)}, u32[]{:S(2)}) collective-permute-start(bf16[128,1280]{1,0:T(8,128)(2,1)S(1)} %copy-done.4), channel_id=1, source_target_pairs={{24,0},{28,4},{32,8},{36,12},{40,16},{44,20},{48,24},{52,28},{56,3... | collective-permute-start | bytes 983048 | tf_op jit(solution)/shard_map/ppermute | solution.py:20
  207.6 2.9 %collective-permute-done.22 = bf16[128,1280]{1,0:T(8,128)(2,1)S(1)} collective-permute-done((bf16[128,1280]{1,0:T(8,128)(2,1)S(1)}, bf16[128,1280]{1,0:T(8,128)(2,1)S(1)}, u32[]{:S(2)}, u32[]{:S(2)}) %collective-permute-start.22) | collective-permute-done | bytes 327712 | tf_op jit(solution)/shard_map/ppermute | solution.py:20
  210.5 4.1 %collective-permute-done.23 = bf16[128,1280]{1,0:T(8,128)(2,1)S(1)} collective-permute-done((bf16[128,1280]{1,0:T(8,128)(2,1)S(1)}, bf16[128,1280]{1,0:T(8,128)(2,1)S(1)}, u32[]{:S(2)}, u32[]{:S(2)}) %collective-permute-start.23) | collective-permute-done | bytes 327712 | tf_op jit(solution)/shard_map/ppermute | solution.py:20
  214.6 2.0 copy-done.2
  216.6 67.1 %while.11 = (s32[]{:T(128)}, bf16[10,128,128]{1,2,0:T(8,128)(2,1)S(1)}, pred[1664]{0:T(1024)(128)(4,1)S(1)}, s32[10]{0:T(128)S(1)}, bf16[128,1280]{0,1:T(8,128)(...) while((s32[]{:T(128)}, ...), condition=%wide.region_14.15_spmd.clone, body=%wide.region_9.14_spmd.clone.sunk | while | flops 127614720 | bytes 4302815 | solution.py:149
  (243 shorter events, 114.3 us)
Async XLA Ops:
  31.3 45.9 %collective-permute-start = (bf16[128,1280]{0,1:T(8,128)(2,1)S(1)}, bf16[128,1280]{0,1:T(8,128)(2,1)}, u32[]{:S(2)}, u32[]{:S(2)}) collective-permute-start(bf16[128,1280]{0,1:T(8,128)(2,1)S(1)} %get-tuple-element.137), channel_id=1, source_target_pairs={{0,4},{4,8},{8,12},{12,16},{16,20},{20,24},{24,28},{28,32},{32,36}... | collective-permute-start | bytes 983048 | tf_op jit(solution)/shard_map/ppermute | solution.py:20
  33.2 52.1 %collective-permute-start.1 = (bf16[128,1280]{0,1:T(8,128)(2,1)S(1)}, bf16[128,1280]{0,1:T(8,128)(2,1)}, u32[]{:S(2)}, u32[]{:S(2)}) collective-permute-start(bf16[128,1280]{0,1:T(8,128)(2,1)S(1)} %get-tuple-element.137), channel_id=1, source_target_pairs={{4,0},{8,4},{12,8},{16,12},{20,16},{24,20},{28,24},{32,28},{36,32}... | collective-permute-start | bytes 983048 | tf_op jit(solution)/shard_map/ppermute | solution.py:20
  36.8 55.5 %collective-permute-start.2 = (bf16[128,1280]{0,1:T(8,128)(2,1)S(1)}, bf16[128,1280]{0,1:T(8,128)(2,1)}, u32[]{:S(2)}, u32[]{:S(2)}) collective-permute-start(bf16[128,1280]{0,1:T(8,128)(2,1)S(1)} %get-tuple-element.137), channel_id=1, source_target_pairs={{0,8},{4,12},{8,16},{12,20},{16,24},{20,28},{24,32},{28,36},{32,40... | collective-permute-start | bytes 983048 | tf_op jit(solution)/shard_map/ppermute | solution.py:20
  40.2 56.8 %collective-permute-start.3 = (bf16[128,1280]{0,1:T(8,128)(2,1)S(1)}, bf16[128,1280]{0,1:T(8,128)(2,1)}, u32[]{:S(2)}, u32[]{:S(2)}) collective-permute-start(bf16[128,1280]{0,1:T(8,128)(2,1)S(1)} %get-tuple-element.137), channel_id=1, source_target_pairs={{8,0},{12,4},{16,8},{20,12},{24,16},{28,20},{32,24},{36,28},{40,32... | collective-permute-start | bytes 983048 | tf_op jit(solution)/shard_map/ppermute | solution.py:20
  43.3 60.3 %collective-permute-start.4 = (bf16[128,1280]{0,1:T(8,128)(2,1)S(1)}, bf16[128,1280]{0,1:T(8,128)(2,1)}, u32[]{:S(2)}, u32[]{:S(2)}) collective-permute-start(bf16[128,1280]{0,1:T(8,128)(2,1)S(1)} %get-tuple-element.137), channel_id=1, source_target_pairs={{0,12},{4,16},{8,20},{12,24},{16,28},{20,32},{24,36},{28,40},{32,4... | collective-permute-start | bytes 983048 | tf_op jit(solution)/shard_map/ppermute | solution.py:20
  77.1 43.8 %collective-permute-start.5 = (bf16[128,1280]{0,1:T(8,128)(2,1)S(1)}, bf16[128,1280]{0,1:T(8,128)(2,1)S(1)}, u32[]{:S(2)}, u32[]{:S(2)}) collective-permute-start(bf16[128,1280]{0,1:T(8,128)(2,1)S(1)} %get-tuple-element.137), channel_id=1, source_target_pairs={{12,0},{16,4},{20,8},{24,12},{28,16},{32,20},{36,24},{40,28},{44,3... | collective-permute-start | bytes 983048 | tf_op jit(solution)/shard_map/ppermute | solution.py:20
  85.3 39.3 %collective-permute-start.6 = (bf16[128,1280]{0,1:T(8,128)(2,1)S(1)}, bf16[128,1280]{0,1:T(8,128)(2,1)S(1)}, u32[]{:S(2)}, u32[]{:S(2)}) collective-permute-start(bf16[128,1280]{0,1:T(8,128)(2,1)S(1)} %get-tuple-element.137), channel_id=1, source_target_pairs={{0,16},{4,20},{8,24},{12,28},{16,32},{20,36},{24,40},{28,44},{32,4... | collective-permute-start | bytes 983048 | tf_op jit(solution)/shard_map/ppermute | solution.py:20
  92.3 36.9 %collective-permute-start.7 = (bf16[128,1280]{0,1:T(8,128)(2,1)S(1)}, bf16[128,1280]{0,1:T(8,128)(2,1)S(1)}, u32[]{:S(2)}, u32[]{:S(2)}) collective-permute-start(bf16[128,1280]{0,1:T(8,128)(2,1)S(1)} %get-tuple-element.137), channel_id=1, source_target_pairs={{16,0},{20,4},{24,8},{28,12},{32,16},{36,20},{40,24},{44,28},{48,3... | collective-permute-start | bytes 983048 | tf_op jit(solution)/shard_map/ppermute | solution.py:20
  97.0 34.9 %collective-permute-start.8 = (bf16[128,1280]{0,1:T(8,128)(2,1)S(1)}, bf16[128,1280]{0,1:T(8,128)(2,1)S(1)}, u32[]{:S(2)}, u32[]{:S(2)}) collective-permute-start(bf16[128,1280]{0,1:T(8,128)(2,1)S(1)} %get-tuple-element.137), channel_id=1, source_target_pairs={{0,20},{4,24},{8,28},{12,32},{16,36},{20,40},{24,44},{28,48},{32,5... | collective-permute-start | bytes 983048 | tf_op jit(solution)/shard_map/ppermute | solution.py:20
  103.6 32.7 %collective-permute-start.9 = (bf16[128,1280]{0,1:T(8,128)(2,1)S(1)}, bf16[128,1280]{0,1:T(8,128)(2,1)S(1)}, u32[]{:S(2)}, u32[]{:S(2)}) collective-permute-start(bf16[128,1280]{0,1:T(8,128)(2,1)S(1)} %get-tuple-element.137), channel_id=1, source_target_pairs={{20,0},{24,4},{28,8},{32,12},{36,16},{40,20},{44,24},{48,28},{52,3... | collective-permute-start | bytes 983048 | tf_op jit(solution)/shard_map/ppermute | solution.py:20
  120.9 18.2 %collective-permute-start.10 = (bf16[128,1280]{0,1:T(8,128)(2,1)S(1)}, bf16[128,1280]{0,1:T(8,128)(2,1)S(1)}, u32[]{:S(2)}, u32[]{:S(2)}) collective-permute-start(bf16[128,1280]{0,1:T(8,128)(2,1)S(1)} %get-tuple-element.137), channel_id=1, source_target_pairs={{0,24},{4,28},{8,32},{12,36},{16,40},{20,44},{24,48},{28,52},{32,5... | collective-permute-start | bytes 983048 | tf_op jit(solution)/shard_map/ppermute | solution.py:20
  124.6 19.2 %collective-permute-start.11 = (bf16[128,1280]{0,1:T(8,128)(2,1)S(1)}, bf16[128,1280]{0,1:T(8,128)(2,1)S(1)}, u32[]{:S(2)}, u32[]{:S(2)}) collective-permute-start(bf16[128,1280]{0,1:T(8,128)(2,1)S(1)} %get-tuple-element.137), channel_id=1, source_target_pairs={{24,0},{28,4},{32,8},{36,12},{40,16},{44,20},{48,24},{52,28},{56,3... | collective-permute-start | bytes 983048 | tf_op jit(solution)/shard_map/ppermute | solution.py:20
  129.2 18.7 %collective-permute-start.12 = (bf16[128,1280]{1,0:T(8,128)(2,1)S(1)}, bf16[128,1280]{1,0:T(8,128)(2,1)S(1)}, u32[]{:S(2)}, u32[]{:S(2)}) collective-permute-start(bf16[128,1280]{1,0:T(8,128)(2,1)S(1)} %copy-done.4), channel_id=1, source_target_pairs={{0,4},{4,8},{8,12},{12,16},{16,20},{20,24},{24,28},{28,32},{32,36}... | collective-permute-start | bytes 983048 | tf_op jit(solution)/shard_map/ppermute | solution.py:20
  131.9 20.6 %collective-permute-start.13 = (bf16[128,1280]{1,0:T(8,128)(2,1)S(1)}, bf16[128,1280]{1,0:T(8,128)(2,1)S(1)}, u32[]{:S(2)}, u32[]{:S(2)}) collective-permute-start(bf16[128,1280]{1,0:T(8,128)(2,1)S(1)} %copy-done.4), channel_id=1, source_target_pairs={{4,0},{8,4},{12,8},{16,12},{20,16},{24,20},{28,24},{32,28},{36,32}... | collective-permute-start | bytes 983048 | tf_op jit(solution)/shard_map/ppermute | solution.py:20
  136.3 24.6 %collective-permute-start.14 = (bf16[128,1280]{1,0:T(8,128)(2,1)S(1)}, bf16[128,1280]{1,0:T(8,128)(2,1)S(1)}, u32[]{:S(2)}, u32[]{:S(2)}) collective-permute-start(bf16[128,1280]{1,0:T(8,128)(2,1)S(1)} %copy-done.4), channel_id=1, source_target_pairs={{0,8},{4,12},{8,16},{12,20},{16,24},{20,28},{24,32},{28,36},{32,40... | collective-permute-start | bytes 983048 | tf_op jit(solution)/shard_map/ppermute | solution.py:20
  139.1 23.8 %collective-permute-start.15 = (bf16[128,1280]{1,0:T(8,128)(2,1)S(1)}, bf16[128,1280]{1,0:T(8,128)(2,1)S(1)}, u32[]{:S(2)}, u32[]{:S(2)}) collective-permute-start(bf16[128,1280]{1,0:T(8,128)(2,1)S(1)} %copy-done.4), channel_id=1, source_target_pairs={{8,0},{12,4},{16,8},{20,12},{24,16},{28,20},{32,24},{36,28},{40,32... | collective-permute-start | bytes 983048 | tf_op jit(solution)/shard_map/ppermute | solution.py:20
  143.8 28.8 %collective-permute-start.16 = (bf16[128,1280]{1,0:T(8,128)(2,1)S(1)}, bf16[128,1280]{1,0:T(8,128)(2,1)S(1)}, u32[]{:S(2)}, u32[]{:S(2)}) collective-permute-start(bf16[128,1280]{1,0:T(8,128)(2,1)S(1)} %copy-done.4), channel_id=1, source_target_pairs={{0,12},{4,16},{8,20},{12,24},{16,28},{20,32},{24,36},{28,40},{32,4... | collective-permute-start | bytes 983048 | tf_op jit(solution)/shard_map/ppermute | solution.py:20
  147.8 52.8 %collective-permute-start.17 = (bf16[128,1280]{1,0:T(8,128)(2,1)S(1)}, bf16[128,1280]{1,0:T(8,128)(2,1)S(1)}, u32[]{:S(2)}, u32[]{:S(2)}) collective-permute-start(bf16[128,1280]{1,0:T(8,128)(2,1)S(1)} %copy-done.4), channel_id=1, source_target_pairs={{12,0},{16,4},{20,8},{24,12},{28,16},{32,20},{36,24},{40,28},{44,3... | collective-permute-start | bytes 983048 | tf_op jit(solution)/shard_map/ppermute | solution.py:20
  152.6 50.0 %collective-permute-start.18 = (bf16[128,1280]{1,0:T(8,128)(2,1)S(1)}, bf16[128,1280]{1,0:T(8,128)(2,1)S(1)}, u32[]{:S(2)}, u32[]{:S(2)}) collective-permute-start(bf16[128,1280]{1,0:T(8,128)(2,1)S(1)} %copy-done.4), channel_id=1, source_target_pairs={{0,16},{4,20},{8,24},{12,28},{16,32},{20,36},{24,40},{28,44},{32,4... | collective-permute-start | bytes 983048 | tf_op jit(solution)/shard_map/ppermute | solution.py:20
  161.0 46.5 %collective-permute-start.19 = (bf16[128,1280]{1,0:T(8,128)(2,1)S(1)}, bf16[128,1280]{1,0:T(8,128)(2,1)S(1)}, u32[]{:S(2)}, u32[]{:S(2)}) collective-permute-start(bf16[128,1280]{1,0:T(8,128)(2,1)S(1)} %copy-done.4), channel_id=1, source_target_pairs={{16,0},{20,4},{24,8},{28,12},{32,16},{36,20},{40,24},{44,28},{48,3... | collective-permute-start | bytes 983048 | tf_op jit(solution)/shard_map/ppermute | solution.py:20
  162.9 44.6 %collective-permute-start.20 = (bf16[128,1280]{1,0:T(8,128)(2,1)S(1)}, bf16[128,1280]{1,0:T(8,128)(2,1)S(1)}, u32[]{:S(2)}, u32[]{:S(2)}) collective-permute-start(bf16[128,1280]{1,0:T(8,128)(2,1)S(1)} %copy-done.4), channel_id=1, source_target_pairs={{0,20},{4,24},{8,28},{12,32},{16,36},{20,40},{24,44},{28,48},{32,5... | collective-permute-start | bytes 983048 | tf_op jit(solution)/shard_map/ppermute | solution.py:20
  172.5 35.0 %collective-permute-start.21 = (bf16[128,1280]{1,0:T(8,128)(2,1)S(1)}, bf16[128,1280]{1,0:T(8,128)(2,1)S(1)}, u32[]{:S(2)}, u32[]{:S(2)}) collective-permute-start(bf16[128,1280]{1,0:T(8,128)(2,1)S(1)} %copy-done.4), channel_id=1, source_target_pairs={{20,0},{24,4},{28,8},{32,12},{36,16},{40,20},{44,24},{48,28},{52,3... | collective-permute-start | bytes 983048 | tf_op jit(solution)/shard_map/ppermute | solution.py:20
  200.6 9.9 %collective-permute-start.22 = (bf16[128,1280]{1,0:T(8,128)(2,1)S(1)}, bf16[128,1280]{1,0:T(8,128)(2,1)S(1)}, u32[]{:S(2)}, u32[]{:S(2)}) collective-permute-start(bf16[128,1280]{1,0:T(8,128)(2,1)S(1)} %copy-done.4), channel_id=1, source_target_pairs={{0,24},{4,28},{8,32},{12,36},{16,40},{20,44},{24,48},{28,52},{32,5... | collective-permute-start | bytes 983048 | tf_op jit(solution)/shard_map/ppermute | solution.py:20
  202.6 12.0 %collective-permute-start.23 = (bf16[128,1280]{1,0:T(8,128)(2,1)S(1)}, bf16[128,1280]{1,0:T(8,128)(2,1)S(1)}, u32[]{:S(2)}, u32[]{:S(2)}) collective-permute-start(bf16[128,1280]{1,0:T(8,128)(2,1)S(1)} %copy-done.4), channel_id=1, source_target_pairs={{24,0},{28,4},{32,8},{36,12},{40,16},{44,20},{48,24},{52,28},{56,3... | collective-permute-start | bytes 983048 | tf_op jit(solution)/shard_map/ppermute | solution.py:20
  (12 other events, 414.3 us)
where the time goes:
time: 288 us; the launch traced here: 285 us
  starting transfers between devices  85.9 us (30%)
  waiting for transfers between devices  50.5 us (18%)
  matrix products  40.8 us (14%)
  local copies, waits for them, and re-layouts  33.8 us (12%)
  other arithmetic  26.3 us (9%)
  blocking collectives  20.4 us (7%)
  between operations  19.9 us (7%)
  loops' own time  7 us (2%)
    ppermute x24, starting transfers between devices, shifted(): return lax.ppermute(value, axis, pairs)  85.9 us
    ppermute x24, waiting for transfers between devices, shifted(): return lax.ppermute(value, axis, pairs)  50.5 us
    dot_general x20, matrix products, attend_head(): jnp.dot(weights.astype(jnp.bfloat16), value_rows, preferred_element_type=...  24.1 us
    unnamed x62, local copies, waits for them, and re-layouts  22.3 us
    psum x1, blocking collectives, per_device(): lax.psum((jnp.sum(query_float * query_float, axis=1), jnp.sum(key_float *...  20.4 us
    dot_general x20, matrix products, attend_head(): lax.dot_general(query, key_rows, (((1,), (1,)), ((), ())), preferred_elem...  16.7 us
    and x13, other arithmetic, live_rows(): same_item & (jnp.arange(row_total, dtype=jnp.int32) < row_count[clipped])  8.12 us
    another operation x1, loops' own time, per_device(): head_outputs = lax.map(per_head, jnp.arange(head_total, dtype=jnp.int32))  7 us
  transfers between devices with their start and end apart: 24, of which 5 were waited for; matrix products, arithmetic and copies ran while one was open for 10% of the time, Pallas kernels for 0%

commit v1 on v0

v1 whole, which is shorter than its diff:
```python
import math

import jax
import jax.numpy as jnp
import numpy as np
from jax import lax
from jax.experimental import pallas as pl
from jax.experimental.pallas import tpu as pltpu
from jax.sharding import PartitionSpec as P

D = 5120
HD = 128
HGT = 30
WID = 52
SPAN = 7
ROWS = 128
EPSILON = 1e-06
SCALE = 1.0 / math.sqrt(HD)
NEG = -1e30


def rope_tables():
    spatial = HD // 6
    temporal = HD // 2 - 2 * spatial
    positions = np.arange(SPAN * ROWS)

    def freq(amount):
        exponent = np.arange(amount, dtype=np.float64) * 2.0 / (2 * amount)
        return (1.0 / 10000.0**exponent).astype(np.float32)

    def part(values, amount):
        return values.astype(np.float32)[:, None] * freq(amount)[None, :]

    angle = np.concatenate(
        [
            part(positions // (HGT * WID), temporal),
            part(positions // WID % HGT, spatial),
            part(positions % WID, spatial),
        ],
        axis=1,
    ).astype(np.float64)
    cosine = np.repeat(np.cos(angle), 2, axis=1).astype(np.float32)
    sine = np.stack([-np.sin(angle), np.sin(angle)], axis=2)
    return cosine, sine.reshape(SPAN * ROWS, HD).astype(np.float32)


def shifted(value, by):
    peers = lax.axis_size("tile")
    return lax.ppermute(
        value, "tile", [(i, i + by) for i in range(peers) if 0 <= i + by < peers]
    )


def swapped(value):
    peers = lax.axis_size("tile")
    return lax.ppermute(value, "tile", [(i, i ^ 1) for i in range(peers)])


def by_rows(total_row):
    factor = lax.rsqrt(total_row / D + EPSILON)
    return jnp.transpose(jnp.broadcast_to(factor, (ROWS, ROWS)))


def rotated(normal, cosine, sine, even):
    partner = jnp.where(even, pltpu.roll(normal, HD - 1, 1), pltpu.roll(normal, 1, 1))
    return normal * cosine + partner * sine


def prefix_live(shape, count):
    return lax.broadcasted_iota(jnp.int32, shape, 1) < count


def sums_kernel(q_ref, k_ref, c_ref, t_ref, out_ref):

    def total(ref, first):
        rows = None
        for head in range(ref.shape[1] // HD):
            x = ref[first : first + ROWS, head * HD : (head + 1) * HD].astype(jnp.float32)
            rows = x * x if rows is None else rows + x * x
        return jnp.sum(jnp.transpose(rows), axis=0, keepdims=True)

    out_ref[0:1, :] = total(q_ref, 0)
    out_ref[1:2, :] = total(k_ref, 0)
    out_ref[2:3, :] = total(c_ref, 0)
    out_ref[3:4, :] = total(t_ref, 0)
    out_ref[4:5, :] = total(t_ref, ROWS)
    out_ref[5:8, :] = jnp.zeros((3, ROWS), jnp.float32)


def cross_kernel(item_ref, len_ref, here_ref, sums_ref, q_ref, k_ref, v_ref, qg_ref, kg_ref, out_ref):
    count = len_ref[item_ref[here_ref[0]]]
    q_factor = by_rows(sums_ref[2:3, :])
    k_factor = [by_rows(sums_ref[3:4, :]), by_rows(sums_ref[4:5, :])]
    live = prefix_live((ROWS, 2 * ROWS), count)
    for head in range(q_ref.shape[1] // HD):
        cols = slice(head * HD, (head + 1) * HD)
        q = (q_ref[:, cols].astype(jnp.float32) * q_factor * qg_ref[:, cols]).astype(jnp.bfloat16)
        keys = [
            (
                k_ref[h * ROWS : (h + 1) * ROWS, cols].astype(jnp.float32)
                * k_factor[h]
                * kg_ref[:, cols]
            ).astype(jnp.bfloat16)
            for h in range(2)
        ]
        k = jnp.concatenate(keys, axis=0)
        s = lax.dot_general(q, k, (((1,), (1,)), ((), ())), preferred_element_type=jnp.float32)
        s = jnp.where(live, s * SCALE, NEG)
        w = jnp.exp(s - jnp.max(s, axis=1, keepdims=True))
        total = jnp.sum(w, axis=1, keepdims=True)
        o = jnp.dot(w.astype(jnp.bfloat16), v_ref[:, cols], preferred_element_type=jnp.float32)
        out_ref[:, cols] = o / total


def self_kernel(
    item_ref,
    count_ref,
    here_ref,
    sums_ref,
    q0_ref,
    q1_ref,
    b0,
    b1,
    b2,
    b3,
    b4,
    b5,
    b6,
    qg_ref,
    kg_ref,
    cos_ref,
    sin_ref,
    out0_ref,
    out1_ref,
    keys,
    values,
    queries,
    scores,
):
    blocks = (b0, b1, b2, b3, b4, b5, b6)
    heads = q0_ref.shape[1] // HD
    here = here_ref[0]
    core = lax.rem(here, 2)
    left = here - core
    base = left - 6
    tiles = item_ref.shape[0]
    even = lax.rem(lax.broadcasted_iota(jnp.int32, (ROWS, HD), 1), 2) == 0

    def extent(tile):
        item = item_ref[tile]
        before = jnp.int32(0)
        after = jnp.int32(0)
        for d in range(1, SPAN):
            lower = item_ref[jnp.maximum(tile - d, 0)] == item
            upper = item_ref[jnp.minimum(tile + d, tiles - 1)] == item
            before += jnp.where(jnp.logical_and(lower, tile - d >= 0), 1, 0)
            after += jnp.where(jnp.logical_and(upper, tile + d < tiles), 1, 0)
        return tile - before, tile + after

    first_a, last_a = extent(left)
    first_b, last_b = extent(left + 1)

    def turn(ref, rows, factor, gain_ref, start, dest, slot):
        cosine = cos_ref[pl.ds(start, ROWS), :]
        sine = sin_ref[pl.ds(start, ROWS), :]
        for head in range(heads):
            cols = slice(head * HD, (head + 1) * HD)
            x = ref[rows, cols].astype(jnp.float32) * factor * gain_ref[:, cols]
            dest[slot, :, cols] = rotated(x, cosine, sine, even).astype(jnp.bfloat16)

    for w in range(14):
        tile = base + w
        parity = w % 2

        @pl.when(jnp.logical_and(tile >= first_a, tile <= last_b))
        def _(w=w, tile=tile, parity=parity):
            first = jnp.where(tile <= last_a, first_a, first_b)
            start = pl.multiple_of((tile - first) * ROWS, ROWS)
            slot = jnp.where(core == parity, 0, 1)
            row = pl.multiple_of(slot * 2 * ROWS, 2 * ROWS)
            block = blocks[w // 2]
            factor = by_rows(sums_ref[pl.ds(2 * (w // 2) + slot, 1), :])
            turn(block, pl.ds(row, ROWS), factor, kg_ref, start, keys, w)
            values[w] = block[pl.ds(row + ROWS, ROWS), :]

    for which, (q_ref, out_ref) in enumerate(((q0_ref, out0_ref), (q1_ref, out1_ref))):
        is_a = core == which
        tile = jnp.where(is_a, left, left + 1)
        first = jnp.where(is_a, first_a, first_b)
        last = jnp.where(is_a, last_a, last_b)
        factor = by_rows(sums_ref[14 + which : 15 + which, :])
        start = pl.multiple_of((tile - first) * ROWS, ROWS)
        turn(q_ref, slice(None), factor, qg_ref, start, queries, 0)
        low, high = first - base, last - base + 1

        def score(w, tops):
            live = prefix_live((ROWS, ROWS), count_ref[base + w])
            found = []
            for head in range(heads):
                cols = slice(head * HD, (head + 1) * HD)
                s = lax.dot_general(
                    queries[0, :, cols],
                    keys[w, :, cols],
                    (((1,), (1,)), ((), ())),
                    preferred_element_type=jnp.float32,
                )
                s = jnp.where(live, s * SCALE, NEG)
                scores[w - low, :, cols] = s
                found.append(jnp.maximum(tops[head], s))
            return tuple(found)

        empty = jnp.full((ROWS, ROWS), NEG, jnp.float32)
        tops = lax.fori_loop(low, high, score, (empty,) * heads)
        tops = [jnp.max(t, axis=1, keepdims=True) for t in tops]

        def mix(w, carry):
            mixed, totals = [], []
            for head in range(heads):
                cols = slice(head * HD, (head + 1) * HD)
                weight = jnp.exp(scores[w - low, :, cols] - tops[head])
                totals.append(carry[1][head] + weight)
                mixed.append(
                    carry[0][head]
                    + jnp.dot(
                        weight.astype(jnp.bfloat16),
                        values[w, :, cols],
                        preferred_element_type=jnp.float32,
                    )
                )
            return tuple(mixed), tuple(totals)

        zero = jnp.zeros((ROWS, ROWS), jnp.float32)
        mixed, totals = lax.fori_loop(low, high, mix, ((zero,) * heads, (zero,) * heads))
        for head in range(heads):
            cols = slice(head * HD, (head + 1) * HD)
            out_ref[:, cols] = mixed[head] / jnp.sum(totals[head], axis=1, keepdims=True)


def join_kernel(here_ref, own_ref, other_ref, text_ref, out_ref):
    core = lax.rem(here_ref[0], 2)
    width = own_ref.shape[1]
    mine = pl.multiple_of(core * width, HD)
    theirs = pl.multiple_of((1 - core) * width, HD)
    out_ref[:, pl.ds(mine, width)] = (own_ref[...] + text_ref[:, pl.ds(mine, width)]).astype(
        jnp.bfloat16
    )
    out_ref[:, pl.ds(theirs, width)] = (other_ref[...] + text_ref[:, pl.ds(theirs, width)]).astype(
        jnp.bfloat16
    )


def call(kernel, out_shape, specs, scratch=(), flops=1000000, limit=40):
    return pl.pallas_call(
        kernel,
        out_shape=out_shape,
        in_specs=specs,
        out_specs=jax.tree.map(lambda _: pl.BlockSpec(memory_space=pltpu.VMEM), out_shape),
        scratch_shapes=list(scratch),
        compiler_params=pltpu.CompilerParams(vmem_limit_bytes=limit << 20),
        cost_estimate=pl.CostEstimate(flops=flops, bytes_accessed=4000000, transcendentals=0),
    )


def per_device(
    self_query,
    self_key,
    self_value,
    cross_query,
    text_key,
    text_value,
    query_gain,
    key_gain,
    cross_gain,
    text_gain,
    tile_item,
    row_count,
    text_len,
):
    smem = pl.BlockSpec(memory_space=pltpu.SMEM)
    vmem = pl.BlockSpec(memory_space=pltpu.VMEM)
    f32 = jnp.float32
    width = self_query.shape[1]
    half = width // 2
    here = lax.axis_index("tile").astype(jnp.int32)
    core = lax.rem(here, 2)
    where = here.reshape(1)

    stacked = jnp.concatenate([self_key, self_value, self_query], axis=0)
    mine = lax.dynamic_slice_in_dim(stacked, core * half, half, 1)
    theirs = lax.dynamic_slice_in_dim(stacked, (1 - core) * half, half, 1)
    got = swapped(theirs)
    block = jnp.concatenate([mine[: 2 * ROWS], got[: 2 * ROWS]], axis=0)
    from_left = shifted(block, 2)
    from_right = shifted(block, -2)
    from_left3 = shifted(block, 6)
    from_right3 = shifted(block, -6)

    sums = call(
        sums_kernel, jax.ShapeDtypeStruct((8, ROWS), f32), [vmem] * 4
    )(self_query, self_key, cross_query, text_key)
    sums = lax.psum(sums, "head")

    from_left2 = shifted(from_left, 2)
    from_right2 = shifted(from_right, -2)

    both = jnp.stack([sums[:2], swapped(sums[:2])])
    k_sums = both[:, 1]
    left_sums = shifted(k_sums, 2)
    right_sums = shifted(k_sums, -2)
    left_far = shifted(jnp.concatenate([left_sums, k_sums]), 4)
    right_far = shifted(jnp.concatenate([k_sums, right_sums]), -4)
    all_sums = jnp.concatenate([left_far, left_sums, k_sums, right_sums, right_far, both[:, 0]])

    text_out = call(
        cross_kernel, jax.ShapeDtypeStruct((ROWS, width), f32), [smem] * 3 + [vmem] * 6, flops=400000000
    )(
        tile_item,
        text_len,
        where,
        sums,
        cross_query,
        text_key,
        text_value,
        cross_gain[None, :],
        text_gain[None, :],
    )

    cosine, sine = rope_tables()
    my_gain = lax.dynamic_slice_in_dim(jnp.stack([query_gain, key_gain]), core * half, half, 1)
    own, other = call(
        self_kernel,
        (jax.ShapeDtypeStruct((ROWS, half), f32),) * 2,
        [smem] * 3 + [vmem] * 14,
        scratch=[
            pltpu.VMEM((14, ROWS, half), jnp.bfloat16),
            pltpu.VMEM((14, ROWS, half), jnp.bfloat16),
            pltpu.VMEM((1, ROWS, half), jnp.bfloat16),
            pltpu.VMEM((SPAN, ROWS, half), f32),
        ],
        flops=600000000,
    )(
        tile_item,
        row_count,
        where,
        all_sums,
        mine[2 * ROWS :],
        got[2 * ROWS :],
        from_left3,
        from_left2,
        from_left,
        block,
        from_right,
        from_right2,
        from_right3,
        my_gain[0:1],
        my_gain[1:2],
        jnp.asarray(cosine),
        jnp.asarray(sine),
    )
    rest = swapped(other)
    return call(
        join_kernel, jax.ShapeDtypeStruct((ROWS, width), jnp.bfloat16), [smem] + [vmem] * 3
    )(where, own, rest, text_out)


def solution(mesh):
    spread = P("tile", "head")
    in_specs = (spread,) * 6 + (P("head"),) * 4 + (P(),) * 3
    return jax.shard_map(
        per_device, mesh=mesh, in_specs=in_specs, out_specs=spread, check_vma=False
    )
```

time: 288 us -> 119 us (0.41)
  the two profiles are of different devices: /device:TPU:58 before, /device:TPU:33 now
where the time goes in v1:
time: 119 us; the launch traced here: 118 us
  starting transfers between devices  51.7 us (43%)
  waiting for transfers between devices  27.2 us (23%)
  blocking collectives  21.3 us (18%)
  Pallas kernels  10.5 us (9%)
  local copies, waits for them, and re-layouts  6.96 us (6%)
    ppermute x10, starting transfers between devices, shifted(): lax.ppermute(value, 'tile', [(i, i + by) for i in range(peers) if 0 <= i...  35.1 us
    ppermute x10, waiting for transfers between devices, shifted(): lax.ppermute(value, 'tile', [(i, i + by) for i in range(peers) if 0 <= i...  25 us
    psum x1, blocking collectives, per_device(): sums = lax.psum(sums, 'head')  21.3 us
    ppermute x3, starting transfers between devices, swapped(): return lax.ppermute(value, 'tile', [(i, i ^ 1) for i in range(peers)])  16.6 us
    pallas_call x1, Pallas kernels, per_device(): call(self_kernel, (jax.ShapeDtypeStruct((ROWS, half), f32),) * 2, [smem]...  7.7 us
    unnamed x34, local copies, waits for them, and re-layouts  4.88 us
  transfers between devices with their start and end apart: 13, of which 6 were waited for; matrix products, arithmetic and copies ran while one was open for 2% of the time, Pallas kernels for 2%

profile of v1, /device:TPU:33, one launch (start us, length us, event | category | flops | bytes accessed | tf_op | source)
XLA Modules:
  0.0 118.2 jit_solution(9281391021603463059)
XLA Ops:
  0.0 1.0 constant_dynamic-update-slice_fusion.2
  2.2 2.6 %collective-permute-start.5 = (bf16[384,640]{1,0:T(8,128)(2,1)S(1)}, bf16[384,640]{1,0:T(8,128)(2,1)S(1)}, u32[]{:S(2)}, u32[]{:S(2)}) collective-permute-start(bf16[384,640]{1,0:T(8,128)(2,1)S(1)} %constant_dynamic-slice_fusion), channel_id=1, source_target_pairs={{0,4},{4,0},{8,12},{12,8},{16,20},{20,16},{24,28},{28,24},{32,36},... | collective-permute-start | bytes 1474568 | tf_op jit(solution)/shard_map/ppermute | solution.py:56
  4.9 1.4 %collective-permute-done.5 = bf16[384,640]{1,0:T(8,128)(2,1)S(1)} collective-permute-done((bf16[384,640]{1,0:T(8,128)(2,1)S(1)}, bf16[384,640]{1,0:T(8,128)(2,1)S(1)}, u32[]{:S(2)}, u32[]{:S(2)}) %collective-permute-start.5) | collective-permute-done | bytes 491552 | tf_op jit(solution)/shard_map/ppermute | solution.py:56
  7.1 3.3 %collective-permute-start.7 = (bf16[512,640]{1,0:T(8,128)(2,1)S(1)}, bf16[512,640]{1,0:T(8,128)(2,1)S(1)}, u32[]{:S(2)}, u32[]{:S(2)}) collective-permute-start(bf16[512,640]{1,0:T(8,128)(2,1)S(1)} %pad_maximum_fusion.b3), channel_id=1, source_target_pairs={{0,8},{4,12},{8,16},{12,20},{16,24},{20,28},{24,32},{28,36},{32,40... | collective-permute-start | bytes 1966088 | tf_op jit(solution)/shard_map/ppermute | solution.py:49
  10.4 6.4 %collective-permute-start.9 = (bf16[512,640]{1,0:T(8,128)(2,1)S(1)}, bf16[512,640]{1,0:T(8,128)(2,1)S(1)}, u32[]{:S(2)}, u32[]{:S(2)}) collective-permute-start(bf16[512,640]{1,0:T(8,128)(2,1)S(1)} %pad_maximum_fusion.b3), channel_id=1, source_target_pairs={{8,0},{12,4},{16,8},{20,12},{24,16},{28,20},{32,24},{36,28},{40,32... | collective-permute-start | bytes 1966088 | tf_op jit(solution)/shard_map/ppermute | solution.py:49
  17.2 21.3 %psum.7.sums_ref = f32[8,128]{1,0:T(8,128)S(1)} all-reduce(f32[8,128]{1,0:T(8,128)S(1)} %shard_map.145), channel_id=1, replica_groups=mesh['tile'=128,'head'=4] {'head'}, use_global_device_ids=true, to_apply=%region_0.0 | all-reduce | flops 1024 | bytes 8192 | tf_op jit(solution)/shard_map/psum | solution.py:301
  38.5 1.9 %collective-permute-start.6 = (bf16[512,640]{1,0:T(8,128)(2,1)S(1)}, bf16[512,640]{1,0:T(8,128)(2,1)}, u32[]{:S(2)}, u32[]{:S(2)}) collective-permute-start(bf16[512,640]{1,0:T(8,128)(2,1)S(1)} %pad_maximum_fusion.b3), channel_id=1, source_target_pairs={{0,24},{4,28},{8,32},{12,36},{16,40},{20,44},{24,48},{28,52},{32,5... | collective-permute-start | bytes 1966088 | tf_op jit(solution)/shard_map/ppermute | solution.py:49
  40.4 6.4 %collective-permute-start.11 = (bf16[512,640]{1,0:T(8,128)(2,1)S(1)}, bf16[512,640]{1,0:T(8,128)(2,1)}, u32[]{:S(2)}, u32[]{:S(2)}) collective-permute-start(bf16[512,640]{1,0:T(8,128)(2,1)S(1)} %pad_maximum_fusion.b3), channel_id=1, source_target_pairs={{24,0},{28,4},{32,8},{36,12},{40,16},{44,20},{48,24},{52,28},{56,3... | collective-permute-start | bytes 1966088 | tf_op jit(solution)/shard_map/ppermute | solution.py:49
  46.8 1.9 %collective-permute-start.8 = (bf16[512,640]{1,0:T(8,128)(2,1)S(1)}, bf16[512,640]{1,0:T(8,128)(2,1)}, u32[]{:S(2)}, u32[]{:S(2)}) collective-permute-start(bf16[512,640]{1,0:T(8,128)(2,1)S(1)} %collective-permute-done.7.b2), channel_id=1, source_target_pairs={{0,8},{4,12},{8,16},{12,20},{16,24},{20,28},{24,32},{28,36},{32,40... | collective-permute-start | bytes 1966088 | tf_op jit(solution)/shard_map/ppermute | solution.py:49
  48.7 7.6 %collective-permute-start.10 = (bf16[512,640]{1,0:T(8,128)(2,1)S(1)}, bf16[512,640]{1,0:T(8,128)(2,1)}, u32[]{:S(2)}, u32[]{:S(2)}) collective-permute-start(bf16[512,640]{1,0:T(8,128)(2,1)S(1)} %collective-permute-done.9.b4), channel_id=1, source_target_pairs={{8,0},{12,4},{16,8},{20,12},{24,16},{28,20},{32,24},{36,28},{40,32... | collective-permute-start | bytes 1966088 | tf_op jit(solution)/shard_map/ppermute | solution.py:49
  56.3 5.4 %collective-permute-start = (f32[2,128]{1,0:T(2,128)S(1)}, f32[2,128]{1,0:T(2,128)S(1)}, u32[]{:S(2)}, u32[]{:S(2)}) collective-permute-start(f32[2,128]{1,0:T(2,128)S(1)} %get-tuple-element.11), channel_id=1, source_target_pairs={{0,4},{4,0},{8,12},{12,8},{16,20},{20,16},{24,28},{28,24},{32,36},... | collective-permute-start | bytes 3080 | tf_op jit(solution)/shard_map/ppermute | solution.py:56
  62.5 1.9 %collective-permute-start.3 = (f32[2,128]{1,0:T(2,128)S(1)}, f32[2,128]{1,0:T(2,128)S(1)}, u32[]{:S(2)}, u32[]{:S(2)}) collective-permute-start(f32[2,128]{1,0:T(2,128)S(1)} %bitcast.6), channel_id=1, source_target_pairs={{8,0},{12,4},{16,8},{20,12},{24,16},{28,20},{32,24},{36,28},{40,32... | collective-permute-start | bytes 3080 | tf_op jit(solution)/shard_map/ppermute | solution.py:49
  64.5 7.8 %collective-permute-done.3 = f32[2,128]{1,0:T(2,128)S(1)} collective-permute-done((f32[2,128]{1,0:T(2,128)S(1)}, f32[2,128]{1,0:T(2,128)S(1)}, u32[]{:S(2)}, u32[]{:S(2)}) %collective-permute-start.3) | collective-permute-done | bytes 1056 | tf_op jit(solution)/shard_map/ppermute | solution.py:49
  72.2 1.9 %collective-permute-start.1 = (f32[2,128]{1,0:T(2,128)S(1)}, f32[2,128]{1,0:T(2,128)S(1)}, u32[]{:S(2)}, u32[]{:S(2)}) collective-permute-start(f32[2,128]{1,0:T(2,128)S(1)} %bitcast.7), channel_id=1, source_target_pairs={{0,8},{4,12},{8,16},{12,20},{16,24},{20,28},{24,32},{28,36},{32,40... | collective-permute-start | bytes 3080 | tf_op jit(solution)/shard_map/ppermute | solution.py:49
  74.2 7.4 %collective-permute-done.1 = f32[2,128]{1,0:T(2,128)S(1)} collective-permute-done((f32[2,128]{1,0:T(2,128)S(1)}, f32[2,128]{1,0:T(2,128)S(1)}, u32[]{:S(2)}, u32[]{:S(2)}) %collective-permute-start.1) | collective-permute-done | bytes 1056 | tf_op jit(solution)/shard_map/ppermute | solution.py:49
  81.6 1.9 %collective-permute-start.2 = (f32[4,128]{1,0:T(4,128)S(1)}, f32[4,128]{1,0:T(4,128)S(1)}, u32[]{:S(2)}, u32[]{:S(2)}) collective-permute-start(f32[4,128]{1,0:T(4,128)S(1)} %get-tuple-element.16), channel_id=1, source_target_pairs={{0,16},{4,20},{8,24},{12,28},{16,32},{20,36},{24,40},{28,44},{32,4... | collective-permute-start | bytes 6152 | tf_op jit(solution)/shard_map/ppermute | solution.py:49
  83.6 6.8 %collective-permute-done.2 = f32[4,128]{1,0:T(4,128)S(1)} collective-permute-done((f32[4,128]{1,0:T(4,128)S(1)}, f32[4,128]{1,0:T(4,128)S(1)}, u32[]{:S(2)}, u32[]{:S(2)}) %collective-permute-start.2) | collective-permute-done | bytes 2080 | tf_op jit(solution)/shard_map/ppermute | solution.py:49
  90.5 1.9 %collective-permute-start.4 = (f32[4,128]{1,0:T(4,128)S(1)}, f32[4,128]{1,0:T(4,128)S(1)}, u32[]{:S(2)}, u32[]{:S(2)}) collective-permute-start(f32[4,128]{1,0:T(4,128)S(1)} %get-tuple-element.15), channel_id=1, source_target_pairs={{16,0},{20,4},{24,8},{28,12},{32,16},{36,20},{40,24},{44,28},{48,3... | collective-permute-start | bytes 6152 | tf_op jit(solution)/shard_map/ppermute | solution.py:49
  93.3 2.9 %collective-permute-done.4 = f32[4,128]{1,0:T(4,128)S(1)} collective-permute-done((f32[4,128]{1,0:T(4,128)S(1)}, f32[4,128]{1,0:T(4,128)S(1)}, u32[]{:S(2)}, u32[]{:S(2)}) %collective-permute-start.4) | collective-permute-done | bytes 2080 | tf_op jit(solution)/shard_map/ppermute | solution.py:49
  97.3 1.0 copy-done.5
  98.3 1.0 copy-done.6
  99.4 7.7 %shard_map.146 = (f32[128,640]{1,0:T(8,128)S(1)}, f32[128,640]{1,0:T(8,128)S(1)}) custom-call(s32[128]{0:T(128)S(1)} %copy-done.7, s32[128]{0:T(128)S(1)} %copy-done.8, s32[1]{0:T(128)} %bitcast.here_ref, f32[16,128]{1,0:T(8,128)S(1)} %concatenate.17.sums_ref, bf16[128,640]{1,0:T(8,128)(2,1)S(1)} %dynamic-slice.q0_ref, bf16[128,640]{1,0:T(8,128)(2,1)S(1)} %slice.39.q1_ref, ...), custom_call_target="tpu_custom_call" | custom-call | flops 600000000 | bytes 4000000 | tf_op jit(solution)/shard_map/pallas_call | solution.py:330
  107.1 8.6 %collective-permute-start.12 = (f32[128,640]{1,0:T(8,128)S(1)}, f32[128,640]{1,0:T(8,128)S(1)}, u32[]{:S(2)}, u32[]{:S(2)}) collective-permute-start(f32[128,640]{1,0:T(8,128)S(1)} %get-tuple-element.8), channel_id=1, source_target_pairs={{0,4},{4,0},{8,12},{12,8},{16,20},{20,16},{24,28},{28,24},{32,36},... | collective-permute-start | bytes 983048 | tf_op jit(solution)/shard_map/ppermute | solution.py:56
  115.8 1.5 %shard_map.147.text_ref = f32[128,1280]{1,0:T(8,128)S(1)} custom-call(s32[128]{0:T(128)S(1)} %copy-done.7, s32[128]{0:T(128)S(1)} %copy-done.9, s32[1]{0:T(128)} %bitcast.here_ref, f32[8,128]{1,0:T(8,128)S(1)} %psum.7.sums_ref, bf16[128,1280]{1,0:T(8,128)(2,1)S(1)} %copy-done.3, bf16[256,1280]{1,0:T(8,128)(2,1)S(1)} %copy-done, ...), custom_call_target="tpu_custom_call" | custom-call | flops 400000000 | bytes 4000000 | tf_op jit(solution)/shard_map/pallas_call | solution.py:314
  (58 shorter events, 6.1 us)
Async XLA Ops:
  2.2 4.1 %collective-permute-start.5 = (bf16[384,640]{1,0:T(8,128)(2,1)S(1)}, bf16[384,640]{1,0:T(8,128)(2,1)S(1)}, u32[]{:S(2)}, u32[]{:S(2)}) collective-permute-start(bf16[384,640]{1,0:T(8,128)(2,1)S(1)} %constant_dynamic-slice_fusion), channel_id=1, source_target_pairs={{0,4},{4,0},{8,12},{12,8},{16,20},{20,16},{24,28},{28,24},{32,36},... | collective-permute-start | bytes 1474568 | tf_op jit(solution)/shard_map/ppermute | solution.py:56
  4.8 11.9 %copy-start = (bf16[256,1280]{1,0:T(8,128)(2,1)S(1)}, bf16[256,1280]{1,0:T(8,128)(2,1)}, u32[]{:S(2)}) copy-start(bf16[256,1280]{1,0:T(8,128)(2,1)} %k_ref.3) | copy-start | bytes 1966084
  4.8 11.9 %copy-start.2 = (bf16[128,1280]{1,0:T(8,128)(2,1)S(1)}, bf16[128,1280]{1,0:T(8,128)(2,1)}, u32[]{:S(2)}) copy-start(bf16[128,1280]{1,0:T(8,128)(2,1)} %k_ref.2) | copy-start | bytes 983044
  4.8 11.9 %copy-start.3 = (bf16[128,1280]{1,0:T(8,128)(2,1)S(1)}, bf16[128,1280]{1,0:T(8,128)(2,1)}, u32[]{:S(2)}) copy-start(bf16[128,1280]{1,0:T(8,128)(2,1)} %q_ref.3) | copy-start | bytes 983044
  7.1 67.1 %copy-start.12 = (f32[1280]{0:T(1024)S(1)}, f32[1280]{0:T(1024)}, u32[]{:S(2)}) copy-start(f32[1280]{0:T(1024)} %param.21) | copy-start | bytes 15364
  7.1 67.1 %copy-start.13 = (f32[1280]{0:T(1024)S(1)}, f32[1280]{0:T(1024)}, u32[]{:S(2)}) copy-start(f32[1280]{0:T(1024)} %param.22) | copy-start | bytes 15364
  7.1 90.2 %copy-start.7 = (s32[128]{0:T(128)S(1)}, s32[128]{0:T(128)}, u32[]{:S(2)}) copy-start(s32[128]{0:T(128)} %item_ref.3) | copy-start | bytes 1540
  7.1 90.2 %copy-start.8 = (s32[128]{0:T(128)S(1)}, s32[128]{0:T(128)}, u32[]{:S(2)}) copy-start(s32[128]{0:T(128)} %count_ref.1) | copy-start | bytes 1540
  7.1 39.7 %collective-permute-start.7 = (bf16[512,640]{1,0:T(8,128)(2,1)S(1)}, bf16[512,640]{1,0:T(8,128)(2,1)S(1)}, u32[]{:S(2)}, u32[]{:S(2)}) collective-permute-start(bf16[512,640]{1,0:T(8,128)(2,1)S(1)} %pad_maximum_fusion.b3), channel_id=1, source_target_pairs={{0,8},{4,12},{8,16},{12,20},{16,24},{20,28},{24,32},{28,36},{32,40... | collective-permute-start | bytes 1966088 | tf_op jit(solution)/shard_map/ppermute | solution.py:49
  10.4 38.3 %collective-permute-start.9 = (bf16[512,640]{1,0:T(8,128)(2,1)S(1)}, bf16[512,640]{1,0:T(8,128)(2,1)S(1)}, u32[]{:S(2)}, u32[]{:S(2)}) collective-permute-start(bf16[512,640]{1,0:T(8,128)(2,1)S(1)} %pad_maximum_fusion.b3), channel_id=1, source_target_pairs={{8,0},{12,4},{16,8},{20,12},{24,16},{28,20},{32,24},{36,28},{40,32... | collective-permute-start | bytes 1966088 | tf_op jit(solution)/shard_map/ppermute | solution.py:49
  38.5 58.8 %collective-permute-start.6 = (bf16[512,640]{1,0:T(8,128)(2,1)S(1)}, bf16[512,640]{1,0:T(8,128)(2,1)}, u32[]{:S(2)}, u32[]{:S(2)}) collective-permute-start(bf16[512,640]{1,0:T(8,128)(2,1)S(1)} %pad_maximum_fusion.b3), channel_id=1, source_target_pairs={{0,24},{4,28},{8,32},{12,36},{16,40},{20,44},{24,48},{28,52},{32,5... | collective-permute-start | bytes 1966088 | tf_op jit(solution)/shard_map/ppermute | solution.py:49
  40.4 56.9 %collective-permute-start.11 = (bf16[512,640]{1,0:T(8,128)(2,1)S(1)}, bf16[512,640]{1,0:T(8,128)(2,1)}, u32[]{:S(2)}, u32[]{:S(2)}) collective-permute-start(bf16[512,640]{1,0:T(8,128)(2,1)S(1)} %pad_maximum_fusion.b3), channel_id=1, source_target_pairs={{24,0},{28,4},{32,8},{36,12},{40,16},{44,20},{48,24},{52,28},{56,3... | collective-permute-start | bytes 1966088 | tf_op jit(solution)/shard_map/ppermute | solution.py:49
  46.8 50.5 %collective-permute-start.8 = (bf16[512,640]{1,0:T(8,128)(2,1)S(1)}, bf16[512,640]{1,0:T(8,128)(2,1)}, u32[]{:S(2)}, u32[]{:S(2)}) collective-permute-start(bf16[512,640]{1,0:T(8,128)(2,1)S(1)} %collective-permute-done.7.b2), channel_id=1, source_target_pairs={{0,8},{4,12},{8,16},{12,20},{16,24},{20,28},{24,32},{28,36},{32,40... | collective-permute-start | bytes 1966088 | tf_op jit(solution)/shard_map/ppermute | solution.py:49
  48.7 48.6 %collective-permute-start.10 = (bf16[512,640]{1,0:T(8,128)(2,1)S(1)}, bf16[512,640]{1,0:T(8,128)(2,1)}, u32[]{:S(2)}, u32[]{:S(2)}) collective-permute-start(bf16[512,640]{1,0:T(8,128)(2,1)S(1)} %collective-permute-done.9.b4), channel_id=1, source_target_pairs={{8,0},{12,4},{16,8},{20,12},{24,16},{28,20},{32,24},{36,28},{40,32... | collective-permute-start | bytes 1966088 | tf_op jit(solution)/shard_map/ppermute | solution.py:49
  56.3 6.2 %collective-permute-start = (f32[2,128]{1,0:T(2,128)S(1)}, f32[2,128]{1,0:T(2,128)S(1)}, u32[]{:S(2)}, u32[]{:S(2)}) collective-permute-start(f32[2,128]{1,0:T(2,128)S(1)} %get-tuple-element.11), channel_id=1, source_target_pairs={{0,4},{4,0},{8,12},{12,8},{16,20},{20,16},{24,28},{28,24},{32,36},... | collective-permute-start | bytes 3080 | tf_op jit(solution)/shard_map/ppermute | solution.py:56
  62.5 9.7 %collective-permute-start.3 = (f32[2,128]{1,0:T(2,128)S(1)}, f32[2,128]{1,0:T(2,128)S(1)}, u32[]{:S(2)}, u32[]{:S(2)}) collective-permute-start(f32[2,128]{1,0:T(2,128)S(1)} %bitcast.6), channel_id=1, source_target_pairs={{8,0},{12,4},{16,8},{20,12},{24,16},{28,20},{32,24},{36,28},{40,32... | collective-permute-start | bytes 3080 | tf_op jit(solution)/shard_map/ppermute | solution.py:49
  72.2 9.4 %collective-permute-start.1 = (f32[2,128]{1,0:T(2,128)S(1)}, f32[2,128]{1,0:T(2,128)S(1)}, u32[]{:S(2)}, u32[]{:S(2)}) collective-permute-start(f32[2,128]{1,0:T(2,128)S(1)} %bitcast.7), channel_id=1, source_target_pairs={{0,8},{4,12},{8,16},{12,20},{16,24},{20,28},{24,32},{28,36},{32,40... | collective-permute-start | bytes 3080 | tf_op jit(solution)/shard_map/ppermute | solution.py:49
  81.6 8.8 %collective-permute-start.2 = (f32[4,128]{1,0:T(4,128)S(1)}, f32[4,128]{1,0:T(4,128)S(1)}, u32[]{:S(2)}, u32[]{:S(2)}) collective-permute-start(f32[4,128]{1,0:T(4,128)S(1)} %get-tuple-element.16), channel_id=1, source_target_pairs={{0,16},{4,20},{8,24},{12,28},{16,32},{20,36},{24,40},{28,44},{32,4... | collective-permute-start | bytes 6152 | tf_op jit(solution)/shard_map/ppermute | solution.py:49
  90.5 5.8 %collective-permute-start.4 = (f32[4,128]{1,0:T(4,128)S(1)}, f32[4,128]{1,0:T(4,128)S(1)}, u32[]{:S(2)}, u32[]{:S(2)}) collective-permute-start(f32[4,128]{1,0:T(4,128)S(1)} %get-tuple-element.15), channel_id=1, source_target_pairs={{16,0},{20,4},{24,8},{28,12},{32,16},{36,20},{40,24},{44,28},{48,3... | collective-permute-start | bytes 6152 | tf_op jit(solution)/shard_map/ppermute | solution.py:49
  99.4 16.3 %copy-start.14 = (f32[1280]{0:T(1024)S(1)}, f32[1280]{0:T(1024)}, u32[]{:S(2)}) copy-start(f32[1280]{0:T(1024)} %param.23) | copy-start | bytes 15364
  99.4 16.4 %copy-start.15 = (f32[1280]{0:T(1024)S(1)}, f32[1280]{0:T(1024)}, u32[]{:S(2)}) copy-start(f32[1280]{0:T(1024)} %param.24) | copy-start | bytes 15364
  99.4 16.4 %copy-start.4 = (bf16[256,1280]{1,0:T(8,128)(2,1)S(1)}, bf16[256,1280]{1,0:T(8,128)(2,1)}, u32[]{:S(2)}) copy-start(bf16[256,1280]{1,0:T(8,128)(2,1)} %v_ref.1) | copy-start | bytes 1966084
  99.4 16.4 %copy-start.9 = (s32[128]{0:T(128)S(1)}, s32[128]{0:T(128)}, u32[]{:S(2)}) copy-start(s32[128]{0:T(128)} %len_ref.1) | copy-start | bytes 1540
  107.1 10.3 %collective-permute-start.12 = (f32[128,640]{1,0:T(8,128)S(1)}, f32[128,640]{1,0:T(8,128)S(1)}, u32[]{:S(2)}, u32[]{:S(2)}) collective-permute-start(f32[128,640]{1,0:T(8,128)S(1)} %get-tuple-element.8), channel_id=1, source_target_pairs={{0,4},{4,0},{8,12},{12,8},{16,20},{20,16},{24,28},{28,24},{32,36},... | collective-permute-start | bytes 983048 | tf_op jit(solution)/shard_map/ppermute | solution.py:56
  (5 other events, 7.5 us)

commit v2 on v1

v2 whole, which is shorter than its diff:
```python
import functools
import math

import jax
import jax.numpy as jnp
import numpy as np
from jax import lax
from jax.experimental import pallas as pl
from jax.experimental.pallas import tpu as pltpu
from jax.sharding import PartitionSpec as P

D = 5120
HD = 128
HGT = 30
WID = 52
SPAN = 7
ROWS = 128
EPSILON = 1e-06
SCALE = 1.0 / math.sqrt(HD)
NEG = -1e30


def rope_tables():
    spatial = HD // 6
    temporal = HD // 2 - 2 * spatial
    positions = np.arange(SPAN * ROWS)

    def freq(amount):
        exponent = np.arange(amount, dtype=np.float64) * 2.0 / (2 * amount)
        return (1.0 / 10000.0**exponent).astype(np.float32)

    def part(values, amount):
        return values.astype(np.float32)[:, None] * freq(amount)[None, :]

    angle = np.concatenate(
        [
            part(positions // (HGT * WID), temporal),
            part(positions // WID % HGT, spatial),
            part(positions % WID, spatial),
        ],
        axis=1,
    ).astype(np.float64)
    cosine = np.repeat(np.cos(angle), 2, axis=1).astype(np.float32)
    sine = np.stack([-np.sin(angle), np.sin(angle)], axis=2)
    return cosine, sine.reshape(SPAN * ROWS, HD).astype(np.float32)


def shifted(value, by):
    peers = lax.axis_size("tile")
    return lax.ppermute(
        value, "tile", [(i, i + by) for i in range(peers) if 0 <= i + by < peers]
    )


def swapped(value):
    peers = lax.axis_size("tile")
    return lax.ppermute(value, "tile", [(i, i ^ 1) for i in range(peers)])


def by_rows(total_row):
    factor = lax.rsqrt(total_row / D + EPSILON)
    return jnp.transpose(jnp.broadcast_to(factor, (ROWS, ROWS)))


def rotated(normal, cosine, sine, even):
    partner = jnp.where(even, pltpu.roll(normal, HD - 1, 1), pltpu.roll(normal, 1, 1))
    return normal * cosine + partner * sine


def prefix_live(shape, count):
    return lax.broadcasted_iota(jnp.int32, shape, 1) < count


def pack_kernel(here_ref, q_ref, k_ref, v_ref, c_ref, t_ref, mine_ref, theirs_ref, sums_ref):
    def total(ref, first):
        rows = None
        for head in range(ref.shape[1] // HD):
            x = ref[first : first + ROWS, head * HD : (head + 1) * HD].astype(jnp.float32)
            rows = x * x if rows is None else rows + x * x
        return jnp.sum(jnp.transpose(rows), axis=0, keepdims=True)

    sums_ref[0:1, :] = total(q_ref, 0)
    sums_ref[1:2, :] = total(k_ref, 0)
    sums_ref[2:3, :] = total(c_ref, 0)
    sums_ref[3:4, :] = total(t_ref, 0)
    sums_ref[4:5, :] = total(t_ref, ROWS)
    sums_ref[5:8, :] = jnp.zeros((3, ROWS), jnp.float32)
    core = lax.rem(here_ref[0], 2)
    half = mine_ref.shape[1]
    for index, ref in enumerate((k_ref, v_ref, q_ref)):
        rows = slice(index * ROWS, (index + 1) * ROWS)
        low, high = ref[:, :half], ref[:, half:]
        mine_ref[rows, :] = jnp.where(core == 0, low, high)
        theirs_ref[rows, :] = jnp.where(core == 0, high, low)


def cross_kernel(item_ref, len_ref, here_ref, sums_ref, q_ref, k_ref, v_ref, qg_ref, kg_ref, out_ref):
    count = len_ref[item_ref[here_ref[0]]]
    q_factor = by_rows(sums_ref[2:3, :])
    k_factor = [by_rows(sums_ref[3:4, :]), by_rows(sums_ref[4:5, :])]
    live = prefix_live((ROWS, 2 * ROWS), count)
    for head in range(q_ref.shape[1] // HD):
        cols = slice(head * HD, (head + 1) * HD)
        q = (q_ref[:, cols].astype(jnp.float32) * q_factor * qg_ref[:, cols]).astype(jnp.bfloat16)
        keys = [
            (
                k_ref[h * ROWS : (h + 1) * ROWS, cols].astype(jnp.float32)
                * k_factor[h]
                * kg_ref[:, cols]
            ).astype(jnp.bfloat16)
            for h in range(2)
        ]
        k = jnp.concatenate(keys, axis=0)
        s = lax.dot_general(q, k, (((1,), (1,)), ((), ())), preferred_element_type=jnp.float32)
        s = jnp.where(live, s * SCALE, NEG)
        w = jnp.exp(s - jnp.max(s, axis=1, keepdims=True))
        total = jnp.sum(w, axis=1, keepdims=True)
        o = jnp.dot(w.astype(jnp.bfloat16), v_ref[:, cols], preferred_element_type=jnp.float32)
        out_ref[:, cols] = o / total


def extent(item_ref, tile):
    tiles = item_ref.shape[0]
    item = item_ref[tile]
    before = jnp.int32(0)
    after = jnp.int32(0)
    for d in range(1, SPAN):
        lower = item_ref[jnp.maximum(tile - d, 0)] == item
        upper = item_ref[jnp.minimum(tile + d, tiles - 1)] == item
        before += jnp.where(jnp.logical_and(lower, tile - d >= 0), 1, 0)
        after += jnp.where(jnp.logical_and(upper, tile + d < tiles), 1, 0)
    return tile - before, tile + after


def turn(ref, rows, factor, gain_ref, cos_ref, sin_ref, start, dest_ref, slot):
    even = lax.rem(lax.broadcasted_iota(jnp.int32, (ROWS, HD), 1), 2) == 0
    cosine = cos_ref[pl.ds(start, ROWS), :]
    sine = sin_ref[pl.ds(start, ROWS), :]
    for head in range(ref.shape[1] // HD):
        cols = slice(head * HD, (head + 1) * HD)
        x = ref[rows, cols].astype(jnp.float32) * factor * gain_ref[:, cols]
        dest_ref[slot, :, cols] = rotated(x, cosine, sine, even).astype(jnp.bfloat16)


def keys_kernel(chips, item_ref, here_ref, sums_ref, gain_ref, cos_ref, sin_ref, *rest):
    blocks, keys_ref = rest[:-1], rest[-1]
    here = here_ref[0]
    core = lax.rem(here, 2)
    left = here - core
    first_a, last_a = extent(item_ref, left)
    first_b, last_b = extent(item_ref, left + 1)
    for index, (chip, block) in enumerate(zip(chips, blocks)):
        for parity in range(2):
            tile = left + 2 * chip + parity

            @pl.when(jnp.logical_and(tile >= first_a, tile <= last_b))
            def _(index=index, parity=parity, tile=tile, block=block):
                first = jnp.where(tile <= last_a, first_a, first_b)
                start = pl.multiple_of((tile - first) * ROWS, ROWS)
                slot = jnp.where(core == parity, 0, 1)
                row = pl.multiple_of(slot * 2 * ROWS, 2 * ROWS)
                factor = by_rows(sums_ref[pl.ds(2 * index + slot, 1), :])
                rows = pl.ds(row, ROWS)
                turn(block, rows, factor, gain_ref, cos_ref, sin_ref, start, keys_ref, 2 * index + parity)


def attend_kernel(
    other,
    item_ref,
    count_ref,
    here_ref,
    sums_ref,
    q_ref,
    near_ref,
    far_ref,
    b0,
    b1,
    b2,
    b3,
    b4,
    b5,
    b6,
    gain_ref,
    cos_ref,
    sin_ref,
    out_ref,
    keys,
    values,
    queries,
    scores,
):
    blocks = (b0, b1, b2, b3, b4, b5, b6)
    heads = q_ref.shape[1] // HD
    here = here_ref[0]
    core = lax.rem(here, 2)
    left = here - core
    base = left - 6
    tile = left + (1 - core if other else core)
    first, last = extent(item_ref, tile)
    factor = by_rows(sums_ref[0:1, :])
    start = pl.multiple_of((tile - first) * ROWS, ROWS)
    turn(q_ref, slice(None), factor, gain_ref, cos_ref, sin_ref, start, queries, 0)
    low, high = first - base, last - base + 1

    for w in range(14):

        @pl.when(jnp.logical_and(w >= low, w < high))
        def _(w=w):
            chip, parity = w // 2, w % 2
            slot = jnp.where(core == parity, 0, 1)
            row = pl.multiple_of(slot * 2 * ROWS + ROWS, ROWS)
            values[w] = blocks[chip][pl.ds(row, ROWS), :]
            keys[w] = near_ref[w - 4] if chip in (2, 3, 4) else far_ref[w if chip < 2 else w - 6]

    def score(w, tops):
        live = prefix_live((ROWS, ROWS), count_ref[base + w])
        found = []
        for head in range(heads):
            cols = slice(head * HD, (head + 1) * HD)
            s = lax.dot_general(
                queries[0, :, cols],
                keys[w, :, cols],
                (((1,), (1,)), ((), ())),
                preferred_element_type=jnp.float32,
            )
            s = jnp.where(live, s * SCALE, NEG)
            scores[w - low, :, cols] = s
            found.append(jnp.maximum(tops[head], s))
        return tuple(found)

    empty = jnp.full((ROWS, ROWS), NEG, jnp.float32)
    tops = lax.fori_loop(low, high, score, (empty,) * heads)
    tops = [jnp.max(t, axis=1, keepdims=True) for t in tops]

    def mix(w, carry):
        mixed, totals = [], []
        for head in range(heads):
            cols = slice(head * HD, (head + 1) * HD)
            weight = jnp.exp(scores[w - low, :, cols] - tops[head])
            totals.append(carry[1][head] + weight)
            mixed.append(
                carry[0][head]
                + jnp.dot(
                    weight.astype(jnp.bfloat16),
                    values[w, :, cols],
                    preferred_element_type=jnp.float32,
                )
            )
        return tuple(mixed), tuple(totals)

    zero = jnp.zeros((ROWS, ROWS), jnp.float32)
    mixed, totals = lax.fori_loop(low, high, mix, ((zero,) * heads, (zero,) * heads))
    for head in range(heads):
        cols = slice(head * HD, (head + 1) * HD)
        out_ref[:, cols] = mixed[head] / jnp.sum(totals[head], axis=1, keepdims=True)


def join_kernel(here_ref, own_ref, other_ref, text_ref, out_ref):
    core = lax.rem(here_ref[0], 2)
    width = own_ref.shape[1]
    mine = pl.multiple_of(core * width, HD)
    theirs = pl.multiple_of((1 - core) * width, HD)
    out_ref[:, pl.ds(mine, width)] = (own_ref[...] + text_ref[:, pl.ds(mine, width)]).astype(
        jnp.bfloat16
    )
    out_ref[:, pl.ds(theirs, width)] = (other_ref[...] + text_ref[:, pl.ds(theirs, width)]).astype(
        jnp.bfloat16
    )


def call(kernel, out_shape, specs, scratch=(), flops=1000000, limit=40):
    return pl.pallas_call(
        kernel,
        out_shape=out_shape,
        in_specs=specs,
        out_specs=jax.tree.map(lambda _: pl.BlockSpec(memory_space=pltpu.VMEM), out_shape),
        scratch_shapes=list(scratch),
        compiler_params=pltpu.CompilerParams(vmem_limit_bytes=limit << 20),
        cost_estimate=pl.CostEstimate(flops=flops, bytes_accessed=4000000, transcendentals=0),
    )


def per_device(
    self_query,
    self_key,
    self_value,
    cross_query,
    text_key,
    text_value,
    query_gain,
    key_gain,
    cross_gain,
    text_gain,
    tile_item,
    row_count,
    text_len,
):
    smem = pl.BlockSpec(memory_space=pltpu.SMEM)
    vmem = pl.BlockSpec(memory_space=pltpu.VMEM)
    f32 = jnp.float32
    width = self_query.shape[1]
    half = width // 2
    here = lax.axis_index("tile").astype(jnp.int32)
    core = lax.rem(here, 2)
    where = here.reshape(1)

    mine, theirs, sums = call(
        pack_kernel,
        (
            jax.ShapeDtypeStruct((3 * ROWS, half), jnp.bfloat16),
            jax.ShapeDtypeStruct((3 * ROWS, half), jnp.bfloat16),
            jax.ShapeDtypeStruct((8, ROWS), f32),
        ),
        [smem] + [vmem] * 5,
    )(where, self_query, self_key, self_value, cross_query, text_key)
    got = swapped(theirs)
    sums = jnp.concatenate([sums[:5], swapped(sums[:2]), sums[7:]])
    block = jnp.concatenate([mine[: 2 * ROWS], got[: 2 * ROWS]], axis=0)
    from_left = shifted(block, 2)
    from_right = shifted(block, -2)
    from_left3 = shifted(block, 6)
    from_right3 = shifted(block, -6)

    sums = lax.psum(sums, "head")
    k_sums = jnp.concatenate([sums[1:2], sums[6:7]])
    left_sums = shifted(k_sums, 2)
    right_sums = shifted(k_sums, -2)

    from_left, from_right, from_left3, from_right3, left_sums, right_sums = lax.optimization_barrier(
        (from_left, from_right, from_left3, from_right3, left_sums, right_sums)
    )
    from_left2 = shifted(from_left, 2)
    from_right2 = shifted(from_right, -2)
    left_far = shifted(jnp.concatenate([left_sums, k_sums]), 4)
    right_far = shifted(jnp.concatenate([k_sums, right_sums]), -4)

    text_out = call(
        cross_kernel, jax.ShapeDtypeStruct((ROWS, width), f32), [smem] * 3 + [vmem] * 6, flops=400000000
    )(
        tile_item,
        text_len,
        where,
        sums,
        cross_query,
        text_key,
        text_value,
        cross_gain[None, :],
        text_gain[None, :],
    )

    cosine, sine = (jnp.asarray(t) for t in rope_tables())
    my_gain = lax.dynamic_slice_in_dim(jnp.stack([query_gain, key_gain]), core * half, half, 1)

    def turned(chips, block_sums, blocks):
        return call(
            functools.partial(keys_kernel, chips),
            jax.ShapeDtypeStruct((2 * len(chips), ROWS, half), jnp.bfloat16),
            [smem] * 2 + [vmem] * (4 + len(chips)),
            flops=200000000,
        )(tile_item, where, block_sums, my_gain[1:2], cosine, sine, *blocks)

    near = turned(
        (-1, 0, 1), jnp.concatenate([left_sums, k_sums, right_sums]), (from_left, block, from_right)
    )
    far = turned(
        (-3, -2, 2, 3),
        jnp.concatenate([left_far, right_far]),
        (from_left3, from_left2, from_right2, from_right3),
    )

    def attended(other, query, query_sums):
        return call(
            functools.partial(attend_kernel, other),
            jax.ShapeDtypeStruct((ROWS, half), f32),
            [smem] * 3 + [vmem] * 14,
            scratch=[
                pltpu.VMEM((14, ROWS, half), jnp.bfloat16),
                pltpu.VMEM((14, ROWS, half), jnp.bfloat16),
                pltpu.VMEM((1, ROWS, half), jnp.bfloat16),
                pltpu.VMEM((SPAN, ROWS, half), f32),
            ],
            flops=300000000,
        )(
            tile_item,
            row_count,
            where,
            query_sums,
            query,
            near,
            far,
            from_left3,
            from_left2,
            from_left,
            block,
            from_right,
            from_right2,
            from_right3,
            my_gain[0:1],
            cosine,
            sine,
        )

    rest = swapped(attended(True, got[2 * ROWS :], sums[5:6]))
    own = attended(False, mine[2 * ROWS :], sums[0:1])
    return call(
        join_kernel, jax.ShapeDtypeStruct((ROWS, width), jnp.bfloat16), [smem] + [vmem] * 3
    )(where, own, rest, text_out)


def solution(mesh):
    spread = P("tile", "head")
    in_specs = (spread,) * 6 + (P("head"),) * 4 + (P(),) * 3
    return jax.shard_map(
        per_device, mesh=mesh, in_specs=in_specs, out_specs=spread, check_vma=False
    )
```

time: 119 us -> 118 us (level)
  waiting for transfers between devices: 27.2 us -> 10.4 us
  blocking collectives: 21.3 us -> 27.3 us
  local copies, waits for them, and re-layouts: 6.96 us -> 10.9 us
  other arithmetic: 0.15 us -> 2.91 us
  Pallas kernels: 10.5 us -> 12.3 us
    ppermute x10, waiting for transfers between devices: 25 us -> 8.25 us  [shifted(): lax.ppermute(value, 'tile', [(i, i + by) for i in range(peers) if 0 <= i...]
    psum x1, blocking collectives: 21.3 us -> 27.3 us  [per_device(): sums = lax.psum(sums, 'head')]
    ppermute x10, starting transfers between devices: 35.1 us -> 37.9 us  [shifted(): lax.ppermute(value, 'tile', [(i, i + by) for i in range(peers) if 0 <= i...]
    another operation x2, local copies, waits for them, and re-layouts: 0.01 us -> 2.59 us  [per_device(): jnp.stack([query_gain, key_gain])]
    concatenate x1 -> x5, other arithmetic: 0.01 us -> 2.07 us  [the longest x1 0.76 us: per_device(): left_far = shifted(jnp.concatenate([left_sums, k_sums]), 4)]
    pallas_call x2 -> x5, Pallas kernels: 8.09 us -> 9.92 us  [the longest x2 6.26 us: attended(): call(functools.partial(attend_kernel, other), jax.ShapeDtypeStruct((ROWS,...]
    ppermute x3, starting transfers between devices: 16.6 us -> 14.9 us  [swapped(): return lax.ppermute(value, 'tile', [(i, i ^ 1) for i in range(peers)])]
    unnamed x34 -> x38, local copies, waits for them, and re-layouts: 4.88 us -> 6.39 us
  transfers between devices with their start and end apart: 13 -> 13, of which waited for: 6 -> 5; matrix products, arithmetic and copies ran while one was open for 2% -> 6% of each run, Pallas kernels for 2% -> 6%
where the time goes in v2:
time: 118 us; the launch traced here: 117 us
  starting transfers between devices  52.8 us (45%)
  blocking collectives  27.3 us (23%)
  Pallas kernels  12.3 us (10%)
  local copies, waits for them, and re-layouts  10.9 us (9%)
  waiting for transfers between devices  10.4 us (9%)
  other arithmetic  2.91 us (2%)
    ppermute x10, starting transfers between devices, shifted(): lax.ppermute(value, 'tile', [(i, i + by) for i in range(peers) if 0 <= i...  37.9 us
    psum x1, blocking collectives, per_device(): sums = lax.psum(sums, 'head')  27.3 us
    ppermute x3, starting transfers between devices, swapped(): return lax.ppermute(value, 'tile', [(i, i ^ 1) for i in range(peers)])  14.9 us
    ppermute x10, waiting for transfers between devices, shifted(): lax.ppermute(value, 'tile', [(i, i + by) for i in range(peers) if 0 <= i...  8.25 us
    unnamed x38, local copies, waits for them, and re-layouts  6.39 us
    pallas_call x2, Pallas kernels, attended(): call(functools.partial(attend_kernel, other), jax.ShapeDtypeStruct((ROWS,...  6.26 us
    pallas_call x2, Pallas kernels, turned(): call(functools.partial(keys_kernel, chips), jax.ShapeDtypeStruct((2 * len...  3.23 us
    another operation x2, local copies, waits for them, and re-layouts, per_device(): jnp.stack([query_gain, key_gain])  2.59 us
  transfers between devices with their start and end apart: 13, of which 5 were waited for; matrix products, arithmetic and copies ran while one was open for 6% of the time, Pallas kernels for 6%

profile of v2, /device:TPU:33, one launch (start us, length us, event | category | flops | bytes accessed | tf_op | source)
XLA Modules:
  0.0 117.2 jit_solution(1716445952456553239)
XLA Ops:
  5.4 2.6 %collective-permute-start.1 = (bf16[384,640]{1,0:T(8,128)(2,1)S(1)}, bf16[384,640]{1,0:T(8,128)(2,1)S(1)}, u32[]{:S(2)}, u32[]{:S(2)}) collective-permute-start(bf16[384,640]{1,0:T(8,128)(2,1)S(1)} %get-tuple-element.16), channel_id=1, source_target_pairs={{0,4},{4,0},{8,12},{12,8},{16,20},{20,16},{24,28},{28,24},{32,36},... | collective-permute-start | bytes 1474568 | tf_op jit(solution)/shard_map/ppermute | solution.py:57
  8.1 1.4 %collective-permute-done.1 = bf16[384,640]{1,0:T(8,128)(2,1)S(1)} collective-permute-done((bf16[384,640]{1,0:T(8,128)(2,1)S(1)}, bf16[384,640]{1,0:T(8,128)(2,1)S(1)}, u32[]{:S(2)}, u32[]{:S(2)}) %collective-permute-start.1) | collective-permute-done | bytes 491552 | tf_op jit(solution)/shard_map/ppermute | solution.py:57
  10.4 3.1 %collective-permute-start.2 = (bf16[512,640]{1,0:T(8,128)(2,1)S(1)}, bf16[512,640]{1,0:T(8,128)(2,1)S(1)}, u32[]{:S(2)}, u32[]{:S(2)}) collective-permute-start(bf16[512,640]{1,0:T(8,128)(2,1)S(1)} %pad_maximum_fusion.rest_1_.b3), channel_id=1, source_target_pairs={{0,8},{4,12},{8,16},{12,20},{16,24},{20,28},{24,32},{28,36},{32,40... | collective-permute-start | bytes 1966088 | tf_op jit(solution)/shard_map/ppermute | solution.py:50
  13.5 6.4 %collective-permute-start.3 = (bf16[512,640]{1,0:T(8,128)(2,1)S(1)}, bf16[512,640]{1,0:T(8,128)(2,1)S(1)}, u32[]{:S(2)}, u32[]{:S(2)}) collective-permute-start(bf16[512,640]{1,0:T(8,128)(2,1)S(1)} %pad_maximum_fusion.rest_1_.b3), channel_id=1, source_target_pairs={{8,0},{12,4},{16,8},{20,12},{24,16},{28,20},{32,24},{36,28},{40,32... | collective-permute-start | bytes 1966088 | tf_op jit(solution)/shard_map/ppermute | solution.py:50
  19.9 1.9 %collective-permute-start.4 = (bf16[512,640]{1,0:T(8,128)(2,1)S(1)}, bf16[512,640]{1,0:T(8,128)(2,1)S(1)}, u32[]{:S(2)}, u32[]{:S(2)}) collective-permute-start(bf16[512,640]{1,0:T(8,128)(2,1)S(1)} %pad_maximum_fusion.rest_1_.b3), channel_id=1, source_target_pairs={{0,24},{4,28},{8,32},{12,36},{16,40},{20,44},{24,48},{28,52},{32,5... | collective-permute-start | bytes 1966088 | tf_op jit(solution)/shard_map/ppermute | solution.py:50
  21.8 6.4 %collective-permute-start.5 = (bf16[512,640]{1,0:T(8,128)(2,1)S(1)}, bf16[512,640]{1,0:T(8,128)(2,1)}, u32[]{:S(2)}, u32[]{:S(2)}) collective-permute-start(bf16[512,640]{1,0:T(8,128)(2,1)S(1)} %pad_maximum_fusion.rest_1_.b3), channel_id=1, source_target_pairs={{24,0},{28,4},{32,8},{36,12},{40,16},{44,20},{48,24},{52,28},{56,3... | collective-permute-start | bytes 1966088 | tf_op jit(solution)/shard_map/ppermute | solution.py:50
  28.2 3.4 %collective-permute-start = (f32[2,128]{1,0:T(2,128)S(1)}, f32[2,128]{1,0:T(2,128)S(1)}, u32[]{:S(2)}, u32[]{:S(2)}) collective-permute-start(f32[2,128]{1,0:T(2,128)S(1)} %slice.42), channel_id=1, source_target_pairs={{0,4},{4,0},{8,12},{12,8},{16,20},{20,16},{24,28},{28,24},{32,36},... | collective-permute-start | bytes 3080 | tf_op jit(solution)/shard_map/ppermute | solution.py:57
  32.4 27.3 %psum.7.sums_ref = f32[8,128]{1,0:T(8,128)S(1)} all-reduce(f32[8,128]{1,0:T(8,128)S(1)} %pad_maximum_fusion.1), channel_id=1, replica_groups=mesh['tile'=128,'head'=4] {'head'}, use_global_device_ids=true, to_apply=%region_0.0 | all-reduce | flops 1024 | bytes 8192 | tf_op jit(solution)/shard_map/psum | solution.py:324
  60.9 1.9 %collective-permute-start.6 = (f32[2,128]{1,0:T(2,128)}, f32[2,128]{1,0:T(2,128)}, u32[]{:S(2)}, u32[]{:S(2)}) collective-permute-start(f32[2,128]{1,0:T(2,128)} %pad_maximum_fusion.6), channel_id=1, source_target_pairs={{0,8},{4,12},{8,16},{12,20},{16,24},{20,28},{24,32},{28,36},{32,40... | collective-permute-start | bytes 3080 | tf_op jit(solution)/shard_map/ppermute | solution.py:50
  62.9 6.9 %collective-permute-done.6 = f32[2,128]{1,0:T(2,128)} collective-permute-done((f32[2,128]{1,0:T(2,128)}, f32[2,128]{1,0:T(2,128)}, u32[]{:S(2)}, u32[]{:S(2)}) %collective-permute-start.6) | collective-permute-done | bytes 1056 | tf_op jit(solution)/shard_map/ppermute | solution.py:50
  69.8 1.9 %collective-permute-start.7 = (f32[2,128]{1,0:T(2,128)}, f32[2,128]{1,0:T(2,128)}, u32[]{:S(2)}, u32[]{:S(2)}) collective-permute-start(f32[2,128]{1,0:T(2,128)} %pad_maximum_fusion.6), channel_id=1, source_target_pairs={{8,0},{12,4},{16,8},{20,12},{24,16},{28,20},{32,24},{36,28},{40,32... | collective-permute-start | bytes 3080 | tf_op jit(solution)/shard_map/ppermute | solution.py:50
  71.7 1.3 %stack.9 = f32[1,1280]{1,0:T(1,128)} reshape(f32[1280]{0:T(1024)} %param.21) | data formatting | bytes 10240 | tf_op jit(solution)/shard_map/stack | solution.py:352
  73.0 1.3 %stack.10 = f32[1,1280]{1,0:T(1,128)} reshape(f32[1280]{0:T(1024)} %param.22) | data formatting | bytes 10240 | tf_op jit(solution)/shard_map/stack | solution.py:352
  74.4 3.3 %collective-permute-start.10 = (bf16[512,640]{1,0:T(8,128)(2,1)S(1)}, bf16[512,640]{1,0:T(8,128)(2,1)S(1)}, u32[]{:S(2)}, u32[]{:S(2)}) collective-permute-start(bf16[512,640]{1,0:T(8,128)(2,1)S(1)} %collective-permute-done.2.rest_0_.b2), channel_id=1, source_target_pairs={{0,8},{4,12},{8,16},{12,20},{16,24},{20,28},{24,32},{28,36},{32,40... | collective-permute-start | bytes 1966088 | tf_op jit(solution)/shard_map/ppermute | solution.py:50
  77.7 6.2 %collective-permute-start.11 = (bf16[512,640]{1,0:T(8,128)(2,1)S(1)}, bf16[512,640]{1,0:T(8,128)(2,1)S(1)}, u32[]{:S(2)}, u32[]{:S(2)}) collective-permute-start(bf16[512,640]{1,0:T(8,128)(2,1)S(1)} %collective-permute-done.3.rest_2_.b4), channel_id=1, source_target_pairs={{8,0},{12,4},{16,8},{20,12},{24,16},{28,20},{32,24},{36,28},{40,32... | collective-permute-start | bytes 1966088 | tf_op jit(solution)/shard_map/ppermute | solution.py:50
  86.4 1.9 %collective-permute-start.9 = (f32[4,128]{1,0:T(4,128)S(1)}, f32[4,128]{1,0:T(4,128)S(1)}, u32[]{:S(2)}, u32[]{:S(2)}) collective-permute-start(f32[4,128]{1,0:T(4,128)S(1)} %get-tuple-element.30), channel_id=1, source_target_pairs={{16,0},{20,4},{24,8},{28,12},{32,16},{36,20},{40,24},{44,28},{48,3... | collective-permute-start | bytes 6152 | tf_op jit(solution)/shard_map/ppermute | solution.py:50
  88.4 4.9 %collective-permute-start.8 = (f32[4,128]{1,0:T(4,128)S(1)}, f32[4,128]{1,0:T(4,128)S(1)}, u32[]{:S(2)}, u32[]{:S(2)}) collective-permute-start(f32[4,128]{1,0:T(4,128)S(1)} %get-tuple-element.29), channel_id=1, source_target_pairs={{0,16},{4,20},{8,24},{12,28},{16,32},{20,36},{24,40},{28,44},{32,4... | collective-permute-start | bytes 6152 | tf_op jit(solution)/shard_map/ppermute | solution.py:50
  94.0 2.0 %shard_map.146.near_ref = bf16[6,128,640]{2,1,0:T(8,128)(2,1)S(1)} custom-call(s32[128]{0:T(128)S(1)} %copy-done.11, s32[1]{0:T(128)} %bitcast.here_ref, f32[6,128]{1,0:T(8,128)S(1)} %pad_maximum_fusion.2.sums_ref, f32[1,640]{1,0:T(1,128)S(1)} %get-tuple-element.24.gain_ref, f32[896,128]{1,0:T(8,128)S(1)} %copy-done, f32[896,128]{1,0:T(8,128)S(1)} %copy-done.1, ...), custom_call_target="tpu_custom_call" | custom-call | flops 200000000 | bytes 4000000 | tf_op jit(solution)/shard_map/pallas_call | solution.py:355
  96.0 1.2 %collective-permute-done.8 = f32[4,128]{1,0:T(4,128)S(1)} collective-permute-done((f32[4,128]{1,0:T(4,128)S(1)}, f32[4,128]{1,0:T(4,128)S(1)}, u32[]{:S(2)}, u32[]{:S(2)}) %collective-permute-start.8) | collective-permute-done | bytes 2080 | tf_op jit(solution)/shard_map/ppermute | solution.py:50
  97.2 1.2 %shard_map.147.far_ref = bf16[8,128,640]{2,1,0:T(8,128)(2,1)S(1)} custom-call(s32[128]{0:T(128)S(1)} %copy-done.11, s32[1]{0:T(128)} %bitcast.here_ref, f32[8,128]{1,0:T(8,128)S(1)} %pad_maximum_fusion.3.sums_ref, f32[1,640]{1,0:T(1,128)S(1)} %get-tuple-element.24.gain_ref, f32[896,128]{1,0:T(8,128)S(1)} %copy-done, f32[896,128]{1,0:T(8,128)S(1)} %copy-done.1, ...), custom_call_target="tpu_custom_call" | custom-call | flops 200000000 | bytes 4000000 | tf_op jit(solution)/shard_map/pallas_call | solution.py:355
  98.6 2.6 %shard_map.149 = f32[128,640]{1,0:T(8,128)S(1)} custom-call(s32[128]{0:T(128)S(1)} %copy-done.11, s32[128]{0:T(128)S(1)} %copy-done.12, s32[1]{0:T(128)} %bitcast.here_ref, f32[1,128]{1,0:T(1,128)S(1)} %get-tuple-element.25.sums_ref, bf16[128,640]{1,0:T(8,128)(2,1)S(1)} %slice.57.q_ref, bf16[6,128,640]{2,1,0:T(8,128)(2,1)S(1)} %shard_map.146.near_ref, ...), custom_call_target="tpu_custom_call" | custom-call | flops 300000000 | bytes 4000000 | tf_op jit(solution)/shard_map/pallas_call | solution.py:372
  101.2 8.9 %collective-permute-start.12 = (f32[128,640]{1,0:T(8,128)S(1)}, f32[128,640]{1,0:T(8,128)S(1)}, u32[]{:S(2)}, u32[]{:S(2)}) collective-permute-start(f32[128,640]{1,0:T(8,128)S(1)} %shard_map.149), channel_id=1, source_target_pairs={{0,4},{4,0},{8,12},{12,8},{16,20},{20,16},{24,28},{28,24},{32,36},... | collective-permute-start | bytes 983048 | tf_op jit(solution)/shard_map/ppermute | solution.py:57
  111.1 1.6 %shard_map.150.text_ref = f32[128,1280]{1,0:T(8,128)S(1)} custom-call(s32[128]{0:T(128)S(1)} %copy-done.11, s32[128]{0:T(128)S(1)} %copy-done.13, s32[1]{0:T(128)} %bitcast.here_ref, f32[8,128]{1,0:T(8,128)S(1)} %psum.7.sums_ref, bf16[128,1280]{1,0:T(8,128)(2,1)S(1)} %copy-done.5, bf16[256,1280]{1,0:T(8,128)(2,1)S(1)} %copy-done.3, ...), custom_call_target="tpu_custom_call" | custom-call | flops 400000000 | bytes 4000000 | tf_op jit(solution)/shard_map/pallas_call | solution.py:337
  112.8 3.6 %shard_map.148.own_ref = f32[128,640]{1,0:T(8,128)S(1)} custom-call(s32[128]{0:T(128)S(1)} %copy-done.11, s32[128]{0:T(128)S(1)} %copy-done.12, s32[1]{0:T(128)} %bitcast.here_ref, f32[1,128]{1,0:T(1,128)S(1)} %get-tuple-element.28.sums_ref, bf16[128,640]{1,0:T(8,128)(2,1)S(1)} %slice.45.q_ref, bf16[6,128,640]{2,1,0:T(8,128)(2,1)S(1)} %shard_map.146.near_ref, ...), custom_call_target="tpu_custom_call" | custom-call | flops 300000000 | bytes 4000000 | tf_op jit(solution)/shard_map/pallas_call | solution.py:372
  (67 shorter events, 13.4 us)
Async XLA Ops:
  5.4 4.9 %copy-start.7 = (bf16[384,640]{1,0:T(8,128)(2,1)}, bf16[384,640]{1,0:T(8,128)(2,1)S(1)}, u32[]{:S(2)}) copy-start(bf16[384,640]{1,0:T(8,128)(2,1)S(1)} %get-tuple-element.15) | copy-start | bytes 1474564
  5.4 4.1 %collective-permute-start.1 = (bf16[384,640]{1,0:T(8,128)(2,1)S(1)}, bf16[384,640]{1,0:T(8,128)(2,1)S(1)}, u32[]{:S(2)}, u32[]{:S(2)}) collective-permute-start(bf16[384,640]{1,0:T(8,128)(2,1)S(1)} %get-tuple-element.16), channel_id=1, source_target_pairs={{0,4},{4,0},{8,12},{12,8},{16,20},{20,16},{24,28},{28,24},{32,36},... | collective-permute-start | bytes 1474568 | tf_op jit(solution)/shard_map/ppermute | solution.py:57
  8.1 85.9 %copy-start = (f32[896,128]{1,0:T(8,128)S(1)}, f32[896,128]{1,0:T(8,128)}, u32[]{:S(2)}) copy-start(f32[896,128]{1,0:T(8,128)} %constant.20.clone.cos_ref) | copy-start | bytes 1376260
  8.1 85.9 %copy-start.1 = (f32[896,128]{1,0:T(8,128)S(1)}, f32[896,128]{1,0:T(8,128)}, u32[]{:S(2)}) copy-start(f32[896,128]{1,0:T(8,128)} %constant.21.clone.sin_ref) | copy-start | bytes 1376260
  8.1 85.9 %copy-start.11 = (s32[128]{0:T(128)S(1)}, s32[128]{0:T(128)}, u32[]{:S(2)}) copy-start(s32[128]{0:T(128)} %item_ref.9) | copy-start | bytes 1540
  10.4 64.0 %collective-permute-start.2 = (bf16[512,640]{1,0:T(8,128)(2,1)S(1)}, bf16[512,640]{1,0:T(8,128)(2,1)S(1)}, u32[]{:S(2)}, u32[]{:S(2)}) collective-permute-start(bf16[512,640]{1,0:T(8,128)(2,1)S(1)} %pad_maximum_fusion.rest_1_.b3), channel_id=1, source_target_pairs={{0,8},{4,12},{8,16},{12,20},{16,24},{20,28},{24,32},{28,36},{32,40... | collective-permute-start | bytes 1966088 | tf_op jit(solution)/shard_map/ppermute | solution.py:50
  13.5 60.9 %collective-permute-start.3 = (bf16[512,640]{1,0:T(8,128)(2,1)S(1)}, bf16[512,640]{1,0:T(8,128)(2,1)S(1)}, u32[]{:S(2)}, u32[]{:S(2)}) collective-permute-start(bf16[512,640]{1,0:T(8,128)(2,1)S(1)} %pad_maximum_fusion.rest_1_.b3), channel_id=1, source_target_pairs={{8,0},{12,4},{16,8},{20,12},{24,16},{28,20},{32,24},{36,28},{40,32... | collective-permute-start | bytes 1966088 | tf_op jit(solution)/shard_map/ppermute | solution.py:50
  19.9 54.5 %collective-permute-start.4 = (bf16[512,640]{1,0:T(8,128)(2,1)S(1)}, bf16[512,640]{1,0:T(8,128)(2,1)S(1)}, u32[]{:S(2)}, u32[]{:S(2)}) collective-permute-start(bf16[512,640]{1,0:T(8,128)(2,1)S(1)} %pad_maximum_fusion.rest_1_.b3), channel_id=1, source_target_pairs={{0,24},{4,28},{8,32},{12,36},{16,40},{20,44},{24,48},{28,52},{32,5... | collective-permute-start | bytes 1966088 | tf_op jit(solution)/shard_map/ppermute | solution.py:50
  21.8 52.6 %collective-permute-start.5 = (bf16[512,640]{1,0:T(8,128)(2,1)S(1)}, bf16[512,640]{1,0:T(8,128)(2,1)}, u32[]{:S(2)}, u32[]{:S(2)}) collective-permute-start(bf16[512,640]{1,0:T(8,128)(2,1)S(1)} %pad_maximum_fusion.rest_1_.b3), channel_id=1, source_target_pairs={{24,0},{28,4},{32,8},{36,12},{40,16},{44,20},{48,24},{52,28},{56,3... | collective-permute-start | bytes 1966088 | tf_op jit(solution)/shard_map/ppermute | solution.py:50
  28.2 4.2 %collective-permute-start = (f32[2,128]{1,0:T(2,128)S(1)}, f32[2,128]{1,0:T(2,128)S(1)}, u32[]{:S(2)}, u32[]{:S(2)}) collective-permute-start(f32[2,128]{1,0:T(2,128)S(1)} %slice.42), channel_id=1, source_target_pairs={{0,4},{4,0},{8,12},{12,8},{16,20},{20,16},{24,28},{28,24},{32,36},... | collective-permute-start | bytes 3080 | tf_op jit(solution)/shard_map/ppermute | solution.py:57
  60.9 8.8 %collective-permute-start.6 = (f32[2,128]{1,0:T(2,128)}, f32[2,128]{1,0:T(2,128)}, u32[]{:S(2)}, u32[]{:S(2)}) collective-permute-start(f32[2,128]{1,0:T(2,128)} %pad_maximum_fusion.6), channel_id=1, source_target_pairs={{0,8},{4,12},{8,16},{12,20},{16,24},{20,28},{24,32},{28,36},{32,40... | collective-permute-start | bytes 3080 | tf_op jit(solution)/shard_map/ppermute | solution.py:50
  69.8 4.6 %collective-permute-start.7 = (f32[2,128]{1,0:T(2,128)}, f32[2,128]{1,0:T(2,128)}, u32[]{:S(2)}, u32[]{:S(2)}) collective-permute-start(f32[2,128]{1,0:T(2,128)} %pad_maximum_fusion.6), channel_id=1, source_target_pairs={{8,0},{12,4},{16,8},{20,12},{24,16},{28,20},{32,24},{36,28},{40,32... | collective-permute-start | bytes 3080 | tf_op jit(solution)/shard_map/ppermute | solution.py:50
  74.4 22.8 %collective-permute-start.10 = (bf16[512,640]{1,0:T(8,128)(2,1)S(1)}, bf16[512,640]{1,0:T(8,128)(2,1)S(1)}, u32[]{:S(2)}, u32[]{:S(2)}) collective-permute-start(bf16[512,640]{1,0:T(8,128)(2,1)S(1)} %collective-permute-done.2.rest_0_.b2), channel_id=1, source_target_pairs={{0,8},{4,12},{8,16},{12,20},{16,24},{20,28},{24,32},{28,36},{32,40... | collective-permute-start | bytes 1966088 | tf_op jit(solution)/shard_map/ppermute | solution.py:50
  77.7 19.5 %collective-permute-start.11 = (bf16[512,640]{1,0:T(8,128)(2,1)S(1)}, bf16[512,640]{1,0:T(8,128)(2,1)S(1)}, u32[]{:S(2)}, u32[]{:S(2)}) collective-permute-start(bf16[512,640]{1,0:T(8,128)(2,1)S(1)} %collective-permute-done.3.rest_2_.b4), channel_id=1, source_target_pairs={{8,0},{12,4},{16,8},{20,12},{24,16},{28,20},{32,24},{36,28},{40,32... | collective-permute-start | bytes 1966088 | tf_op jit(solution)/shard_map/ppermute | solution.py:50
  86.4 9.6 %collective-permute-start.9 = (f32[4,128]{1,0:T(4,128)S(1)}, f32[4,128]{1,0:T(4,128)S(1)}, u32[]{:S(2)}, u32[]{:S(2)}) collective-permute-start(f32[4,128]{1,0:T(4,128)S(1)} %get-tuple-element.30), channel_id=1, source_target_pairs={{16,0},{20,4},{24,8},{28,12},{32,16},{36,20},{40,24},{44,28},{48,3... | collective-permute-start | bytes 6152 | tf_op jit(solution)/shard_map/ppermute | solution.py:50
  88.4 8.8 %collective-permute-start.8 = (f32[4,128]{1,0:T(4,128)S(1)}, f32[4,128]{1,0:T(4,128)S(1)}, u32[]{:S(2)}, u32[]{:S(2)}) collective-permute-start(f32[4,128]{1,0:T(4,128)S(1)} %get-tuple-element.29), channel_id=1, source_target_pairs={{0,16},{4,20},{8,24},{12,28},{16,32},{20,36},{24,40},{28,44},{32,4... | collective-permute-start | bytes 6152 | tf_op jit(solution)/shard_map/ppermute | solution.py:50
  97.2 1.3 %copy-start.12 = (s32[128]{0:T(128)S(1)}, s32[128]{0:T(128)}, u32[]{:S(2)}) copy-start(s32[128]{0:T(128)} %count_ref.3) | copy-start | bytes 1540
  98.5 12.6 %copy-start.17 = (f32[1280]{0:T(1024)S(1)}, f32[1280]{0:T(1024)}, u32[]{:S(2)}) copy-start(f32[1280]{0:T(1024)} %param.23) | copy-start | bytes 15364
  98.5 12.6 %copy-start.18 = (f32[1280]{0:T(1024)S(1)}, f32[1280]{0:T(1024)}, u32[]{:S(2)}) copy-start(f32[1280]{0:T(1024)} %param.24) | copy-start | bytes 15364
  98.5 12.6 %copy-start.3 = (bf16[256,1280]{1,0:T(8,128)(2,1)S(1)}, bf16[256,1280]{1,0:T(8,128)(2,1)}, u32[]{:S(2)}) copy-start(bf16[256,1280]{1,0:T(8,128)(2,1)} %k_ref.3) | copy-start | bytes 1966084
  98.5 12.6 %copy-start.5 = (bf16[128,1280]{1,0:T(8,128)(2,1)S(1)}, bf16[128,1280]{1,0:T(8,128)(2,1)}, u32[]{:S(2)}) copy-start(bf16[128,1280]{1,0:T(8,128)(2,1)} %q_ref.3) | copy-start | bytes 983044
  98.5 12.6 %copy-start.6 = (bf16[256,1280]{1,0:T(8,128)(2,1)S(1)}, bf16[256,1280]{1,0:T(8,128)(2,1)}, u32[]{:S(2)}) copy-start(bf16[256,1280]{1,0:T(8,128)(2,1)} %v_ref.3) | copy-start | bytes 1966084
  98.5 12.6 %copy-start.13 = (s32[128]{0:T(128)S(1)}, s32[128]{0:T(128)}, u32[]{:S(2)}) copy-start(s32[128]{0:T(128)} %len_ref.1) | copy-start | bytes 1540
  101.2 15.2 %collective-permute-start.12 = (f32[128,640]{1,0:T(8,128)S(1)}, f32[128,640]{1,0:T(8,128)S(1)}, u32[]{:S(2)}, u32[]{:S(2)}) collective-permute-start(f32[128,640]{1,0:T(8,128)S(1)} %shard_map.149), channel_id=1, source_target_pairs={{0,4},{4,0},{8,12},{12,8},{16,20},{20,16},{24,28},{28,24},{32,36},... | collective-permute-start | bytes 983048 | tf_op jit(solution)/shard_map/ppermute | solution.py:57
  (8 other events, 7.5 us)

commit v3 on v2

--- a/solution.py
+++ b/solution.py
@@ -71,7 +71,20 @@
     return lax.broadcasted_iota(jnp.int32, shape, 1) < count
 
 
-def pack_kernel(here_ref, q_ref, k_ref, v_ref, c_ref, t_ref, mine_ref, theirs_ref, sums_ref):
+def pack_kernel(
+    here_ref, q_hbm, k_hbm, v_hbm, c_hbm, t_hbm, kv_ref, theirs_ref, q_mine_ref, sums_ref,
+    q_ref, k_ref, v_ref, c_ref, t_ref, arrived
+):
+    pairs = ((k_hbm, k_ref), (v_hbm, v_ref), (q_hbm, q_ref), (c_hbm, c_ref), (t_hbm, t_ref))
+    copies = [
+        pltpu.make_async_copy(source, target, arrived.at[index])
+        for index, (source, target) in enumerate(pairs)
+    ]
+    for copy in copies:
+        copy.start()
+    core = lax.rem(here_ref[0], 2)
+    half = theirs_ref.shape[1]
+
     def total(ref, first):
         rows = None
         for head in range(ref.shape[1] // HD):
@@ -79,19 +92,25 @@
             rows = x * x if rows is None else rows + x * x
         return jnp.sum(jnp.transpose(rows), axis=0, keepdims=True)
 
-    sums_ref[0:1, :] = total(q_ref, 0)
-    sums_ref[1:2, :] = total(k_ref, 0)
+    def split(ref, mine_ref, first, index):
+        low, high = ref[:, :half], ref[:, half:]
+        mine_ref[first : first + ROWS, :] = jnp.where(core == 0, low, high)
+        theirs_ref[index * ROWS : (index + 1) * ROWS, :] = jnp.where(core == 0, high, low)
+
+    sums_ref[...] = jnp.zeros((8, ROWS), jnp.float32)
+    copies[0].wait()
+    split(k_ref, kv_ref, 0, 0)
+    sums_ref[0:1, :] = total(k_ref, 0)
+    copies[1].wait()
+    split(v_ref, kv_ref, ROWS, 1)
+    copies[2].wait()
+    split(q_ref, q_mine_ref, 0, 2)
+    sums_ref[1:2, :] = total(q_ref, 0)
+    copies[3].wait()
     sums_ref[2:3, :] = total(c_ref, 0)
+    copies[4].wait()
     sums_ref[3:4, :] = total(t_ref, 0)
     sums_ref[4:5, :] = total(t_ref, ROWS)
-    sums_ref[5:8, :] = jnp.zeros((3, ROWS), jnp.float32)
-    core = lax.rem(here_ref[0], 2)
-    half = mine_ref.shape[1]
-    for index, ref in enumerate((k_ref, v_ref, q_ref)):
-        rows = slice(index * ROWS, (index + 1) * ROWS)
-        low, high = ref[:, :half], ref[:, half:]
-        mine_ref[rows, :] = jnp.where(core == 0, low, high)
-        theirs_ref[rows, :] = jnp.where(core == 0, high, low)
 
 
 def cross_kernel(item_ref, len_ref, here_ref, sums_ref, q_ref, k_ref, v_ref, qg_ref, kg_ref, out_ref):
@@ -142,26 +161,30 @@
         dest_ref[slot, :, cols] = rotated(x, cosine, sine, even).astype(jnp.bfloat16)
 
 
-def keys_kernel(chips, item_ref, here_ref, sums_ref, gain_ref, cos_ref, sin_ref, *rest):
-    blocks, keys_ref = rest[:-1], rest[-1]
+def keys_kernel(item_ref, here_ref, gain_ref, cos_ref, sin_ref, *rest):
+    blocks, keys_ref = rest[:7], rest[12]
+    left_far, left_sums, own_sums, right_sums, right_far = rest[7:12]
+    sums = (left_far, left_far, left_sums, own_sums, right_sums, right_far, right_far)
+    starts = (0, 8, 0, 0, 0, 0, 8)
     here = here_ref[0]
     core = lax.rem(here, 2)
     left = here - core
     first_a, last_a = extent(item_ref, left)
     first_b, last_b = extent(item_ref, left + 1)
-    for index, (chip, block) in enumerate(zip(chips, blocks)):
-        for parity in range(2):
-            tile = left + 2 * chip + parity
-
-            @pl.when(jnp.logical_and(tile >= first_a, tile <= last_b))
-            def _(index=index, parity=parity, tile=tile, block=block):
-                first = jnp.where(tile <= last_a, first_a, first_b)
-                start = pl.multiple_of((tile - first) * ROWS, ROWS)
-                slot = jnp.where(core == parity, 0, 1)
-                row = pl.multiple_of(slot * 2 * ROWS, 2 * ROWS)
-                factor = by_rows(sums_ref[pl.ds(2 * index + slot, 1), :])
-                rows = pl.ds(row, ROWS)
-                turn(block, rows, factor, gain_ref, cos_ref, sin_ref, start, keys_ref, 2 * index + parity)
+    half = keys_ref.shape[2]
+    for w in range(14):
+        tile = left - 6 + w
+
+        @pl.when(jnp.logical_and(tile >= first_a, tile <= last_b))
+        def _(w=w, tile=tile):
+            chip, parity = w // 2, w % 2
+            first = jnp.where(tile <= last_a, first_a, first_b)
+            start = pl.multiple_of((tile - first) * ROWS, ROWS)
+            slot = jnp.where(core == parity, 0, 1)
+            row = pl.multiple_of(slot * 2 * ROWS, 2 * ROWS)
+            factor = by_rows(sums[chip][pl.ds(starts[chip] + 5 * slot, 1), :])
+            gains = gain_ref.at[:, pl.ds(pl.multiple_of(core * half, HD), half)]
+            turn(blocks[chip], pl.ds(row, ROWS), factor, gains, cos_ref, sin_ref, start, keys_ref, w)
 
 
 def attend_kernel(
@@ -171,8 +194,7 @@
     here_ref,
     sums_ref,
     q_ref,
-    near_ref,
-    far_ref,
+    keys,
     b0,
     b1,
     b2,
@@ -184,22 +206,24 @@
     cos_ref,
     sin_ref,
     out_ref,
-    keys,
     values,
     queries,
     scores,
 ):
     blocks = (b0, b1, b2, b3, b4, b5, b6)
-    heads = q_ref.shape[1] // HD
+    half = q_ref.shape[1]
+    heads = half // HD
     here = here_ref[0]
     core = lax.rem(here, 2)
     left = here - core
     base = left - 6
     tile = left + (1 - core if other else core)
     first, last = extent(item_ref, tile)
-    factor = by_rows(sums_ref[0:1, :])
+    factor = by_rows(sums_ref[6:7, :] if other else sums_ref[1:2, :])
     start = pl.multiple_of((tile - first) * ROWS, ROWS)
-    turn(q_ref, slice(None), factor, gain_ref, cos_ref, sin_ref, start, queries, 0)
+    rows = slice(2 * ROWS, 3 * ROWS) if other else slice(0, ROWS)
+    gains = gain_ref.at[:, pl.ds(pl.multiple_of(core * half, HD), half)]
+    turn(q_ref, rows, factor, gains, cos_ref, sin_ref, start, queries, 0)
     low, high = first - base, last - base + 1
 
     for w in range(14):
@@ -210,7 +234,6 @@
             slot = jnp.where(core == parity, 0, 1)
             row = pl.multiple_of(slot * 2 * ROWS + ROWS, ROWS)
             values[w] = blocks[chip][pl.ds(row, ROWS), :]
-            keys[w] = near_ref[w - 4] if chip in (2, 3, 4) else far_ref[w if chip < 2 else w - 6]
 
     def score(w, tops):
         live = prefix_live((ROWS, ROWS), count_ref[base + w])
@@ -304,35 +327,35 @@
     core = lax.rem(here, 2)
     where = here.reshape(1)
 
-    mine, theirs, sums = call(
+    bf16 = jnp.bfloat16
+    hbm = pl.BlockSpec(memory_space=pltpu.HBM)
+    kv, theirs, q_mine, sums = call(
         pack_kernel,
         (
-            jax.ShapeDtypeStruct((3 * ROWS, half), jnp.bfloat16),
-            jax.ShapeDtypeStruct((3 * ROWS, half), jnp.bfloat16),
+            jax.ShapeDtypeStruct((2 * ROWS, half), bf16),
+            jax.ShapeDtypeStruct((3 * ROWS, half), bf16),
+            jax.ShapeDtypeStruct((ROWS, half), bf16),
             jax.ShapeDtypeStruct((8, ROWS), f32),
         ),
-        [smem] + [vmem] * 5,
+        [smem] + [hbm] * 5,
+        scratch=[pltpu.VMEM((ROWS, width), bf16)] * 4
+        + [pltpu.VMEM((2 * ROWS, width), bf16), pltpu.SemaphoreType.DMA((5,))],
     )(where, self_query, self_key, self_value, cross_query, text_key)
     got = swapped(theirs)
     sums = jnp.concatenate([sums[:5], swapped(sums[:2]), sums[7:]])
-    block = jnp.concatenate([mine[: 2 * ROWS], got[: 2 * ROWS]], axis=0)
-    from_left = shifted(block, 2)
-    from_right = shifted(block, -2)
-    from_left3 = shifted(block, 6)
-    from_right3 = shifted(block, -6)
+    block = jnp.concatenate([kv, got[: 2 * ROWS]], axis=0)
+    near = [shifted(block, -2 * chip) for chip in (-1, 1, -3, 3)]
 
     sums = lax.psum(sums, "head")
-    k_sums = jnp.concatenate([sums[1:2], sums[6:7]])
-    left_sums = shifted(k_sums, 2)
-    right_sums = shifted(k_sums, -2)
-
-    from_left, from_right, from_left3, from_right3, left_sums, right_sums = lax.optimization_barrier(
-        (from_left, from_right, from_left3, from_right3, left_sums, right_sums)
-    )
-    from_left2 = shifted(from_left, 2)
-    from_right2 = shifted(from_right, -2)
-    left_far = shifted(jnp.concatenate([left_sums, k_sums]), 4)
-    right_far = shifted(jnp.concatenate([k_sums, right_sums]), -4)
+    left_sums = shifted(sums, 2)
+    right_sums = shifted(sums, -2)
+    left, right, left3, right3, left_sums, right_sums = lax.optimization_barrier(
+        (*near, left_sums, right_sums)
+    )
+    left2 = shifted(left, 2)
+    right2 = shifted(right, -2)
+    left_far = shifted(jnp.concatenate([left_sums, sums]), 4)
+    right_far = shifted(jnp.concatenate([sums, right_sums]), -4)
 
     text_out = call(
         cross_kernel, jax.ShapeDtypeStruct((ROWS, width), f32), [smem] * 3 + [vmem] * 6, flops=400000000
@@ -347,36 +370,29 @@
         cross_gain[None, :],
         text_gain[None, :],
     )
+    q_gain, k_gain = query_gain[None, :], key_gain[None, :]
+    left_far, right_far, text_out, q_gain, k_gain = lax.optimization_barrier(
+        (left_far, right_far, text_out, q_gain, k_gain)
+    )
+    all_sums = [left_far, left_sums, sums, right_sums, right_far]
 
     cosine, sine = (jnp.asarray(t) for t in rope_tables())
-    my_gain = lax.dynamic_slice_in_dim(jnp.stack([query_gain, key_gain]), core * half, half, 1)
-
-    def turned(chips, block_sums, blocks):
-        return call(
-            functools.partial(keys_kernel, chips),
-            jax.ShapeDtypeStruct((2 * len(chips), ROWS, half), jnp.bfloat16),
-            [smem] * 2 + [vmem] * (4 + len(chips)),
-            flops=200000000,
-        )(tile_item, where, block_sums, my_gain[1:2], cosine, sine, *blocks)
-
-    near = turned(
-        (-1, 0, 1), jnp.concatenate([left_sums, k_sums, right_sums]), (from_left, block, from_right)
-    )
-    far = turned(
-        (-3, -2, 2, 3),
-        jnp.concatenate([left_far, right_far]),
-        (from_left3, from_left2, from_right2, from_right3),
-    )
-
-    def attended(other, query, query_sums):
+    blocks = [left3, left2, left, block, right, right2, right3]
+    keys = call(
+        keys_kernel,
+        jax.ShapeDtypeStruct((14, ROWS, half), bf16),
+        [smem] * 2 + [vmem] * 15,
+        flops=200000000,
+    )(tile_item, where, k_gain, cosine, sine, *blocks, *all_sums)
+
+    def attended(other, query):
         return call(
             functools.partial(attend_kernel, other),
             jax.ShapeDtypeStruct((ROWS, half), f32),
-            [smem] * 3 + [vmem] * 14,
+            [smem] * 3 + [vmem] * 13,
             scratch=[
-                pltpu.VMEM((14, ROWS, half), jnp.bfloat16),
-                pltpu.VMEM((14, ROWS, half), jnp.bfloat16),
-                pltpu.VMEM((1, ROWS, half), jnp.bfloat16),
+                pltpu.VMEM((14, ROWS, half), bf16),
+                pltpu.VMEM((1, ROWS, half), bf16),
                 pltpu.VMEM((SPAN, ROWS, half), f32),
             ],
             flops=300000000,
@@ -384,26 +400,19 @@
             tile_item,
             row_count,
             where,
-            query_sums,
+            sums,
             query,
-            near,
-            far,
-            from_left3,
-            from_left2,
-            from_left,
-            block,
-            from_right,
-            from_right2,
-            from_right3,
-            my_gain[0:1],
+            keys,
+            *blocks,
+            q_gain,
             cosine,
             sine,
         )
 
-    rest = swapped(attended(True, got[2 * ROWS :], sums[5:6]))
-    own = attended(False, mine[2 * ROWS :], sums[0:1])
+    rest = swapped(attended(True, got))
+    own = attended(False, q_mine)
     return call(
-        join_kernel, jax.ShapeDtypeStruct((ROWS, width), jnp.bfloat16), [smem] + [vmem] * 3
+        join_kernel, jax.ShapeDtypeStruct((ROWS, width), bf16), [smem] + [vmem] * 3
     )(where, own, rest, text_out)
 
 

time: 118 us -> 119 us (level)
  the two profiles are of different devices: /device:TPU:33 before, /device:TPU:61 now
where the time goes in v3:
time: 119 us; the launch traced here: 118 us
  starting transfers between devices  56.8 us (48%)
  waiting for transfers between devices  19.8 us (17%)
  blocking collectives  18.5 us (16%)
  Pallas kernels  13.4 us (11%)
  local copies, waits for them, and re-layouts  8.99 us (8%)
    ppermute x10, starting transfers between devices, shifted(): lax.ppermute(value, 'tile', [(i, i + by) for i in range(peers) if 0 <= i...  41.8 us
    psum x1, blocking collectives, per_device(): sums = lax.psum(sums, 'head')  18.5 us
    ppermute x10, waiting for transfers between devices, shifted(): lax.ppermute(value, 'tile', [(i, i + by) for i in range(peers) if 0 <= i...  17.6 us
    ppermute x3, starting transfers between devices, swapped(): return lax.ppermute(value, 'tile', [(i, i ^ 1) for i in range(peers)])  15 us
    unnamed x38, local copies, waits for them, and re-layouts  8.93 us
    pallas_call x2, Pallas kernels, attended(): call(functools.partial(attend_kernel, other), jax.ShapeDtypeStruct((ROWS,...  6.58 us
    pallas_call x1, Pallas kernels, per_device(): call(keys_kernel, jax.ShapeDtypeStruct((14, ROWS, half), bf16), [smem] *...  3.12 us
  transfers between devices with their start and end apart: 13, of which 5 were waited for; matrix products, arithmetic and copies ran while one was open for 0% of the time, Pallas kernels for 4%

profile of v3, /device:TPU:61, one launch (start us, length us, event | category | flops | bytes accessed | tf_op | source)
XLA Modules:
  0.0 118.0 jit_solution(17511743930047671744)
XLA Ops:
  0.0 1.1 copy-done.2
  5.0 1.4 %shard_map.145 = (bf16[256,640]{1,0:T(8,128)(2,1)S(1)}, bf16[384,640]{1,0:T(8,128)(2,1)S(1)}, bf16[128,640]{1,0:T(8,128)(2,1)S(1)}, f32[8,128]{1,0:T(8,128)S(1)}) custom-call(s32[1]{0:T(128)} %bitcast.here_ref, bf16[128,1280]{1,0:T(8,128)(2,1)S(1)} %copy-done.9, bf16[128,1280]{1,0:T(8,128)(2,1)S(1)} %copy-done.10, bf16[128,1280]{1,0:T(8,128)(2,1)S(1)} %copy-done.11, ...), custom_call_target="tpu_custom_call" | custom-call | flops 1000000 | bytes 4000000 | tf_op jit(solution)/shard_map/pallas_call | solution.py:332
  6.4 2.7 %collective-permute-start.1 = (bf16[384,640]{1,0:T(8,128)(2,1)S(1)}, bf16[384,640]{1,0:T(8,128)(2,1)S(1)}, u32[]{:S(2)}, u32[]{:S(2)}) collective-permute-start(bf16[384,640]{1,0:T(8,128)(2,1)S(1)} %get-tuple-element.23), channel_id=1, source_target_pairs={{0,4},{4,0},{8,12},{12,8},{16,20},{20,16},{24,28},{28,24},{32,36},... | collective-permute-start | bytes 1474568 | tf_op jit(solution)/shard_map/ppermute | solution.py:57
  9.2 1.5 %collective-permute-done.1.q_ref = bf16[384,640]{1,0:T(8,128)(2,1)S(1)} collective-permute-done((bf16[384,640]{1,0:T(8,128)(2,1)S(1)}, bf16[384,640]{1,0:T(8,128)(2,1)S(1)}, u32[]{:S(2)}, u32[]{:S(2)}) %collective-permute-start.1) | collective-permute-done | bytes 491552 | tf_op jit(solution)/shard_map/ppermute | solution.py:57
  11.5 3.0 %collective-permute-start.5 = (bf16[512,640]{1,0:T(8,128)(2,1)S(1)}, bf16[512,640]{1,0:T(8,128)(2,1)S(1)}, u32[]{:S(2)}, u32[]{:S(2)}) collective-permute-start(bf16[512,640]{1,0:T(8,128)(2,1)S(1)} %pad_maximum_fusion.rest_3_.b3), channel_id=1, source_target_pairs={{24,0},{28,4},{32,8},{36,12},{40,16},{44,20},{48,24},{52,28},{56,3... | collective-permute-start | bytes 1966088 | tf_op jit(solution)/shard_map/ppermute | solution.py:50
  14.5 5.3 %collective-permute-start.4 = (bf16[512,640]{1,0:T(8,128)(2,1)S(1)}, bf16[512,640]{1,0:T(8,128)(2,1)S(1)}, u32[]{:S(2)}, u32[]{:S(2)}) collective-permute-start(bf16[512,640]{1,0:T(8,128)(2,1)S(1)} %pad_maximum_fusion.rest_3_.b3), channel_id=1, source_target_pairs={{0,24},{4,28},{8,32},{12,36},{16,40},{20,44},{24,48},{28,52},{32,5... | collective-permute-start | bytes 1966088 | tf_op jit(solution)/shard_map/ppermute | solution.py:50
  19.8 2.2 %collective-permute-start.3 = (bf16[512,640]{1,0:T(8,128)(2,1)S(1)}, bf16[512,640]{1,0:T(8,128)(2,1)S(1)}, u32[]{:S(2)}, u32[]{:S(2)}) collective-permute-start(bf16[512,640]{1,0:T(8,128)(2,1)S(1)} %pad_maximum_fusion.rest_3_.b3), channel_id=1, source_target_pairs={{8,0},{12,4},{16,8},{20,12},{24,16},{28,20},{32,24},{36,28},{40,32... | collective-permute-start | bytes 1966088 | tf_op jit(solution)/shard_map/ppermute | solution.py:50
  22.0 3.1 %collective-permute-start.2 = (bf16[512,640]{1,0:T(8,128)(2,1)S(1)}, bf16[512,640]{1,0:T(8,128)(2,1)S(1)}, u32[]{:S(2)}, u32[]{:S(2)}) collective-permute-start(bf16[512,640]{1,0:T(8,128)(2,1)S(1)} %pad_maximum_fusion.rest_3_.b3), channel_id=1, source_target_pairs={{0,8},{4,12},{8,16},{12,20},{16,24},{20,28},{24,32},{28,36},{32,40... | collective-permute-start | bytes 1966088 | tf_op jit(solution)/shard_map/ppermute | solution.py:50
  25.1 3.4 %collective-permute-start = (f32[2,128]{1,0:T(2,128)S(1)}, f32[2,128]{1,0:T(2,128)S(1)}, u32[]{:S(2)}, u32[]{:S(2)}) collective-permute-start(f32[2,128]{1,0:T(2,128)S(1)} %slice.13), channel_id=1, source_target_pairs={{0,4},{4,0},{8,12},{12,8},{16,20},{20,16},{24,28},{28,24},{32,36},... | collective-permute-start | bytes 3080 | tf_op jit(solution)/shard_map/ppermute | solution.py:57
  29.3 18.5 %psum.7.sums_ref.rest_9_ = f32[8,128]{1,0:T(8,128)S(1)} all-reduce(f32[8,128]{1,0:T(8,128)S(1)} %pad_maximum_fusion.3), channel_id=1, replica_groups=mesh['tile'=128,'head'=4] {'head'}, use_global_device_ids=true, to_apply=%region_0.0 | all-reduce | flops 1024 | bytes 8192 | tf_op jit(solution)/shard_map/psum | solution.py:349
  47.8 2.3 %collective-permute-start.7 = (f32[8,128]{1,0:T(8,128)S(1)}, f32[8,128]{1,0:T(8,128)S(1)}, u32[]{:S(2)}, u32[]{:S(2)}) collective-permute-start(f32[8,128]{1,0:T(8,128)S(1)} %psum.7.sums_ref.rest_9_), channel_id=1, source_target_pairs={{8,0},{12,4},{16,8},{20,12},{24,16},{28,20},{32,24},{36,28},{40,32... | collective-permute-start | bytes 12296 | tf_op jit(solution)/shard_map/ppermute | solution.py:50
  50.1 15.9 %collective-permute-done.7.rest_10_ = f32[8,128]{1,0:T(8,128)S(1)} collective-permute-done((f32[8,128]{1,0:T(8,128)S(1)}, f32[8,128]{1,0:T(8,128)S(1)}, u32[]{:S(2)}, u32[]{:S(2)}) %collective-permute-start.7) | collective-permute-done | bytes 4128 | tf_op jit(solution)/shard_map/ppermute | solution.py:50
  66.0 7.6 %collective-permute-start.6 = (f32[8,128]{1,0:T(8,128)S(1)}, f32[8,128]{1,0:T(8,128)S(1)}, u32[]{:S(2)}, u32[]{:S(2)}) collective-permute-start(f32[8,128]{1,0:T(8,128)S(1)} %psum.7.sums_ref.rest_9_), channel_id=1, source_target_pairs={{0,8},{4,12},{8,16},{12,20},{16,24},{20,28},{24,32},{28,36},{32,40... | collective-permute-start | bytes 12296 | tf_op jit(solution)/shard_map/ppermute | solution.py:50
  74.3 3.6 %collective-permute-start.10 = (bf16[512,640]{1,0:T(8,128)(2,1)S(1)}, bf16[512,640]{1,0:T(8,128)(2,1)S(1)}, u32[]{:S(2)}, u32[]{:S(2)}) collective-permute-start(bf16[512,640]{1,0:T(8,128)(2,1)S(1)} %collective-permute-done.2.rest_2_.b2), channel_id=1, source_target_pairs={{0,8},{4,12},{8,16},{12,20},{16,24},{20,28},{24,32},{28,36},{32,40... | collective-permute-start | bytes 1966088 | tf_op jit(solution)/shard_map/ppermute | solution.py:50
  77.9 1.9 %collective-permute-start.11 = (bf16[512,640]{1,0:T(8,128)(2,1)S(1)}, bf16[512,640]{1,0:T(8,128)(2,1)S(1)}, u32[]{:S(2)}, u32[]{:S(2)}) collective-permute-start(bf16[512,640]{1,0:T(8,128)(2,1)S(1)} %collective-permute-done.3.rest_4_.b4), channel_id=1, source_target_pairs={{8,0},{12,4},{16,8},{20,12},{24,16},{28,20},{32,24},{36,28},{40,32... | collective-permute-start | bytes 1966088 | tf_op jit(solution)/shard_map/ppermute | solution.py:50
  79.9 1.9 %collective-permute-start.9 = (f32[16,128]{1,0:T(8,128)S(1)}, f32[16,128]{1,0:T(8,128)S(1)}, u32[]{:S(2)}, u32[]{:S(2)}) collective-permute-start(f32[16,128]{1,0:T(8,128)S(1)} %get-tuple-element.35), channel_id=1, source_target_pairs={{16,0},{20,4},{24,8},{28,12},{32,16},{36,20},{40,24},{44,28},{48,3... | collective-permute-start | bytes 24584 | tf_op jit(solution)/shard_map/ppermute | solution.py:50
  81.9 10.9 %collective-permute-start.8 = (f32[16,128]{1,0:T(8,128)S(1)}, f32[16,128]{1,0:T(8,128)S(1)}, u32[]{:S(2)}, u32[]{:S(2)}) collective-permute-start(f32[16,128]{1,0:T(8,128)S(1)} %get-tuple-element.36), channel_id=1, source_target_pairs={{0,16},{4,20},{8,24},{12,28},{16,32},{20,36},{24,40},{28,44},{32,4... | collective-permute-start | bytes 24584 | tf_op jit(solution)/shard_map/ppermute | solution.py:50
  92.8 1.1 copy-done.3
  94.9 1.1 copy-done.8
  96.0 1.6 %shard_map.146.text_ref = f32[128,1280]{1,0:T(8,128)S(1)} custom-call(s32[128]{0:T(128)S(1)} %copy-done.12, s32[128]{0:T(128)S(1)} %copy-done.14, s32[1]{0:T(128)} %bitcast.here_ref, f32[8,128]{1,0:T(8,128)S(1)} %psum.7.sums_ref.rest_9_, bf16[128,1280]{1,0:T(8,128)(2,1)S(1)} %copy-done.7, bf16[256,1280]{1,0:T(8,128)(2,1)S(1)} %copy-done.3, ...), custom_call_target="tpu_custom_call" | custom-call | flops 400000000 | bytes 4000000 | tf_op jit(solution)/shard_map/pallas_call | solution.py:360
  98.5 3.1 %shard_map.147.keys = bf16[14,128,640]{2,1,0:T(8,128)(2,1)S(1)} custom-call(s32[128]{0:T(128)S(1)} %copy-done.12, s32[1]{0:T(128)} %bitcast.here_ref, f32[1,1280]{1,0:T(1,128)S(1)} %broadcast_in_dim.15.gain_ref, f32[896,128]{1,0:T(8,128)S(1)} %copy-done.1, f32[896,128]{1,0:T(8,128)S(1)} %copy-done, bf16[512,640]{1,0:T(8,128)(2,1)S(1)} %collective-permute-done.4.rest_0_.b0, ...), custom_call_target="tpu_custom_call" | custom-call | flops 200000000 | bytes 4000000 | tf_op jit(solution)/shard_map/pallas_call | solution.py:381
  101.7 3.0 %shard_map.149 = f32[128,640]{1,0:T(8,128)S(1)} custom-call(s32[128]{0:T(128)S(1)} %copy-done.12, s32[128]{0:T(128)S(1)} %copy-done.13, s32[1]{0:T(128)} %bitcast.here_ref, f32[8,128]{1,0:T(8,128)S(1)} %psum.7.sums_ref.rest_9_, bf16[384,640]{1,0:T(8,128)(2,1)S(1)} %copy-done.5, bf16[14,128,640]{2,1,0:T(8,128)(2,1)S(1)} %shard_map.147.keys, ...), custom_call_target="tpu_custom_call" | custom-call | flops 300000000 | bytes 4000000 | tf_op jit(solution)/shard_map/pallas_call | solution.py:389
  104.7 8.8 %collective-permute-start.12 = (f32[128,640]{1,0:T(8,128)S(1)}, f32[128,640]{1,0:T(8,128)S(1)}, u32[]{:S(2)}, u32[]{:S(2)}) collective-permute-start(f32[128,640]{1,0:T(8,128)S(1)} %shard_map.149), channel_id=1, source_target_pairs={{0,4},{4,0},{8,12},{12,8},{16,20},{20,16},{24,28},{28,24},{32,36},... | collective-permute-start | bytes 983048 | tf_op jit(solution)/shard_map/ppermute | solution.py:57
  113.6 3.6 %shard_map.148.own_ref = f32[128,640]{1,0:T(8,128)S(1)} custom-call(s32[128]{0:T(128)S(1)} %copy-done.12, s32[128]{0:T(128)S(1)} %copy-done.13, s32[1]{0:T(128)} %bitcast.here_ref, f32[8,128]{1,0:T(8,128)S(1)} %psum.7.sums_ref.rest_9_, bf16[128,640]{1,0:T(8,128)(2,1)S(1)} %get-tuple-element.21.q_ref, bf16[14,128,640]{2,1,0:T(8,128)(2,1)S(1)} %shard_map.147.keys, ...), custom_call_target="tpu_custom_call" | custom-call | flops 300000000 | bytes 4000000 | tf_op jit(solution)/shard_map/pallas_call | solution.py:389
  (57 shorter events, 9.1 us)
Async XLA Ops:
  6.4 73.5 %copy-start.15 = (f32[1280]{0:T(1024)S(1)}, f32[1280]{0:T(1024)}, u32[]{:S(2)}) copy-start(f32[1280]{0:T(1024)} %param.21) | copy-start | bytes 15364
  6.4 73.5 %copy-start.16 = (f32[1280]{0:T(1024)S(1)}, f32[1280]{0:T(1024)}, u32[]{:S(2)}) copy-start(f32[1280]{0:T(1024)} %param.22) | copy-start | bytes 15364
  6.4 73.5 %copy-start.17 = (f32[1280]{0:T(1024)S(1)}, f32[1280]{0:T(1024)}, u32[]{:S(2)}) copy-start(f32[1280]{0:T(1024)} %param.23) | copy-start | bytes 15364
  6.4 73.5 %copy-start.18 = (f32[1280]{0:T(1024)S(1)}, f32[1280]{0:T(1024)}, u32[]{:S(2)}) copy-start(f32[1280]{0:T(1024)} %param.24) | copy-start | bytes 15364
  6.4 86.4 %copy-start.12 = (s32[128]{0:T(128)S(1)}, s32[128]{0:T(128)}, u32[]{:S(2)}) copy-start(s32[128]{0:T(128)} %item_ref.7) | copy-start | bytes 1540
  6.4 86.4 %copy-start.14 = (s32[128]{0:T(128)S(1)}, s32[128]{0:T(128)}, u32[]{:S(2)}) copy-start(s32[128]{0:T(128)} %len_ref.1) | copy-start | bytes 1540
  6.4 4.2 %collective-permute-start.1 = (bf16[384,640]{1,0:T(8,128)(2,1)S(1)}, bf16[384,640]{1,0:T(8,128)(2,1)S(1)}, u32[]{:S(2)}, u32[]{:S(2)}) collective-permute-start(bf16[384,640]{1,0:T(8,128)(2,1)S(1)} %get-tuple-element.23), channel_id=1, source_target_pairs={{0,4},{4,0},{8,12},{12,8},{16,20},{20,16},{24,28},{28,24},{32,36},... | collective-permute-start | bytes 1474568 | tf_op jit(solution)/shard_map/ppermute | solution.py:57
  11.5 62.8 %collective-permute-start.5 = (bf16[512,640]{1,0:T(8,128)(2,1)S(1)}, bf16[512,640]{1,0:T(8,128)(2,1)S(1)}, u32[]{:S(2)}, u32[]{:S(2)}) collective-permute-start(bf16[512,640]{1,0:T(8,128)(2,1)S(1)} %pad_maximum_fusion.rest_3_.b3), channel_id=1, source_target_pairs={{24,0},{28,4},{32,8},{36,12},{40,16},{44,20},{48,24},{52,28},{56,3... | collective-permute-start | bytes 1966088 | tf_op jit(solution)/shard_map/ppermute | solution.py:50
  14.5 59.8 %collective-permute-start.4 = (bf16[512,640]{1,0:T(8,128)(2,1)S(1)}, bf16[512,640]{1,0:T(8,128)(2,1)S(1)}, u32[]{:S(2)}, u32[]{:S(2)}) collective-permute-start(bf16[512,640]{1,0:T(8,128)(2,1)S(1)} %pad_maximum_fusion.rest_3_.b3), channel_id=1, source_target_pairs={{0,24},{4,28},{8,32},{12,36},{16,40},{20,44},{24,48},{28,52},{32,5... | collective-permute-start | bytes 1966088 | tf_op jit(solution)/shard_map/ppermute | solution.py:50
  19.8 54.5 %collective-permute-start.3 = (bf16[512,640]{1,0:T(8,128)(2,1)S(1)}, bf16[512,640]{1,0:T(8,128)(2,1)S(1)}, u32[]{:S(2)}, u32[]{:S(2)}) collective-permute-start(bf16[512,640]{1,0:T(8,128)(2,1)S(1)} %pad_maximum_fusion.rest_3_.b3), channel_id=1, source_target_pairs={{8,0},{12,4},{16,8},{20,12},{24,16},{28,20},{32,24},{36,28},{40,32... | collective-permute-start | bytes 1966088 | tf_op jit(solution)/shard_map/ppermute | solution.py:50
  22.0 52.3 %collective-permute-start.2 = (bf16[512,640]{1,0:T(8,128)(2,1)S(1)}, bf16[512,640]{1,0:T(8,128)(2,1)S(1)}, u32[]{:S(2)}, u32[]{:S(2)}) collective-permute-start(bf16[512,640]{1,0:T(8,128)(2,1)S(1)} %pad_maximum_fusion.rest_3_.b3), channel_id=1, source_target_pairs={{0,8},{4,12},{8,16},{12,20},{16,24},{20,28},{24,32},{28,36},{32,40... | collective-permute-start | bytes 1966088 | tf_op jit(solution)/shard_map/ppermute | solution.py:50
  25.1 4.2 %collective-permute-start = (f32[2,128]{1,0:T(2,128)S(1)}, f32[2,128]{1,0:T(2,128)S(1)}, u32[]{:S(2)}, u32[]{:S(2)}) collective-permute-start(f32[2,128]{1,0:T(2,128)S(1)} %slice.13), channel_id=1, source_target_pairs={{0,4},{4,0},{8,12},{12,8},{16,20},{20,16},{24,28},{28,24},{32,36},... | collective-permute-start | bytes 3080 | tf_op jit(solution)/shard_map/ppermute | solution.py:57
  47.8 50.7 %copy-start = (f32[896,128]{1,0:T(8,128)S(1)}, f32[896,128]{1,0:T(8,128)}, u32[]{:S(2)}) copy-start(f32[896,128]{1,0:T(8,128)} %constant.11.clone.sin_ref) | copy-start | bytes 1376260
  47.8 50.7 %copy-start.1 = (f32[896,128]{1,0:T(8,128)S(1)}, f32[896,128]{1,0:T(8,128)}, u32[]{:S(2)}) copy-start(f32[896,128]{1,0:T(8,128)} %constant.10.clone.cos_ref) | copy-start | bytes 1376260
  47.8 18.2 %collective-permute-start.7 = (f32[8,128]{1,0:T(8,128)S(1)}, f32[8,128]{1,0:T(8,128)S(1)}, u32[]{:S(2)}, u32[]{:S(2)}) collective-permute-start(f32[8,128]{1,0:T(8,128)S(1)} %psum.7.sums_ref.rest_9_), channel_id=1, source_target_pairs={{8,0},{12,4},{16,8},{20,12},{24,16},{28,20},{32,24},{36,28},{40,32... | collective-permute-start | bytes 12296 | tf_op jit(solution)/shard_map/ppermute | solution.py:50
  66.0 8.3 %collective-permute-start.6 = (f32[8,128]{1,0:T(8,128)S(1)}, f32[8,128]{1,0:T(8,128)S(1)}, u32[]{:S(2)}, u32[]{:S(2)}) collective-permute-start(f32[8,128]{1,0:T(8,128)S(1)} %psum.7.sums_ref.rest_9_), channel_id=1, source_target_pairs={{0,8},{4,12},{8,16},{12,20},{16,24},{20,28},{24,32},{28,36},{32,40... | collective-permute-start | bytes 12296 | tf_op jit(solution)/shard_map/ppermute | solution.py:50
  74.3 24.2 %collective-permute-start.10 = (bf16[512,640]{1,0:T(8,128)(2,1)S(1)}, bf16[512,640]{1,0:T(8,128)(2,1)S(1)}, u32[]{:S(2)}, u32[]{:S(2)}) collective-permute-start(bf16[512,640]{1,0:T(8,128)(2,1)S(1)} %collective-permute-done.2.rest_2_.b2), channel_id=1, source_target_pairs={{0,8},{4,12},{8,16},{12,20},{16,24},{20,28},{24,32},{28,36},{32,40... | collective-permute-start | bytes 1966088 | tf_op jit(solution)/shard_map/ppermute | solution.py:50
  77.9 20.6 %collective-permute-start.11 = (bf16[512,640]{1,0:T(8,128)(2,1)S(1)}, bf16[512,640]{1,0:T(8,128)(2,1)S(1)}, u32[]{:S(2)}, u32[]{:S(2)}) collective-permute-start(bf16[512,640]{1,0:T(8,128)(2,1)S(1)} %collective-permute-done.3.rest_4_.b4), channel_id=1, source_target_pairs={{8,0},{12,4},{16,8},{20,12},{24,16},{28,20},{32,24},{36,28},{40,32... | collective-permute-start | bytes 1966088 | tf_op jit(solution)/shard_map/ppermute | solution.py:50
  79.9 18.6 %collective-permute-start.9 = (f32[16,128]{1,0:T(8,128)S(1)}, f32[16,128]{1,0:T(8,128)S(1)}, u32[]{:S(2)}, u32[]{:S(2)}) collective-permute-start(f32[16,128]{1,0:T(8,128)S(1)} %get-tuple-element.35), channel_id=1, source_target_pairs={{16,0},{20,4},{24,8},{28,12},{32,16},{36,20},{40,24},{44,28},{48,3... | collective-permute-start | bytes 24584 | tf_op jit(solution)/shard_map/ppermute | solution.py:50
  81.9 16.6 %collective-permute-start.8 = (f32[16,128]{1,0:T(8,128)S(1)}, f32[16,128]{1,0:T(8,128)S(1)}, u32[]{:S(2)}, u32[]{:S(2)}) collective-permute-start(f32[16,128]{1,0:T(8,128)S(1)} %get-tuple-element.36), channel_id=1, source_target_pairs={{0,16},{4,20},{8,24},{12,28},{16,32},{20,36},{24,40},{28,44},{32,4... | collective-permute-start | bytes 24584 | tf_op jit(solution)/shard_map/ppermute | solution.py:50
  92.8 1.1 copy-start.3
  97.5 4.1 %copy-start.5 = (bf16[384,640]{1,0:T(8,128)(2,1)S(1)}, bf16[384,640]{1,0:T(8,128)(2,1)}, u32[]{:S(2)}) copy-start(bf16[384,640]{1,0:T(8,128)(2,1)} %copy-done.4) | copy-start | bytes 1474564
  97.6 4.1 %copy-start.13 = (s32[128]{0:T(128)S(1)}, s32[128]{0:T(128)}, u32[]{:S(2)}) copy-start(s32[128]{0:T(128)} %count_ref.3) | copy-start | bytes 1540
  104.7 12.4 %collective-permute-start.12 = (f32[128,640]{1,0:T(8,128)S(1)}, f32[128,640]{1,0:T(8,128)S(1)}, u32[]{:S(2)}, u32[]{:S(2)}) collective-permute-start(f32[128,640]{1,0:T(8,128)S(1)} %shard_map.149), channel_id=1, source_target_pairs={{0,4},{4,0},{8,12},{12,8},{16,20},{20,16},{24,28},{28,24},{32,36},... | collective-permute-start | bytes 983048 | tf_op jit(solution)/shard_map/ppermute | solution.py:57
  (8 other events, 7.8 us)

commit v4 on v3

--- a/solution.py
+++ b/solution.py
@@ -18,6 +18,7 @@
 EPSILON = 1e-06
 SCALE = 1.0 / math.sqrt(HD)
 NEG = -1e30
+KEY_LINES = (5, 6, 7, 0, 8, 9, 10)
 
 
 def rope_tables():
@@ -111,6 +112,17 @@
     copies[4].wait()
     sums_ref[3:4, :] = total(t_ref, 0)
     sums_ref[4:5, :] = total(t_ref, ROWS)
+
+
+def table_kernel(own_ref, left_ref, right_ref, left_far_ref, right_far_ref, out_ref):
+    out_ref[0:8, :] = own_ref[...]
+    out_ref[8:16, :] = jnp.zeros((8, ROWS), jnp.float32)
+    out_ref[5:6, :] = left_far_ref[0:1, :]
+    out_ref[6:7, :] = left_far_ref[8:9, :]
+    out_ref[7:8, :] = left_ref[0:1, :]
+    out_ref[8:9, :] = right_ref[0:1, :]
+    out_ref[9:10, :] = right_far_ref[0:1, :]
+    out_ref[10:11, :] = right_far_ref[8:9, :]
 
 
 def cross_kernel(item_ref, len_ref, here_ref, sums_ref, q_ref, k_ref, v_ref, qg_ref, kg_ref, out_ref):
@@ -162,10 +174,7 @@
 
 
 def keys_kernel(item_ref, here_ref, gain_ref, cos_ref, sin_ref, *rest):
-    blocks, keys_ref = rest[:7], rest[12]
-    left_far, left_sums, own_sums, right_sums, right_far = rest[7:12]
-    sums = (left_far, left_far, left_sums, own_sums, right_sums, right_far, right_far)
-    starts = (0, 8, 0, 0, 0, 0, 8)
+    blocks, own_ref, mate_ref, keys_ref = rest[:7], rest[7], rest[8], rest[9]
     here = here_ref[0]
     core = lax.rem(here, 2)
     left = here - core
@@ -182,7 +191,9 @@
             start = pl.multiple_of((tile - first) * ROWS, ROWS)
             slot = jnp.where(core == parity, 0, 1)
             row = pl.multiple_of(slot * 2 * ROWS, 2 * ROWS)
-            factor = by_rows(sums[chip][pl.ds(starts[chip] + 5 * slot, 1), :])
+            line = KEY_LINES[chip]
+            sums = jnp.where(core == parity, own_ref[line : line + 1, :], mate_ref[line : line + 1, :])
+            factor = by_rows(sums)
             gains = gain_ref.at[:, pl.ds(pl.multiple_of(core * half, HD), half)]
             turn(blocks[chip], pl.ds(row, ROWS), factor, gains, cos_ref, sin_ref, start, keys_ref, w)
 
@@ -219,7 +230,7 @@
     base = left - 6
     tile = left + (1 - core if other else core)
     first, last = extent(item_ref, tile)
-    factor = by_rows(sums_ref[6:7, :] if other else sums_ref[1:2, :])
+    factor = by_rows(sums_ref[1:2, :])
     start = pl.multiple_of((tile - first) * ROWS, ROWS)
     rows = slice(2 * ROWS, 3 * ROWS) if other else slice(0, ROWS)
     gains = gain_ref.at[:, pl.ds(pl.multiple_of(core * half, HD), half)]
@@ -340,22 +351,24 @@
         [smem] + [hbm] * 5,
         scratch=[pltpu.VMEM((ROWS, width), bf16)] * 4
         + [pltpu.VMEM((2 * ROWS, width), bf16), pltpu.SemaphoreType.DMA((5,))],
+        limit=60,
     )(where, self_query, self_key, self_value, cross_query, text_key)
     got = swapped(theirs)
-    sums = jnp.concatenate([sums[:5], swapped(sums[:2]), sums[7:]])
-    block = jnp.concatenate([kv, got[: 2 * ROWS]], axis=0)
-    near = [shifted(block, -2 * chip) for chip in (-1, 1, -3, 3)]
-
-    sums = lax.psum(sums, "head")
     left_sums = shifted(sums, 2)
     right_sums = shifted(sums, -2)
-    left, right, left3, right3, left_sums, right_sums = lax.optimization_barrier(
-        (*near, left_sums, right_sums)
-    )
+    block = jnp.concatenate([kv, got[: 2 * ROWS]], axis=0)
+    left_far = shifted(jnp.concatenate([left_sums, sums]), 4)
+    right_far = shifted(jnp.concatenate([sums, right_sums]), -4)
+    table = call(table_kernel, jax.ShapeDtypeStruct((16, ROWS), f32), [vmem] * 5)(
+        sums, left_sums, right_sums, left_far, right_far
+    )
+    block, table = lax.optimization_barrier((block, table))
+    near = [shifted(block, -2 * chip) for chip in (-1, 1, -3, 3)]
+    sums = lax.psum(table, "head")
+    left, right, left3, right3, sums = lax.optimization_barrier((*near, sums))
     left2 = shifted(left, 2)
     right2 = shifted(right, -2)
-    left_far = shifted(jnp.concatenate([left_sums, sums]), 4)
-    right_far = shifted(jnp.concatenate([sums, right_sums]), -4)
+    mate_sums = swapped(sums)
 
     text_out = call(
         cross_kernel, jax.ShapeDtypeStruct((ROWS, width), f32), [smem] * 3 + [vmem] * 6, flops=400000000
@@ -371,21 +384,20 @@
         text_gain[None, :],
     )
     q_gain, k_gain = query_gain[None, :], key_gain[None, :]
-    left_far, right_far, text_out, q_gain, k_gain = lax.optimization_barrier(
-        (left_far, right_far, text_out, q_gain, k_gain)
-    )
-    all_sums = [left_far, left_sums, sums, right_sums, right_far]
+    mate_sums, text_out, q_gain, k_gain = lax.optimization_barrier(
+        (mate_sums, text_out, q_gain, k_gain)
+    )
 
     cosine, sine = (jnp.asarray(t) for t in rope_tables())
     blocks = [left3, left2, left, block, right, right2, right3]
     keys = call(
         keys_kernel,
         jax.ShapeDtypeStruct((14, ROWS, half), bf16),
-        [smem] * 2 + [vmem] * 15,
+        [smem] * 2 + [vmem] * 12,
         flops=200000000,
-    )(tile_item, where, k_gain, cosine, sine, *blocks, *all_sums)
-
-    def attended(other, query):
+    )(tile_item, where, k_gain, cosine, sine, *blocks, sums, mate_sums)
+
+    def attended(other, query, query_sums):
         return call(
             functools.partial(attend_kernel, other),
             jax.ShapeDtypeStruct((ROWS, half), f32),
@@ -400,7 +412,7 @@
             tile_item,
             row_count,
             where,
-            sums,
+            query_sums,
             query,
             keys,
             *blocks,
@@ -409,8 +421,8 @@
             sine,
         )
 
-    rest = swapped(attended(True, got))
-    own = attended(False, q_mine)
+    rest = swapped(attended(True, got, mate_sums))
+    own = attended(False, q_mine, sums)
     return call(
         join_kernel, jax.ShapeDtypeStruct((ROWS, width), bf16), [smem] + [vmem] * 3
     )(where, own, rest, text_out)

time: 119 us -> 116 us (0.975)
  the two profiles are of different devices: /device:TPU:61 before, /device:TPU:31 now
where the time goes in v4:
time: 116 us
  starting transfers between devices  60.3 us (52%)
  blocking collectives  32.7 us (28%)
  Pallas kernels  12.6 us (11%)
  local copies, waits for them, and re-layouts  3.95 us (3%)
  waiting for transfers between devices  3.48 us (3%)
  other arithmetic  1.95 us (2%)
    ppermute x10, starting transfers between devices, shifted(): lax.ppermute(value, 'tile', [(i, i + by) for i in range(peers) if 0 <= i...  42.5 us
    psum x1, blocking collectives, per_device(): sums = lax.psum(table, 'head')  32.7 us
    ppermute x3, starting transfers between devices, swapped(): return lax.ppermute(value, 'tile', [(i, i ^ 1) for i in range(peers)])  17.9 us
    pallas_call x2, Pallas kernels, attended(): call(functools.partial(attend_kernel, other), jax.ShapeDtypeStruct((ROWS,...  6.04 us
    unnamed x32, local copies, waits for them, and re-layouts  3.9 us
    ppermute x10, waiting for transfers between devices, shifted(): lax.ppermute(value, 'tile', [(i, i + by) for i in range(peers) if 0 <= i...  3.48 us
    pallas_call x1, Pallas kernels, per_device(): call(pack_kernel, (jax.ShapeDtypeStruct((2 * ROWS, half), bf16), jax.Shap...  2.47 us
  transfers between devices with their start and end apart: 13, of which 3 were waited for; matrix products, arithmetic and copies ran while one was open for 1% of the time, Pallas kernels for 4%

profile of v4, /device:TPU:31, one launch (start us, length us, event | category | flops | bytes accessed | tf_op | source)
XLA Modules:
  0.0 115.5 jit_solution(15882891163214840671)
XLA Ops:
  0.0 2.5 %shard_map.145 = (bf16[256,640]{1,0:T(8,128)(2,1)}, bf16[384,640]{1,0:T(8,128)(2,1)}, bf16[128,640]{1,0:T(8,128)(2,1)}, f32[8,128]{1,0:T(8,128)}) custom-call(s32[1]{0:T(128)} %bitcast.here_ref, bf16[128,1280]{1,0:T(8,128)(2,1)} %q_hbm.1, bf16[128,1280]{1,0:T(8,128)(2,1)} %k_hbm.1, bf16[128,1280]{1,0:T(8,128)(2,1)} %v_hbm.1, bf16[128,1280]{1,0:T(8,128)(2,1)} %q_ref.1, ...), custom_call_target="tpu_custom_call" | custom-call | flops 1000000 | bytes 4000000 | tf_op jit(solution)/shard_map/pallas_call | solution.py:343
  2.6 2.7 %collective-permute-start = (bf16[384,640]{1,0:T(8,128)(2,1)}, bf16[384,640]{1,0:T(8,128)(2,1)S(1)}, u32[]{:S(2)}, u32[]{:S(2)}) collective-permute-start(bf16[384,640]{1,0:T(8,128)(2,1)} %get-tuple-element.21), channel_id=1, source_target_pairs={{0,4},{4,0},{8,12},{12,8},{16,20},{20,16},{24,28},{28,24},{32,36},... | collective-permute-start | bytes 1474568 | tf_op jit(solution)/shard_map/ppermute | solution.py:58
  5.3 2.5 %collective-permute-start.2 = (f32[8,128]{1,0:T(8,128)}, f32[8,128]{1,0:T(8,128)S(1)}, u32[]{:S(2)}, u32[]{:S(2)}) collective-permute-start(f32[8,128]{1,0:T(8,128)} %get-tuple-element.22.own_ref), channel_id=1, source_target_pairs={{8,0},{12,4},{16,8},{20,12},{24,16},{28,20},{32,24},{36,28},{40,32... | collective-permute-start | bytes 12296 | tf_op jit(solution)/shard_map/ppermute | solution.py:51
  7.7 7.0 %collective-permute-start.1 = (f32[8,128]{1,0:T(8,128)}, f32[8,128]{1,0:T(8,128)S(1)}, u32[]{:S(2)}, u32[]{:S(2)}) collective-permute-start(f32[8,128]{1,0:T(8,128)} %get-tuple-element.22.own_ref), channel_id=1, source_target_pairs={{0,8},{4,12},{8,16},{12,20},{16,24},{20,28},{24,32},{28,36},{32,40... | collective-permute-start | bytes 12296 | tf_op jit(solution)/shard_map/ppermute | solution.py:51
  16.5 1.9 %collective-permute-start.4 = (f32[16,128]{1,0:T(8,128)S(1)}, f32[16,128]{1,0:T(8,128)S(1)}, u32[]{:S(2)}, u32[]{:S(2)}) collective-permute-start(f32[16,128]{1,0:T(8,128)S(1)} %get-tuple-element.35), channel_id=1, source_target_pairs={{16,0},{20,4},{24,8},{28,12},{32,16},{36,20},{40,24},{44,28},{48,3... | collective-permute-start | bytes 24584 | tf_op jit(solution)/shard_map/ppermute | solution.py:51
  18.4 7.9 %collective-permute-start.3 = (f32[16,128]{1,0:T(8,128)S(1)}, f32[16,128]{1,0:T(8,128)S(1)}, u32[]{:S(2)}, u32[]{:S(2)}) collective-permute-start(f32[16,128]{1,0:T(8,128)S(1)} %get-tuple-element.36), channel_id=1, source_target_pairs={{0,16},{4,20},{8,24},{12,28},{16,32},{20,36},{24,40},{28,44},{32,4... | collective-permute-start | bytes 24584 | tf_op jit(solution)/shard_map/ppermute | solution.py:51
  27.8 1.2 %pad_maximum_fusion.rest_3_.b3 = bf16[512,640]{1,0:T(8,128)(2,1)S(1)} fusion(bf16[256,640]{1,0:T(8,128)(2,1)S(1)} %slice.4, bf16[256,640]{1,0:T(8,128)(2,1)} %get-tuple-element.20), kind=kLoop, calls=%fused_computation | loop fusion | flops 1310720 | bytes 1310720 | tf_op jit(solution)/shard_map/concatenate | solution.py:359
  29.0 1.9 %collective-permute-start.8 = (bf16[512,640]{1,0:T(8,128)(2,1)S(1)}, bf16[512,640]{1,0:T(8,128)(2,1)S(1)}, u32[]{:S(2)}, u32[]{:S(2)}) collective-permute-start(bf16[512,640]{1,0:T(8,128)(2,1)S(1)} %pad_maximum_fusion.rest_3_.b3), channel_id=1, source_target_pairs={{24,0},{28,4},{32,8},{36,12},{40,16},{44,20},{48,24},{52,28},{56,3... | collective-permute-start | bytes 1966088 | tf_op jit(solution)/shard_map/ppermute | solution.py:51
  30.9 6.4 %collective-permute-start.7 = (bf16[512,640]{1,0:T(8,128)(2,1)S(1)}, bf16[512,640]{1,0:T(8,128)(2,1)S(1)}, u32[]{:S(2)}, u32[]{:S(2)}) collective-permute-start(bf16[512,640]{1,0:T(8,128)(2,1)S(1)} %pad_maximum_fusion.rest_3_.b3), channel_id=1, source_target_pairs={{0,24},{4,28},{8,32},{12,36},{16,40},{20,44},{24,48},{28,52},{32,5... | collective-permute-start | bytes 1966088 | tf_op jit(solution)/shard_map/ppermute | solution.py:51
  37.3 3.3 %collective-permute-start.6 = (bf16[512,640]{1,0:T(8,128)(2,1)S(1)}, bf16[512,640]{1,0:T(8,128)(2,1)S(1)}, u32[]{:S(2)}, u32[]{:S(2)}) collective-permute-start(bf16[512,640]{1,0:T(8,128)(2,1)S(1)} %pad_maximum_fusion.rest_3_.b3), channel_id=1, source_target_pairs={{8,0},{12,4},{16,8},{20,12},{24,16},{28,20},{32,24},{36,28},{40,32... | collective-permute-start | bytes 1966088 | tf_op jit(solution)/shard_map/ppermute | solution.py:51
  40.7 6.2 %collective-permute-start.5 = (bf16[512,640]{1,0:T(8,128)(2,1)S(1)}, bf16[512,640]{1,0:T(8,128)(2,1)S(1)}, u32[]{:S(2)}, u32[]{:S(2)}) collective-permute-start(bf16[512,640]{1,0:T(8,128)(2,1)S(1)} %pad_maximum_fusion.rest_3_.b3), channel_id=1, source_target_pairs={{0,8},{4,12},{8,16},{12,20},{16,24},{20,28},{24,32},{28,36},{32,40... | collective-permute-start | bytes 1966088 | tf_op jit(solution)/shard_map/ppermute | solution.py:51
  46.8 32.7 %psum.7.sums_ref.rest_7_ = f32[16,128]{1,0:T(8,128)S(1)} all-reduce(f32[16,128]{1,0:T(8,128)S(1)} %shard_map.146), channel_id=1, replica_groups=mesh['tile'=128,'head'=4] {'head'}, use_global_device_ids=true, to_apply=%region_0.0 | all-reduce | flops 2048 | bytes 16384 | tf_op jit(solution)/shard_map/psum | solution.py:367
  79.6 2.1 %collective-permute-start.10 = (bf16[512,640]{1,0:T(8,128)(2,1)S(1)}, bf16[512,640]{1,0:T(8,128)(2,1)S(1)}, u32[]{:S(2)}, u32[]{:S(2)}) collective-permute-start(bf16[512,640]{1,0:T(8,128)(2,1)S(1)} %collective-permute-done.5.rest_2_.b2), channel_id=1, source_target_pairs={{0,8},{4,12},{8,16},{12,20},{16,24},{20,28},{24,32},{28,36},{32,40... | collective-permute-start | bytes 1966088 | tf_op jit(solution)/shard_map/ppermute | solution.py:51
  81.7 3.4 %collective-permute-start.11 = (bf16[512,640]{1,0:T(8,128)(2,1)S(1)}, bf16[512,640]{1,0:T(8,128)(2,1)S(1)}, u32[]{:S(2)}, u32[]{:S(2)}) collective-permute-start(bf16[512,640]{1,0:T(8,128)(2,1)S(1)} %collective-permute-done.6.rest_4_.b4), channel_id=1, source_target_pairs={{8,0},{12,4},{16,8},{20,12},{24,16},{28,20},{32,24},{36,28},{40,32... | collective-permute-start | bytes 1966088 | tf_op jit(solution)/shard_map/ppermute | solution.py:51
  85.2 7.4 %collective-permute-start.9 = (f32[16,128]{1,0:T(8,128)S(1)}, f32[16,128]{1,0:T(8,128)S(1)}, u32[]{:S(2)}, u32[]{:S(2)}) collective-permute-start(f32[16,128]{1,0:T(8,128)S(1)} %psum.7.sums_ref.rest_7_), channel_id=1, source_target_pairs={{0,4},{4,0},{8,12},{12,8},{16,20},{20,16},{24,28},{28,24},{32,36},... | collective-permute-start | bytes 24584 | tf_op jit(solution)/shard_map/ppermute | solution.py:58
  92.6 1.1 copy-done.2
  93.7 1.0 copy-done.5
  94.6 1.1 copy-done.6
  95.7 1.6 %shard_map.147.text_ref = f32[128,1280]{1,0:T(8,128)S(1)} custom-call(s32[128]{0:T(128)S(1)} %copy-done.9, s32[128]{0:T(128)S(1)} %copy-done.11, s32[1]{0:T(128)} %bitcast.here_ref, f32[16,128]{1,0:T(8,128)S(1)} %psum.7.sums_ref.rest_7_, bf16[128,1280]{1,0:T(8,128)(2,1)S(1)} %copy-done.5, bf16[256,1280]{1,0:T(8,128)(2,1)S(1)} %copy-done.2, ...), custom_call_target="tpu_custom_call" | custom-call | flops 400000000 | bytes 4000000 | tf_op jit(solution)/shard_map/pallas_call | solution.py:373
  97.4 1.8 %collective-permute-done.11.rest_5_.b5 = bf16[512,640]{1,0:T(8,128)(2,1)S(1)} collective-permute-done((bf16[512,640]{1,0:T(8,128)(2,1)S(1)}, bf16[512,640]{1,0:T(8,128)(2,1)S(1)}, u32[]{:S(2)}, u32[]{:S(2)}) %collective-permute-start.11) | collective-permute-done | bytes 655392 | tf_op jit(solution)/shard_map/ppermute | solution.py:51
  99.1 1.7 %shard_map.148.keys = bf16[14,128,640]{2,1,0:T(8,128)(2,1)S(1)} custom-call(s32[128]{0:T(128)S(1)} %copy-done.9, s32[1]{0:T(128)} %bitcast.here_ref, f32[1,1280]{1,0:T(1,128)S(1)} %broadcast_in_dim.15.gain_ref, f32[896,128]{1,0:T(8,128)S(1)} %copy-done.1, f32[896,128]{1,0:T(8,128)S(1)} %copy-done, bf16[512,640]{1,0:T(8,128)(2,1)S(1)} %collective-permute-done.7.rest_0_.b0, ...), custom_call_target="tpu_custom_call" | custom-call | flops 200000000 | bytes 4000000 | tf_op jit(solution)/shard_map/pallas_call | solution.py:393
  100.9 3.0 %shard_map.150 = f32[128,640]{1,0:T(8,128)S(1)} custom-call(s32[128]{0:T(128)S(1)} %copy-done.9, s32[128]{0:T(128)S(1)} %copy-done.10, s32[1]{0:T(128)} %bitcast.here_ref, f32[16,128]{1,0:T(8,128)S(1)} %collective-permute-done.9.rest_8_.sums_ref, bf16[384,640]{1,0:T(8,128)(2,1)S(1)} %copy-done.4, bf16[14,128,640]{2,1,0:T(8,128)(2,1)S(1)} %shard_map.148.keys, ...), custom_call_target="tpu_custom_call" | custom-call | flops 300000000 | bytes 4000000 | tf_op jit(solution)/shard_map/pallas_call | solution.py:401
  103.9 7.8 %collective-permute-start.12 = (f32[128,640]{1,0:T(8,128)S(1)}, f32[128,640]{1,0:T(8,128)S(1)}, u32[]{:S(2)}, u32[]{:S(2)}) collective-permute-start(f32[128,640]{1,0:T(8,128)S(1)} %shard_map.150), channel_id=1, source_target_pairs={{0,4},{4,0},{8,12},{12,8},{16,20},{20,16},{24,28},{28,24},{32,36},... | collective-permute-start | bytes 983048 | tf_op jit(solution)/shard_map/ppermute | solution.py:58
  111.7 3.0 %shard_map.149.own_ref = f32[128,640]{1,0:T(8,128)S(1)} custom-call(s32[128]{0:T(128)S(1)} %copy-done.9, s32[128]{0:T(128)S(1)} %copy-done.10, s32[1]{0:T(128)} %bitcast.here_ref, f32[16,128]{1,0:T(8,128)S(1)} %psum.7.sums_ref.rest_7_, bf16[128,640]{1,0:T(8,128)(2,1)S(1)} %copy-done.7, bf16[14,128,640]{2,1,0:T(8,128)(2,1)S(1)} %shard_map.148.keys, ...), custom_call_target="tpu_custom_call" | custom-call | flops 300000000 | bytes 4000000 | tf_op jit(solution)/shard_map/pallas_call | solution.py:401
  (49 shorter events, 4.1 us)
Async XLA Ops:
  2.5 82.6 %copy-start.12 = (f32[1280]{0:T(1024)S(1)}, f32[1280]{0:T(1024)}, u32[]{:S(2)}) copy-start(f32[1280]{0:T(1024)} %param.21) | copy-start | bytes 15364
  2.5 82.6 %copy-start.13 = (f32[1280]{0:T(1024)S(1)}, f32[1280]{0:T(1024)}, u32[]{:S(2)}) copy-start(f32[1280]{0:T(1024)} %param.22) | copy-start | bytes 15364
  2.5 82.6 %copy-start.14 = (f32[1280]{0:T(1024)S(1)}, f32[1280]{0:T(1024)}, u32[]{:S(2)}) copy-start(f32[1280]{0:T(1024)} %param.23) | copy-start | bytes 15364
  2.5 82.6 %copy-start.15 = (f32[1280]{0:T(1024)S(1)}, f32[1280]{0:T(1024)}, u32[]{:S(2)}) copy-start(f32[1280]{0:T(1024)} %param.24) | copy-start | bytes 15364
  2.5 90.0 %copy-start.9 = (s32[128]{0:T(128)S(1)}, s32[128]{0:T(128)}, u32[]{:S(2)}) copy-start(s32[128]{0:T(128)} %item_ref.7) | copy-start | bytes 1540
  2.5 90.0 %copy-start.11 = (s32[128]{0:T(128)S(1)}, s32[128]{0:T(128)}, u32[]{:S(2)}) copy-start(s32[128]{0:T(128)} %len_ref.1) | copy-start | bytes 1540
  2.6 25.2 %collective-permute-start = (bf16[384,640]{1,0:T(8,128)(2,1)}, bf16[384,640]{1,0:T(8,128)(2,1)S(1)}, u32[]{:S(2)}, u32[]{:S(2)}) collective-permute-start(bf16[384,640]{1,0:T(8,128)(2,1)} %get-tuple-element.21), channel_id=1, source_target_pairs={{0,4},{4,0},{8,12},{12,8},{16,20},{20,16},{24,28},{28,24},{32,36},... | collective-permute-start | bytes 1474568 | tf_op jit(solution)/shard_map/ppermute | solution.py:58
  5.3 9.5 %collective-permute-start.2 = (f32[8,128]{1,0:T(8,128)}, f32[8,128]{1,0:T(8,128)S(1)}, u32[]{:S(2)}, u32[]{:S(2)}) collective-permute-start(f32[8,128]{1,0:T(8,128)} %get-tuple-element.22.own_ref), channel_id=1, source_target_pairs={{8,0},{12,4},{16,8},{20,12},{24,16},{28,20},{32,24},{36,28},{40,32... | collective-permute-start | bytes 12296 | tf_op jit(solution)/shard_map/ppermute | solution.py:51
  7.7 8.0 %collective-permute-start.1 = (f32[8,128]{1,0:T(8,128)}, f32[8,128]{1,0:T(8,128)S(1)}, u32[]{:S(2)}, u32[]{:S(2)}) collective-permute-start(f32[8,128]{1,0:T(8,128)} %get-tuple-element.22.own_ref), channel_id=1, source_target_pairs={{0,8},{4,12},{8,16},{12,20},{16,24},{20,28},{24,32},{28,36},{32,40... | collective-permute-start | bytes 12296 | tf_op jit(solution)/shard_map/ppermute | solution.py:51
  16.5 9.8 %collective-permute-start.4 = (f32[16,128]{1,0:T(8,128)S(1)}, f32[16,128]{1,0:T(8,128)S(1)}, u32[]{:S(2)}, u32[]{:S(2)}) collective-permute-start(f32[16,128]{1,0:T(8,128)S(1)} %get-tuple-element.35), channel_id=1, source_target_pairs={{16,0},{20,4},{24,8},{28,12},{32,16},{36,20},{40,24},{44,28},{48,3... | collective-permute-start | bytes 24584 | tf_op jit(solution)/shard_map/ppermute | solution.py:51
  18.4 8.7 %collective-permute-start.3 = (f32[16,128]{1,0:T(8,128)S(1)}, f32[16,128]{1,0:T(8,128)S(1)}, u32[]{:S(2)}, u32[]{:S(2)}) collective-permute-start(f32[16,128]{1,0:T(8,128)S(1)} %get-tuple-element.36), channel_id=1, source_target_pairs={{0,16},{4,20},{8,24},{12,28},{16,32},{20,36},{24,40},{28,44},{32,4... | collective-permute-start | bytes 24584 | tf_op jit(solution)/shard_map/ppermute | solution.py:51
  27.8 9.5 %copy-start.3 = (bf16[384,640]{1,0:T(8,128)(2,1)}, bf16[384,640]{1,0:T(8,128)(2,1)S(1)}, u32[]{:S(2)}) copy-start(bf16[384,640]{1,0:T(8,128)(2,1)S(1)} %collective-permute-done.q_ref) | copy-start | bytes 1474564
  29.0 50.6 %collective-permute-start.8 = (bf16[512,640]{1,0:T(8,128)(2,1)S(1)}, bf16[512,640]{1,0:T(8,128)(2,1)S(1)}, u32[]{:S(2)}, u32[]{:S(2)}) collective-permute-start(bf16[512,640]{1,0:T(8,128)(2,1)S(1)} %pad_maximum_fusion.rest_3_.b3), channel_id=1, source_target_pairs={{24,0},{28,4},{32,8},{36,12},{40,16},{44,20},{48,24},{52,28},{56,3... | collective-permute-start | bytes 1966088 | tf_op jit(solution)/shard_map/ppermute | solution.py:51
  30.9 48.7 %collective-permute-start.7 = (bf16[512,640]{1,0:T(8,128)(2,1)S(1)}, bf16[512,640]{1,0:T(8,128)(2,1)S(1)}, u32[]{:S(2)}, u32[]{:S(2)}) collective-permute-start(bf16[512,640]{1,0:T(8,128)(2,1)S(1)} %pad_maximum_fusion.rest_3_.b3), channel_id=1, source_target_pairs={{0,24},{4,28},{8,32},{12,36},{16,40},{20,44},{24,48},{28,52},{32,5... | collective-permute-start | bytes 1966088 | tf_op jit(solution)/shard_map/ppermute | solution.py:51
  37.3 42.3 %collective-permute-start.6 = (bf16[512,640]{1,0:T(8,128)(2,1)S(1)}, bf16[512,640]{1,0:T(8,128)(2,1)S(1)}, u32[]{:S(2)}, u32[]{:S(2)}) collective-permute-start(bf16[512,640]{1,0:T(8,128)(2,1)S(1)} %pad_maximum_fusion.rest_3_.b3), channel_id=1, source_target_pairs={{8,0},{12,4},{16,8},{20,12},{24,16},{28,20},{32,24},{36,28},{40,32... | collective-permute-start | bytes 1966088 | tf_op jit(solution)/shard_map/ppermute | solution.py:51
  40.7 39.0 %collective-permute-start.5 = (bf16[512,640]{1,0:T(8,128)(2,1)S(1)}, bf16[512,640]{1,0:T(8,128)(2,1)S(1)}, u32[]{:S(2)}, u32[]{:S(2)}) collective-permute-start(bf16[512,640]{1,0:T(8,128)(2,1)S(1)} %pad_maximum_fusion.rest_3_.b3), channel_id=1, source_target_pairs={{0,8},{4,12},{8,16},{12,20},{16,24},{20,28},{24,32},{28,36},{32,40... | collective-permute-start | bytes 1966088 | tf_op jit(solution)/shard_map/ppermute | solution.py:51
  79.6 19.5 %copy-start = (f32[896,128]{1,0:T(8,128)S(1)}, f32[896,128]{1,0:T(8,128)}, u32[]{:S(2)}) copy-start(f32[896,128]{1,0:T(8,128)} %constant.11.clone.sin_ref) | copy-start | bytes 1376260
  79.6 19.5 %copy-start.1 = (f32[896,128]{1,0:T(8,128)S(1)}, f32[896,128]{1,0:T(8,128)}, u32[]{:S(2)}) copy-start(f32[896,128]{1,0:T(8,128)} %constant.10.clone.cos_ref) | copy-start | bytes 1376260
  79.6 17.7 %collective-permute-start.10 = (bf16[512,640]{1,0:T(8,128)(2,1)S(1)}, bf16[512,640]{1,0:T(8,128)(2,1)S(1)}, u32[]{:S(2)}, u32[]{:S(2)}) collective-permute-start(bf16[512,640]{1,0:T(8,128)(2,1)S(1)} %collective-permute-done.5.rest_2_.b2), channel_id=1, source_target_pairs={{0,8},{4,12},{8,16},{12,20},{16,24},{20,28},{24,32},{28,36},{32,40... | collective-permute-start | bytes 1966088 | tf_op jit(solution)/shard_map/ppermute | solution.py:51
  81.7 17.4 %collective-permute-start.11 = (bf16[512,640]{1,0:T(8,128)(2,1)S(1)}, bf16[512,640]{1,0:T(8,128)(2,1)S(1)}, u32[]{:S(2)}, u32[]{:S(2)}) collective-permute-start(bf16[512,640]{1,0:T(8,128)(2,1)S(1)} %collective-permute-done.6.rest_4_.b4), channel_id=1, source_target_pairs={{8,0},{12,4},{16,8},{20,12},{24,16},{28,20},{32,24},{36,28},{40,32... | collective-permute-start | bytes 1966088 | tf_op jit(solution)/shard_map/ppermute | solution.py:51
  85.2 12.2 %collective-permute-start.9 = (f32[16,128]{1,0:T(8,128)S(1)}, f32[16,128]{1,0:T(8,128)S(1)}, u32[]{:S(2)}, u32[]{:S(2)}) collective-permute-start(f32[16,128]{1,0:T(8,128)S(1)} %psum.7.sums_ref.rest_7_), channel_id=1, source_target_pairs={{0,4},{4,0},{8,12},{12,8},{16,20},{20,16},{24,28},{28,24},{32,36},... | collective-permute-start | bytes 24584 | tf_op jit(solution)/shard_map/ppermute | solution.py:58
  97.3 3.6 %copy-start.4 = (bf16[384,640]{1,0:T(8,128)(2,1)S(1)}, bf16[384,640]{1,0:T(8,128)(2,1)}, u32[]{:S(2)}) copy-start(bf16[384,640]{1,0:T(8,128)(2,1)} %copy-done.3) | copy-start | bytes 1474564
  100.9 10.8 %copy-start.7 = (bf16[128,640]{1,0:T(8,128)(2,1)S(1)}, bf16[128,640]{1,0:T(8,128)(2,1)}, u32[]{:S(2)}) copy-start(bf16[128,640]{1,0:T(8,128)(2,1)} %get-tuple-element.26.q_ref) | copy-start | bytes 491524
  103.9 10.8 %collective-permute-start.12 = (f32[128,640]{1,0:T(8,128)S(1)}, f32[128,640]{1,0:T(8,128)S(1)}, u32[]{:S(2)}, u32[]{:S(2)}) collective-permute-start(f32[128,640]{1,0:T(8,128)S(1)} %shard_map.150), channel_id=1, source_target_pairs={{0,4},{4,0},{8,12},{12,8},{16,20},{20,16},{24,28},{28,24},{32,36},... | collective-permute-start | bytes 983048 | tf_op jit(solution)/shard_map/ppermute | solution.py:58
  (5 other events, 7.4 us)

commit v5 on v4

--- a/solution.py
+++ b/solution.py
@@ -163,130 +163,119 @@
     return tile - before, tile + after
 
 
-def turn(ref, rows, factor, gain_ref, cos_ref, sin_ref, start, dest_ref, slot):
+def turn(ref, rows, factor, gain_ref, cos_ref, sin_ref, start, dest_ref, goal):
     even = lax.rem(lax.broadcasted_iota(jnp.int32, (ROWS, HD), 1), 2) == 0
     cosine = cos_ref[pl.ds(start, ROWS), :]
     sine = sin_ref[pl.ds(start, ROWS), :]
     for head in range(ref.shape[1] // HD):
         cols = slice(head * HD, (head + 1) * HD)
         x = ref[rows, cols].astype(jnp.float32) * factor * gain_ref[:, cols]
-        dest_ref[slot, :, cols] = rotated(x, cosine, sine, even).astype(jnp.bfloat16)
-
-
-def keys_kernel(item_ref, here_ref, gain_ref, cos_ref, sin_ref, *rest):
-    blocks, own_ref, mate_ref, keys_ref = rest[:7], rest[7], rest[8], rest[9]
-    here = here_ref[0]
-    core = lax.rem(here, 2)
-    left = here - core
-    first_a, last_a = extent(item_ref, left)
-    first_b, last_b = extent(item_ref, left + 1)
-    half = keys_ref.shape[2]
-    for w in range(14):
-        tile = left - 6 + w
+        dest_ref[goal, cols] = rotated(x, cosine, sine, even).astype(jnp.bfloat16)
+
+
+def gather_block(chip, block, core, left, bounds, sums, gains, tables, keys_ref, values_ref, place):
+    first_a, last_a, first_b, last_b = bounds
+    cos_ref, sin_ref = tables
+    own_ref, mate_ref = sums
+    line = KEY_LINES[chip + SPAN // 2]
+    for parity in range(2):
+        tile = left + 2 * chip + parity
+        slot = jnp.where(core == parity, 0, 1)
+        key_rows = pl.ds(pl.multiple_of(slot * 2 * ROWS, 2 * ROWS), ROWS)
+        value_rows = pl.ds(pl.multiple_of(slot * 2 * ROWS + ROWS, ROWS), ROWS)
+        goal = slice((place + parity) * ROWS, (place + parity + 1) * ROWS)
+        values_ref[goal, :] = block[value_rows, :]
 
         @pl.when(jnp.logical_and(tile >= first_a, tile <= last_b))
-        def _(w=w, tile=tile):
-            chip, parity = w // 2, w % 2
+        def _(parity=parity, tile=tile, key_rows=key_rows, goal=goal):
             first = jnp.where(tile <= last_a, first_a, first_b)
             start = pl.multiple_of((tile - first) * ROWS, ROWS)
-            slot = jnp.where(core == parity, 0, 1)
-            row = pl.multiple_of(slot * 2 * ROWS, 2 * ROWS)
-            line = KEY_LINES[chip]
-            sums = jnp.where(core == parity, own_ref[line : line + 1, :], mate_ref[line : line + 1, :])
-            factor = by_rows(sums)
-            gains = gain_ref.at[:, pl.ds(pl.multiple_of(core * half, HD), half)]
-            turn(blocks[chip], pl.ds(row, ROWS), factor, gains, cos_ref, sin_ref, start, keys_ref, w)
-
-
-def attend_kernel(
-    other,
-    item_ref,
-    count_ref,
-    here_ref,
-    sums_ref,
-    q_ref,
-    keys,
-    b0,
-    b1,
-    b2,
-    b3,
-    b4,
-    b5,
-    b6,
-    gain_ref,
-    cos_ref,
-    sin_ref,
-    out_ref,
-    values,
-    queries,
-    scores,
-):
-    blocks = (b0, b1, b2, b3, b4, b5, b6)
-    half = q_ref.shape[1]
-    heads = half // HD
-    here = here_ref[0]
-    core = lax.rem(here, 2)
-    left = here - core
-    base = left - 6
-    tile = left + (1 - core if other else core)
+            total = jnp.where(core == parity, own_ref[line : line + 1, :], mate_ref[line : line + 1, :])
+            turn(block, key_rows, by_rows(total), gains, cos_ref, sin_ref, start, keys_ref, goal)
+
+
+def near_kernel(chips, item_ref, here_ref, *rest):
+    own_ref, mate_ref, k_gain_ref, q_gain_ref, cos_ref, sin_ref, q_own_ref, q_mate_ref = rest[:8]
+    blocks = rest[8 : 8 + len(chips)]
+    keys_ref, values_ref, own_turned_ref, mate_turned_ref = rest[8 + len(chips) :]
+    core = lax.rem(here_ref[0], 2)
+    left = here_ref[0] - core
+    half = keys_ref.shape[1]
+    bounds = (*extent(item_ref, left), *extent(item_ref, left + 1))
+    part = pl.ds(pl.multiple_of(core * half, HD), half)
+    k_gains, q_gains = k_gain_ref.at[:, part], q_gain_ref.at[:, part]
+    for which, (source, rows, sums, goal) in enumerate(
+        (
+            (q_own_ref, slice(0, ROWS), own_ref, own_turned_ref),
+            (q_mate_ref, slice(2 * ROWS, 3 * ROWS), mate_ref, mate_turned_ref),
+        )
+    ):
+        is_a = core == which
+        first = jnp.where(is_a, bounds[0], bounds[2])
+        tile = jnp.where(is_a, left, left + 1)
+        start = pl.multiple_of((tile - first) * ROWS, ROWS)
+        factor = by_rows(sums[1:2, :])
+        turn(source, rows, factor, q_gains, cos_ref, sin_ref, start, goal, slice(None))
+    for index, (chip, block) in enumerate(zip(chips, blocks)):
+        gather_block(
+            chip, block, core, left, bounds, (own_ref, mate_ref), k_gains, (cos_ref, sin_ref),
+            keys_ref, values_ref, 2 * index,
+        )
+
+
+def attend(mate, item_ref, count_ref, here_ref, q_ref, keys_ref, values_ref, out_ref):
+    core = lax.rem(here_ref[0], 2)
+    left = here_ref[0] - core
+    tile = left + (1 - core if mate else core)
     first, last = extent(item_ref, tile)
-    factor = by_rows(sums_ref[1:2, :])
-    start = pl.multiple_of((tile - first) * ROWS, ROWS)
-    rows = slice(2 * ROWS, 3 * ROWS) if other else slice(0, ROWS)
-    gains = gain_ref.at[:, pl.ds(pl.multiple_of(core * half, HD), half)]
-    turn(q_ref, rows, factor, gains, cos_ref, sin_ref, start, queries, 0)
-    low, high = first - base, last - base + 1
-
-    for w in range(14):
-
-        @pl.when(jnp.logical_and(w >= low, w < high))
-        def _(w=w):
-            chip, parity = w // 2, w % 2
-            slot = jnp.where(core == parity, 0, 1)
-            row = pl.multiple_of(slot * 2 * ROWS + ROWS, ROWS)
-            values[w] = blocks[chip][pl.ds(row, ROWS), :]
-
-    def score(w, tops):
-        live = prefix_live((ROWS, ROWS), count_ref[base + w])
-        found = []
-        for head in range(heads):
-            cols = slice(head * HD, (head + 1) * HD)
-            s = lax.dot_general(
-                queries[0, :, cols],
-                keys[w, :, cols],
-                (((1,), (1,)), ((), ())),
-                preferred_element_type=jnp.float32,
-            )
-            s = jnp.where(live, s * SCALE, NEG)
-            scores[w - low, :, cols] = s
-            found.append(jnp.maximum(tops[head], s))
-        return tuple(found)
-
-    empty = jnp.full((ROWS, ROWS), NEG, jnp.float32)
-    tops = lax.fori_loop(low, high, score, (empty,) * heads)
-    tops = [jnp.max(t, axis=1, keepdims=True) for t in tops]
-
-    def mix(w, carry):
-        mixed, totals = [], []
-        for head in range(heads):
-            cols = slice(head * HD, (head + 1) * HD)
-            weight = jnp.exp(scores[w - low, :, cols] - tops[head])
-            totals.append(carry[1][head] + weight)
-            mixed.append(
-                carry[0][head]
-                + jnp.dot(
-                    weight.astype(jnp.bfloat16),
-                    values[w, :, cols],
-                    preferred_element_type=jnp.float32,
-                )
-            )
-        return tuple(mixed), tuple(totals)
-
-    zero = jnp.zeros((ROWS, ROWS), jnp.float32)
-    mixed, totals = lax.fori_loop(low, high, mix, ((zero,) * heads, (zero,) * heads))
-    for head in range(heads):
+    window = pl.ds(pl.multiple_of((first - left + 6) * ROWS, ROWS), SPAN * ROWS)
+    tiles = item_ref.shape[0]
+    lanes = lax.broadcasted_iota(jnp.int32, (ROWS, ROWS), 1)
+    live = []
+    for slot in range(SPAN):
+        count = count_ref[jnp.minimum(first + slot, tiles - 1)]
+        live.append(lanes < jnp.where(first + slot <= last, count, 0))
+    for head in range(q_ref.shape[1] // HD):
         cols = slice(head * HD, (head + 1) * HD)
-        out_ref[:, cols] = mixed[head] / jnp.sum(totals[head], axis=1, keepdims=True)
+        s = lax.dot_general(
+            q_ref[:, cols],
+            keys_ref[window, cols],
+            (((1,), (1,)), ((), ())),
+            preferred_element_type=jnp.float32,
+        )
+        parts = [
+            jnp.where(live[slot], s[:, slot * ROWS : (slot + 1) * ROWS] * SCALE, NEG)
+            for slot in range(SPAN)
+        ]
+        top = functools.reduce(jnp.maximum, parts)
+        top = jnp.max(top, axis=1, keepdims=True)
+        parts = [jnp.exp(part - top) for part in parts]
+        total = jnp.sum(functools.reduce(jnp.add, parts), axis=1, keepdims=True)
+        weights = jnp.concatenate([part.astype(jnp.bfloat16) for part in parts], axis=1)
+        mixed = jnp.dot(weights, values_ref[window, cols], preferred_element_type=jnp.float32)
+        out_ref[:, cols] = mixed / total
+
+
+def far_kernel(near_chips, far_chips, item_ref, count_ref, here_ref, *rest):
+    own_ref, mate_ref, k_gain_ref, cos_ref, sin_ref, q_ref, near_keys_ref, near_values_ref = rest[:8]
+    blocks = rest[8 : 8 + len(far_chips)]
+    out_ref, keys_ref, values_ref = rest[8 + len(far_chips) :]
+    core = lax.rem(here_ref[0], 2)
+    left = here_ref[0] - core
+    half = keys_ref.shape[1]
+    bounds = (*extent(item_ref, left), *extent(item_ref, left + 1))
+    k_gains = k_gain_ref.at[:, pl.ds(pl.multiple_of(core * half, HD), half)]
+    for index, chip in enumerate(near_chips):
+        source = slice(2 * index * ROWS, 2 * (index + 1) * ROWS)
+        goal = slice(2 * (chip + 3) * ROWS, 2 * (chip + 4) * ROWS)
+        keys_ref[goal, :] = near_keys_ref[source, :]
+        values_ref[goal, :] = near_values_ref[source, :]
+    for chip, block in zip(far_chips, blocks):
+        gather_block(
+            chip, block, core, left, bounds, (own_ref, mate_ref), k_gains, (cos_ref, sin_ref),
+            keys_ref, values_ref, 2 * (chip + 3),
+        )
+    attend(True, item_ref, count_ref, here_ref, q_ref, keys_ref, values_ref, out_ref)
 
 
 def join_kernel(here_ref, own_ref, other_ref, text_ref, out_ref):
@@ -389,40 +378,55 @@
     )
 
     cosine, sine = (jnp.asarray(t) for t in rope_tables())
-    blocks = [left3, left2, left, block, right, right2, right3]
-    keys = call(
-        keys_kernel,
-        jax.ShapeDtypeStruct((14, ROWS, half), bf16),
-        [smem] * 2 + [vmem] * 12,
+    arrived = {-3: left3, -2: left2, -1: left, 0: block, 1: right, 2: right2, 3: right3}
+    near_chips, far_chips = (-3, -1, 0, 1, 3), (-2, 2)
+    near_rows = 2 * len(near_chips) * ROWS
+    near_keys, near_values, q_own, q_mate = call(
+        functools.partial(near_kernel, near_chips),
+        (jax.ShapeDtypeStruct((near_rows, half), bf16),) * 2
+        + (jax.ShapeDtypeStruct((ROWS, half), bf16),) * 2,
+        [smem] * 2 + [vmem] * (8 + len(near_chips)),
         flops=200000000,
-    )(tile_item, where, k_gain, cosine, sine, *blocks, sums, mate_sums)
-
-    def attended(other, query, query_sums):
-        return call(
-            functools.partial(attend_kernel, other),
-            jax.ShapeDtypeStruct((ROWS, half), f32),
-            [smem] * 3 + [vmem] * 13,
-            scratch=[
-                pltpu.VMEM((14, ROWS, half), bf16),
-                pltpu.VMEM((1, ROWS, half), bf16),
-                pltpu.VMEM((SPAN, ROWS, half), f32),
-            ],
-            flops=300000000,
-        )(
-            tile_item,
-            row_count,
-            where,
-            query_sums,
-            query,
-            keys,
-            *blocks,
-            q_gain,
-            cosine,
-            sine,
-        )
-
-    rest = swapped(attended(True, got, mate_sums))
-    own = attended(False, q_mine, sums)
+    )(
+        tile_item,
+        where,
+        sums,
+        mate_sums,
+        k_gain,
+        q_gain,
+        cosine,
+        sine,
+        q_mine,
+        got,
+        *[arrived[chip] for chip in near_chips],
+    )
+    window = jax.ShapeDtypeStruct((14 * ROWS, half), bf16)
+    mate_out, keys, values = call(
+        functools.partial(far_kernel, near_chips, far_chips),
+        (jax.ShapeDtypeStruct((ROWS, half), f32), window, window),
+        [smem] * 3 + [vmem] * (8 + len(far_chips)),
+        flops=300000000,
+    )(
+        tile_item,
+        row_count,
+        where,
+        sums,
+        mate_sums,
+        k_gain,
+        cosine,
+        sine,
+        q_mate,
+        near_keys,
+        near_values,
+        *[arrived[chip] for chip in far_chips],
+    )
+    rest = swapped(mate_out)
+    own = call(
+        functools.partial(attend, False),
+        jax.ShapeDtypeStruct((ROWS, half), f32),
+        [smem] * 3 + [vmem] * 3,
+        flops=300000000,
+    )(tile_item, row_count, where, q_own, keys, values)
     return call(
         join_kernel, jax.ShapeDtypeStruct((ROWS, width), bf16), [smem] + [vmem] * 3
     )(where, own, rest, text_out)

time: 116 us -> 113 us (0.974)
  local copies, waits for them, and re-layouts: 3.95 us -> 1.86 us
  waiting for transfers between devices: 3.48 us -> 2.31 us
    unnamed x32 -> x28, local copies, waits for them, and re-layouts: 3.9 us -> 1.81 us
    ppermute x10, waiting for transfers between devices: 3.48 us -> 2.3 us  [shifted(): lax.ppermute(value, 'tile', [(i, i + by) for i in range(peers) if 0 <= i...]
  transfers between devices with their start and end apart: 13 -> 13, of which waited for: 3 -> 3; matrix products, arithmetic and copies ran while one was open for 1% -> 1% of each run, Pallas kernels for 4% -> 6%
where the time goes in v5:
time: 113 us
  starting transfers between devices  60.4 us (53%)
  blocking collectives  32.6 us (29%)
  Pallas kernels  13.3 us (12%)
  waiting for transfers between devices  2.31 us (2%)
  local copies, waits for them, and re-layouts  1.86 us (2%)
  other arithmetic  1.86 us (2%)
    ppermute x10, starting transfers between devices, shifted(): lax.ppermute(value, 'tile', [(i, i + by) for i in range(peers) if 0 <= i...  42.4 us
    psum x1, blocking collectives, per_device(): sums = lax.psum(table, 'head')  32.6 us
    ppermute x3, starting transfers between devices, swapped(): return lax.ppermute(value, 'tile', [(i, i ^ 1) for i in range(peers)])  18 us
    pallas_call x1, Pallas kernels, per_device(): call(functools.partial(near_kernel, near_chips), (jax.ShapeDtypeStruct((n...  3.08 us
    pallas_call x1, Pallas kernels, per_device(): call(functools.partial(far_kernel, near_chips, far_chips), (jax.ShapeDtyp...  2.8 us
    pallas_call x1, Pallas kernels, per_device(): call(pack_kernel, (jax.ShapeDtypeStruct((2 * ROWS, half), bf16), jax.Shap...  2.57 us
    pallas_call x1, Pallas kernels, per_device(): call(functools.partial(attend, False), jax.ShapeDtypeStruct((ROWS, half),...  2.47 us
    ppermute x10, waiting for transfers between devices, shifted(): lax.ppermute(value, 'tile', [(i, i + by) for i in range(peers) if 0 <= i...  2.3 us
  transfers between devices with their start and end apart: 13, of which 3 were waited for; matrix products, arithmetic and copies ran while one was open for 1% of the time, Pallas kernels for 6%

profile of v5, /device:TPU:31, one launch (start us, length us, event | category | flops | bytes accessed | tf_op | source)
XLA Modules:
  0.0 112.8 jit_solution(9782341379826573839)
XLA Ops:
  0.1 2.6 %shard_map.145 = (bf16[256,640]{1,0:T(8,128)(2,1)}, bf16[384,640]{1,0:T(8,128)(2,1)}, bf16[128,640]{1,0:T(8,128)(2,1)}, f32[8,128]{1,0:T(8,128)}) custom-call(s32[1]{0:T(128)} %bitcast.here_ref, bf16[128,1280]{1,0:T(8,128)(2,1)} %q_hbm.1, bf16[128,1280]{1,0:T(8,128)(2,1)} %k_hbm.1, bf16[128,1280]{1,0:T(8,128)(2,1)} %v_hbm.1, bf16[128,1280]{1,0:T(8,128)(2,1)} %q_ref.1, ...), custom_call_target="tpu_custom_call" | custom-call | flops 1000000 | bytes 4000000 | tf_op jit(solution)/shard_map/pallas_call | solution.py:332
  2.6 2.6 %collective-permute-start = (bf16[384,640]{1,0:T(8,128)(2,1)}, bf16[384,640]{1,0:T(8,128)(2,1)S(1)}, u32[]{:S(2)}, u32[]{:S(2)}) collective-permute-start(bf16[384,640]{1,0:T(8,128)(2,1)} %get-tuple-element.28), channel_id=1, source_target_pairs={{0,4},{4,0},{8,12},{12,8},{16,20},{20,16},{24,28},{28,24},{32,36},... | collective-permute-start | bytes 1474568 | tf_op jit(solution)/shard_map/ppermute | solution.py:58
  5.2 2.5 %collective-permute-start.2 = (f32[8,128]{1,0:T(8,128)}, f32[8,128]{1,0:T(8,128)S(1)}, u32[]{:S(2)}, u32[]{:S(2)}) collective-permute-start(f32[8,128]{1,0:T(8,128)} %get-tuple-element.29.own_ref), channel_id=1, source_target_pairs={{8,0},{12,4},{16,8},{20,12},{24,16},{28,20},{32,24},{36,28},{40,32... | collective-permute-start | bytes 12296 | tf_op jit(solution)/shard_map/ppermute | solution.py:51
  7.7 7.0 %collective-permute-start.1 = (f32[8,128]{1,0:T(8,128)}, f32[8,128]{1,0:T(8,128)S(1)}, u32[]{:S(2)}, u32[]{:S(2)}) collective-permute-start(f32[8,128]{1,0:T(8,128)} %get-tuple-element.29.own_ref), channel_id=1, source_target_pairs={{0,8},{4,12},{8,16},{12,20},{16,24},{20,28},{24,32},{28,36},{32,40... | collective-permute-start | bytes 12296 | tf_op jit(solution)/shard_map/ppermute | solution.py:51
  14.8 0.9 collective-permute-done.1.left_ref
  16.4 1.9 %collective-permute-start.4 = (f32[16,128]{1,0:T(8,128)S(1)}, f32[16,128]{1,0:T(8,128)S(1)}, u32[]{:S(2)}, u32[]{:S(2)}) collective-permute-start(f32[16,128]{1,0:T(8,128)S(1)} %get-tuple-element.49), channel_id=1, source_target_pairs={{16,0},{20,4},{24,8},{28,12},{32,16},{36,20},{40,24},{44,28},{48,3... | collective-permute-start | bytes 24584 | tf_op jit(solution)/shard_map/ppermute | solution.py:51
  18.4 7.9 %collective-permute-start.3 = (f32[16,128]{1,0:T(8,128)S(1)}, f32[16,128]{1,0:T(8,128)S(1)}, u32[]{:S(2)}, u32[]{:S(2)}) collective-permute-start(f32[16,128]{1,0:T(8,128)S(1)} %get-tuple-element.50), channel_id=1, source_target_pairs={{0,16},{4,20},{8,24},{12,28},{16,32},{20,36},{24,40},{28,44},{32,4... | collective-permute-start | bytes 24584 | tf_op jit(solution)/shard_map/ppermute | solution.py:51
  26.2 0.8 collective-permute-done.3.left_far_ref
  27.8 1.1 pad_maximum_fusion.rest_10_
  28.9 1.9 %collective-permute-start.8 = (bf16[512,640]{1,0:T(8,128)(2,1)S(1)}, bf16[512,640]{1,0:T(8,128)(2,1)}, u32[]{:S(2)}, u32[]{:S(2)}) collective-permute-start(bf16[512,640]{1,0:T(8,128)(2,1)S(1)} %pad_maximum_fusion.rest_10_), channel_id=1, source_target_pairs={{24,0},{28,4},{32,8},{36,12},{40,16},{44,20},{48,24},{52,28},{56,3... | collective-permute-start | bytes 1966088 | tf_op jit(solution)/shard_map/ppermute | solution.py:51
  30.8 6.4 %collective-permute-start.7 = (bf16[512,640]{1,0:T(8,128)(2,1)S(1)}, bf16[512,640]{1,0:T(8,128)(2,1)}, u32[]{:S(2)}, u32[]{:S(2)}) collective-permute-start(bf16[512,640]{1,0:T(8,128)(2,1)S(1)} %pad_maximum_fusion.rest_10_), channel_id=1, source_target_pairs={{0,24},{4,28},{8,32},{12,36},{16,40},{20,44},{24,48},{28,52},{32,5... | collective-permute-start | bytes 1966088 | tf_op jit(solution)/shard_map/ppermute | solution.py:51
  37.2 3.3 %collective-permute-start.6 = (bf16[512,640]{1,0:T(8,128)(2,1)S(1)}, bf16[512,640]{1,0:T(8,128)(2,1)}, u32[]{:S(2)}, u32[]{:S(2)}) collective-permute-start(bf16[512,640]{1,0:T(8,128)(2,1)S(1)} %pad_maximum_fusion.rest_10_), channel_id=1, source_target_pairs={{8,0},{12,4},{16,8},{20,12},{24,16},{28,20},{32,24},{36,28},{40,32... | collective-permute-start | bytes 1966088 | tf_op jit(solution)/shard_map/ppermute | solution.py:51
  40.5 6.2 %collective-permute-start.5 = (bf16[512,640]{1,0:T(8,128)(2,1)S(1)}, bf16[512,640]{1,0:T(8,128)(2,1)}, u32[]{:S(2)}, u32[]{:S(2)}) collective-permute-start(bf16[512,640]{1,0:T(8,128)(2,1)S(1)} %pad_maximum_fusion.rest_10_), channel_id=1, source_target_pairs={{0,8},{4,12},{8,16},{12,20},{16,24},{20,28},{24,32},{28,36},{32,40... | collective-permute-start | bytes 1966088 | tf_op jit(solution)/shard_map/ppermute | solution.py:51
  46.7 32.6 %psum.7.sums_ref.rest_0_ = f32[16,128]{1,0:T(8,128)S(1)} all-reduce(f32[16,128]{1,0:T(8,128)S(1)} %shard_map.146), channel_id=1, replica_groups=mesh['tile'=128,'head'=4] {'head'}, use_global_device_ids=true, to_apply=%region_0.0 | all-reduce | flops 2048 | bytes 16384 | tf_op jit(solution)/shard_map/psum | solution.py:356
  79.3 1.9 %collective-permute-start.10 = (bf16[512,640]{1,0:T(8,128)(2,1)}, bf16[512,640]{1,0:T(8,128)(2,1)S(1)}, u32[]{:S(2)}, u32[]{:S(2)}) collective-permute-start(bf16[512,640]{1,0:T(8,128)(2,1)} %collective-permute-done.5.rest_9_), channel_id=1, source_target_pairs={{0,8},{4,12},{8,16},{12,20},{16,24},{20,28},{24,32},{28,36},{32,40... | collective-permute-start | bytes 1966088 | tf_op jit(solution)/shard_map/ppermute | solution.py:51
  81.3 3.4 %collective-permute-start.11 = (bf16[512,640]{1,0:T(8,128)(2,1)}, bf16[512,640]{1,0:T(8,128)(2,1)S(1)}, u32[]{:S(2)}, u32[]{:S(2)}) collective-permute-start(bf16[512,640]{1,0:T(8,128)(2,1)} %collective-permute-done.6.rest_11_), channel_id=1, source_target_pairs={{8,0},{12,4},{16,8},{20,12},{24,16},{28,20},{32,24},{36,28},{40,32... | collective-permute-start | bytes 1966088 | tf_op jit(solution)/shard_map/ppermute | solution.py:51
  84.7 7.5 %collective-permute-start.9 = (f32[16,128]{1,0:T(8,128)S(1)}, f32[16,128]{1,0:T(8,128)S(1)}, u32[]{:S(2)}, u32[]{:S(2)}) collective-permute-start(f32[16,128]{1,0:T(8,128)S(1)} %psum.7.sums_ref.rest_0_), channel_id=1, source_target_pairs={{0,4},{4,0},{8,12},{12,8},{16,20},{20,16},{24,28},{28,24},{32,36},... | collective-permute-start | bytes 24584 | tf_op jit(solution)/shard_map/ppermute | solution.py:58
  92.3 1.1 copy-done.4
  93.4 1.6 %shard_map.147.text_ref = f32[128,1280]{1,0:T(8,128)S(1)} custom-call(s32[128]{0:T(128)S(1)} %copy-done.7, s32[128]{0:T(128)S(1)} %copy-done.9, s32[1]{0:T(128)} %bitcast.here_ref, f32[16,128]{1,0:T(8,128)S(1)} %psum.7.sums_ref.rest_0_, bf16[128,1280]{1,0:T(8,128)(2,1)S(1)} %copy-done.3, bf16[256,1280]{1,0:T(8,128)(2,1)S(1)} %copy-done, ...), custom_call_target="tpu_custom_call" | custom-call | flops 400000000 | bytes 4000000 | tf_op jit(solution)/shard_map/pallas_call | solution.py:362
  95.0 3.1 %shard_map.148 = (bf16[1280,640]{1,0:T(8,128)(2,1)S(1)}, bf16[1280,640]{1,0:T(8,128)(2,1)S(1)}, bf16[128,640]{1,0:T(8,128)(2,1)S(1)}, bf16[128,640]{1,0:T(8,128)(2,1)S(1)}) custom-call(s32[128]{0:T(128)S(1)} %copy-done.7, s32[1]{0:T(128)} %bitcast.here_ref, f32[16,128]{1,0:T(8,128)S(1)} %psum.7.sums_ref.rest_0_, ...), custom_call_target="tpu_custom_call" | custom-call | flops 200000000 | bytes 4000000 | tf_op jit(solution)/shard_map/pallas_call | solution.py:384
  98.7 2.8 %shard_map.149 = (f32[128,640]{1,0:T(8,128)S(1)}, bf16[1792,640]{1,0:T(8,128)(2,1)S(1)}, bf16[1792,640]{1,0:T(8,128)(2,1)S(1)}) custom-call(s32[128]{0:T(128)S(1)} %copy-done.7, s32[128]{0:T(128)S(1)} %copy-done.8, s32[1]{0:T(128)} %bitcast.here_ref, f32[16,128]{1,0:T(8,128)S(1)} %psum.7.sums_ref.rest_0_, f32[16,128]{1,0:T(8,128)S(1)} %collective-permute-done.9.rest_1_, ...), custom_call_target="tpu_custom_call" | custom-call | flops 300000000 | bytes 4000000 | tf_op jit(solution)/shard_map/pallas_call | solution.py:404
  101.5 7.9 %collective-permute-start.12 = (f32[128,640]{1,0:T(8,128)S(1)}, f32[128,640]{1,0:T(8,128)S(1)}, u32[]{:S(2)}, u32[]{:S(2)}) collective-permute-start(f32[128,640]{1,0:T(8,128)S(1)} %get-tuple-element.47), channel_id=1, source_target_pairs={{0,4},{4,0},{8,12},{12,8},{16,20},{20,16},{24,28},{28,24},{32,36},... | collective-permute-start | bytes 983048 | tf_op jit(solution)/shard_map/ppermute | solution.py:58
  109.5 2.5 %shard_map.150.own_ref = f32[128,640]{1,0:T(8,128)S(1)} custom-call(s32[128]{0:T(128)S(1)} %copy-done.7, s32[128]{0:T(128)S(1)} %copy-done.8, s32[1]{0:T(128)} %bitcast.here_ref, bf16[128,640]{1,0:T(8,128)(2,1)S(1)} %get-tuple-element.41.q_ref, bf16[1792,640]{1,0:T(8,128)(2,1)S(1)} %get-tuple-element.45.keys_ref, ...), custom_call_target="tpu_custom_call" | custom-call | flops 300000000 | bytes 4000000 | tf_op jit(solution)/shard_map/pallas_call | solution.py:424
  111.9 0.8 shard_map.151
  (45 shorter events, 2.1 us)
Async XLA Ops:
  0.0 84.6 %copy-start.10 = (f32[1280]{0:T(1024)S(1)}, f32[1280]{0:T(1024)}, u32[]{:S(2)}) copy-start(f32[1280]{0:T(1024)} %param.21) | copy-start | bytes 15364
  0.0 84.7 %copy-start.11 = (f32[1280]{0:T(1024)S(1)}, f32[1280]{0:T(1024)}, u32[]{:S(2)}) copy-start(f32[1280]{0:T(1024)} %param.22) | copy-start | bytes 15364
  0.0 84.7 %copy-start.12 = (f32[1280]{0:T(1024)S(1)}, f32[1280]{0:T(1024)}, u32[]{:S(2)}) copy-start(f32[1280]{0:T(1024)} %param.23) | copy-start | bytes 15364
  0.0 84.7 %copy-start.13 = (f32[1280]{0:T(1024)S(1)}, f32[1280]{0:T(1024)}, u32[]{:S(2)}) copy-start(f32[1280]{0:T(1024)} %param.24) | copy-start | bytes 15364
  0.0 92.3 %copy-start = (bf16[256,1280]{1,0:T(8,128)(2,1)S(1)}, bf16[256,1280]{1,0:T(8,128)(2,1)}, u32[]{:S(2)}) copy-start(bf16[256,1280]{1,0:T(8,128)(2,1)} %k_ref.1) | copy-start | bytes 1966084
  0.0 92.3 %copy-start.3 = (bf16[128,1280]{1,0:T(8,128)(2,1)S(1)}, bf16[128,1280]{1,0:T(8,128)(2,1)}, u32[]{:S(2)}) copy-start(bf16[128,1280]{1,0:T(8,128)(2,1)} %q_ref.1) | copy-start | bytes 983044
  0.0 92.3 %copy-start.7 = (s32[128]{0:T(128)S(1)}, s32[128]{0:T(128)}, u32[]{:S(2)}) copy-start(s32[128]{0:T(128)} %item_ref.7) | copy-start | bytes 1540
  0.0 92.3 %copy-start.9 = (s32[128]{0:T(128)S(1)}, s32[128]{0:T(128)}, u32[]{:S(2)}) copy-start(s32[128]{0:T(128)} %len_ref.1) | copy-start | bytes 1540
  2.6 25.0 %collective-permute-start = (bf16[384,640]{1,0:T(8,128)(2,1)}, bf16[384,640]{1,0:T(8,128)(2,1)S(1)}, u32[]{:S(2)}, u32[]{:S(2)}) collective-permute-start(bf16[384,640]{1,0:T(8,128)(2,1)} %get-tuple-element.28), channel_id=1, source_target_pairs={{0,4},{4,0},{8,12},{12,8},{16,20},{20,16},{24,28},{28,24},{32,36},... | collective-permute-start | bytes 1474568 | tf_op jit(solution)/shard_map/ppermute | solution.py:58
  5.2 9.5 %collective-permute-start.2 = (f32[8,128]{1,0:T(8,128)}, f32[8,128]{1,0:T(8,128)S(1)}, u32[]{:S(2)}, u32[]{:S(2)}) collective-permute-start(f32[8,128]{1,0:T(8,128)} %get-tuple-element.29.own_ref), channel_id=1, source_target_pairs={{8,0},{12,4},{16,8},{20,12},{24,16},{28,20},{32,24},{36,28},{40,32... | collective-permute-start | bytes 12296 | tf_op jit(solution)/shard_map/ppermute | solution.py:51
  7.7 8.0 %collective-permute-start.1 = (f32[8,128]{1,0:T(8,128)}, f32[8,128]{1,0:T(8,128)S(1)}, u32[]{:S(2)}, u32[]{:S(2)}) collective-permute-start(f32[8,128]{1,0:T(8,128)} %get-tuple-element.29.own_ref), channel_id=1, source_target_pairs={{0,8},{4,12},{8,16},{12,20},{16,24},{20,28},{24,32},{28,36},{32,40... | collective-permute-start | bytes 12296 | tf_op jit(solution)/shard_map/ppermute | solution.py:51
  16.4 9.8 %collective-permute-start.4 = (f32[16,128]{1,0:T(8,128)S(1)}, f32[16,128]{1,0:T(8,128)S(1)}, u32[]{:S(2)}, u32[]{:S(2)}) collective-permute-start(f32[16,128]{1,0:T(8,128)S(1)} %get-tuple-element.49), channel_id=1, source_target_pairs={{16,0},{20,4},{24,8},{28,12},{32,16},{36,20},{40,24},{44,28},{48,3... | collective-permute-start | bytes 24584 | tf_op jit(solution)/shard_map/ppermute | solution.py:51
  18.4 8.7 %collective-permute-start.3 = (f32[16,128]{1,0:T(8,128)S(1)}, f32[16,128]{1,0:T(8,128)S(1)}, u32[]{:S(2)}, u32[]{:S(2)}) collective-permute-start(f32[16,128]{1,0:T(8,128)S(1)} %get-tuple-element.50), channel_id=1, source_target_pairs={{0,16},{4,20},{8,24},{12,28},{16,32},{20,36},{24,40},{28,44},{32,4... | collective-permute-start | bytes 24584 | tf_op jit(solution)/shard_map/ppermute | solution.py:51
  27.7 67.3 %copy-start.1 = (f32[896,128]{1,0:T(8,128)S(1)}, f32[896,128]{1,0:T(8,128)}, u32[]{:S(2)}) copy-start(f32[896,128]{1,0:T(8,128)} %constant.11.clone.rest_5_.rest_4_) | copy-start | bytes 1376260
  27.7 67.3 %copy-start.2 = (f32[896,128]{1,0:T(8,128)S(1)}, f32[896,128]{1,0:T(8,128)}, u32[]{:S(2)}) copy-start(f32[896,128]{1,0:T(8,128)} %constant.10.clone.rest_4_.rest_3_) | copy-start | bytes 1376260
  27.7 67.3 %copy-start.5 = (bf16[128,640]{1,0:T(8,128)(2,1)S(1)}, bf16[128,640]{1,0:T(8,128)(2,1)}, u32[]{:S(2)}) copy-start(bf16[128,640]{1,0:T(8,128)(2,1)} %get-tuple-element.36.rest_6_) | copy-start | bytes 491524
  28.9 50.4 %collective-permute-start.8 = (bf16[512,640]{1,0:T(8,128)(2,1)S(1)}, bf16[512,640]{1,0:T(8,128)(2,1)}, u32[]{:S(2)}, u32[]{:S(2)}) collective-permute-start(bf16[512,640]{1,0:T(8,128)(2,1)S(1)} %pad_maximum_fusion.rest_10_), channel_id=1, source_target_pairs={{24,0},{28,4},{32,8},{36,12},{40,16},{44,20},{48,24},{52,28},{56,3... | collective-permute-start | bytes 1966088 | tf_op jit(solution)/shard_map/ppermute | solution.py:51
  30.8 48.5 %collective-permute-start.7 = (bf16[512,640]{1,0:T(8,128)(2,1)S(1)}, bf16[512,640]{1,0:T(8,128)(2,1)}, u32[]{:S(2)}, u32[]{:S(2)}) collective-permute-start(bf16[512,640]{1,0:T(8,128)(2,1)S(1)} %pad_maximum_fusion.rest_10_), channel_id=1, source_target_pairs={{0,24},{4,28},{8,32},{12,36},{16,40},{20,44},{24,48},{28,52},{32,5... | collective-permute-start | bytes 1966088 | tf_op jit(solution)/shard_map/ppermute | solution.py:51
  37.2 42.1 %collective-permute-start.6 = (bf16[512,640]{1,0:T(8,128)(2,1)S(1)}, bf16[512,640]{1,0:T(8,128)(2,1)}, u32[]{:S(2)}, u32[]{:S(2)}) collective-permute-start(bf16[512,640]{1,0:T(8,128)(2,1)S(1)} %pad_maximum_fusion.rest_10_), channel_id=1, source_target_pairs={{8,0},{12,4},{16,8},{20,12},{24,16},{28,20},{32,24},{36,28},{40,32... | collective-permute-start | bytes 1966088 | tf_op jit(solution)/shard_map/ppermute | solution.py:51
  40.5 38.8 %collective-permute-start.5 = (bf16[512,640]{1,0:T(8,128)(2,1)S(1)}, bf16[512,640]{1,0:T(8,128)(2,1)}, u32[]{:S(2)}, u32[]{:S(2)}) collective-permute-start(bf16[512,640]{1,0:T(8,128)(2,1)S(1)} %pad_maximum_fusion.rest_10_), channel_id=1, source_target_pairs={{0,8},{4,12},{8,16},{12,20},{16,24},{20,28},{24,32},{28,36},{32,40... | collective-permute-start | bytes 1966088 | tf_op jit(solution)/shard_map/ppermute | solution.py:51
  79.3 18.8 %collective-permute-start.10 = (bf16[512,640]{1,0:T(8,128)(2,1)}, bf16[512,640]{1,0:T(8,128)(2,1)S(1)}, u32[]{:S(2)}, u32[]{:S(2)}) collective-permute-start(bf16[512,640]{1,0:T(8,128)(2,1)} %collective-permute-done.5.rest_9_), channel_id=1, source_target_pairs={{0,8},{4,12},{8,16},{12,20},{16,24},{20,28},{24,32},{28,36},{32,40... | collective-permute-start | bytes 1966088 | tf_op jit(solution)/shard_map/ppermute | solution.py:51
  81.3 17.5 %collective-permute-start.11 = (bf16[512,640]{1,0:T(8,128)(2,1)}, bf16[512,640]{1,0:T(8,128)(2,1)S(1)}, u32[]{:S(2)}, u32[]{:S(2)}) collective-permute-start(bf16[512,640]{1,0:T(8,128)(2,1)} %collective-permute-done.6.rest_11_), channel_id=1, source_target_pairs={{8,0},{12,4},{16,8},{20,12},{24,16},{28,20},{32,24},{36,28},{40,32... | collective-permute-start | bytes 1966088 | tf_op jit(solution)/shard_map/ppermute | solution.py:51
  84.7 10.3 %collective-permute-start.9 = (f32[16,128]{1,0:T(8,128)S(1)}, f32[16,128]{1,0:T(8,128)S(1)}, u32[]{:S(2)}, u32[]{:S(2)}) collective-permute-start(f32[16,128]{1,0:T(8,128)S(1)} %psum.7.sums_ref.rest_0_), channel_id=1, source_target_pairs={{0,4},{4,0},{8,12},{12,8},{16,20},{20,16},{24,28},{28,24},{32,36},... | collective-permute-start | bytes 24584 | tf_op jit(solution)/shard_map/ppermute | solution.py:58
  101.5 10.4 %collective-permute-start.12 = (f32[128,640]{1,0:T(8,128)S(1)}, f32[128,640]{1,0:T(8,128)S(1)}, u32[]{:S(2)}, u32[]{:S(2)}) collective-permute-start(f32[128,640]{1,0:T(8,128)S(1)} %get-tuple-element.47), channel_id=1, source_target_pairs={{0,4},{4,0},{8,12},{12,8},{16,20},{20,16},{24,28},{28,24},{32,36},... | collective-permute-start | bytes 983048 | tf_op jit(solution)/shard_map/ppermute | solution.py:58
  (3 other events, 5.5 us)

commit v6 on v5

--- a/solution.py
+++ b/solution.py
@@ -18,7 +18,8 @@
 EPSILON = 1e-06
 SCALE = 1.0 / math.sqrt(HD)
 NEG = -1e30
-KEY_LINES = (5, 6, 7, 0, 8, 9, 10)
+KEY_LINES = {-1: (7, 8), 0: (0, 5), 1: (9, 10)}
+SPARE = 16
 
 
 def rope_tables():
@@ -46,11 +47,10 @@
     return cosine, sine.reshape(SPAN * ROWS, HD).astype(np.float32)
 
 
-def shifted(value, by):
+def shifted(value, by, wrapped=()):
     peers = lax.axis_size("tile")
-    return lax.ppermute(
-        value, "tile", [(i, i + by) for i in range(peers) if 0 <= i + by < peers]
-    )
+    pairs = [(i, i + by) for i in range(peers) if 0 <= i + by < peers]
+    return lax.ppermute(value, "tile", pairs + [(i, (i + by) % peers) for i in wrapped])
 
 
 def swapped(value):
@@ -114,15 +114,32 @@
     sums_ref[4:5, :] = total(t_ref, ROWS)
 
 
-def table_kernel(own_ref, left_ref, right_ref, left_far_ref, right_far_ref, out_ref):
+def mate_kernel(own_ref, mate_ref, out_ref):
+    out_ref[...] = own_ref[...]
+    out_ref[5:7, :] = mate_ref[0:2, :]
+
+
+def table_kernel(own_ref, left_ref, right_ref, out_ref):
     out_ref[0:8, :] = own_ref[...]
     out_ref[8:16, :] = jnp.zeros((8, ROWS), jnp.float32)
-    out_ref[5:6, :] = left_far_ref[0:1, :]
-    out_ref[6:7, :] = left_far_ref[8:9, :]
     out_ref[7:8, :] = left_ref[0:1, :]
-    out_ref[8:9, :] = right_ref[0:1, :]
-    out_ref[9:10, :] = right_far_ref[0:1, :]
-    out_ref[10:11, :] = right_far_ref[8:9, :]
+    out_ref[8:9, :] = left_ref[5:6, :]
+    out_ref[9:10, :] = right_ref[0:1, :]
+    out_ref[10:11, :] = right_ref[5:6, :]
+
+
+def pieces_kernel(sums_ref, left_ref, right_ref):
+    for chip, out_ref in ((-1, left_ref), (1, right_ref)):
+        out_ref[...] = jnp.zeros(out_ref.shape, jnp.bfloat16)
+        rows = []
+        for line in KEY_LINES[chip]:
+            rest = sums_ref[line : line + 1, :]
+            for _ in range(3):
+                piece = rest.astype(jnp.bfloat16)
+                rows.append(piece.astype(jnp.float32))
+                rest = rest - rows[-1]
+        rows.append(jnp.zeros((SPARE - len(rows), ROWS), jnp.float32))
+        out_ref[:, 0:ROWS] = jnp.concatenate(rows, axis=0).astype(jnp.bfloat16)
 
 
 def cross_kernel(item_ref, len_ref, here_ref, sums_ref, q_ref, k_ref, v_ref, qg_ref, kg_ref, out_ref):
@@ -173,11 +190,9 @@
         dest_ref[goal, cols] = rotated(x, cosine, sine, even).astype(jnp.bfloat16)
 
 
-def gather_block(chip, block, core, left, bounds, sums, gains, tables, keys_ref, values_ref, place):
+def gather_block(chip, block, core, left, bounds, sums_ref, gains, tables, keys_ref, values_ref, place):
     first_a, last_a, first_b, last_b = bounds
     cos_ref, sin_ref = tables
-    own_ref, mate_ref = sums
-    line = KEY_LINES[chip + SPAN // 2]
     for parity in range(2):
         tile = left + 2 * chip + parity
         slot = jnp.where(core == parity, 0, 1)
@@ -190,35 +205,43 @@
         def _(parity=parity, tile=tile, key_rows=key_rows, goal=goal):
             first = jnp.where(tile <= last_a, first_a, first_b)
             start = pl.multiple_of((tile - first) * ROWS, ROWS)
-            total = jnp.where(core == parity, own_ref[line : line + 1, :], mate_ref[line : line + 1, :])
+            if chip in KEY_LINES:
+                own, mate = (sums_ref[line : line + 1, :] for line in KEY_LINES[chip])
+            else:
+                spare = block[4 * ROWS : 4 * ROWS + SPARE, 0:ROWS].astype(jnp.float32)
+                own, mate = (
+                    spare[3 * i : 3 * i + 1] + spare[3 * i + 1 : 3 * i + 2] + spare[3 * i + 2 : 3 * i + 3]
+                    for i in range(2)
+                )
+            total = jnp.where(core == parity, own, mate)
             turn(block, key_rows, by_rows(total), gains, cos_ref, sin_ref, start, keys_ref, goal)
 
 
 def near_kernel(chips, item_ref, here_ref, *rest):
-    own_ref, mate_ref, k_gain_ref, q_gain_ref, cos_ref, sin_ref, q_own_ref, q_mate_ref = rest[:8]
-    blocks = rest[8 : 8 + len(chips)]
-    keys_ref, values_ref, own_turned_ref, mate_turned_ref = rest[8 + len(chips) :]
+    sums_ref, k_gain_ref, q_gain_ref, cos_ref, sin_ref, q_own_ref, q_mate_ref = rest[:7]
+    blocks = rest[7 : 7 + len(chips)]
+    keys_ref, values_ref, own_turned_ref, mate_turned_ref = rest[7 + len(chips) :]
     core = lax.rem(here_ref[0], 2)
     left = here_ref[0] - core
     half = keys_ref.shape[1]
     bounds = (*extent(item_ref, left), *extent(item_ref, left + 1))
     part = pl.ds(pl.multiple_of(core * half, HD), half)
     k_gains, q_gains = k_gain_ref.at[:, part], q_gain_ref.at[:, part]
-    for which, (source, rows, sums, goal) in enumerate(
+    for which, (source, rows, line, goal) in enumerate(
         (
-            (q_own_ref, slice(0, ROWS), own_ref, own_turned_ref),
-            (q_mate_ref, slice(2 * ROWS, 3 * ROWS), mate_ref, mate_turned_ref),
+            (q_own_ref, slice(0, ROWS), 1, own_turned_ref),
+            (q_mate_ref, slice(2 * ROWS, 3 * ROWS), 6, mate_turned_ref),
         )
     ):
         is_a = core == which
         first = jnp.where(is_a, bounds[0], bounds[2])
         tile = jnp.where(is_a, left, left + 1)
         start = pl.multiple_of((tile - first) * ROWS, ROWS)
-        factor = by_rows(sums[1:2, :])
+        factor = by_rows(sums_ref[line : line + 1, :])
         turn(source, rows, factor, q_gains, cos_ref, sin_ref, start, goal, slice(None))
     for index, (chip, block) in enumerate(zip(chips, blocks)):
         gather_block(
-            chip, block, core, left, bounds, (own_ref, mate_ref), k_gains, (cos_ref, sin_ref),
+            chip, block, core, left, bounds, sums_ref, k_gains, (cos_ref, sin_ref),
             keys_ref, values_ref, 2 * index,
         )
 
@@ -257,9 +280,9 @@
 
 
 def far_kernel(near_chips, far_chips, item_ref, count_ref, here_ref, *rest):
-    own_ref, mate_ref, k_gain_ref, cos_ref, sin_ref, q_ref, near_keys_ref, near_values_ref = rest[:8]
-    blocks = rest[8 : 8 + len(far_chips)]
-    out_ref, keys_ref, values_ref = rest[8 + len(far_chips) :]
+    sums_ref, k_gain_ref, cos_ref, sin_ref, q_ref, near_keys_ref, near_values_ref = rest[:7]
+    blocks = rest[7 : 7 + len(far_chips)]
+    out_ref, keys_ref, values_ref = rest[7 + len(far_chips) :]
     core = lax.rem(here_ref[0], 2)
     left = here_ref[0] - core
     half = keys_ref.shape[1]
@@ -272,7 +295,7 @@
         values_ref[goal, :] = near_values_ref[source, :]
     for chip, block in zip(far_chips, blocks):
         gather_block(
-            chip, block, core, left, bounds, (own_ref, mate_ref), k_gains, (cos_ref, sin_ref),
+            chip, block, core, left, bounds, sums_ref, k_gains, (cos_ref, sin_ref),
             keys_ref, values_ref, 2 * (chip + 3),
         )
     attend(True, item_ref, count_ref, here_ref, q_ref, keys_ref, values_ref, out_ref)
@@ -343,21 +366,28 @@
         limit=60,
     )(where, self_query, self_key, self_value, cross_query, text_key)
     got = swapped(theirs)
-    left_sums = shifted(sums, 2)
-    right_sums = shifted(sums, -2)
-    block = jnp.concatenate([kv, got[: 2 * ROWS]], axis=0)
-    left_far = shifted(jnp.concatenate([left_sums, sums]), 4)
-    right_far = shifted(jnp.concatenate([sums, right_sums]), -4)
-    table = call(table_kernel, jax.ShapeDtypeStruct((16, ROWS), f32), [vmem] * 5)(
-        sums, left_sums, right_sums, left_far, right_far
-    )
-    block, table = lax.optimization_barrier((block, table))
-    near = [shifted(block, -2 * chip) for chip in (-1, 1, -3, 3)]
-    sums = lax.psum(table, "head")
-    left, right, left3, right3, sums = lax.optimization_barrier((*near, sums))
+    peers = lax.axis_size("tile")
+    low_pair, high_pair = (0, 1), (peers - 2, peers - 1)
+    table = jax.ShapeDtypeStruct((8, ROWS), f32)
+    sums = call(mate_kernel, table, [vmem] * 2)(sums, swapped(sums))
+    block = jnp.concatenate([kv, got[: 2 * ROWS], jnp.zeros((SPARE, half), bf16)], axis=0)
+    left_sums = shifted(sums, 2, high_pair)
+    right_sums = shifted(sums, -2, low_pair)
+    block, left_sums, right_sums = lax.optimization_barrier((block, left_sums, right_sums))
+    left = shifted(block, 2, high_pair)
+    right = shifted(block, -2, low_pair)
+    table = jax.ShapeDtypeStruct((16, ROWS), f32)
+    sums = call(table_kernel, table, [vmem] * 3)(sums, left_sums, right_sums)
+    sums = lax.psum(sums, "head")
+    left, right, sums = lax.optimization_barrier((left, right, sums))
+    spare = jax.ShapeDtypeStruct((SPARE, half), bf16)
+    left_pieces, right_pieces = call(pieces_kernel, (spare, spare), [vmem])(sums)
+    left = lax.dynamic_update_slice(left, left_pieces, (4 * ROWS, 0))
+    right = lax.dynamic_update_slice(right, right_pieces, (4 * ROWS, 0))
+    right3 = shifted(left, -8, low_pair)
+    left3 = shifted(right, 8, high_pair)
     left2 = shifted(left, 2)
     right2 = shifted(right, -2)
-    mate_sums = swapped(sums)
 
     text_out = call(
         cross_kernel, jax.ShapeDtypeStruct((ROWS, width), f32), [smem] * 3 + [vmem] * 6, flops=400000000
@@ -373,25 +403,22 @@
         text_gain[None, :],
     )
     q_gain, k_gain = query_gain[None, :], key_gain[None, :]
-    mate_sums, text_out, q_gain, k_gain = lax.optimization_barrier(
-        (mate_sums, text_out, q_gain, k_gain)
-    )
+    text_out, q_gain, k_gain = lax.optimization_barrier((text_out, q_gain, k_gain))
 
     cosine, sine = (jnp.asarray(t) for t in rope_tables())
     arrived = {-3: left3, -2: left2, -1: left, 0: block, 1: right, 2: right2, 3: right3}
-    near_chips, far_chips = (-3, -1, 0, 1, 3), (-2, 2)
+    near_chips, far_chips = (-1, 0, 1), (-3, -2, 2, 3)
     near_rows = 2 * len(near_chips) * ROWS
     near_keys, near_values, q_own, q_mate = call(
         functools.partial(near_kernel, near_chips),
         (jax.ShapeDtypeStruct((near_rows, half), bf16),) * 2
         + (jax.ShapeDtypeStruct((ROWS, half), bf16),) * 2,
-        [smem] * 2 + [vmem] * (8 + len(near_chips)),
+        [smem] * 2 + [vmem] * (7 + len(near_chips)),
         flops=200000000,
     )(
         tile_item,
         where,
         sums,
-        mate_sums,
         k_gain,
         q_gain,
         cosine,
@@ -404,14 +431,13 @@
     mate_out, keys, values = call(
         functools.partial(far_kernel, near_chips, far_chips),
         (jax.ShapeDtypeStruct((ROWS, half), f32), window, window),
-        [smem] * 3 + [vmem] * (8 + len(far_chips)),
+        [smem] * 3 + [vmem] * (7 + len(far_chips)),
         flops=300000000,
     )(
         tile_item,
         row_count,
         where,
         sums,
-        mate_sums,
         k_gain,
         cosine,
         sine,

time: 113 us -> 111 us (0.982)
  the two profiles are of different devices: /device:TPU:31 before, /device:TPU:33 now
where the time goes in v6:
time: 111 us; the launch traced here: 110 us
  starting transfers between devices  42.3 us (38%)
  blocking collectives  27.3 us (25%)
  waiting for transfers between devices  23.2 us (21%)
  Pallas kernels  12.8 us (12%)
  local copies, waits for them, and re-layouts  3.11 us (3%)
  other arithmetic  1.19 us (1%)
    ppermute x8, starting transfers between devices, shifted(): lax.ppermute(value, 'tile', pairs + [(i, (i + by) % peers) for i in wrapp...  31.4 us
    psum x1, blocking collectives, per_device(): sums = lax.psum(sums, 'head')  27.3 us
    ppermute x8, waiting for transfers between devices, shifted(): lax.ppermute(value, 'tile', pairs + [(i, (i + by) % peers) for i in wrapp...  21.9 us
    ppermute x3, starting transfers between devices, swapped(): return lax.ppermute(value, 'tile', [(i, i ^ 1) for i in range(peers)])  10.9 us
    pallas_call x1, Pallas kernels, per_device(): call(functools.partial(far_kernel, near_chips, far_chips), (jax.ShapeDtyp...  2.77 us
    pallas_call x1, Pallas kernels, per_device(): call(functools.partial(near_kernel, near_chips), (jax.ShapeDtypeStruct((n...  2.64 us
    pallas_call x1, Pallas kernels, per_device(): call(pack_kernel, (jax.ShapeDtypeStruct((2 * ROWS, half), bf16), jax.Shap...  2.51 us
    pallas_call x1, Pallas kernels, per_device(): call(functools.partial(attend, False), jax.ShapeDtypeStruct((ROWS, half),...  2.47 us
  transfers between devices with their start and end apart: 11, of which 5 were waited for; matrix products, arithmetic and copies ran while one was open for 2% of the time, Pallas kernels for 6%

profile of v6, /device:TPU:33, one launch (start us, length us, event | category | flops | bytes accessed | tf_op | source)
XLA Modules:
  0.0 110.4 jit_solution(4542428119776152083)
XLA Ops:
  0.0 2.5 %shard_map.145 = (bf16[256,640]{1,0:T(8,128)(2,1)}, bf16[384,640]{1,0:T(8,128)(2,1)}, bf16[128,640]{1,0:T(8,128)(2,1)}, f32[8,128]{1,0:T(8,128)}) custom-call(s32[1]{0:T(128)} %bitcast.here_ref, bf16[128,1280]{1,0:T(8,128)(2,1)} %q_hbm.1, bf16[128,1280]{1,0:T(8,128)(2,1)} %k_hbm.1, bf16[128,1280]{1,0:T(8,128)(2,1)} %v_hbm.1, bf16[128,1280]{1,0:T(8,128)(2,1)} %q_ref.1, ...), custom_call_target="tpu_custom_call" | custom-call | flops 1000000 | bytes 4000000 | tf_op jit(solution)/shard_map/pallas_call | solution.py:355
  2.6 2.7 %collective-permute-start = (bf16[384,640]{1,0:T(8,128)(2,1)}, bf16[384,640]{1,0:T(8,128)(2,1)S(1)}, u32[]{:S(2)}, u32[]{:S(2)}) collective-permute-start(bf16[384,640]{1,0:T(8,128)(2,1)} %get-tuple-element.28), channel_id=1, source_target_pairs={{0,4},{4,0},{8,12},{12,8},{16,20},{20,16},{24,28},{28,24},{32,36},... | collective-permute-start | bytes 1474568 | tf_op jit(solution)/shard_map/ppermute | solution.py:58
  5.3 1.9 %collective-permute-start.1 = (f32[8,128]{1,0:T(8,128)}, f32[8,128]{1,0:T(8,128)S(1)}, u32[]{:S(2)}, u32[]{:S(2)}) collective-permute-start(f32[8,128]{1,0:T(8,128)} %get-tuple-element.29.own_ref), channel_id=1, source_target_pairs={{0,4},{4,0},{8,12},{12,8},{16,20},{20,16},{24,28},{28,24},{32,36},... | collective-permute-start | bytes 12296 | tf_op jit(solution)/shard_map/ppermute | solution.py:58
  7.3 1.3 %collective-permute-done.1.mate_ref = f32[8,128]{1,0:T(8,128)S(1)} collective-permute-done((f32[8,128]{1,0:T(8,128)}, f32[8,128]{1,0:T(8,128)S(1)}, u32[]{:S(2)}, u32[]{:S(2)}) %collective-permute-start.1) | collective-permute-done | bytes 4128 | tf_op jit(solution)/shard_map/ppermute | solution.py:58
  9.3 6.4 %collective-permute-start.3 = (f32[8,128]{1,0:T(8,128)S(1)}, f32[8,128]{1,0:T(8,128)S(1)}, u32[]{:S(2)}, u32[]{:S(2)}) collective-permute-start(f32[8,128]{1,0:T(8,128)S(1)} %shard_map.146.own_ref), channel_id=1, source_target_pairs={{8,0},{12,4},{16,8},{20,12},{24,16},{28,20},{32,24},{36,28},{40,32... | collective-permute-start | bytes 12296 | tf_op jit(solution)/shard_map/ppermute | solution.py:53
  15.6 1.9 %collective-permute-start.2 = (f32[8,128]{1,0:T(8,128)S(1)}, f32[8,128]{1,0:T(8,128)S(1)}, u32[]{:S(2)}, u32[]{:S(2)}) collective-permute-start(f32[8,128]{1,0:T(8,128)S(1)} %shard_map.146.own_ref), channel_id=1, source_target_pairs={{0,8},{4,12},{8,16},{12,20},{16,24},{20,28},{24,32},{28,36},{32,40... | collective-permute-start | bytes 12296 | tf_op jit(solution)/shard_map/ppermute | solution.py:53
  17.6 1.2 %maximum_maximum_fusion.rest_8_ = bf16[528,640]{1,0:T(8,128)(2,1)S(1)} fusion(bf16[256,640]{1,0:T(8,128)(2,1)S(1)} %slice.4, bf16[256,640]{1,0:T(8,128)(2,1)} %get-tuple-element.27, bf16[528]{0:T(1024)(128)(2,1)S(1)} %pad.2.clone), kind=kLoop, calls=%fused_computation | loop fusion | flops 2027520 | bytes 1332256 | tf_op jit(solution)/shard_map/concatenate | solution.py:373
  18.9 5.3 %collective-permute-done.2.left_ref = f32[8,128]{1,0:T(8,128)S(1)} collective-permute-done((f32[8,128]{1,0:T(8,128)S(1)}, f32[8,128]{1,0:T(8,128)S(1)}, u32[]{:S(2)}, u32[]{:S(2)}) %collective-permute-start.2) | collective-permute-done | bytes 4128 | tf_op jit(solution)/shard_map/ppermute | solution.py:53
  24.2 2.4 %collective-permute-start.5 = (bf16[528,640]{1,0:T(8,128)(2,1)S(1)}, bf16[528,640]{1,0:T(8,128)(2,1)}, u32[]{:S(2)}, u32[]{:S(2)}) collective-permute-start(bf16[528,640]{1,0:T(8,128)(2,1)S(1)} %maximum_maximum_fusion.rest_8_), channel_id=1, source_target_pairs={{8,0},{12,4},{16,8},{20,12},{24,16},{28,20},{32,24},{36,28},{40,32... | collective-permute-start | bytes 2027528 | tf_op jit(solution)/shard_map/ppermute | solution.py:53
  26.6 2.9 %collective-permute-start.4 = (bf16[528,640]{1,0:T(8,128)(2,1)S(1)}, bf16[528,640]{1,0:T(8,128)(2,1)}, u32[]{:S(2)}, u32[]{:S(2)}) collective-permute-start(bf16[528,640]{1,0:T(8,128)(2,1)S(1)} %maximum_maximum_fusion.rest_8_), channel_id=1, source_target_pairs={{0,8},{4,12},{8,16},{12,20},{16,24},{20,28},{24,32},{28,36},{32,40... | collective-permute-start | bytes 2027528 | tf_op jit(solution)/shard_map/ppermute | solution.py:53
  29.5 27.3 %psum.7.sums_ref.rest_0_ = f32[16,128]{1,0:T(8,128)S(1)} all-reduce(f32[16,128]{1,0:T(8,128)S(1)} %shard_map.147), channel_id=1, replica_groups=mesh['tile'=128,'head'=4] {'head'}, use_global_device_ids=true, to_apply=%region_0.0 | all-reduce | flops 2048 | bytes 16384 | tf_op jit(solution)/shard_map/psum | solution.py:381
  57.5 8.6 %collective-permute-start.8 = (bf16[528,640]{1,0:T(8,128)(2,1)}, bf16[528,640]{1,0:T(8,128)(2,1)S(1)}, u32[]{:S(2)}, u32[]{:S(2)}) collective-permute-start(bf16[528,640]{1,0:T(8,128)(2,1)} %constant_dynamic-update-slice_fusion.rest_9_), channel_id=1, source_target_pairs={{8,0},{12,4},{16,8},{20,12},{24,16},{28,20},{32,24},{36,28},{40,32... | collective-permute-start | bytes 2027528 | tf_op jit(solution)/shard_map/ppermute | solution.py:53
  66.1 1.9 %collective-permute-start.6 = (bf16[528,640]{1,0:T(8,128)(2,1)}, bf16[528,640]{1,0:T(8,128)(2,1)S(1)}, u32[]{:S(2)}, u32[]{:S(2)}) collective-permute-start(bf16[528,640]{1,0:T(8,128)(2,1)} %constant_dynamic-update-slice_fusion.rest_9_), channel_id=1, source_target_pairs={{0,32},{4,36},{8,40},{12,44},{16,48},{20,52},{24,56},{28,60},{32,6... | collective-permute-start | bytes 2027528 | tf_op jit(solution)/shard_map/ppermute | solution.py:53
  68.6 5.5 %collective-permute-start.9 = (bf16[528,640]{1,0:T(8,128)(2,1)}, bf16[528,640]{1,0:T(8,128)(2,1)S(1)}, u32[]{:S(2)}, u32[]{:S(2)}) collective-permute-start(bf16[528,640]{1,0:T(8,128)(2,1)} %constant_dynamic-update-slice_fusion.1.rest_7_), channel_id=1, source_target_pairs={{32,0},{36,4},{40,8},{44,12},{48,16},{52,20},{56,24},{60,28},{64,3... | collective-permute-start | bytes 2027528 | tf_op jit(solution)/shard_map/ppermute | solution.py:53
  74.1 1.9 %collective-permute-start.7 = (bf16[528,640]{1,0:T(8,128)(2,1)}, bf16[528,640]{1,0:T(8,128)(2,1)S(1)}, u32[]{:S(2)}, u32[]{:S(2)}) collective-permute-start(bf16[528,640]{1,0:T(8,128)(2,1)} %constant_dynamic-update-slice_fusion.1.rest_7_), channel_id=1, source_target_pairs={{0,8},{4,12},{8,16},{12,20},{16,24},{20,28},{24,32},{28,36},{32,40... | collective-permute-start | bytes 2027528 | tf_op jit(solution)/shard_map/ppermute | solution.py:53
  76.2 1.1 copy-done.4
  77.3 1.6 %shard_map.148.text_ref = f32[128,1280]{1,0:T(8,128)S(1)} custom-call(s32[128]{0:T(128)S(1)} %copy-done.6, s32[128]{0:T(128)S(1)} %copy-done.9, s32[1]{0:T(128)} %bitcast.here_ref, f32[16,128]{1,0:T(8,128)S(1)} %psum.7.sums_ref.rest_0_, bf16[128,1280]{1,0:T(8,128)(2,1)S(1)} %copy-done.3, bf16[256,1280]{1,0:T(8,128)(2,1)S(1)} %copy-done, ...), custom_call_target="tpu_custom_call" | custom-call | flops 400000000 | bytes 4000000 | tf_op jit(solution)/shard_map/pallas_call | solution.py:392
  78.9 2.6 %shard_map.150 = (bf16[768,640]{1,0:T(8,128)(2,1)S(1)}, bf16[768,640]{1,0:T(8,128)(2,1)S(1)}, bf16[128,640]{1,0:T(8,128)(2,1)S(1)}, bf16[128,640]{1,0:T(8,128)(2,1)S(1)}) custom-call(s32[128]{0:T(128)S(1)} %copy-done.6, s32[1]{0:T(128)} %bitcast.here_ref, f32[16,128]{1,0:T(8,128)S(1)} %psum.7.sums_ref.rest_0_, f32[1,1280]{1,0:T(1,128)S(1)} %broadcast_in_dim.19.rest_1_, ...), custom_call_target="tpu_custom_call" | custom-call | flops 200000000 | bytes 4000000 | tf_op jit(solution)/shard_map/pallas_call | solution.py:412
  81.5 12.1 %collective-permute-done.6.rest_7_ = bf16[528,640]{1,0:T(8,128)(2,1)S(1)} collective-permute-done((bf16[528,640]{1,0:T(8,128)(2,1)}, bf16[528,640]{1,0:T(8,128)(2,1)S(1)}, u32[]{:S(2)}, u32[]{:S(2)}) %collective-permute-start.6) | collective-permute-done | bytes 675872 | tf_op jit(solution)/shard_map/ppermute | solution.py:53
  93.6 1.2 %collective-permute-done.9.rest_10_ = bf16[528,640]{1,0:T(8,128)(2,1)S(1)} collective-permute-done((bf16[528,640]{1,0:T(8,128)(2,1)}, bf16[528,640]{1,0:T(8,128)(2,1)S(1)}, u32[]{:S(2)}, u32[]{:S(2)}) %collective-permute-start.9) | collective-permute-done | bytes 675872 | tf_op jit(solution)/shard_map/ppermute | solution.py:53
  94.8 3.3 %collective-permute-done.7.rest_8_ = bf16[528,640]{1,0:T(8,128)(2,1)S(1)} collective-permute-done((bf16[528,640]{1,0:T(8,128)(2,1)}, bf16[528,640]{1,0:T(8,128)(2,1)S(1)}, u32[]{:S(2)}, u32[]{:S(2)}) %collective-permute-start.7) | collective-permute-done | bytes 675872 | tf_op jit(solution)/shard_map/ppermute | solution.py:53
  98.0 2.8 %shard_map.151 = (f32[128,640]{1,0:T(8,128)S(1)}, bf16[1792,640]{1,0:T(8,128)(2,1)S(1)}, bf16[1792,640]{1,0:T(8,128)(2,1)S(1)}) custom-call(s32[128]{0:T(128)S(1)} %copy-done.6, s32[128]{0:T(128)S(1)} %copy-done.8, s32[1]{0:T(128)} %bitcast.here_ref, f32[16,128]{1,0:T(8,128)S(1)} %psum.7.sums_ref.rest_0_, f32[1,1280]{1,0:T(1,128)S(1)} %broadcast_in_dim.19.rest_1_, ...), custom_call_target="tpu_custom_call" | custom-call | flops 300000000 | bytes 4000000 | tf_op jit(solution)/shard_map/pallas_call | solution.py:431
  100.8 6.3 %collective-permute-start.10 = (f32[128,640]{1,0:T(8,128)S(1)}, f32[128,640]{1,0:T(8,128)S(1)}, u32[]{:S(2)}, u32[]{:S(2)}) collective-permute-start(f32[128,640]{1,0:T(8,128)S(1)} %get-tuple-element.47), channel_id=1, source_target_pairs={{0,4},{4,0},{8,12},{12,8},{16,20},{20,16},{24,28},{28,24},{32,36},... | collective-permute-start | bytes 983048 | tf_op jit(solution)/shard_map/ppermute | solution.py:58
  107.1 2.5 %shard_map.152.own_ref = f32[128,640]{1,0:T(8,128)S(1)} custom-call(s32[128]{0:T(128)S(1)} %copy-done.6, s32[128]{0:T(128)S(1)} %copy-done.8, s32[1]{0:T(128)} %bitcast.here_ref, bf16[128,640]{1,0:T(8,128)(2,1)S(1)} %get-tuple-element.41.q_ref, bf16[1792,640]{1,0:T(8,128)(2,1)S(1)} %get-tuple-element.45.keys_ref, ...), custom_call_target="tpu_custom_call" | custom-call | flops 300000000 | bytes 4000000 | tf_op jit(solution)/shard_map/pallas_call | solution.py:450
  (46 shorter events, 2.9 us)
Async XLA Ops:
  0.0 76.0 %copy-start.10 = (f32[1280]{0:T(1024)S(1)}, f32[1280]{0:T(1024)}, u32[]{:S(2)}) copy-start(f32[1280]{0:T(1024)} %param.21) | copy-start | bytes 15364
  0.0 76.1 %copy-start.11 = (f32[1280]{0:T(1024)S(1)}, f32[1280]{0:T(1024)}, u32[]{:S(2)}) copy-start(f32[1280]{0:T(1024)} %param.22) | copy-start | bytes 15364
  0.0 76.1 %copy-start.12 = (f32[1280]{0:T(1024)S(1)}, f32[1280]{0:T(1024)}, u32[]{:S(2)}) copy-start(f32[1280]{0:T(1024)} %param.23) | copy-start | bytes 15364
  0.0 76.1 %copy-start.13 = (f32[1280]{0:T(1024)S(1)}, f32[1280]{0:T(1024)}, u32[]{:S(2)}) copy-start(f32[1280]{0:T(1024)} %param.24) | copy-start | bytes 15364
  0.0 76.1 %copy-start.9 = (s32[128]{0:T(128)S(1)}, s32[128]{0:T(128)}, u32[]{:S(2)}) copy-start(s32[128]{0:T(128)} %len_ref.1) | copy-start | bytes 1540
  2.6 73.6 %copy-start = (bf16[256,1280]{1,0:T(8,128)(2,1)S(1)}, bf16[256,1280]{1,0:T(8,128)(2,1)}, u32[]{:S(2)}) copy-start(bf16[256,1280]{1,0:T(8,128)(2,1)} %k_ref.1) | copy-start | bytes 1966084
  2.6 73.6 %copy-start.3 = (bf16[128,1280]{1,0:T(8,128)(2,1)S(1)}, bf16[128,1280]{1,0:T(8,128)(2,1)}, u32[]{:S(2)}) copy-start(bf16[128,1280]{1,0:T(8,128)(2,1)} %q_ref.1) | copy-start | bytes 983044
  2.6 73.6 %copy-start.6 = (s32[128]{0:T(128)S(1)}, s32[128]{0:T(128)}, u32[]{:S(2)}) copy-start(s32[128]{0:T(128)} %item_ref.7) | copy-start | bytes 1540
  2.6 15.0 %collective-permute-start = (bf16[384,640]{1,0:T(8,128)(2,1)}, bf16[384,640]{1,0:T(8,128)(2,1)S(1)}, u32[]{:S(2)}, u32[]{:S(2)}) collective-permute-start(bf16[384,640]{1,0:T(8,128)(2,1)} %get-tuple-element.28), channel_id=1, source_target_pairs={{0,4},{4,0},{8,12},{12,8},{16,20},{20,16},{24,28},{28,24},{32,36},... | collective-permute-start | bytes 1474568 | tf_op jit(solution)/shard_map/ppermute | solution.py:58
  5.3 3.3 %collective-permute-start.1 = (f32[8,128]{1,0:T(8,128)}, f32[8,128]{1,0:T(8,128)S(1)}, u32[]{:S(2)}, u32[]{:S(2)}) collective-permute-start(f32[8,128]{1,0:T(8,128)} %get-tuple-element.29.own_ref), channel_id=1, source_target_pairs={{0,4},{4,0},{8,12},{12,8},{16,20},{20,16},{24,28},{28,24},{32,36},... | collective-permute-start | bytes 12296 | tf_op jit(solution)/shard_map/ppermute | solution.py:58
  9.3 9.6 %collective-permute-start.3 = (f32[8,128]{1,0:T(8,128)S(1)}, f32[8,128]{1,0:T(8,128)S(1)}, u32[]{:S(2)}, u32[]{:S(2)}) collective-permute-start(f32[8,128]{1,0:T(8,128)S(1)} %shard_map.146.own_ref), channel_id=1, source_target_pairs={{8,0},{12,4},{16,8},{20,12},{24,16},{28,20},{32,24},{36,28},{40,32... | collective-permute-start | bytes 12296 | tf_op jit(solution)/shard_map/ppermute | solution.py:53
  15.6 8.6 %collective-permute-start.2 = (f32[8,128]{1,0:T(8,128)S(1)}, f32[8,128]{1,0:T(8,128)S(1)}, u32[]{:S(2)}, u32[]{:S(2)}) collective-permute-start(f32[8,128]{1,0:T(8,128)S(1)} %shard_map.146.own_ref), channel_id=1, source_target_pairs={{0,8},{4,12},{8,16},{12,20},{16,24},{20,28},{24,32},{28,36},{32,40... | collective-permute-start | bytes 12296 | tf_op jit(solution)/shard_map/ppermute | solution.py:53
  17.6 61.2 %copy-start.5 = (bf16[128,640]{1,0:T(8,128)(2,1)S(1)}, bf16[128,640]{1,0:T(8,128)(2,1)}, u32[]{:S(2)}) copy-start(bf16[128,640]{1,0:T(8,128)(2,1)} %get-tuple-element.36.rest_5_) | copy-start | bytes 491524
  18.8 60.0 %copy-start.1 = (f32[896,128]{1,0:T(8,128)S(1)}, f32[896,128]{1,0:T(8,128)}, u32[]{:S(2)}) copy-start(f32[896,128]{1,0:T(8,128)} %constant.17.clone.rest_4_.rest_3_) | copy-start | bytes 1376260
  18.8 60.0 %copy-start.2 = (f32[896,128]{1,0:T(8,128)S(1)}, f32[896,128]{1,0:T(8,128)}, u32[]{:S(2)}) copy-start(f32[896,128]{1,0:T(8,128)} %constant.16.clone.rest_3_.rest_2_) | copy-start | bytes 1376260
  24.2 32.7 %collective-permute-start.5 = (bf16[528,640]{1,0:T(8,128)(2,1)S(1)}, bf16[528,640]{1,0:T(8,128)(2,1)}, u32[]{:S(2)}, u32[]{:S(2)}) collective-permute-start(bf16[528,640]{1,0:T(8,128)(2,1)S(1)} %maximum_maximum_fusion.rest_8_), channel_id=1, source_target_pairs={{8,0},{12,4},{16,8},{20,12},{24,16},{28,20},{32,24},{36,28},{40,32... | collective-permute-start | bytes 2027528 | tf_op jit(solution)/shard_map/ppermute | solution.py:53
  26.6 30.3 %collective-permute-start.4 = (bf16[528,640]{1,0:T(8,128)(2,1)S(1)}, bf16[528,640]{1,0:T(8,128)(2,1)}, u32[]{:S(2)}, u32[]{:S(2)}) collective-permute-start(bf16[528,640]{1,0:T(8,128)(2,1)S(1)} %maximum_maximum_fusion.rest_8_), channel_id=1, source_target_pairs={{0,8},{4,12},{8,16},{12,20},{16,24},{20,28},{24,32},{28,36},{32,40... | collective-permute-start | bytes 2027528 | tf_op jit(solution)/shard_map/ppermute | solution.py:53
  57.5 24.0 %collective-permute-start.8 = (bf16[528,640]{1,0:T(8,128)(2,1)}, bf16[528,640]{1,0:T(8,128)(2,1)S(1)}, u32[]{:S(2)}, u32[]{:S(2)}) collective-permute-start(bf16[528,640]{1,0:T(8,128)(2,1)} %constant_dynamic-update-slice_fusion.rest_9_), channel_id=1, source_target_pairs={{8,0},{12,4},{16,8},{20,12},{24,16},{28,20},{32,24},{36,28},{40,32... | collective-permute-start | bytes 2027528 | tf_op jit(solution)/shard_map/ppermute | solution.py:53
  66.1 27.5 %collective-permute-start.6 = (bf16[528,640]{1,0:T(8,128)(2,1)}, bf16[528,640]{1,0:T(8,128)(2,1)S(1)}, u32[]{:S(2)}, u32[]{:S(2)}) collective-permute-start(bf16[528,640]{1,0:T(8,128)(2,1)} %constant_dynamic-update-slice_fusion.rest_9_), channel_id=1, source_target_pairs={{0,32},{4,36},{8,40},{12,44},{16,48},{20,52},{24,56},{28,60},{32,6... | collective-permute-start | bytes 2027528 | tf_op jit(solution)/shard_map/ppermute | solution.py:53
  68.6 26.1 %collective-permute-start.9 = (bf16[528,640]{1,0:T(8,128)(2,1)}, bf16[528,640]{1,0:T(8,128)(2,1)S(1)}, u32[]{:S(2)}, u32[]{:S(2)}) collective-permute-start(bf16[528,640]{1,0:T(8,128)(2,1)} %constant_dynamic-update-slice_fusion.1.rest_7_), channel_id=1, source_target_pairs={{32,0},{36,4},{40,8},{44,12},{48,16},{52,20},{56,24},{60,28},{64,3... | collective-permute-start | bytes 2027528 | tf_op jit(solution)/shard_map/ppermute | solution.py:53
  74.1 23.9 %collective-permute-start.7 = (bf16[528,640]{1,0:T(8,128)(2,1)}, bf16[528,640]{1,0:T(8,128)(2,1)S(1)}, u32[]{:S(2)}, u32[]{:S(2)}) collective-permute-start(bf16[528,640]{1,0:T(8,128)(2,1)} %constant_dynamic-update-slice_fusion.1.rest_7_), channel_id=1, source_target_pairs={{0,8},{4,12},{8,16},{12,20},{16,24},{20,28},{24,32},{28,36},{32,40... | collective-permute-start | bytes 2027528 | tf_op jit(solution)/shard_map/ppermute | solution.py:53
  76.2 1.1 copy-start.4
  78.9 19.2 %copy-start.8 = (s32[128]{0:T(128)S(1)}, s32[128]{0:T(128)}, u32[]{:S(2)}) copy-start(s32[128]{0:T(128)} %count_ref.3) | copy-start | bytes 1540
  100.8 8.8 %collective-permute-start.10 = (f32[128,640]{1,0:T(8,128)S(1)}, f32[128,640]{1,0:T(8,128)S(1)}, u32[]{:S(2)}, u32[]{:S(2)}) collective-permute-start(f32[128,640]{1,0:T(8,128)S(1)} %get-tuple-element.47), channel_id=1, source_target_pairs={{0,4},{4,0},{8,12},{12,8},{16,20},{20,16},{24,28},{28,24},{32,36},... | collective-permute-start | bytes 983048 | tf_op jit(solution)/shard_map/ppermute | solution.py:58
  (1 other events, 0.7 us)

commit v7 on v6

--- a/solution.py
+++ b/solution.py
@@ -18,8 +18,12 @@
 EPSILON = 1e-06
 SCALE = 1.0 / math.sqrt(HD)
 NEG = -1e30
-KEY_LINES = {-1: (7, 8), 0: (0, 5), 1: (9, 10)}
+KEY_LINES = {0: (0, 1), -1: (2, 3), 1: (4, 5), -3: (8, 9), -2: (10, 11), 2: (12, 13), 3: (14, 15)}
+QUERY_LINES = (6, 7)
+CROSS_LINE = 16
+TEXT_LINES = (17, 18)
 SPARE = 16
+TILE_ROWS = 2 * ROWS + SPARE
 
 
 def rope_tables():
@@ -93,20 +97,32 @@
             rows = x * x if rows is None else rows + x * x
         return jnp.sum(jnp.transpose(rows), axis=0, keepdims=True)
 
-    def split(ref, mine_ref, first, index):
+    def split(ref, mine_ref, mine_first, first):
         low, high = ref[:, :half], ref[:, half:]
-        mine_ref[first : first + ROWS, :] = jnp.where(core == 0, low, high)
-        theirs_ref[index * ROWS : (index + 1) * ROWS, :] = jnp.where(core == 0, high, low)
+        mine_ref[mine_first : mine_first + ROWS, :] = jnp.where(core == 0, low, high)
+        theirs_ref[first : first + ROWS, :] = jnp.where(core == 0, high, low)
 
     sums_ref[...] = jnp.zeros((8, ROWS), jnp.float32)
     copies[0].wait()
     split(k_ref, kv_ref, 0, 0)
-    sums_ref[0:1, :] = total(k_ref, 0)
+    k_total = total(k_ref, 0)
     copies[1].wait()
-    split(v_ref, kv_ref, ROWS, 1)
+    split(v_ref, kv_ref, ROWS, ROWS)
     copies[2].wait()
-    split(q_ref, q_mine_ref, 0, 2)
-    sums_ref[1:2, :] = total(q_ref, 0)
+    split(q_ref, q_mine_ref, 0, TILE_ROWS)
+    q_total = total(q_ref, 0)
+    sums_ref[0:1, :] = k_total
+    sums_ref[1:2, :] = q_total
+    rows = []
+    for rest in (k_total, q_total):
+        for _ in range(3):
+            rows.append(rest.astype(jnp.bfloat16).astype(jnp.float32))
+            rest = rest - rows[-1]
+    rows.append(jnp.zeros((SPARE - len(rows), ROWS), jnp.float32))
+    spare = jnp.concatenate(rows, axis=0).astype(jnp.bfloat16)
+    for ref in (kv_ref, theirs_ref):
+        ref[2 * ROWS : TILE_ROWS, 0:ROWS] = spare
+        ref[2 * ROWS : TILE_ROWS, ROWS:] = jnp.zeros((SPARE, half - ROWS), jnp.bfloat16)
     copies[3].wait()
     sums_ref[2:3, :] = total(c_ref, 0)
     copies[4].wait()
@@ -114,38 +130,36 @@
     sums_ref[4:5, :] = total(t_ref, ROWS)
 
 
-def mate_kernel(own_ref, mate_ref, out_ref):
-    out_ref[...] = own_ref[...]
-    out_ref[5:7, :] = mate_ref[0:2, :]
-
-
-def table_kernel(own_ref, left_ref, right_ref, out_ref):
-    out_ref[0:8, :] = own_ref[...]
-    out_ref[8:16, :] = jnp.zeros((8, ROWS), jnp.float32)
-    out_ref[7:8, :] = left_ref[0:1, :]
-    out_ref[8:9, :] = left_ref[5:6, :]
-    out_ref[9:10, :] = right_ref[0:1, :]
-    out_ref[10:11, :] = right_ref[5:6, :]
-
-
-def pieces_kernel(sums_ref, left_ref, right_ref):
-    for chip, out_ref in ((-1, left_ref), (1, right_ref)):
-        out_ref[...] = jnp.zeros(out_ref.shape, jnp.bfloat16)
-        rows = []
-        for line in KEY_LINES[chip]:
-            rest = sums_ref[line : line + 1, :]
-            for _ in range(3):
-                piece = rest.astype(jnp.bfloat16)
-                rows.append(piece.astype(jnp.float32))
-                rest = rest - rows[-1]
-        rows.append(jnp.zeros((SPARE - len(rows), ROWS), jnp.float32))
-        out_ref[:, 0:ROWS] = jnp.concatenate(rows, axis=0).astype(jnp.bfloat16)
+def pieced(spare_ref, first):
+    rows = spare_ref[...].astype(jnp.float32)
+    return rows[first : first + 1] + rows[first + 1 : first + 2] + rows[first + 2 : first + 3]
+
+
+def close_kernel(own_ref, mate_ref, left_own_ref, left_mate_ref, right_own_ref, right_mate_ref, out_ref):
+    out_ref[0:1, :] = own_ref[0:1, :]
+    out_ref[1:2, :] = pieced(mate_ref, 0)
+    out_ref[2:3, :] = pieced(left_own_ref, 0)
+    out_ref[3:4, :] = pieced(left_mate_ref, 0)
+    out_ref[4:5, :] = pieced(right_own_ref, 0)
+    out_ref[5:6, :] = pieced(right_mate_ref, 0)
+    out_ref[6:7, :] = own_ref[1:2, :]
+    out_ref[7:8, :] = pieced(mate_ref, 3)
+
+
+def table_kernel(own_ref, close_ref, left_ref, right_ref, out_ref):
+    out_ref[0:8, :] = close_ref[...]
+    out_ref[8:10, :] = left_ref[2:4, :]
+    out_ref[10:12, :] = left_ref[0:2, :]
+    out_ref[12:14, :] = right_ref[0:2, :]
+    out_ref[14:16, :] = right_ref[4:6, :]
+    out_ref[16:24, :] = jnp.zeros((8, ROWS), jnp.float32)
+    out_ref[16:19, :] = own_ref[2:5, :]
 
 
 def cross_kernel(item_ref, len_ref, here_ref, sums_ref, q_ref, k_ref, v_ref, qg_ref, kg_ref, out_ref):
     count = len_ref[item_ref[here_ref[0]]]
-    q_factor = by_rows(sums_ref[2:3, :])
-    k_factor = [by_rows(sums_ref[3:4, :]), by_rows(sums_ref[4:5, :])]
+    q_factor = by_rows(sums_ref[CROSS_LINE : CROSS_LINE + 1, :])
+    k_factor = [by_rows(sums_ref[line : line + 1, :]) for line in TEXT_LINES]
     live = prefix_live((ROWS, 2 * ROWS), count)
     for head in range(q_ref.shape[1] // HD):
         cols = slice(head * HD, (head + 1) * HD)
@@ -196,8 +210,8 @@
     for parity in range(2):
         tile = left + 2 * chip + parity
         slot = jnp.where(core == parity, 0, 1)
-        key_rows = pl.ds(pl.multiple_of(slot * 2 * ROWS, 2 * ROWS), ROWS)
-        value_rows = pl.ds(pl.multiple_of(slot * 2 * ROWS + ROWS, ROWS), ROWS)
+        key_rows = pl.ds(pl.multiple_of(slot * TILE_ROWS, SPARE), ROWS)
+        value_rows = pl.ds(pl.multiple_of(slot * TILE_ROWS + ROWS, SPARE), ROWS)
         goal = slice((place + parity) * ROWS, (place + parity + 1) * ROWS)
         values_ref[goal, :] = block[value_rows, :]
 
@@ -205,14 +219,7 @@
         def _(parity=parity, tile=tile, key_rows=key_rows, goal=goal):
             first = jnp.where(tile <= last_a, first_a, first_b)
             start = pl.multiple_of((tile - first) * ROWS, ROWS)
-            if chip in KEY_LINES:
-                own, mate = (sums_ref[line : line + 1, :] for line in KEY_LINES[chip])
-            else:
-                spare = block[4 * ROWS : 4 * ROWS + SPARE, 0:ROWS].astype(jnp.float32)
-                own, mate = (
-                    spare[3 * i : 3 * i + 1] + spare[3 * i + 1 : 3 * i + 2] + spare[3 * i + 2 : 3 * i + 3]
-                    for i in range(2)
-                )
+            own, mate = (sums_ref[line : line + 1, :] for line in KEY_LINES[chip])
             total = jnp.where(core == parity, own, mate)
             turn(block, key_rows, by_rows(total), gains, cos_ref, sin_ref, start, keys_ref, goal)
 
@@ -229,8 +236,8 @@
     k_gains, q_gains = k_gain_ref.at[:, part], q_gain_ref.at[:, part]
     for which, (source, rows, line, goal) in enumerate(
         (
-            (q_own_ref, slice(0, ROWS), 1, own_turned_ref),
-            (q_mate_ref, slice(2 * ROWS, 3 * ROWS), 6, mate_turned_ref),
+            (q_own_ref, slice(0, ROWS), QUERY_LINES[0], own_turned_ref),
+            (q_mate_ref, slice(TILE_ROWS, TILE_ROWS + ROWS), QUERY_LINES[1], mate_turned_ref),
         )
     ):
         is_a = core == which
@@ -355,8 +362,8 @@
     kv, theirs, q_mine, sums = call(
         pack_kernel,
         (
-            jax.ShapeDtypeStruct((2 * ROWS, half), bf16),
-            jax.ShapeDtypeStruct((3 * ROWS, half), bf16),
+            jax.ShapeDtypeStruct((TILE_ROWS, half), bf16),
+            jax.ShapeDtypeStruct((TILE_ROWS + ROWS, half), bf16),
             jax.ShapeDtypeStruct((ROWS, half), bf16),
             jax.ShapeDtypeStruct((8, ROWS), f32),
         ),
@@ -368,26 +375,34 @@
     got = swapped(theirs)
     peers = lax.axis_size("tile")
     low_pair, high_pair = (0, 1), (peers - 2, peers - 1)
-    table = jax.ShapeDtypeStruct((8, ROWS), f32)
-    sums = call(mate_kernel, table, [vmem] * 2)(sums, swapped(sums))
-    block = jnp.concatenate([kv, got[: 2 * ROWS], jnp.zeros((SPARE, half), bf16)], axis=0)
-    left_sums = shifted(sums, 2, high_pair)
-    right_sums = shifted(sums, -2, low_pair)
-    block, left_sums, right_sums = lax.optimization_barrier((block, left_sums, right_sums))
+    block = jnp.concatenate([kv, got[:TILE_ROWS]], axis=0)
     left = shifted(block, 2, high_pair)
     right = shifted(block, -2, low_pair)
-    table = jax.ShapeDtypeStruct((16, ROWS), f32)
-    sums = call(table_kernel, table, [vmem] * 3)(sums, left_sums, right_sums)
-    sums = lax.psum(sums, "head")
-    left, right, sums = lax.optimization_barrier((left, right, sums))
-    spare = jax.ShapeDtypeStruct((SPARE, half), bf16)
-    left_pieces, right_pieces = call(pieces_kernel, (spare, spare), [vmem])(sums)
-    left = lax.dynamic_update_slice(left, left_pieces, (4 * ROWS, 0))
-    right = lax.dynamic_update_slice(right, right_pieces, (4 * ROWS, 0))
+
+    def spare(tile):
+        return pl.BlockSpec((SPARE, ROWS), lambda i: ((tile * TILE_ROWS + 2 * ROWS) // SPARE, 0))
+
+    few = pl.BlockSpec((8, ROWS), lambda i: (0, 0))
+    close = pl.pallas_call(
+        close_kernel,
+        grid=(1,),
+        out_shape=jax.ShapeDtypeStruct((8, ROWS), f32),
+        in_specs=[few, spare(0), spare(0), spare(1), spare(0), spare(1)],
+        out_specs=few,
+    )(sums, got, left, left, right, right)
+    left_sums = shifted(close, 4)
+    right_sums = shifted(close, -4)
+    left, right, left_sums, right_sums = lax.optimization_barrier(
+        (left, right, left_sums, right_sums)
+    )
     right3 = shifted(left, -8, low_pair)
     left3 = shifted(right, 8, high_pair)
     left2 = shifted(left, 2)
     right2 = shifted(right, -2)
+    sums = call(table_kernel, jax.ShapeDtypeStruct((24, ROWS), f32), [vmem] * 4)(
+        sums, close, left_sums, right_sums
+    )
+    sums = lax.psum(sums, "head")
 
     text_out = call(
         cross_kernel, jax.ShapeDtypeStruct((ROWS, width), f32), [smem] * 3 + [vmem] * 6, flops=400000000

time: 111 us -> 131 us (1.18)
  the two profiles are of different devices: /device:TPU:33 before, /device:TPU:25 now
where the time goes in v7:
time: 131 us; the launch traced here: 130 us
  starting transfers between devices  44.3 us (34%)
  blocking collectives  43 us (33%)
  waiting for transfers between devices  22.4 us (17%)
  Pallas kernels  14.5 us (11%)
  local copies, waits for them, and re-layouts  4.73 us (4%)
    psum x1, blocking collectives, per_device(): sums = lax.psum(sums, 'head')  43 us
    ppermute x8, starting transfers between devices, shifted(): lax.ppermute(value, 'tile', pairs + [(i, (i + by) % peers) for i in wrapp...  34.1 us
    ppermute x8, waiting for transfers between devices, shifted(): lax.ppermute(value, 'tile', pairs + [(i, (i + by) % peers) for i in wrapp...  20.7 us
    ppermute x2, starting transfers between devices, swapped(): return lax.ppermute(value, 'tile', [(i, i ^ 1) for i in range(peers)])  10.2 us
    unnamed x44, local copies, waits for them, and re-layouts  4.67 us
    pallas_call x1, Pallas kernels, per_device(): call(functools.partial(far_kernel, near_chips, far_chips), (jax.ShapeDtyp...  3.95 us
  transfers between devices with their start and end apart: 10, of which 4 were waited for; matrix products, arithmetic and copies ran while one was open for 0% of the time, Pallas kernels for 5%

profile of v7, /device:TPU:25, one launch (start us, length us, event | category | flops | bytes accessed | tf_op | source)
XLA Modules:
  0.0 130.5 jit_solution(5641408469132336297)
XLA Ops:
  0.0 2.5 %shard_map.145 = (bf16[272,640]{1,0:T(8,128)(2,1)}, bf16[400,640]{1,0:T(8,128)(2,1)}, bf16[128,640]{1,0:T(8,128)(2,1)}, f32[8,128]{1,0:T(8,128)}) custom-call(s32[1]{0:T(128)} %bitcast.here_ref, bf16[128,1280]{1,0:T(8,128)(2,1)} %q_hbm.1, bf16[128,1280]{1,0:T(8,128)(2,1)} %k_hbm.1, bf16[128,1280]{1,0:T(8,128)(2,1)} %v_hbm.1, bf16[128,1280]{1,0:T(8,128)(2,1)} %q_ref.1, ...), custom_call_target="tpu_custom_call" | custom-call | flops 1000000 | bytes 4000000 | tf_op jit(solution)/shard_map/pallas_call | solution.py:362
  2.5 2.6 %collective-permute-start = (bf16[400,640]{1,0:T(8,128)(2,1)}, bf16[400,640]{1,0:T(8,128)(2,1)S(1)}, u32[]{:S(2)}, u32[]{:S(2)}) collective-permute-start(bf16[400,640]{1,0:T(8,128)(2,1)} %get-tuple-element.24), channel_id=1, source_target_pairs={{0,4},{4,0},{8,12},{12,8},{16,20},{20,16},{24,28},{28,24},{32,36},... | collective-permute-start | bytes 1536008 | tf_op jit(solution)/shard_map/ppermute | solution.py:62
  5.1 1.7 %collective-permute-done.mate_ref.rest_6_ = bf16[400,640]{1,0:T(8,128)(2,1)S(1)} collective-permute-done((bf16[400,640]{1,0:T(8,128)(2,1)}, bf16[400,640]{1,0:T(8,128)(2,1)S(1)}, u32[]{:S(2)}, u32[]{:S(2)}) %collective-permute-start) | collective-permute-done | bytes 512032 | tf_op jit(solution)/shard_map/ppermute | solution.py:62
  6.8 1.2 pad_maximum_fusion.rest_8_
  8.0 4.6 %collective-permute-start.2 = (bf16[544,640]{1,0:T(8,128)(2,1)S(1)}, bf16[544,640]{1,0:T(8,128)(2,1)S(1)}, u32[]{:S(2)}, u32[]{:S(2)}) collective-permute-start(bf16[544,640]{1,0:T(8,128)(2,1)S(1)} %pad_maximum_fusion.rest_8_), channel_id=1, source_target_pairs={{8,0},{12,4},{16,8},{20,12},{24,16},{28,20},{32,24},{36,28},{40,32... | collective-permute-start | bytes 2088968 | tf_op jit(solution)/shard_map/ppermute | solution.py:57
  12.6 1.9 %collective-permute-start.1 = (bf16[544,640]{1,0:T(8,128)(2,1)S(1)}, bf16[544,640]{1,0:T(8,128)(2,1)S(1)}, u32[]{:S(2)}, u32[]{:S(2)}) collective-permute-start(bf16[544,640]{1,0:T(8,128)(2,1)S(1)} %pad_maximum_fusion.rest_8_), channel_id=1, source_target_pairs={{0,8},{4,12},{8,16},{12,20},{16,24},{20,28},{24,32},{28,36},{32,40... | collective-permute-start | bytes 2088968 | tf_op jit(solution)/shard_map/ppermute | solution.py:57
  14.5 12.7 %collective-permute-done.2.right_own_ref.right_mate_ref.rest_9_ = bf16[544,640]{1,0:T(8,128)(2,1)S(1)} collective-permute-done((bf16[544,640]{1,0:T(8,128)(2,1)S(1)}, bf16[544,640]{1,0:T(8,128)(2,1)S(1)}, u32[]{:S(2)}, u32[]{:S(2)}) %collective-permute-start.2) | collective-permute-done | bytes 696352 | tf_op jit(solution)/shard_map/ppermute | solution.py:57
  27.2 5.9 %collective-permute-done.1.left_own_ref.left_mate_ref.rest_7_ = bf16[544,640]{1,0:T(8,128)(2,1)S(1)} collective-permute-done((bf16[544,640]{1,0:T(8,128)(2,1)S(1)}, bf16[544,640]{1,0:T(8,128)(2,1)S(1)}, u32[]{:S(2)}, u32[]{:S(2)}) %collective-permute-start.1) | collective-permute-done | bytes 696352 | tf_op jit(solution)/shard_map/ppermute | solution.py:57
  34.1 1.4 %shard_map.146.close_ref = f32[8,128]{1,0:T(8,128)} custom-call(f32[8,128]{1,0:T(8,128)} %get-tuple-element.23.own_ref, bf16[400,640]{1,0:T(8,128)(2,1)} %copy-done.4, bf16[544,640]{1,0:T(8,128)(2,1)} %copy-done.2, bf16[544,640]{1,0:T(8,128)(2,1)} %copy-done.2, bf16[544,640]{1,0:T(8,128)(2,1)} %copy-done, bf16[544,640]{1,0:T(8,128)(2,1)} %copy-done), custom_call_target="tpu_custom_call" | custom-call | tf_op jit(solution)/shard_map/pallas_call | solution.py:386
  35.4 2.1 %collective-permute-start.4 = (f32[8,128]{1,0:T(8,128)}, f32[8,128]{1,0:T(8,128)S(1)}, u32[]{:S(2)}, u32[]{:S(2)}) collective-permute-start(f32[8,128]{1,0:T(8,128)} %shard_map.146.close_ref), channel_id=1, source_target_pairs={{16,0},{20,4},{24,8},{28,12},{32,16},{36,20},{40,24},{44,28},{48,3... | collective-permute-start | bytes 12296 | tf_op jit(solution)/shard_map/ppermute | solution.py:57
  37.5 4.9 %collective-permute-start.3 = (f32[8,128]{1,0:T(8,128)}, f32[8,128]{1,0:T(8,128)S(1)}, u32[]{:S(2)}, u32[]{:S(2)}) collective-permute-start(f32[8,128]{1,0:T(8,128)} %shard_map.146.close_ref), channel_id=1, source_target_pairs={{0,16},{4,20},{8,24},{12,28},{16,32},{20,36},{24,40},{28,44},{32,4... | collective-permute-start | bytes 12296 | tf_op jit(solution)/shard_map/ppermute | solution.py:57
  42.4 2.1 %collective-permute-done.3.left_ref = f32[8,128]{1,0:T(8,128)S(1)} collective-permute-done((f32[8,128]{1,0:T(8,128)}, f32[8,128]{1,0:T(8,128)S(1)}, u32[]{:S(2)}, u32[]{:S(2)}) %collective-permute-start.3) | collective-permute-done | bytes 4128 | tf_op jit(solution)/shard_map/ppermute | solution.py:57
  44.5 2.1 %collective-permute-start.8 = (bf16[544,640]{1,0:T(8,128)(2,1)}, bf16[544,640]{1,0:T(8,128)(2,1)}, u32[]{:S(2)}, u32[]{:S(2)}) collective-permute-start(bf16[544,640]{1,0:T(8,128)(2,1)} %copy-done.2), channel_id=1, source_target_pairs={{32,0},{36,4},{40,8},{44,12},{48,16},{52,20},{56,24},{60,28},{64,3... | collective-permute-start | bytes 2088968 | tf_op jit(solution)/shard_map/ppermute | solution.py:57
  46.5 1.9 %collective-permute-start.6 = (bf16[544,640]{1,0:T(8,128)(2,1)}, bf16[544,640]{1,0:T(8,128)(2,1)}, u32[]{:S(2)}, u32[]{:S(2)}) collective-permute-start(bf16[544,640]{1,0:T(8,128)(2,1)} %copy-done.2), channel_id=1, source_target_pairs={{0,8},{4,12},{8,16},{12,20},{16,24},{20,28},{24,32},{28,36},{32,40... | collective-permute-start | bytes 2088968 | tf_op jit(solution)/shard_map/ppermute | solution.py:57
  48.5 5.5 %collective-permute-start.7 = (bf16[544,640]{1,0:T(8,128)(2,1)}, bf16[544,640]{1,0:T(8,128)(2,1)}, u32[]{:S(2)}, u32[]{:S(2)}) collective-permute-start(bf16[544,640]{1,0:T(8,128)(2,1)} %copy-done), channel_id=1, source_target_pairs={{8,0},{12,4},{16,8},{20,12},{24,16},{28,20},{32,24},{36,28},{40,32... | collective-permute-start | bytes 2088968 | tf_op jit(solution)/shard_map/ppermute | solution.py:57
  54.0 11.2 %collective-permute-start.5 = (bf16[544,640]{1,0:T(8,128)(2,1)}, bf16[544,640]{1,0:T(8,128)(2,1)}, u32[]{:S(2)}, u32[]{:S(2)}) collective-permute-start(bf16[544,640]{1,0:T(8,128)(2,1)} %copy-done), channel_id=1, source_target_pairs={{0,32},{4,36},{8,40},{12,44},{16,48},{20,52},{24,56},{28,60},{32,6... | collective-permute-start | bytes 2088968 | tf_op jit(solution)/shard_map/ppermute | solution.py:57
  65.9 43.0 %psum.7.sums_ref.rest_0_ = f32[24,128]{1,0:T(8,128)S(1)} all-reduce(f32[24,128]{1,0:T(8,128)S(1)} %shard_map.147), channel_id=1, replica_groups=mesh['tile'=128,'head'=4] {'head'}, use_global_device_ids=true, to_apply=%region_0.0 | all-reduce | flops 3072 | bytes 24576 | tf_op jit(solution)/shard_map/psum | solution.py:405
  109.9 1.1 copy-done.11
  111.0 1.6 %shard_map.148.text_ref = f32[128,1280]{1,0:T(8,128)S(1)} custom-call(s32[128]{0:T(128)S(1)} %copy-done.15, s32[128]{0:T(128)S(1)} %copy-done.17, s32[1]{0:T(128)} %bitcast.here_ref, f32[24,128]{1,0:T(8,128)S(1)} %psum.7.sums_ref.rest_0_, bf16[128,1280]{1,0:T(8,128)(2,1)S(1)} %copy-done.10, bf16[256,1280]{1,0:T(8,128)(2,1)S(1)} %copy-done.6, ...), custom_call_target="tpu_custom_call" | custom-call | flops 400000000 | bytes 4000000 | tf_op jit(solution)/shard_map/pallas_call | solution.py:407
  112.6 1.0 copy-done.8
  113.6 1.9 %shard_map.149 = (bf16[768,640]{1,0:T(8,128)(2,1)S(1)}, bf16[768,640]{1,0:T(8,128)(2,1)S(1)}, bf16[128,640]{1,0:T(8,128)(2,1)S(1)}, bf16[128,640]{1,0:T(8,128)(2,1)S(1)}) custom-call(s32[128]{0:T(128)S(1)} %copy-done.15, s32[1]{0:T(128)} %bitcast.here_ref, f32[24,128]{1,0:T(8,128)S(1)} %psum.7.sums_ref.rest_0_, f32[1,1280]{1,0:T(1,128)S(1)} %broadcast_in_dim.15.rest_1_, ...), custom_call_target="tpu_custom_call" | custom-call | flops 200000000 | bytes 4000000 | tf_op jit(solution)/shard_map/pallas_call | solution.py:427
  115.6 3.9 %shard_map.150 = (f32[128,640]{1,0:T(8,128)S(1)}, bf16[1792,640]{1,0:T(8,128)(2,1)S(1)}, bf16[1792,640]{1,0:T(8,128)(2,1)S(1)}) custom-call(s32[128]{0:T(128)S(1)} %copy-done.15, s32[128]{0:T(128)S(1)} %copy-done.16, s32[1]{0:T(128)} %bitcast.here_ref, f32[24,128]{1,0:T(8,128)S(1)} %psum.7.sums_ref.rest_0_, f32[1,1280]{1,0:T(1,128)S(1)} %broadcast_in_dim.15.rest_1_, ...), custom_call_target="tpu_custom_call" | custom-call | flops 300000000 | bytes 4000000 | tf_op jit(solution)/shard_map/pallas_call | solution.py:446
  119.5 7.6 %collective-permute-start.9 = (f32[128,640]{1,0:T(8,128)S(1)}, f32[128,640]{1,0:T(8,128)S(1)}, u32[]{:S(2)}, u32[]{:S(2)}) collective-permute-start(f32[128,640]{1,0:T(8,128)S(1)} %get-tuple-element.39), channel_id=1, source_target_pairs={{0,4},{4,0},{8,12},{12,8},{16,20},{20,16},{24,28},{28,24},{32,36},... | collective-permute-start | bytes 983048 | tf_op jit(solution)/shard_map/ppermute | solution.py:62
  127.2 2.5 %shard_map.151.own_ref = f32[128,640]{1,0:T(8,128)S(1)} custom-call(s32[128]{0:T(128)S(1)} %copy-done.15, s32[128]{0:T(128)S(1)} %copy-done.16, s32[1]{0:T(128)} %bitcast.here_ref, bf16[128,640]{1,0:T(8,128)(2,1)S(1)} %get-tuple-element.33.q_ref, bf16[1792,640]{1,0:T(8,128)(2,1)S(1)} %get-tuple-element.37.keys_ref, ...), custom_call_target="tpu_custom_call" | custom-call | flops 300000000 | bytes 4000000 | tf_op jit(solution)/shard_map/pallas_call | solution.py:465
  (55 shorter events, 3.5 us)
Async XLA Ops:
  2.5 4.3 %collective-permute-start = (bf16[400,640]{1,0:T(8,128)(2,1)}, bf16[400,640]{1,0:T(8,128)(2,1)S(1)}, u32[]{:S(2)}, u32[]{:S(2)}) collective-permute-start(bf16[400,640]{1,0:T(8,128)(2,1)} %get-tuple-element.24), channel_id=1, source_target_pairs={{0,4},{4,0},{8,12},{12,8},{16,20},{20,16},{24,28},{28,24},{32,36},... | collective-permute-start | bytes 1536008 | tf_op jit(solution)/shard_map/ppermute | solution.py:62
  6.8 26.3 %copy-start.4 = (bf16[400,640]{1,0:T(8,128)(2,1)}, bf16[400,640]{1,0:T(8,128)(2,1)S(1)}, u32[]{:S(2)}) copy-start(bf16[400,640]{1,0:T(8,128)(2,1)S(1)} %collective-permute-done.mate_ref.rest_6_) | copy-start | bytes 1536004
  8.0 19.2 %collective-permute-start.2 = (bf16[544,640]{1,0:T(8,128)(2,1)S(1)}, bf16[544,640]{1,0:T(8,128)(2,1)S(1)}, u32[]{:S(2)}, u32[]{:S(2)}) collective-permute-start(bf16[544,640]{1,0:T(8,128)(2,1)S(1)} %pad_maximum_fusion.rest_8_), channel_id=1, source_target_pairs={{8,0},{12,4},{16,8},{20,12},{24,16},{28,20},{32,24},{36,28},{40,32... | collective-permute-start | bytes 2088968 | tf_op jit(solution)/shard_map/ppermute | solution.py:57
  12.6 20.5 %collective-permute-start.1 = (bf16[544,640]{1,0:T(8,128)(2,1)S(1)}, bf16[544,640]{1,0:T(8,128)(2,1)S(1)}, u32[]{:S(2)}, u32[]{:S(2)}) collective-permute-start(bf16[544,640]{1,0:T(8,128)(2,1)S(1)} %pad_maximum_fusion.rest_8_), channel_id=1, source_target_pairs={{0,8},{4,12},{8,16},{12,20},{16,24},{20,28},{24,32},{28,36},{32,40... | collective-permute-start | bytes 2088968 | tf_op jit(solution)/shard_map/ppermute | solution.py:57
  27.2 5.9 %copy-start = (bf16[544,640]{1,0:T(8,128)(2,1)}, bf16[544,640]{1,0:T(8,128)(2,1)S(1)}, u32[]{:S(2)}) copy-start(bf16[544,640]{1,0:T(8,128)(2,1)S(1)} %collective-permute-done.2.right_own_ref.right_mate_ref.rest_9_) | copy-start | bytes 2088964
  34.0 31.2 %copy-start.18 = (f32[1280]{0:T(1024)S(1)}, f32[1280]{0:T(1024)}, u32[]{:S(2)}) copy-start(f32[1280]{0:T(1024)} %param.21) | copy-start | bytes 15364
  34.0 31.2 %copy-start.19 = (f32[1280]{0:T(1024)S(1)}, f32[1280]{0:T(1024)}, u32[]{:S(2)}) copy-start(f32[1280]{0:T(1024)} %param.22) | copy-start | bytes 15364
  34.0 31.2 %copy-start.20 = (f32[1280]{0:T(1024)S(1)}, f32[1280]{0:T(1024)}, u32[]{:S(2)}) copy-start(f32[1280]{0:T(1024)} %param.23) | copy-start | bytes 15364
  34.0 31.2 %copy-start.21 = (f32[1280]{0:T(1024)S(1)}, f32[1280]{0:T(1024)}, u32[]{:S(2)}) copy-start(f32[1280]{0:T(1024)} %param.24) | copy-start | bytes 15364
  34.0 31.2 %copy-start.13 = (f32[8,128]{1,0:T(8,128)S(1)}, f32[8,128]{1,0:T(8,128)}, u32[]{:S(2)}) copy-start(f32[8,128]{1,0:T(8,128)} %get-tuple-element.23.own_ref) | copy-start | bytes 12292
  34.0 74.9 %copy-start.6 = (bf16[256,1280]{1,0:T(8,128)(2,1)S(1)}, bf16[256,1280]{1,0:T(8,128)(2,1)}, u32[]{:S(2)}) copy-start(bf16[256,1280]{1,0:T(8,128)(2,1)} %k_ref.1) | copy-start | bytes 1966084
  34.0 74.9 %copy-start.15 = (s32[128]{0:T(128)S(1)}, s32[128]{0:T(128)}, u32[]{:S(2)}) copy-start(s32[128]{0:T(128)} %item_ref.7) | copy-start | bytes 1540
  34.0 74.9 %copy-start.17 = (s32[128]{0:T(128)S(1)}, s32[128]{0:T(128)}, u32[]{:S(2)}) copy-start(s32[128]{0:T(128)} %len_ref.1) | copy-start | bytes 1540
  34.1 78.5 %copy-start.12 = (bf16[128,640]{1,0:T(8,128)(2,1)S(1)}, bf16[128,640]{1,0:T(8,128)(2,1)}, u32[]{:S(2)}) copy-start(bf16[128,640]{1,0:T(8,128)(2,1)} %get-tuple-element.30.rest_5_) | copy-start | bytes 491524
  35.4 77.1 %copy-start.1 = (bf16[544,640]{1,0:T(8,128)(2,1)S(1)}, bf16[544,640]{1,0:T(8,128)(2,1)}, u32[]{:S(2)}) copy-start(bf16[544,640]{1,0:T(8,128)(2,1)} %copy-done) | copy-start | bytes 2088964
  35.4 77.2 %copy-start.3 = (bf16[544,640]{1,0:T(8,128)(2,1)S(1)}, bf16[544,640]{1,0:T(8,128)(2,1)}, u32[]{:S(2)}) copy-start(bf16[544,640]{1,0:T(8,128)(2,1)} %copy-done.2) | copy-start | bytes 2088964
  35.4 77.2 %copy-start.5 = (bf16[400,640]{1,0:T(8,128)(2,1)S(1)}, bf16[400,640]{1,0:T(8,128)(2,1)}, u32[]{:S(2)}) copy-start(bf16[400,640]{1,0:T(8,128)(2,1)} %copy-done.4) | copy-start | bytes 1536004
  35.4 6.9 %collective-permute-start.4 = (f32[8,128]{1,0:T(8,128)}, f32[8,128]{1,0:T(8,128)S(1)}, u32[]{:S(2)}, u32[]{:S(2)}) collective-permute-start(f32[8,128]{1,0:T(8,128)} %shard_map.146.close_ref), channel_id=1, source_target_pairs={{16,0},{20,4},{24,8},{28,12},{32,16},{36,20},{40,24},{44,28},{48,3... | collective-permute-start | bytes 12296 | tf_op jit(solution)/shard_map/ppermute | solution.py:57
  37.5 7.0 %collective-permute-start.3 = (f32[8,128]{1,0:T(8,128)}, f32[8,128]{1,0:T(8,128)S(1)}, u32[]{:S(2)}, u32[]{:S(2)}) collective-permute-start(f32[8,128]{1,0:T(8,128)} %shard_map.146.close_ref), channel_id=1, source_target_pairs={{0,16},{4,20},{8,24},{12,28},{16,32},{20,36},{24,40},{28,44},{32,4... | collective-permute-start | bytes 12296 | tf_op jit(solution)/shard_map/ppermute | solution.py:57
  44.5 71.0 %collective-permute-start.8 = (bf16[544,640]{1,0:T(8,128)(2,1)}, bf16[544,640]{1,0:T(8,128)(2,1)}, u32[]{:S(2)}, u32[]{:S(2)}) collective-permute-start(bf16[544,640]{1,0:T(8,128)(2,1)} %copy-done.2), channel_id=1, source_target_pairs={{32,0},{36,4},{40,8},{44,12},{48,16},{52,20},{56,24},{60,28},{64,3... | collective-permute-start | bytes 2088968 | tf_op jit(solution)/shard_map/ppermute | solution.py:57
  46.5 69.0 %collective-permute-start.6 = (bf16[544,640]{1,0:T(8,128)(2,1)}, bf16[544,640]{1,0:T(8,128)(2,1)}, u32[]{:S(2)}, u32[]{:S(2)}) collective-permute-start(bf16[544,640]{1,0:T(8,128)(2,1)} %copy-done.2), channel_id=1, source_target_pairs={{0,8},{4,12},{8,16},{12,20},{16,24},{20,28},{24,32},{28,36},{32,40... | collective-permute-start | bytes 2088968 | tf_op jit(solution)/shard_map/ppermute | solution.py:57
  48.5 67.1 %collective-permute-start.7 = (bf16[544,640]{1,0:T(8,128)(2,1)}, bf16[544,640]{1,0:T(8,128)(2,1)}, u32[]{:S(2)}, u32[]{:S(2)}) collective-permute-start(bf16[544,640]{1,0:T(8,128)(2,1)} %copy-done), channel_id=1, source_target_pairs={{8,0},{12,4},{16,8},{20,12},{24,16},{28,20},{32,24},{36,28},{40,32... | collective-permute-start | bytes 2088968 | tf_op jit(solution)/shard_map/ppermute | solution.py:57
  54.0 61.6 %collective-permute-start.5 = (bf16[544,640]{1,0:T(8,128)(2,1)}, bf16[544,640]{1,0:T(8,128)(2,1)}, u32[]{:S(2)}, u32[]{:S(2)}) collective-permute-start(bf16[544,640]{1,0:T(8,128)(2,1)} %copy-done), channel_id=1, source_target_pairs={{0,32},{4,36},{8,40},{12,44},{16,48},{20,52},{24,56},{28,60},{32,6... | collective-permute-start | bytes 2088968 | tf_op jit(solution)/shard_map/ppermute | solution.py:57
  119.5 10.1 %collective-permute-start.9 = (f32[128,640]{1,0:T(8,128)S(1)}, f32[128,640]{1,0:T(8,128)S(1)}, u32[]{:S(2)}, u32[]{:S(2)}) collective-permute-start(f32[128,640]{1,0:T(8,128)S(1)} %get-tuple-element.39), channel_id=1, source_target_pairs={{0,4},{4,0},{8,12},{12,8},{16,20},{20,16},{24,28},{28,24},{32,36},... | collective-permute-start | bytes 983048 | tf_op jit(solution)/shard_map/ppermute | solution.py:62
  (8 other events, 10.1 us)

commit v8 on v6

--- a/solution.py
+++ b/solution.py
@@ -70,6 +70,20 @@
 
 def prefix_live(shape, count):
     return lax.broadcasted_iota(jnp.int32, shape, 1) < count
+
+
+def pieces(*totals):
+    rows = []
+    for rest in totals:
+        for _ in range(3):
+            rows.append(rest.astype(jnp.bfloat16).astype(jnp.float32))
+            rest = rest - rows[-1]
+    rows.append(jnp.zeros((SPARE - len(rows), ROWS), jnp.float32))
+    return jnp.concatenate(rows, axis=0).astype(jnp.bfloat16)
+
+
+def joined(rows, first):
+    return rows[first : first + 1] + rows[first + 1 : first + 2] + rows[first + 2 : first + 3]
 
 
 def pack_kernel(
@@ -101,12 +115,16 @@
     sums_ref[...] = jnp.zeros((8, ROWS), jnp.float32)
     copies[0].wait()
     split(k_ref, kv_ref, 0, 0)
-    sums_ref[0:1, :] = total(k_ref, 0)
+    k_total = total(k_ref, 0)
     copies[1].wait()
     split(v_ref, kv_ref, ROWS, 1)
     copies[2].wait()
     split(q_ref, q_mine_ref, 0, 2)
-    sums_ref[1:2, :] = total(q_ref, 0)
+    q_total = total(q_ref, 0)
+    sums_ref[0:1, :] = k_total
+    sums_ref[1:2, :] = q_total
+    theirs_ref[3 * ROWS :, 0:ROWS] = pieces(k_total, q_total)
+    theirs_ref[3 * ROWS :, ROWS:] = jnp.zeros((SPARE, half - ROWS), jnp.bfloat16)
     copies[3].wait()
     sums_ref[2:3, :] = total(c_ref, 0)
     copies[4].wait()
@@ -114,9 +132,11 @@
     sums_ref[4:5, :] = total(t_ref, ROWS)
 
 
-def mate_kernel(own_ref, mate_ref, out_ref):
+def mate_kernel(own_ref, got_ref, out_ref):
+    rows = got_ref[3 * ROWS : 3 * ROWS + SPARE, 0:ROWS].astype(jnp.float32)
     out_ref[...] = own_ref[...]
-    out_ref[5:7, :] = mate_ref[0:2, :]
+    out_ref[5:6, :] = joined(rows, 0)
+    out_ref[6:7, :] = joined(rows, 3)
 
 
 def table_kernel(own_ref, left_ref, right_ref, out_ref):
@@ -131,15 +151,7 @@
 def pieces_kernel(sums_ref, left_ref, right_ref):
     for chip, out_ref in ((-1, left_ref), (1, right_ref)):
         out_ref[...] = jnp.zeros(out_ref.shape, jnp.bfloat16)
-        rows = []
-        for line in KEY_LINES[chip]:
-            rest = sums_ref[line : line + 1, :]
-            for _ in range(3):
-                piece = rest.astype(jnp.bfloat16)
-                rows.append(piece.astype(jnp.float32))
-                rest = rest - rows[-1]
-        rows.append(jnp.zeros((SPARE - len(rows), ROWS), jnp.float32))
-        out_ref[:, 0:ROWS] = jnp.concatenate(rows, axis=0).astype(jnp.bfloat16)
+        out_ref[:, 0:ROWS] = pieces(*(sums_ref[line : line + 1, :] for line in KEY_LINES[chip]))
 
 
 def cross_kernel(item_ref, len_ref, here_ref, sums_ref, q_ref, k_ref, v_ref, qg_ref, kg_ref, out_ref):
@@ -209,10 +221,7 @@
                 own, mate = (sums_ref[line : line + 1, :] for line in KEY_LINES[chip])
             else:
                 spare = block[4 * ROWS : 4 * ROWS + SPARE, 0:ROWS].astype(jnp.float32)
-                own, mate = (
-                    spare[3 * i : 3 * i + 1] + spare[3 * i + 1 : 3 * i + 2] + spare[3 * i + 2 : 3 * i + 3]
-                    for i in range(2)
-                )
+                own, mate = joined(spare, 0), joined(spare, 3)
             total = jnp.where(core == parity, own, mate)
             turn(block, key_rows, by_rows(total), gains, cos_ref, sin_ref, start, keys_ref, goal)
 
@@ -356,7 +365,7 @@
         pack_kernel,
         (
             jax.ShapeDtypeStruct((2 * ROWS, half), bf16),
-            jax.ShapeDtypeStruct((3 * ROWS, half), bf16),
+            jax.ShapeDtypeStruct((3 * ROWS + SPARE, half), bf16),
             jax.ShapeDtypeStruct((ROWS, half), bf16),
             jax.ShapeDtypeStruct((8, ROWS), f32),
         ),
@@ -368,11 +377,10 @@
     got = swapped(theirs)
     peers = lax.axis_size("tile")
     low_pair, high_pair = (0, 1), (peers - 2, peers - 1)
-    table = jax.ShapeDtypeStruct((8, ROWS), f32)
-    sums = call(mate_kernel, table, [vmem] * 2)(sums, swapped(sums))
-    block = jnp.concatenate([kv, got[: 2 * ROWS], jnp.zeros((SPARE, half), bf16)], axis=0)
+    sums = call(mate_kernel, jax.ShapeDtypeStruct((8, ROWS), f32), [vmem] * 2)(sums, got)
     left_sums = shifted(sums, 2, high_pair)
     right_sums = shifted(sums, -2, low_pair)
+    block = jnp.concatenate([kv, got[: 2 * ROWS], jnp.zeros((SPARE, half), bf16)], axis=0)
     block, left_sums, right_sums = lax.optimization_barrier((block, left_sums, right_sums))
     left = shifted(block, 2, high_pair)
     right = shifted(block, -2, low_pair)

time: 111 us -> 109 us (0.982)
  starting transfers between devices: 42.3 us -> 40.3 us
    ppermute x3 -> x2, starting transfers between devices: 10.9 us -> 9.06 us  [swapped(): return lax.ppermute(value, 'tile', [(i, i ^ 1) for i in range(peers)])]
  transfers between devices with their start and end apart: 11 -> 10, of which waited for: 5 -> 5; matrix products, arithmetic and copies ran while one was open for 2% -> 2% of each run, Pallas kernels for 6% -> 6%
where the time goes in v8:
time: 109 us
  starting transfers between devices  40.3 us (37%)
  blocking collectives  27.3 us (25%)
  waiting for transfers between devices  23.1 us (21%)
  Pallas kernels  13.2 us (12%)
  local copies, waits for them, and re-layouts  3.08 us (3%)
  other arithmetic  1.19 us (1%)
    ppermute x8, starting transfers between devices, shifted(): lax.ppermute(value, 'tile', pairs + [(i, (i + by) % peers) for i in wrapp...  31.2 us
    psum x1, blocking collectives, per_device(): sums = lax.psum(sums, 'head')  27.3 us
    ppermute x8, waiting for transfers between devices, shifted(): lax.ppermute(value, 'tile', pairs + [(i, (i + by) % peers) for i in wrapp...  21.4 us
    ppermute x2, starting transfers between devices, swapped(): return lax.ppermute(value, 'tile', [(i, i ^ 1) for i in range(peers)])  9.06 us
    pallas_call x1, Pallas kernels, per_device(): call(functools.partial(near_kernel, near_chips), (jax.ShapeDtypeStruct((n...  2.99 us
    pallas_call x1, Pallas kernels, per_device(): call(functools.partial(far_kernel, near_chips, far_chips), (jax.ShapeDtyp...  2.77 us
    pallas_call x1, Pallas kernels, per_device(): call(pack_kernel, (jax.ShapeDtypeStruct((2 * ROWS, half), bf16), jax.Shap...  2.52 us
    pallas_call x1, Pallas kernels, per_device(): call(functools.partial(attend, False), jax.ShapeDtypeStruct((ROWS, half),...  2.47 us
  transfers between devices with their start and end apart: 10, of which 5 were waited for; matrix products, arithmetic and copies ran while one was open for 2% of the time, Pallas kernels for 6%

profile of v8, /device:TPU:33, one launch (start us, length us, event | category | flops | bytes accessed | tf_op | source)
XLA Modules:
  0.0 108.6 jit_solution(4511317312375114501)
XLA Ops:
  0.0 2.5 %shard_map.145 = (bf16[256,640]{1,0:T(8,128)(2,1)}, bf16[400,640]{1,0:T(8,128)(2,1)}, bf16[128,640]{1,0:T(8,128)(2,1)}, f32[8,128]{1,0:T(8,128)}) custom-call(s32[1]{0:T(128)} %bitcast.here_ref, bf16[128,1280]{1,0:T(8,128)(2,1)} %q_hbm.1, bf16[128,1280]{1,0:T(8,128)(2,1)} %k_hbm.1, bf16[128,1280]{1,0:T(8,128)(2,1)} %v_hbm.1, bf16[128,1280]{1,0:T(8,128)(2,1)} %q_ref.1, ...), custom_call_target="tpu_custom_call" | custom-call | flops 1000000 | bytes 4000000 | tf_op jit(solution)/shard_map/pallas_call | solution.py:364
  2.6 2.7 %collective-permute-start = (bf16[400,640]{1,0:T(8,128)(2,1)}, bf16[400,640]{1,0:T(8,128)(2,1)S(1)}, u32[]{:S(2)}, u32[]{:S(2)}) collective-permute-start(bf16[400,640]{1,0:T(8,128)(2,1)} %get-tuple-element.28), channel_id=1, source_target_pairs={{0,4},{4,0},{8,12},{12,8},{16,20},{20,16},{24,28},{28,24},{32,36},... | collective-permute-start | bytes 1536008 | tf_op jit(solution)/shard_map/ppermute | solution.py:58
  5.3 1.7 %collective-permute-done.got_ref.rest_6_ = bf16[400,640]{1,0:T(8,128)(2,1)S(1)} collective-permute-done((bf16[400,640]{1,0:T(8,128)(2,1)}, bf16[400,640]{1,0:T(8,128)(2,1)S(1)}, u32[]{:S(2)}, u32[]{:S(2)}) %collective-permute-start) | collective-permute-done | bytes 512032 | tf_op jit(solution)/shard_map/ppermute | solution.py:58
  7.7 6.4 %collective-permute-start.2 = (f32[8,128]{1,0:T(8,128)S(1)}, f32[8,128]{1,0:T(8,128)S(1)}, u32[]{:S(2)}, u32[]{:S(2)}) collective-permute-start(f32[8,128]{1,0:T(8,128)S(1)} %shard_map.146.own_ref), channel_id=1, source_target_pairs={{8,0},{12,4},{16,8},{20,12},{24,16},{28,20},{32,24},{36,28},{40,32... | collective-permute-start | bytes 12296 | tf_op jit(solution)/shard_map/ppermute | solution.py:53
  14.1 1.9 %collective-permute-start.1 = (f32[8,128]{1,0:T(8,128)S(1)}, f32[8,128]{1,0:T(8,128)S(1)}, u32[]{:S(2)}, u32[]{:S(2)}) collective-permute-start(f32[8,128]{1,0:T(8,128)S(1)} %shard_map.146.own_ref), channel_id=1, source_target_pairs={{0,8},{4,12},{8,16},{12,20},{16,24},{20,28},{24,32},{28,36},{32,40... | collective-permute-start | bytes 12296 | tf_op jit(solution)/shard_map/ppermute | solution.py:53
  16.1 1.2 %maximum_maximum_fusion.rest_8_ = bf16[528,640]{1,0:T(8,128)(2,1)S(1)} fusion(bf16[256,640]{1,0:T(8,128)(2,1)S(1)} %slice.4, bf16[256,640]{1,0:T(8,128)(2,1)} %get-tuple-element.27, bf16[528]{0:T(1024)(128)(2,1)S(1)} %pad.2.clone), kind=kLoop, calls=%fused_computation | loop fusion | flops 2027520 | bytes 1332256 | tf_op jit(solution)/shard_map/concatenate | solution.py:383
  17.3 5.4 %collective-permute-done.1.left_ref = f32[8,128]{1,0:T(8,128)S(1)} collective-permute-done((f32[8,128]{1,0:T(8,128)S(1)}, f32[8,128]{1,0:T(8,128)S(1)}, u32[]{:S(2)}, u32[]{:S(2)}) %collective-permute-start.1) | collective-permute-done | bytes 4128 | tf_op jit(solution)/shard_map/ppermute | solution.py:53
  22.7 2.4 %collective-permute-start.4 = (bf16[528,640]{1,0:T(8,128)(2,1)S(1)}, bf16[528,640]{1,0:T(8,128)(2,1)}, u32[]{:S(2)}, u32[]{:S(2)}) collective-permute-start(bf16[528,640]{1,0:T(8,128)(2,1)S(1)} %maximum_maximum_fusion.rest_8_), channel_id=1, source_target_pairs={{8,0},{12,4},{16,8},{20,12},{24,16},{28,20},{32,24},{36,28},{40,32... | collective-permute-start | bytes 2027528 | tf_op jit(solution)/shard_map/ppermute | solution.py:53
  25.0 2.9 %collective-permute-start.3 = (bf16[528,640]{1,0:T(8,128)(2,1)S(1)}, bf16[528,640]{1,0:T(8,128)(2,1)}, u32[]{:S(2)}, u32[]{:S(2)}) collective-permute-start(bf16[528,640]{1,0:T(8,128)(2,1)S(1)} %maximum_maximum_fusion.rest_8_), channel_id=1, source_target_pairs={{0,8},{4,12},{8,16},{12,20},{16,24},{20,28},{24,32},{28,36},{32,40... | collective-permute-start | bytes 2027528 | tf_op jit(solution)/shard_map/ppermute | solution.py:53
  28.0 27.3 %psum.7.sums_ref.rest_0_ = f32[16,128]{1,0:T(8,128)S(1)} all-reduce(f32[16,128]{1,0:T(8,128)S(1)} %shard_map.147), channel_id=1, replica_groups=mesh['tile'=128,'head'=4] {'head'}, use_global_device_ids=true, to_apply=%region_0.0 | all-reduce | flops 2048 | bytes 16384 | tf_op jit(solution)/shard_map/psum | solution.py:389
  55.9 8.4 %collective-permute-start.7 = (bf16[528,640]{1,0:T(8,128)(2,1)}, bf16[528,640]{1,0:T(8,128)(2,1)S(1)}, u32[]{:S(2)}, u32[]{:S(2)}) collective-permute-start(bf16[528,640]{1,0:T(8,128)(2,1)} %constant_dynamic-update-slice_fusion.rest_9_), channel_id=1, source_target_pairs={{8,0},{12,4},{16,8},{20,12},{24,16},{28,20},{32,24},{36,28},{40,32... | collective-permute-start | bytes 2027528 | tf_op jit(solution)/shard_map/ppermute | solution.py:53
  64.3 1.9 %collective-permute-start.5 = (bf16[528,640]{1,0:T(8,128)(2,1)}, bf16[528,640]{1,0:T(8,128)(2,1)S(1)}, u32[]{:S(2)}, u32[]{:S(2)}) collective-permute-start(bf16[528,640]{1,0:T(8,128)(2,1)} %constant_dynamic-update-slice_fusion.rest_9_), channel_id=1, source_target_pairs={{0,32},{4,36},{8,40},{12,44},{16,48},{20,52},{24,56},{28,60},{32,6... | collective-permute-start | bytes 2027528 | tf_op jit(solution)/shard_map/ppermute | solution.py:53
  66.8 5.5 %collective-permute-start.8 = (bf16[528,640]{1,0:T(8,128)(2,1)}, bf16[528,640]{1,0:T(8,128)(2,1)S(1)}, u32[]{:S(2)}, u32[]{:S(2)}) collective-permute-start(bf16[528,640]{1,0:T(8,128)(2,1)} %constant_dynamic-update-slice_fusion.1.rest_7_), channel_id=1, source_target_pairs={{32,0},{36,4},{40,8},{44,12},{48,16},{52,20},{56,24},{60,28},{64,3... | collective-permute-start | bytes 2027528 | tf_op jit(solution)/shard_map/ppermute | solution.py:53
  72.3 1.9 %collective-permute-start.6 = (bf16[528,640]{1,0:T(8,128)(2,1)}, bf16[528,640]{1,0:T(8,128)(2,1)S(1)}, u32[]{:S(2)}, u32[]{:S(2)}) collective-permute-start(bf16[528,640]{1,0:T(8,128)(2,1)} %constant_dynamic-update-slice_fusion.1.rest_7_), channel_id=1, source_target_pairs={{0,8},{4,12},{8,16},{12,20},{16,24},{20,28},{24,32},{28,36},{32,40... | collective-permute-start | bytes 2027528 | tf_op jit(solution)/shard_map/ppermute | solution.py:53
  74.4 1.1 copy-done.4
  75.5 1.6 %shard_map.148.text_ref = f32[128,1280]{1,0:T(8,128)S(1)} custom-call(s32[128]{0:T(128)S(1)} %copy-done.6, s32[128]{0:T(128)S(1)} %copy-done.9, s32[1]{0:T(128)} %bitcast.here_ref, f32[16,128]{1,0:T(8,128)S(1)} %psum.7.sums_ref.rest_0_, bf16[128,1280]{1,0:T(8,128)(2,1)S(1)} %copy-done.3, bf16[256,1280]{1,0:T(8,128)(2,1)S(1)} %copy-done, ...), custom_call_target="tpu_custom_call" | custom-call | flops 400000000 | bytes 4000000 | tf_op jit(solution)/shard_map/pallas_call | solution.py:400
  77.1 3.0 %shard_map.150 = (bf16[768,640]{1,0:T(8,128)(2,1)S(1)}, bf16[768,640]{1,0:T(8,128)(2,1)S(1)}, bf16[128,640]{1,0:T(8,128)(2,1)S(1)}, bf16[128,640]{1,0:T(8,128)(2,1)S(1)}) custom-call(s32[128]{0:T(128)S(1)} %copy-done.6, s32[1]{0:T(128)} %bitcast.here_ref, f32[16,128]{1,0:T(8,128)S(1)} %psum.7.sums_ref.rest_0_, f32[1,1280]{1,0:T(1,128)S(1)} %broadcast_in_dim.19.rest_1_, ...), custom_call_target="tpu_custom_call" | custom-call | flops 200000000 | bytes 4000000 | tf_op jit(solution)/shard_map/pallas_call | solution.py:420
  80.1 11.5 %collective-permute-done.5.rest_7_ = bf16[528,640]{1,0:T(8,128)(2,1)S(1)} collective-permute-done((bf16[528,640]{1,0:T(8,128)(2,1)}, bf16[528,640]{1,0:T(8,128)(2,1)S(1)}, u32[]{:S(2)}, u32[]{:S(2)}) %collective-permute-start.5) | collective-permute-done | bytes 675872 | tf_op jit(solution)/shard_map/ppermute | solution.py:53
  91.6 1.1 collective-permute-done.8.rest_10_
  92.7 3.5 %collective-permute-done.6.rest_8_ = bf16[528,640]{1,0:T(8,128)(2,1)S(1)} collective-permute-done((bf16[528,640]{1,0:T(8,128)(2,1)}, bf16[528,640]{1,0:T(8,128)(2,1)S(1)}, u32[]{:S(2)}, u32[]{:S(2)}) %collective-permute-start.6) | collective-permute-done | bytes 675872 | tf_op jit(solution)/shard_map/ppermute | solution.py:53
  96.2 2.8 %shard_map.151 = (f32[128,640]{1,0:T(8,128)S(1)}, bf16[1792,640]{1,0:T(8,128)(2,1)S(1)}, bf16[1792,640]{1,0:T(8,128)(2,1)S(1)}) custom-call(s32[128]{0:T(128)S(1)} %copy-done.6, s32[128]{0:T(128)S(1)} %copy-done.8, s32[1]{0:T(128)} %bitcast.here_ref, f32[16,128]{1,0:T(8,128)S(1)} %psum.7.sums_ref.rest_0_, f32[1,1280]{1,0:T(1,128)S(1)} %broadcast_in_dim.19.rest_1_, ...), custom_call_target="tpu_custom_call" | custom-call | flops 300000000 | bytes 4000000 | tf_op jit(solution)/shard_map/pallas_call | solution.py:439
  98.9 6.3 %collective-permute-start.9 = (f32[128,640]{1,0:T(8,128)S(1)}, f32[128,640]{1,0:T(8,128)S(1)}, u32[]{:S(2)}, u32[]{:S(2)}) collective-permute-start(f32[128,640]{1,0:T(8,128)S(1)} %get-tuple-element.47), channel_id=1, source_target_pairs={{0,4},{4,0},{8,12},{12,8},{16,20},{20,16},{24,28},{28,24},{32,36},... | collective-permute-start | bytes 983048 | tf_op jit(solution)/shard_map/ppermute | solution.py:58
  105.3 2.5 %shard_map.152.own_ref = f32[128,640]{1,0:T(8,128)S(1)} custom-call(s32[128]{0:T(128)S(1)} %copy-done.6, s32[128]{0:T(128)S(1)} %copy-done.8, s32[1]{0:T(128)} %bitcast.here_ref, bf16[128,640]{1,0:T(8,128)(2,1)S(1)} %get-tuple-element.41.q_ref, bf16[1792,640]{1,0:T(8,128)(2,1)S(1)} %get-tuple-element.45.keys_ref, ...), custom_call_target="tpu_custom_call" | custom-call | flops 300000000 | bytes 4000000 | tf_op jit(solution)/shard_map/pallas_call | solution.py:458
  107.8 0.8 shard_map.153
  (44 shorter events, 2.0 us)
Async XLA Ops:
  0.0 74.2 %copy-start.10 = (f32[1280]{0:T(1024)S(1)}, f32[1280]{0:T(1024)}, u32[]{:S(2)}) copy-start(f32[1280]{0:T(1024)} %param.21) | copy-start | bytes 15364
  0.0 74.3 %copy-start.11 = (f32[1280]{0:T(1024)S(1)}, f32[1280]{0:T(1024)}, u32[]{:S(2)}) copy-start(f32[1280]{0:T(1024)} %param.22) | copy-start | bytes 15364
  0.0 74.3 %copy-start.12 = (f32[1280]{0:T(1024)S(1)}, f32[1280]{0:T(1024)}, u32[]{:S(2)}) copy-start(f32[1280]{0:T(1024)} %param.23) | copy-start | bytes 15364
  0.0 74.3 %copy-start.13 = (f32[1280]{0:T(1024)S(1)}, f32[1280]{0:T(1024)}, u32[]{:S(2)}) copy-start(f32[1280]{0:T(1024)} %param.24) | copy-start | bytes 15364
  0.0 74.3 %copy-start.9 = (s32[128]{0:T(128)S(1)}, s32[128]{0:T(128)}, u32[]{:S(2)}) copy-start(s32[128]{0:T(128)} %len_ref.1) | copy-start | bytes 1540
  2.6 71.8 %copy-start = (bf16[256,1280]{1,0:T(8,128)(2,1)S(1)}, bf16[256,1280]{1,0:T(8,128)(2,1)}, u32[]{:S(2)}) copy-start(bf16[256,1280]{1,0:T(8,128)(2,1)} %k_ref.1) | copy-start | bytes 1966084
  2.6 71.8 %copy-start.3 = (bf16[128,1280]{1,0:T(8,128)(2,1)S(1)}, bf16[128,1280]{1,0:T(8,128)(2,1)}, u32[]{:S(2)}) copy-start(bf16[128,1280]{1,0:T(8,128)(2,1)} %q_ref.1) | copy-start | bytes 983044
  2.6 71.8 %copy-start.6 = (s32[128]{0:T(128)S(1)}, s32[128]{0:T(128)}, u32[]{:S(2)}) copy-start(s32[128]{0:T(128)} %item_ref.7) | copy-start | bytes 1540
  2.6 4.4 %collective-permute-start = (bf16[400,640]{1,0:T(8,128)(2,1)}, bf16[400,640]{1,0:T(8,128)(2,1)S(1)}, u32[]{:S(2)}, u32[]{:S(2)}) collective-permute-start(bf16[400,640]{1,0:T(8,128)(2,1)} %get-tuple-element.28), channel_id=1, source_target_pairs={{0,4},{4,0},{8,12},{12,8},{16,20},{20,16},{24,28},{28,24},{32,36},... | collective-permute-start | bytes 1536008 | tf_op jit(solution)/shard_map/ppermute | solution.py:58
  7.0 0.7 copy-start.7
  7.7 9.6 %collective-permute-start.2 = (f32[8,128]{1,0:T(8,128)S(1)}, f32[8,128]{1,0:T(8,128)S(1)}, u32[]{:S(2)}, u32[]{:S(2)}) collective-permute-start(f32[8,128]{1,0:T(8,128)S(1)} %shard_map.146.own_ref), channel_id=1, source_target_pairs={{8,0},{12,4},{16,8},{20,12},{24,16},{28,20},{32,24},{36,28},{40,32... | collective-permute-start | bytes 12296 | tf_op jit(solution)/shard_map/ppermute | solution.py:53
  14.1 8.6 %collective-permute-start.1 = (f32[8,128]{1,0:T(8,128)S(1)}, f32[8,128]{1,0:T(8,128)S(1)}, u32[]{:S(2)}, u32[]{:S(2)}) collective-permute-start(f32[8,128]{1,0:T(8,128)S(1)} %shard_map.146.own_ref), channel_id=1, source_target_pairs={{0,8},{4,12},{8,16},{12,20},{16,24},{20,28},{24,32},{28,36},{32,40... | collective-permute-start | bytes 12296 | tf_op jit(solution)/shard_map/ppermute | solution.py:53
  16.0 61.0 %copy-start.5 = (bf16[128,640]{1,0:T(8,128)(2,1)S(1)}, bf16[128,640]{1,0:T(8,128)(2,1)}, u32[]{:S(2)}) copy-start(bf16[128,640]{1,0:T(8,128)(2,1)} %get-tuple-element.36.rest_5_) | copy-start | bytes 491524
  17.3 59.8 %copy-start.1 = (f32[896,128]{1,0:T(8,128)S(1)}, f32[896,128]{1,0:T(8,128)}, u32[]{:S(2)}) copy-start(f32[896,128]{1,0:T(8,128)} %constant.17.clone.rest_4_.rest_3_) | copy-start | bytes 1376260
  17.3 59.8 %copy-start.2 = (f32[896,128]{1,0:T(8,128)S(1)}, f32[896,128]{1,0:T(8,128)}, u32[]{:S(2)}) copy-start(f32[896,128]{1,0:T(8,128)} %constant.16.clone.rest_3_.rest_2_) | copy-start | bytes 1376260
  22.7 32.6 %collective-permute-start.4 = (bf16[528,640]{1,0:T(8,128)(2,1)S(1)}, bf16[528,640]{1,0:T(8,128)(2,1)}, u32[]{:S(2)}, u32[]{:S(2)}) collective-permute-start(bf16[528,640]{1,0:T(8,128)(2,1)S(1)} %maximum_maximum_fusion.rest_8_), channel_id=1, source_target_pairs={{8,0},{12,4},{16,8},{20,12},{24,16},{28,20},{32,24},{36,28},{40,32... | collective-permute-start | bytes 2027528 | tf_op jit(solution)/shard_map/ppermute | solution.py:53
  25.0 30.3 %collective-permute-start.3 = (bf16[528,640]{1,0:T(8,128)(2,1)S(1)}, bf16[528,640]{1,0:T(8,128)(2,1)}, u32[]{:S(2)}, u32[]{:S(2)}) collective-permute-start(bf16[528,640]{1,0:T(8,128)(2,1)S(1)} %maximum_maximum_fusion.rest_8_), channel_id=1, source_target_pairs={{0,8},{4,12},{8,16},{12,20},{16,24},{20,28},{24,32},{28,36},{32,40... | collective-permute-start | bytes 2027528 | tf_op jit(solution)/shard_map/ppermute | solution.py:53
  55.9 24.2 %collective-permute-start.7 = (bf16[528,640]{1,0:T(8,128)(2,1)}, bf16[528,640]{1,0:T(8,128)(2,1)S(1)}, u32[]{:S(2)}, u32[]{:S(2)}) collective-permute-start(bf16[528,640]{1,0:T(8,128)(2,1)} %constant_dynamic-update-slice_fusion.rest_9_), channel_id=1, source_target_pairs={{8,0},{12,4},{16,8},{20,12},{24,16},{28,20},{32,24},{36,28},{40,32... | collective-permute-start | bytes 2027528 | tf_op jit(solution)/shard_map/ppermute | solution.py:53
  64.3 27.3 %collective-permute-start.5 = (bf16[528,640]{1,0:T(8,128)(2,1)}, bf16[528,640]{1,0:T(8,128)(2,1)S(1)}, u32[]{:S(2)}, u32[]{:S(2)}) collective-permute-start(bf16[528,640]{1,0:T(8,128)(2,1)} %constant_dynamic-update-slice_fusion.rest_9_), channel_id=1, source_target_pairs={{0,32},{4,36},{8,40},{12,44},{16,48},{20,52},{24,56},{28,60},{32,6... | collective-permute-start | bytes 2027528 | tf_op jit(solution)/shard_map/ppermute | solution.py:53
  66.8 25.8 %collective-permute-start.8 = (bf16[528,640]{1,0:T(8,128)(2,1)}, bf16[528,640]{1,0:T(8,128)(2,1)S(1)}, u32[]{:S(2)}, u32[]{:S(2)}) collective-permute-start(bf16[528,640]{1,0:T(8,128)(2,1)} %constant_dynamic-update-slice_fusion.1.rest_7_), channel_id=1, source_target_pairs={{32,0},{36,4},{40,8},{44,12},{48,16},{52,20},{56,24},{60,28},{64,3... | collective-permute-start | bytes 2027528 | tf_op jit(solution)/shard_map/ppermute | solution.py:53
  72.3 23.8 %collective-permute-start.6 = (bf16[528,640]{1,0:T(8,128)(2,1)}, bf16[528,640]{1,0:T(8,128)(2,1)S(1)}, u32[]{:S(2)}, u32[]{:S(2)}) collective-permute-start(bf16[528,640]{1,0:T(8,128)(2,1)} %constant_dynamic-update-slice_fusion.1.rest_7_), channel_id=1, source_target_pairs={{0,8},{4,12},{8,16},{12,20},{16,24},{20,28},{24,32},{28,36},{32,40... | collective-permute-start | bytes 2027528 | tf_op jit(solution)/shard_map/ppermute | solution.py:53
  74.4 1.1 %copy-start.4 = (bf16[256,1280]{1,0:T(8,128)(2,1)S(1)}, bf16[256,1280]{1,0:T(8,128)(2,1)}, u32[]{:S(2)}) copy-start(bf16[256,1280]{1,0:T(8,128)(2,1)} %v_ref.1) | copy-start | bytes 1966084
  77.1 19.1 %copy-start.8 = (s32[128]{0:T(128)S(1)}, s32[128]{0:T(128)}, u32[]{:S(2)}) copy-start(s32[128]{0:T(128)} %count_ref.3) | copy-start | bytes 1540
  98.9 8.8 %collective-permute-start.9 = (f32[128,640]{1,0:T(8,128)S(1)}, f32[128,640]{1,0:T(8,128)S(1)}, u32[]{:S(2)}, u32[]{:S(2)}) collective-permute-start(f32[128,640]{1,0:T(8,128)S(1)} %get-tuple-element.47), channel_id=1, source_target_pairs={{0,4},{4,0},{8,12},{12,8},{16,20},{20,16},{24,28},{28,24},{32,36},... | collective-permute-start | bytes 983048 | tf_op jit(solution)/shard_map/ppermute | solution.py:58

commit v9 on v8

--- a/solution.py
+++ b/solution.py
@@ -18,8 +18,10 @@
 EPSILON = 1e-06
 SCALE = 1.0 / math.sqrt(HD)
 NEG = -1e30
-KEY_LINES = {-1: (7, 8), 0: (0, 5), 1: (9, 10)}
+OWN_LINES, SIDE_LINES, QUERY_LINES = (0, 5), (7, 8), (1, 6)
 SPARE = 16
+HALF_ROWS = 2 * ROWS + SPARE
+PART_ROWS = 4 * ROWS + SPARE
 
 
 def rope_tables():
@@ -49,8 +51,12 @@
 
 def shifted(value, by, wrapped=()):
     peers = lax.axis_size("tile")
-    pairs = [(i, i + by) for i in range(peers) if 0 <= i + by < peers]
-    return lax.ppermute(value, "tile", pairs + [(i, (i + by) % peers) for i in wrapped])
+    pairs = []
+    for i in range(peers):
+        goal = i - by if i % 2 else i + by
+        if 0 <= goal < peers or i in wrapped:
+            pairs.append((i, goal % peers))
+    return lax.ppermute(value, "tile", pairs)
 
 
 def swapped(value):
@@ -87,7 +93,7 @@
 
 
 def pack_kernel(
-    here_ref, q_hbm, k_hbm, v_hbm, c_hbm, t_hbm, kv_ref, theirs_ref, q_mine_ref, sums_ref,
+    here_ref, q_hbm, k_hbm, v_hbm, c_hbm, t_hbm, theirs_ref, q_mine_ref, sums_ref,
     q_ref, k_ref, v_ref, c_ref, t_ref, arrived
 ):
     pairs = ((k_hbm, k_ref), (v_hbm, v_ref), (q_hbm, q_ref), (c_hbm, c_ref), (t_hbm, t_ref))
@@ -107,24 +113,28 @@
             rows = x * x if rows is None else rows + x * x
         return jnp.sum(jnp.transpose(rows), axis=0, keepdims=True)
 
-    def split(ref, mine_ref, first, index):
-        low, high = ref[:, :half], ref[:, half:]
-        mine_ref[first : first + ROWS, :] = jnp.where(core == 0, low, high)
-        theirs_ref[index * ROWS : (index + 1) * ROWS, :] = jnp.where(core == 0, high, low)
+    def split(ref, first):
+        for side in range(2):
+            row = side * HALF_ROWS + first
+            theirs_ref[row : row + ROWS, :] = ref[:, side * half : (side + 1) * half]
 
     sums_ref[...] = jnp.zeros((8, ROWS), jnp.float32)
     copies[0].wait()
-    split(k_ref, kv_ref, 0, 0)
+    split(k_ref, 0)
     k_total = total(k_ref, 0)
     copies[1].wait()
-    split(v_ref, kv_ref, ROWS, 1)
+    split(v_ref, ROWS)
     copies[2].wait()
-    split(q_ref, q_mine_ref, 0, 2)
+    low, high = q_ref[:, :half], q_ref[:, half:]
+    q_mine_ref[...] = jnp.where(core == 0, low, high)
+    theirs_ref[2 * HALF_ROWS :, :] = jnp.where(core == 0, high, low)
     q_total = total(q_ref, 0)
     sums_ref[0:1, :] = k_total
     sums_ref[1:2, :] = q_total
-    theirs_ref[3 * ROWS :, 0:ROWS] = pieces(k_total, q_total)
-    theirs_ref[3 * ROWS :, ROWS:] = jnp.zeros((SPARE, half - ROWS), jnp.bfloat16)
+    for side in range(2):
+        rows = slice(side * HALF_ROWS + 2 * ROWS, (side + 1) * HALF_ROWS)
+        theirs_ref[rows, 0:ROWS] = pieces(k_total, q_total)
+        theirs_ref[rows, ROWS:] = jnp.zeros((SPARE, half - ROWS), jnp.bfloat16)
     copies[3].wait()
     sums_ref[2:3, :] = total(c_ref, 0)
     copies[4].wait()
@@ -133,25 +143,41 @@
 
 
 def mate_kernel(own_ref, got_ref, out_ref):
-    rows = got_ref[3 * ROWS : 3 * ROWS + SPARE, 0:ROWS].astype(jnp.float32)
+    rows = got_ref[2 * ROWS : HALF_ROWS, 0:ROWS].astype(jnp.float32)
     out_ref[...] = own_ref[...]
     out_ref[5:6, :] = joined(rows, 0)
     out_ref[6:7, :] = joined(rows, 3)
 
 
-def table_kernel(own_ref, left_ref, right_ref, out_ref):
+def table_kernel(own_ref, side_ref, out_ref):
     out_ref[0:8, :] = own_ref[...]
     out_ref[8:16, :] = jnp.zeros((8, ROWS), jnp.float32)
-    out_ref[7:8, :] = left_ref[0:1, :]
-    out_ref[8:9, :] = left_ref[5:6, :]
-    out_ref[9:10, :] = right_ref[0:1, :]
-    out_ref[10:11, :] = right_ref[5:6, :]
-
-
-def pieces_kernel(sums_ref, left_ref, right_ref):
-    for chip, out_ref in ((-1, left_ref), (1, right_ref)):
-        out_ref[...] = jnp.zeros(out_ref.shape, jnp.bfloat16)
-        out_ref[:, 0:ROWS] = pieces(*(sums_ref[line : line + 1, :] for line in KEY_LINES[chip]))
+    out_ref[7:8, :] = side_ref[0:1, :]
+    out_ref[8:9, :] = side_ref[5:6, :]
+
+
+def pieces_kernel(sums_ref, out_ref):
+    out_ref[...] = jnp.zeros(out_ref.shape, jnp.bfloat16)
+    out_ref[:, 0:ROWS] = pieces(*(sums_ref[line : line + 1, :] for line in SIDE_LINES))
+
+
+def part_kernel(here_ref, *rest):
+    blocks, out_ref, arrived = rest[:-2], rest[-2], rest[-1]
+    side = 1 - lax.rem(here_ref[0], 2)
+    copies = []
+    for index, block in enumerate(blocks):
+        first = index * PART_ROWS
+        for slot in range(2):
+            row = pl.multiple_of((2 * slot + side) * HALF_ROWS, SPARE)
+            goal = first + slot * 2 * ROWS
+            copies.append((block.at[pl.ds(row, 2 * ROWS)], out_ref.at[goal : goal + 2 * ROWS]))
+        goal = first + 4 * ROWS
+        copies.append((block.at[2 * ROWS : HALF_ROWS], out_ref.at[goal : goal + SPARE]))
+    copies = [pltpu.make_async_copy(*pair, arrived.at[i]) for i, pair in enumerate(copies)]
+    for copy in copies:
+        copy.start()
+    for copy in copies:
+        copy.wait()
 
 
 def cross_kernel(item_ref, len_ref, here_ref, sums_ref, q_ref, k_ref, v_ref, qg_ref, kg_ref, out_ref):
@@ -202,44 +228,68 @@
         dest_ref[goal, cols] = rotated(x, cosine, sine, even).astype(jnp.bfloat16)
 
 
-def gather_block(chip, block, core, left, bounds, sums_ref, gains, tables, keys_ref, values_ref, place):
+def gather(chip, rows_of, totals, block, core, left, bounds, gains, tables, keys_ref, values_ref, first_chip):
     first_a, last_a, first_b, last_b = bounds
-    cos_ref, sin_ref = tables
     for parity in range(2):
         tile = left + 2 * chip + parity
-        slot = jnp.where(core == parity, 0, 1)
-        key_rows = pl.ds(pl.multiple_of(slot * 2 * ROWS, 2 * ROWS), ROWS)
-        value_rows = pl.ds(pl.multiple_of(slot * 2 * ROWS + ROWS, ROWS), ROWS)
-        goal = slice((place + parity) * ROWS, (place + parity + 1) * ROWS)
+        slot, row = rows_of(parity)
+        key_rows = pl.ds(pl.multiple_of(row, SPARE), ROWS)
+        value_rows = pl.ds(pl.multiple_of(row + ROWS, SPARE), ROWS)
+        goal = pl.ds(pl.multiple_of((2 * (chip - first_chip) + parity) * ROWS, ROWS), ROWS)
         values_ref[goal, :] = block[value_rows, :]
 
         @pl.when(jnp.logical_and(tile >= first_a, tile <= last_b))
-        def _(parity=parity, tile=tile, key_rows=key_rows, goal=goal):
+        def _(tile=tile, slot=slot, key_rows=key_rows, goal=goal):
             first = jnp.where(tile <= last_a, first_a, first_b)
             start = pl.multiple_of((tile - first) * ROWS, ROWS)
-            if chip in KEY_LINES:
-                own, mate = (sums_ref[line : line + 1, :] for line in KEY_LINES[chip])
-            else:
-                spare = block[4 * ROWS : 4 * ROWS + SPARE, 0:ROWS].astype(jnp.float32)
-                own, mate = joined(spare, 0), joined(spare, 3)
-            total = jnp.where(core == parity, own, mate)
-            turn(block, key_rows, by_rows(total), gains, cos_ref, sin_ref, start, keys_ref, goal)
-
-
-def near_kernel(chips, item_ref, here_ref, *rest):
-    sums_ref, k_gain_ref, q_gain_ref, cos_ref, sin_ref, q_own_ref, q_mate_ref = rest[:7]
-    blocks = rest[7 : 7 + len(chips)]
-    keys_ref, values_ref, own_turned_ref, mate_turned_ref = rest[7 + len(chips) :]
+            total = jnp.where(slot == 0, *totals())
+            turn(block, key_rows, by_rows(total), gains, *tables, start, keys_ref, goal)
+
+
+def kept_rows(core):
+    def rows_of(parity):
+        slot = jnp.where(core == parity, 0, 1)
+        return slot, (2 * slot + core) * HALF_ROWS
+
+    return rows_of
+
+
+def part_rows(core, index):
+    def rows_of(parity):
+        slot = jnp.where(core == parity, 1, 0)
+        return slot, index * PART_ROWS + slot * 2 * ROWS
+
+    return rows_of
+
+
+def lines(ref, pair):
+    return lambda: tuple(ref[line : line + 1, :] for line in pair)
+
+
+def spares(ref, first):
+    def totals():
+        rows = ref[first : first + SPARE, 0:ROWS].astype(jnp.float32)
+        return joined(rows, 0), joined(rows, 3)
+
+    return totals
+
+
+def near_kernel(
+    item_ref, here_ref, sums_ref, mate_sums_ref, k_gain_ref, q_gain_ref, cos_ref, sin_ref, q_own_ref, got_ref,
+    block_ref, kept_ref, part_ref, keys_ref, values_ref, own_turned_ref, mate_turned_ref
+):
     core = lax.rem(here_ref[0], 2)
     left = here_ref[0] - core
+    sign = 2 * core - 1
     half = keys_ref.shape[1]
     bounds = (*extent(item_ref, left), *extent(item_ref, left + 1))
-    part = pl.ds(pl.multiple_of(core * half, HD), half)
-    k_gains, q_gains = k_gain_ref.at[:, part], q_gain_ref.at[:, part]
+    columns = pl.ds(pl.multiple_of(core * half, HD), half)
+    k_gains, q_gains = k_gain_ref.at[:, columns], q_gain_ref.at[:, columns]
+    tables = (cos_ref, sin_ref)
     for which, (source, rows, line, goal) in enumerate(
         (
-            (q_own_ref, slice(0, ROWS), 1, own_turned_ref),
-            (q_mate_ref, slice(2 * ROWS, 3 * ROWS), 6, mate_turned_ref),
+            (q_own_ref, slice(0, ROWS), QUERY_LINES[0], own_turned_ref),
+            (got_ref, slice(2 * HALF_ROWS, 2 * HALF_ROWS + ROWS), QUERY_LINES[1], mate_turned_ref),
         )
     ):
         is_a = core == which
@@ -247,12 +297,13 @@
         tile = jnp.where(is_a, left, left + 1)
         start = pl.multiple_of((tile - first) * ROWS, ROWS)
         factor = by_rows(sums_ref[line : line + 1, :])
-        turn(source, rows, factor, q_gains, cos_ref, sin_ref, start, goal, slice(None))
-    for index, (chip, block) in enumerate(zip(chips, blocks)):
-        gather_block(
-            chip, block, core, left, bounds, sums_ref, k_gains, (cos_ref, sin_ref),
-            keys_ref, values_ref, 2 * index,
-        )
+        turn(source, rows, factor, q_gains, *tables, start, goal, slice(None))
+    for chip, rows_of, totals, block in (
+        (0, kept_rows(core), lines(sums_ref, OWN_LINES), block_ref),
+        (sign, kept_rows(core), lines(sums_ref, SIDE_LINES), kept_ref),
+        (-sign, part_rows(core, 0), lines(mate_sums_ref, SIDE_LINES), part_ref),
+    ):
+        gather(chip, rows_of, totals, block, core, left, bounds, k_gains, tables, keys_ref, values_ref, -1)
 
 
 def attend(mate, item_ref, count_ref, here_ref, q_ref, keys_ref, values_ref, out_ref):
@@ -288,24 +339,27 @@
         out_ref[:, cols] = mixed / total
 
 
-def far_kernel(near_chips, far_chips, item_ref, count_ref, here_ref, *rest):
-    sums_ref, k_gain_ref, cos_ref, sin_ref, q_ref, near_keys_ref, near_values_ref = rest[:7]
-    blocks = rest[7 : 7 + len(far_chips)]
-    out_ref, keys_ref, values_ref = rest[7 + len(far_chips) :]
+def far_kernel(
+    item_ref, count_ref, here_ref, k_gain_ref, cos_ref, sin_ref, q_ref, near_keys_ref, near_values_ref,
+    second_ref, third_ref, part_ref, out_ref, keys_ref, values_ref
+):
     core = lax.rem(here_ref[0], 2)
     left = here_ref[0] - core
+    sign = 2 * core - 1
     half = keys_ref.shape[1]
     bounds = (*extent(item_ref, left), *extent(item_ref, left + 1))
     k_gains = k_gain_ref.at[:, pl.ds(pl.multiple_of(core * half, HD), half)]
-    for index, chip in enumerate(near_chips):
-        source = slice(2 * index * ROWS, 2 * (index + 1) * ROWS)
-        goal = slice(2 * (chip + 3) * ROWS, 2 * (chip + 4) * ROWS)
-        keys_ref[goal, :] = near_keys_ref[source, :]
-        values_ref[goal, :] = near_values_ref[source, :]
-    for chip, block in zip(far_chips, blocks):
-        gather_block(
-            chip, block, core, left, bounds, sums_ref, k_gains, (cos_ref, sin_ref),
-            keys_ref, values_ref, 2 * (chip + 3),
+    near = slice(4 * ROWS, 10 * ROWS)
+    keys_ref[near, :] = near_keys_ref[...]
+    values_ref[near, :] = near_values_ref[...]
+    for chip, rows_of, totals, block in (
+        (2 * sign, kept_rows(core), spares(second_ref, 2 * ROWS), second_ref),
+        (-3 * sign, kept_rows(core), spares(third_ref, 2 * ROWS), third_ref),
+        (-2 * sign, part_rows(core, 0), spares(part_ref, 4 * ROWS), part_ref),
+        (3 * sign, part_rows(core, 1), spares(part_ref, PART_ROWS + 4 * ROWS), part_ref),
+    ):
+        gather(
+            chip, rows_of, totals, block, core, left, bounds, k_gains, (cos_ref, sin_ref), keys_ref, values_ref, -3
         )
     attend(True, item_ref, count_ref, here_ref, q_ref, keys_ref, values_ref, out_ref)
 
@@ -361,11 +415,10 @@
 
     bf16 = jnp.bfloat16
     hbm = pl.BlockSpec(memory_space=pltpu.HBM)
-    kv, theirs, q_mine, sums = call(
+    theirs, q_mine, sums = call(
         pack_kernel,
         (
-            jax.ShapeDtypeStruct((2 * ROWS, half), bf16),
-            jax.ShapeDtypeStruct((3 * ROWS + SPARE, half), bf16),
+            jax.ShapeDtypeStruct((2 * HALF_ROWS + ROWS, half), bf16),
             jax.ShapeDtypeStruct((ROWS, half), bf16),
             jax.ShapeDtypeStruct((8, ROWS), f32),
         ),
@@ -376,26 +429,32 @@
     )(where, self_query, self_key, self_value, cross_query, text_key)
     got = swapped(theirs)
     peers = lax.axis_size("tile")
-    low_pair, high_pair = (0, 1), (peers - 2, peers - 1)
+    ends = (peers - 2, 1)
     sums = call(mate_kernel, jax.ShapeDtypeStruct((8, ROWS), f32), [vmem] * 2)(sums, got)
-    left_sums = shifted(sums, 2, high_pair)
-    right_sums = shifted(sums, -2, low_pair)
-    block = jnp.concatenate([kv, got[: 2 * ROWS], jnp.zeros((SPARE, half), bf16)], axis=0)
-    block, left_sums, right_sums = lax.optimization_barrier((block, left_sums, right_sums))
-    left = shifted(block, 2, high_pair)
-    right = shifted(block, -2, low_pair)
-    table = jax.ShapeDtypeStruct((16, ROWS), f32)
-    sums = call(table_kernel, table, [vmem] * 3)(sums, left_sums, right_sums)
+    side_sums = shifted(sums, 2, ends)
+    block = jnp.concatenate([theirs[: 2 * HALF_ROWS], got[: 2 * HALF_ROWS]], axis=0)
+    block, side_sums = lax.optimization_barrier((block, side_sums))
+    side = shifted(block, 2, ends)
+    sums = call(table_kernel, jax.ShapeDtypeStruct((16, ROWS), f32), [vmem] * 2)(sums, side_sums)
     sums = lax.psum(sums, "head")
-    left, right, sums = lax.optimization_barrier((left, right, sums))
-    spare = jax.ShapeDtypeStruct((SPARE, half), bf16)
-    left_pieces, right_pieces = call(pieces_kernel, (spare, spare), [vmem])(sums)
-    left = lax.dynamic_update_slice(left, left_pieces, (4 * ROWS, 0))
-    right = lax.dynamic_update_slice(right, right_pieces, (4 * ROWS, 0))
-    right3 = shifted(left, -8, low_pair)
-    left3 = shifted(right, 8, high_pair)
-    left2 = shifted(left, 2)
-    right2 = shifted(right, -2)
+    side, sums = lax.optimization_barrier((side, sums))
+    marks = call(pieces_kernel, jax.ShapeDtypeStruct((SPARE, half), bf16), [vmem])(sums)
+    side = lax.dynamic_update_slice(side, marks, (2 * ROWS, 0))
+    second = shifted(side, 2)
+    third = shifted(side, -8, (0, peers - 1))
+
+    def parts(*blocks):
+        return swapped(
+            call(
+                part_kernel,
+                jax.ShapeDtypeStruct((len(blocks) * PART_ROWS, half), bf16),
+                [smem] + [hbm] * len(blocks),
+                scratch=[pltpu.SemaphoreType.DMA((3 * len(blocks),))],
+            )(where, *blocks)
+        )
+
+    near_part = parts(side)
+    mate_sums = swapped(sums)
 
     text_out = call(
         cross_kernel, jax.ShapeDtypeStruct((ROWS, width), f32), [smem] * 3 + [vmem] * 6, flops=400000000
@@ -414,45 +473,26 @@
     text_out, q_gain, k_gain = lax.optimization_barrier((text_out, q_gain, k_gain))
 
     cosine, sine = (jnp.asarray(t) for t in rope_tables())
-    arrived = {-3: left3, -2: left2, -1: left, 0: block, 1: right, 2: right2, 3: right3}
-    near_chips, far_chips = (-1, 0, 1), (-3, -2, 2, 3)
-    near_rows = 2 * len(near_chips) * ROWS
     near_keys, near_values, q_own, q_mate = call(
-        functools.partial(near_kernel, near_chips),
-        (jax.ShapeDtypeStruct((near_rows, half), bf16),) * 2
-        + (jax.ShapeDtypeStruct((ROWS, half), bf16),) * 2,
-        [smem] * 2 + [vmem] * (7 + len(near_chips)),
+        near_kernel,
+        (jax.ShapeDtypeStruct((6 * ROWS, half), bf16),) * 2 + (jax.ShapeDtypeStruct((ROWS, half), bf16),) * 2,
+        [smem] * 2 + [vmem] * 11,
         flops=200000000,
     )(
-        tile_item,
-        where,
-        sums,
-        k_gain,
-        q_gain,
-        cosine,
-        sine,
-        q_mine,
-        got,
-        *[arrived[chip] for chip in near_chips],
-    )
+        tile_item, where, sums, mate_sums, k_gain, q_gain, cosine, sine, q_mine, got, block, side, near_part
+    )
+    second, third, near_keys, near_values, text_out = lax.optimization_barrier(
+        (second, third, near_keys, near_values, text_out)
+    )
+    far_part = parts(second, third)
     window = jax.ShapeDtypeStruct((14 * ROWS, half), bf16)
     mate_out, keys, values = call(
-        functools.partial(far_kernel, near_chips, far_chips),
+        far_kernel,
         (jax.ShapeDtypeStruct((ROWS, half), f32), window, window),
-        [smem] * 3 + [vmem] * (7 + len(far_chips)),
+        [smem] * 3 + [vmem] * 9,
         flops=300000000,
     )(
-        tile_item,
-        row_count,
-        where,
-        sums,
-        k_gain,
-        cosine,
-        sine,
-        q_mate,
-        near_keys,
-        near_values,
-        *[arrived[chip] for chip in far_chips],
+        tile_item, row_count, where, k_gain, cosine, sine, q_mate, near_keys, near_values, second, third, far_part
     )
     rest = swapped(mate_out)
     own = call(

time: 109 us -> 105 us (0.963)
  the two profiles are of different devices: /device:TPU:33 before, /device:TPU:31 now
where the time goes in v9:
time: 105 us; the launch traced here: 104 us
  starting transfers between devices  35.4 us (34%)
  waiting for transfers between devices  32.6 us (31%)
  blocking collectives  19.6 us (19%)
  Pallas kernels  13.7 us (13%)
  local copies, waits for them, and re-layouts  1.33 us (1%)
  other arithmetic  1.22 us (1%)
    ppermute x4, waiting for transfers between devices, shifted(): return lax.ppermute(value, 'tile', pairs)  28.9 us
    ppermute x5, starting transfers between devices, swapped(): return lax.ppermute(value, 'tile', [(i, i ^ 1) for i in range(peers)])  27.2 us
    psum x1, blocking collectives, per_device(): sums = lax.psum(sums, 'head')  19.6 us
    ppermute x4, starting transfers between devices, shifted(): return lax.ppermute(value, 'tile', pairs)  8.19 us
    ppermute x5, waiting for transfers between devices, swapped(): return lax.ppermute(value, 'tile', [(i, i ^ 1) for i in range(peers)])  3.75 us
    pallas_call x1, Pallas kernels, per_device(): call(far_kernel, (jax.ShapeDtypeStruct((ROWS, half), f32), window, window...  2.78 us
    pallas_call x1, Pallas kernels, per_device(): call(near_kernel, (jax.ShapeDtypeStruct((6 * ROWS, half), bf16),) * 2 + (...  2.7 us
    pallas_call x1, Pallas kernels, per_device(): call(pack_kernel, (jax.ShapeDtypeStruct((2 * HALF_ROWS + ROWS, half), bf1...  2.51 us
  transfers between devices with their start and end apart: 9, of which 5 were waited for; matrix products, arithmetic and copies ran while one was open for 2% of the time, Pallas kernels for 7%

profile of v9, /device:TPU:31, one launch (start us, length us, event | category | flops | bytes accessed | tf_op | source)
XLA Modules:
  0.0 104.2 jit_solution(1146790293356942605)
XLA Ops:
  0.0 2.5 %shard_map.145 = (bf16[672,640]{1,0:T(8,128)(2,1)}, bf16[128,640]{1,0:T(8,128)(2,1)}, f32[8,128]{1,0:T(8,128)}) custom-call(s32[1]{0:T(128)} %bitcast.here_ref, bf16[128,1280]{1,0:T(8,128)(2,1)} %q_hbm.1, bf16[128,1280]{1,0:T(8,128)(2,1)} %k_hbm.1, bf16[128,1280]{1,0:T(8,128)(2,1)} %v_hbm.1, bf16[128,1280]{1,0:T(8,128)(2,1)} %q_ref.1, bf16[256,1280]{1,0:T(8,128)(2,1)} %k_ref.1), custom_call_target="tpu_custom_call" | custom-call | flops 1000000 | bytes 4000000 | tf_op jit(solution)/shard_map/pallas_call | solution.py:418
  2.5 2.6 %collective-permute-start = (bf16[672,640]{1,0:T(8,128)(2,1)}, bf16[672,640]{1,0:T(8,128)(2,1)S(1)}, u32[]{:S(2)}, u32[]{:S(2)}) collective-permute-start(bf16[672,640]{1,0:T(8,128)(2,1)} %get-tuple-element.27), channel_id=1, source_target_pairs={{0,4},{4,0},{8,12},{12,8},{16,20},{20,16},{24,28},{28,24},{32,36},... | collective-permute-start | bytes 2580488 | tf_op jit(solution)/shard_map/ppermute | solution.py:64
  5.1 1.2 %slice.6 = bf16[544,640]{1,0:T(8,128)(2,1)S(1)} slice(bf16[672,640]{1,0:T(8,128)(2,1)} %get-tuple-element.27), slice={[0:544], [0:640]} | slice | bytes 1392640 | tf_op jit(solution)/shard_map/slice | solution.py:435
  6.3 1.0 collective-permute-done.got_ref
  7.3 2.4 %collective-permute-start.1 = (f32[8,128]{1,0:T(8,128)S(1)}, f32[8,128]{1,0:T(8,128)S(1)}, u32[]{:S(2)}, u32[]{:S(2)}) collective-permute-start(f32[8,128]{1,0:T(8,128)S(1)} %shard_map.146.own_ref), channel_id=1, source_target_pairs={{0,8},{4,508},{8,16},{12,4},{16,24},{20,12},{24,32},{28,20},{32,40... | collective-permute-start | bytes 12296 | tf_op jit(solution)/shard_map/ppermute | solution.py:59
  9.9 1.2 %pad_maximum_fusion.block_ref = bf16[1088,640]{1,0:T(8,128)(2,1)} fusion(bf16[544,640]{1,0:T(8,128)(2,1)S(1)} %slice.8, bf16[544,640]{1,0:T(8,128)(2,1)S(1)} %slice.6), kind=kLoop, calls=%fused_computation | loop fusion | flops 2785280 | bytes 2785280 | tf_op jit(solution)/shard_map/concatenate | solution.py:435
  11.1 4.8 %collective-permute-done.1.side_ref = f32[8,128]{1,0:T(8,128)S(1)} collective-permute-done((f32[8,128]{1,0:T(8,128)S(1)}, f32[8,128]{1,0:T(8,128)S(1)}, u32[]{:S(2)}, u32[]{:S(2)}) %collective-permute-start.1) | collective-permute-done | bytes 4128 | tf_op jit(solution)/shard_map/ppermute | solution.py:59
  15.9 1.9 %collective-permute-start.2 = (bf16[1088,640]{1,0:T(8,128)(2,1)}, bf16[1088,640]{1,0:T(8,128)(2,1)S(1)}, u32[]{:S(2)}, u32[]{:S(2)}) collective-permute-start(bf16[1088,640]{1,0:T(8,128)(2,1)} %pad_maximum_fusion.block_ref), channel_id=1, source_target_pairs={{0,8},{4,508},{8,16},{12,4},{16,24},{20,12},{24,32},{28,20},{32,40... | collective-permute-start | bytes 4177928 | tf_op jit(solution)/shard_map/ppermute | solution.py:59
  17.8 19.6 %psum.7.sums_ref = f32[16,128]{1,0:T(8,128)S(1)} all-reduce(f32[16,128]{1,0:T(8,128)S(1)} %shard_map.147), channel_id=1, replica_groups=mesh['tile'=128,'head'=4] {'head'}, use_global_device_ids=true, to_apply=%region_0.0 | all-reduce | flops 2048 | bytes 16384 | tf_op jit(solution)/shard_map/psum | solution.py:439
  37.4 2.4 %collective-permute-done.2 = bf16[1088,640]{1,0:T(8,128)(2,1)S(1)} collective-permute-done((bf16[1088,640]{1,0:T(8,128)(2,1)}, bf16[1088,640]{1,0:T(8,128)(2,1)S(1)}, u32[]{:S(2)}, u32[]{:S(2)}) %collective-permute-start.2) | collective-permute-done | bytes 1392672 | tf_op jit(solution)/shard_map/ppermute | solution.py:59
  39.9 1.9 %collective-permute-start.6 = (bf16[1088,640]{1,0:T(8,128)(2,1)S(1)}, bf16[1088,640]{1,0:T(8,128)(2,1)S(1)}, u32[]{:S(2)}, u32[]{:S(2)}) collective-permute-start(bf16[1088,640]{1,0:T(8,128)(2,1)S(1)} %constant_dynamic-update-slice_fusion.rest_0_.kept_ref), channel_id=1, source_target_pairs={{0,480},{4,36},{12,44},{20,52},{28,60},{32,0},{36,68},{40,8},{44,7... | collective-permute-start | bytes 4177928 | tf_op jit(solution)/shard_map/ppermute | solution.py:59
  41.9 1.9 %collective-permute-start.5 = (bf16[1088,640]{1,0:T(8,128)(2,1)S(1)}, bf16[1088,640]{1,0:T(8,128)(2,1)S(1)}, u32[]{:S(2)}, u32[]{:S(2)}) collective-permute-start(bf16[1088,640]{1,0:T(8,128)(2,1)S(1)} %constant_dynamic-update-slice_fusion.rest_0_.kept_ref), channel_id=1, source_target_pairs={{0,8},{8,16},{12,4},{16,24},{20,12},{24,32},{28,20},{32,40},{36,28... | collective-permute-start | bytes 4177928 | tf_op jit(solution)/shard_map/ppermute | solution.py:59
  44.1 17.4 %collective-permute-start.4 = (bf16[528,640]{1,0:T(8,128)(2,1)S(1)}, bf16[528,640]{1,0:T(8,128)(2,1)S(1)}, u32[]{:S(2)}, u32[]{:S(2)}) collective-permute-start(bf16[528,640]{1,0:T(8,128)(2,1)S(1)} %shard_map.150), channel_id=1, source_target_pairs={{0,4},{4,0},{8,12},{12,8},{16,20},{20,16},{24,28},{28,24},{32,36},... | collective-permute-start | bytes 2027528 | tf_op jit(solution)/shard_map/ppermute | solution.py:64
  61.6 1.9 %collective-permute-start.3 = (f32[16,128]{1,0:T(8,128)S(1)}, f32[16,128]{1,0:T(8,128)S(1)}, u32[]{:S(2)}, u32[]{:S(2)}) collective-permute-start(f32[16,128]{1,0:T(8,128)S(1)} %psum.7.sums_ref), channel_id=1, source_target_pairs={{0,4},{4,0},{8,12},{12,8},{16,20},{20,16},{24,28},{28,24},{32,36},... | collective-permute-start | bytes 24584 | tf_op jit(solution)/shard_map/ppermute | solution.py:64
  63.6 1.6 %shard_map.148.text_ref = f32[128,1280]{1,0:T(8,128)S(1)} custom-call(s32[128]{0:T(128)S(1)} %copy-done.6, s32[128]{0:T(128)S(1)} %copy-done.9, s32[1]{0:T(128)} %bitcast.here_ref, f32[16,128]{1,0:T(8,128)S(1)} %psum.7.sums_ref, bf16[128,1280]{1,0:T(8,128)(2,1)S(1)} %copy-done.3, bf16[256,1280]{1,0:T(8,128)(2,1)S(1)} %copy-done, ...), custom_call_target="tpu_custom_call" | custom-call | flops 400000000 | bytes 4000000 | tf_op jit(solution)/shard_map/pallas_call | solution.py:459
  65.3 2.7 %shard_map.151 = (bf16[768,640]{1,0:T(8,128)(2,1)S(1)}, bf16[768,640]{1,0:T(8,128)(2,1)S(1)}, bf16[128,640]{1,0:T(8,128)(2,1)S(1)}, bf16[128,640]{1,0:T(8,128)(2,1)S(1)}) custom-call(s32[128]{0:T(128)S(1)} %copy-done.6, s32[1]{0:T(128)} %bitcast.here_ref, f32[16,128]{1,0:T(8,128)S(1)} %psum.7.sums_ref, f32[16,128]{1,0:T(8,128)S(1)} %collective-permute-done.3.mate_sums_ref, ...), custom_call_target="tpu_custom_call" | custom-call | flops 200000000 | bytes 4000000 | tf_op jit(solution)/shard_map/pallas_call | solution.py:476
  68.0 21.7 %collective-permute-done.5.rest_0_.second_ref = bf16[1088,640]{1,0:T(8,128)(2,1)S(1)} collective-permute-done((bf16[1088,640]{1,0:T(8,128)(2,1)S(1)}, bf16[1088,640]{1,0:T(8,128)(2,1)S(1)}, u32[]{:S(2)}, u32[]{:S(2)}) %collective-permute-start.5) | collective-permute-done | bytes 1392672 | tf_op jit(solution)/shard_map/ppermute | solution.py:59
  89.7 0.5 shard_map.152
  90.2 2.9 %collective-permute-start.7 = (bf16[1056,640]{1,0:T(8,128)(2,1)S(1)}, bf16[1056,640]{1,0:T(8,128)(2,1)S(1)}, u32[]{:S(2)}, u32[]{:S(2)}) collective-permute-start(bf16[1056,640]{1,0:T(8,128)(2,1)S(1)} %shard_map.152), channel_id=1, source_target_pairs={{0,4},{4,0},{8,12},{12,8},{16,20},{20,16},{24,28},{28,24},{32,36},... | collective-permute-start | bytes 4055048 | tf_op jit(solution)/shard_map/ppermute | solution.py:64
  93.2 2.7 %collective-permute-done.7.part_ref = bf16[1056,640]{1,0:T(8,128)(2,1)S(1)} collective-permute-done((bf16[1056,640]{1,0:T(8,128)(2,1)S(1)}, bf16[1056,640]{1,0:T(8,128)(2,1)S(1)}, u32[]{:S(2)}, u32[]{:S(2)}) %collective-permute-start.7) | collective-permute-done | bytes 1351712 | tf_op jit(solution)/shard_map/ppermute | solution.py:64
  95.9 2.8 %shard_map.153 = (f32[128,640]{1,0:T(8,128)S(1)}, bf16[1792,640]{1,0:T(8,128)(2,1)S(1)}, bf16[1792,640]{1,0:T(8,128)(2,1)S(1)}) custom-call(s32[128]{0:T(128)S(1)} %copy-done.6, s32[128]{0:T(128)S(1)} %copy-done.8, s32[1]{0:T(128)} %bitcast.here_ref, f32[1,1280]{1,0:T(1,128)S(1)} %broadcast_in_dim.15.k_gain_ref, f32[896,128]{1,0:T(8,128)S(1)} %copy-done.2, ...), custom_call_target="tpu_custom_call" | custom-call | flops 300000000 | bytes 4000000 | tf_op jit(solution)/shard_map/pallas_call | solution.py:489
  98.6 2.3 %collective-permute-start.8 = (f32[128,640]{1,0:T(8,128)S(1)}, f32[128,640]{1,0:T(8,128)S(1)}, u32[]{:S(2)}, u32[]{:S(2)}) collective-permute-start(f32[128,640]{1,0:T(8,128)S(1)} %get-tuple-element.47), channel_id=1, source_target_pairs={{0,4},{4,0},{8,12},{12,8},{16,20},{20,16},{24,28},{28,24},{32,36},... | collective-permute-start | bytes 983048 | tf_op jit(solution)/shard_map/ppermute | solution.py:64
  100.9 2.5 %shard_map.154.own_ref = f32[128,640]{1,0:T(8,128)S(1)} custom-call(s32[128]{0:T(128)S(1)} %copy-done.6, s32[128]{0:T(128)S(1)} %copy-done.8, s32[1]{0:T(128)} %bitcast.here_ref, bf16[128,640]{1,0:T(8,128)(2,1)S(1)} %get-tuple-element.36.q_ref, bf16[1792,640]{1,0:T(8,128)(2,1)S(1)} %get-tuple-element.45.keys_ref, ...), custom_call_target="tpu_custom_call" | custom-call | flops 300000000 | bytes 4000000 | tf_op jit(solution)/shard_map/pallas_call | solution.py:498
  103.4 0.8 shard_map.155
  (42 shorter events, 0.5 us)
Async XLA Ops:
  2.5 4.8 %copy-start.7 = (f32[8,128]{1,0:T(8,128)S(1)}, f32[8,128]{1,0:T(8,128)}, u32[]{:S(2)}) copy-start(f32[8,128]{1,0:T(8,128)} %get-tuple-element.28.own_ref) | copy-start | bytes 12292
  2.5 4.8 %collective-permute-start = (bf16[672,640]{1,0:T(8,128)(2,1)}, bf16[672,640]{1,0:T(8,128)(2,1)S(1)}, u32[]{:S(2)}, u32[]{:S(2)}) collective-permute-start(bf16[672,640]{1,0:T(8,128)(2,1)} %get-tuple-element.27), channel_id=1, source_target_pairs={{0,4},{4,0},{8,12},{12,8},{16,20},{20,16},{24,28},{28,24},{32,36},... | collective-permute-start | bytes 2580488 | tf_op jit(solution)/shard_map/ppermute | solution.py:64
  7.3 8.6 %collective-permute-start.1 = (f32[8,128]{1,0:T(8,128)S(1)}, f32[8,128]{1,0:T(8,128)S(1)}, u32[]{:S(2)}, u32[]{:S(2)}) collective-permute-start(f32[8,128]{1,0:T(8,128)S(1)} %shard_map.146.own_ref), channel_id=1, source_target_pairs={{0,8},{4,508},{8,16},{12,4},{16,24},{20,12},{24,32},{28,20},{32,40... | collective-permute-start | bytes 12296 | tf_op jit(solution)/shard_map/ppermute | solution.py:59
  11.1 50.5 %copy-start.10 = (f32[1280]{0:T(1024)S(1)}, f32[1280]{0:T(1024)}, u32[]{:S(2)}) copy-start(f32[1280]{0:T(1024)} %param.21) | copy-start | bytes 15364
  11.1 50.5 %copy-start.11 = (f32[1280]{0:T(1024)S(1)}, f32[1280]{0:T(1024)}, u32[]{:S(2)}) copy-start(f32[1280]{0:T(1024)} %param.22) | copy-start | bytes 15364
  11.1 50.5 %copy-start.12 = (f32[1280]{0:T(1024)S(1)}, f32[1280]{0:T(1024)}, u32[]{:S(2)}) copy-start(f32[1280]{0:T(1024)} %param.23) | copy-start | bytes 15364
  11.1 50.5 %copy-start.13 = (f32[1280]{0:T(1024)S(1)}, f32[1280]{0:T(1024)}, u32[]{:S(2)}) copy-start(f32[1280]{0:T(1024)} %param.24) | copy-start | bytes 15364
  11.1 52.5 %copy-start = (bf16[256,1280]{1,0:T(8,128)(2,1)S(1)}, bf16[256,1280]{1,0:T(8,128)(2,1)}, u32[]{:S(2)}) copy-start(bf16[256,1280]{1,0:T(8,128)(2,1)} %k_ref.1) | copy-start | bytes 1966084
  11.1 52.5 %copy-start.3 = (bf16[128,1280]{1,0:T(8,128)(2,1)S(1)}, bf16[128,1280]{1,0:T(8,128)(2,1)}, u32[]{:S(2)}) copy-start(bf16[128,1280]{1,0:T(8,128)(2,1)} %q_ref.1) | copy-start | bytes 983044
  11.1 52.5 %copy-start.6 = (s32[128]{0:T(128)S(1)}, s32[128]{0:T(128)}, u32[]{:S(2)}) copy-start(s32[128]{0:T(128)} %item_ref.7) | copy-start | bytes 1540
  11.1 52.5 %copy-start.9 = (s32[128]{0:T(128)S(1)}, s32[128]{0:T(128)}, u32[]{:S(2)}) copy-start(s32[128]{0:T(128)} %len_ref.1) | copy-start | bytes 1540
  15.9 24.0 %collective-permute-start.2 = (bf16[1088,640]{1,0:T(8,128)(2,1)}, bf16[1088,640]{1,0:T(8,128)(2,1)S(1)}, u32[]{:S(2)}, u32[]{:S(2)}) collective-permute-start(bf16[1088,640]{1,0:T(8,128)(2,1)} %pad_maximum_fusion.block_ref), channel_id=1, source_target_pairs={{0,8},{4,508},{8,16},{12,4},{16,24},{20,12},{24,32},{28,20},{32,40... | collective-permute-start | bytes 4177928 | tf_op jit(solution)/shard_map/ppermute | solution.py:59
  37.4 26.2 %copy-start.4 = (bf16[256,1280]{1,0:T(8,128)(2,1)S(1)}, bf16[256,1280]{1,0:T(8,128)(2,1)}, u32[]{:S(2)}) copy-start(bf16[256,1280]{1,0:T(8,128)(2,1)} %v_ref.1) | copy-start | bytes 1966084
  39.9 28.1 %collective-permute-start.6 = (bf16[1088,640]{1,0:T(8,128)(2,1)S(1)}, bf16[1088,640]{1,0:T(8,128)(2,1)S(1)}, u32[]{:S(2)}, u32[]{:S(2)}) collective-permute-start(bf16[1088,640]{1,0:T(8,128)(2,1)S(1)} %constant_dynamic-update-slice_fusion.rest_0_.kept_ref), channel_id=1, source_target_pairs={{0,480},{4,36},{12,44},{20,52},{28,60},{32,0},{36,68},{40,8},{44,7... | collective-permute-start | bytes 4177928 | tf_op jit(solution)/shard_map/ppermute | solution.py:59
  41.9 47.8 %collective-permute-start.5 = (bf16[1088,640]{1,0:T(8,128)(2,1)S(1)}, bf16[1088,640]{1,0:T(8,128)(2,1)S(1)}, u32[]{:S(2)}, u32[]{:S(2)}) collective-permute-start(bf16[1088,640]{1,0:T(8,128)(2,1)S(1)} %constant_dynamic-update-slice_fusion.rest_0_.kept_ref), channel_id=1, source_target_pairs={{0,8},{8,16},{12,4},{16,24},{20,12},{24,32},{28,20},{32,40},{36,28... | collective-permute-start | bytes 4177928 | tf_op jit(solution)/shard_map/ppermute | solution.py:59
  44.1 21.2 %copy-start.1 = (f32[896,128]{1,0:T(8,128)S(1)}, f32[896,128]{1,0:T(8,128)}, u32[]{:S(2)}) copy-start(f32[896,128]{1,0:T(8,128)} %constant.15.clone.sin_ref) | copy-start | bytes 1376260
  44.1 21.2 %copy-start.2 = (f32[896,128]{1,0:T(8,128)S(1)}, f32[896,128]{1,0:T(8,128)}, u32[]{:S(2)}) copy-start(f32[896,128]{1,0:T(8,128)} %constant.14.clone.cos_ref) | copy-start | bytes 1376260
  44.1 21.2 %copy-start.5 = (bf16[128,640]{1,0:T(8,128)(2,1)S(1)}, bf16[128,640]{1,0:T(8,128)(2,1)}, u32[]{:S(2)}) copy-start(bf16[128,640]{1,0:T(8,128)(2,1)} %get-tuple-element.34.q_own_ref) | copy-start | bytes 491524
  44.1 21.1 %collective-permute-start.4 = (bf16[528,640]{1,0:T(8,128)(2,1)S(1)}, bf16[528,640]{1,0:T(8,128)(2,1)S(1)}, u32[]{:S(2)}, u32[]{:S(2)}) collective-permute-start(bf16[528,640]{1,0:T(8,128)(2,1)S(1)} %shard_map.150), channel_id=1, source_target_pairs={{0,4},{4,0},{8,12},{12,8},{16,20},{20,16},{24,28},{28,24},{32,36},... | collective-permute-start | bytes 2027528 | tf_op jit(solution)/shard_map/ppermute | solution.py:64
  61.6 3.6 %collective-permute-start.3 = (f32[16,128]{1,0:T(8,128)S(1)}, f32[16,128]{1,0:T(8,128)S(1)}, u32[]{:S(2)}, u32[]{:S(2)}) collective-permute-start(f32[16,128]{1,0:T(8,128)S(1)} %psum.7.sums_ref), channel_id=1, source_target_pairs={{0,4},{4,0},{8,12},{12,8},{16,20},{20,16},{24,28},{28,24},{32,36},... | collective-permute-start | bytes 24584 | tf_op jit(solution)/shard_map/ppermute | solution.py:64
  89.7 6.2 %copy-start.8 = (s32[128]{0:T(128)S(1)}, s32[128]{0:T(128)}, u32[]{:S(2)}) copy-start(s32[128]{0:T(128)} %count_ref.3) | copy-start | bytes 1540
  90.2 5.6 %collective-permute-start.7 = (bf16[1056,640]{1,0:T(8,128)(2,1)S(1)}, bf16[1056,640]{1,0:T(8,128)(2,1)S(1)}, u32[]{:S(2)}, u32[]{:S(2)}) collective-permute-start(bf16[1056,640]{1,0:T(8,128)(2,1)S(1)} %shard_map.152), channel_id=1, source_target_pairs={{0,4},{4,0},{8,12},{12,8},{16,20},{20,16},{24,28},{28,24},{32,36},... | collective-permute-start | bytes 4055048 | tf_op jit(solution)/shard_map/ppermute | solution.py:64
  98.6 4.8 %collective-permute-start.8 = (f32[128,640]{1,0:T(8,128)S(1)}, f32[128,640]{1,0:T(8,128)S(1)}, u32[]{:S(2)}, u32[]{:S(2)}) collective-permute-start(f32[128,640]{1,0:T(8,128)S(1)} %get-tuple-element.47), channel_id=1, source_target_pairs={{0,4},{4,0},{8,12},{12,8},{16,20},{20,16},{24,28},{28,24},{32,36},... | collective-permute-start | bytes 983048 | tf_op jit(solution)/shard_map/ppermute | solution.py:64

commit v10 on v9

--- a/solution.py
+++ b/solution.py
@@ -272,6 +272,18 @@
         return joined(rows, 0), joined(rows, 3)
 
     return totals
+
+
+def block_kernel(own_ref, mate_ref, out_ref, arrived):
+    tile = 2 * HALF_ROWS
+    copies = [
+        pltpu.make_async_copy(ref.at[0:tile], out_ref.at[slot * tile : (slot + 1) * tile], arrived.at[slot])
+        for slot, ref in enumerate((own_ref, mate_ref))
+    ]
+    for copy in copies:
+        copy.start()
+    for copy in copies:
+        copy.wait()
 
 
 def near_kernel(
@@ -341,7 +353,7 @@
 
 def far_kernel(
     item_ref, count_ref, here_ref, k_gain_ref, cos_ref, sin_ref, q_ref, near_keys_ref, near_values_ref,
-    second_ref, third_ref, part_ref, out_ref, keys_ref, values_ref
+    second_ref, third_ref, part_ref, out_ref, keys_ref, values_ref, arrived
 ):
     core = lax.rem(here_ref[0], 2)
     left = here_ref[0] - core
@@ -350,8 +362,12 @@
     bounds = (*extent(item_ref, left), *extent(item_ref, left + 1))
     k_gains = k_gain_ref.at[:, pl.ds(pl.multiple_of(core * half, HD), half)]
     near = slice(4 * ROWS, 10 * ROWS)
-    keys_ref[near, :] = near_keys_ref[...]
-    values_ref[near, :] = near_values_ref[...]
+    copies = [
+        pltpu.make_async_copy(near_keys_ref, keys_ref.at[near], arrived.at[0]),
+        pltpu.make_async_copy(near_values_ref, values_ref.at[near], arrived.at[1]),
+    ]
+    for copy in copies:
+        copy.start()
     for chip, rows_of, totals, block in (
         (2 * sign, kept_rows(core), spares(second_ref, 2 * ROWS), second_ref),
         (-3 * sign, kept_rows(core), spares(third_ref, 2 * ROWS), third_ref),
@@ -361,6 +377,8 @@
         gather(
             chip, rows_of, totals, block, core, left, bounds, k_gains, (cos_ref, sin_ref), keys_ref, values_ref, -3
         )
+    for copy in copies:
+        copy.wait()
     attend(True, item_ref, count_ref, here_ref, q_ref, keys_ref, values_ref, out_ref)
 
 
@@ -432,7 +450,12 @@
     ends = (peers - 2, 1)
     sums = call(mate_kernel, jax.ShapeDtypeStruct((8, ROWS), f32), [vmem] * 2)(sums, got)
     side_sums = shifted(sums, 2, ends)
-    block = jnp.concatenate([theirs[: 2 * HALF_ROWS], got[: 2 * HALF_ROWS]], axis=0)
+    block = call(
+        block_kernel,
+        jax.ShapeDtypeStruct((4 * HALF_ROWS, half), bf16),
+        [hbm] * 2,
+        scratch=[pltpu.SemaphoreType.DMA((2,))],
+    )(theirs, got)
     block, side_sums = lax.optimization_barrier((block, side_sums))
     side = shifted(block, 2, ends)
     sums = call(table_kernel, jax.ShapeDtypeStruct((16, ROWS), f32), [vmem] * 2)(sums, side_sums)
@@ -490,6 +513,7 @@
         far_kernel,
         (jax.ShapeDtypeStruct((ROWS, half), f32), window, window),
         [smem] * 3 + [vmem] * 9,
+        scratch=[pltpu.SemaphoreType.DMA((2,))],
         flops=300000000,
     )(
         tile_item, row_count, where, k_gain, cosine, sine, q_mate, near_keys, near_values, second, third, far_part

time: 105 us -> 107 us (1.019)
  the two profiles are of different devices: /device:TPU:31 before, /device:TPU:1 now
where the time goes in v10:
time: 107 us; the launch traced here: 106 us
  starting transfers between devices  35.1 us (33%)
  blocking collectives  29 us (27%)
  waiting for transfers between devices  24.1 us (23%)
  Pallas kernels  16.1 us (15%)
  local copies, waits for them, and re-layouts  1.38 us (1%)
    psum x1, blocking collectives, per_device(): sums = lax.psum(sums, 'head')  29 us
    ppermute x4, waiting for transfers between devices, shifted(): return lax.ppermute(value, 'tile', pairs)  18.9 us
    ppermute x4, starting transfers between devices, shifted(): return lax.ppermute(value, 'tile', pairs)  17.8 us
    ppermute x5, starting transfers between devices, swapped(): return lax.ppermute(value, 'tile', [(i, i ^ 1) for i in range(peers)])  17.3 us
    ppermute x5, waiting for transfers between devices, swapped(): return lax.ppermute(value, 'tile', [(i, i ^ 1) for i in range(peers)])  5.27 us
    pallas_call x1, Pallas kernels, per_device(): call(far_kernel, (jax.ShapeDtypeStruct((ROWS, half), f32), window, window...  3.45 us
    pallas_call x1, Pallas kernels, per_device(): call(near_kernel, (jax.ShapeDtypeStruct((6 * ROWS, half), bf16),) * 2 + (...  3.04 us
    pallas_call x1, Pallas kernels, per_device(): call(pack_kernel, (jax.ShapeDtypeStruct((2 * HALF_ROWS + ROWS, half), bf1...  2.51 us
  transfers between devices with their start and end apart: 9, of which 4 were waited for; matrix products, arithmetic and copies ran while one was open for 0% of the time, Pallas kernels for 8%

profile of v10, /device:TPU:1, one launch (start us, length us, event | category | flops | bytes accessed | tf_op | source)
XLA Modules:
  0.0 106.1 jit_solution(16427760030364104317)
XLA Ops:
  0.0 2.5 %shard_map.145 = (bf16[672,640]{1,0:T(8,128)(2,1)}, bf16[128,640]{1,0:T(8,128)(2,1)}, f32[8,128]{1,0:T(8,128)}) custom-call(s32[1]{0:T(128)} %bitcast.here_ref, bf16[128,1280]{1,0:T(8,128)(2,1)} %q_hbm.1, bf16[128,1280]{1,0:T(8,128)(2,1)} %k_hbm.1, bf16[128,1280]{1,0:T(8,128)(2,1)} %v_hbm.1, bf16[128,1280]{1,0:T(8,128)(2,1)} %q_ref.1, bf16[256,1280]{1,0:T(8,128)(2,1)} %k_ref.1), custom_call_target="tpu_custom_call" | custom-call | flops 1000000 | bytes 4000000 | tf_op jit(solution)/shard_map/pallas_call | solution.py:436
  2.5 8.9 %collective-permute-start = (bf16[672,640]{1,0:T(8,128)(2,1)}, bf16[672,640]{1,0:T(8,128)(2,1)S(1)}, u32[]{:S(2)}, u32[]{:S(2)}) collective-permute-start(bf16[672,640]{1,0:T(8,128)(2,1)} %get-tuple-element.27.own_ref), channel_id=1, source_target_pairs={{0,4},{4,0},{8,12},{12,8},{16,20},{20,16},{24,28},{28,24},{32,36},... | collective-permute-start | bytes 2580488 | tf_op jit(solution)/shard_map/ppermute | solution.py:64
  11.5 2.2 %collective-permute-done.mate_ref.got_ref = bf16[672,640]{1,0:T(8,128)(2,1)S(1)} collective-permute-done((bf16[672,640]{1,0:T(8,128)(2,1)}, bf16[672,640]{1,0:T(8,128)(2,1)S(1)}, u32[]{:S(2)}, u32[]{:S(2)}) %collective-permute-start) | collective-permute-done | bytes 860192 | tf_op jit(solution)/shard_map/ppermute | solution.py:64
  13.7 0.7 copy-done.8
  14.3 5.5 %collective-permute-start.1 = (f32[8,128]{1,0:T(8,128)S(1)}, f32[8,128]{1,0:T(8,128)S(1)}, u32[]{:S(2)}, u32[]{:S(2)}) collective-permute-start(f32[8,128]{1,0:T(8,128)S(1)} %shard_map.147.own_ref), channel_id=1, source_target_pairs={{0,8},{4,508},{8,16},{12,4},{16,24},{20,12},{24,32},{28,20},{32,40... | collective-permute-start | bytes 12296 | tf_op jit(solution)/shard_map/ppermute | solution.py:59
  19.9 0.5 shard_map.146.block_ref
  20.6 9.6 %collective-permute-start.2 = (bf16[1088,640]{1,0:T(8,128)(2,1)S(1)}, bf16[1088,640]{1,0:T(8,128)(2,1)}, u32[]{:S(2)}, u32[]{:S(2)}) collective-permute-start(bf16[1088,640]{1,0:T(8,128)(2,1)S(1)} %shard_map.146.block_ref), channel_id=1, source_target_pairs={{0,8},{4,508},{8,16},{12,4},{16,24},{20,12},{24,32},{28,20},{32,40... | collective-permute-start | bytes 4177928 | tf_op jit(solution)/shard_map/ppermute | solution.py:59
  30.2 29.0 %psum.7.sums_ref = f32[16,128]{1,0:T(8,128)S(1)} all-reduce(f32[16,128]{1,0:T(8,128)S(1)} %shard_map.148), channel_id=1, replica_groups=mesh['tile'=128,'head'=4] {'head'}, use_global_device_ids=true, to_apply=%region_0.0 | all-reduce | flops 2048 | bytes 16384 | tf_op jit(solution)/shard_map/psum | solution.py:462
  59.2 0.6 constant_dynamic-update-slice_fusion.rest_0_.kept_ref
  59.8 1.4 %collective-permute-start.6 = (bf16[1088,640]{1,0:T(8,128)(2,1)}, bf16[1088,640]{1,0:T(8,128)(2,1)S(1)}, u32[]{:S(2)}, u32[]{:S(2)}) collective-permute-start(bf16[1088,640]{1,0:T(8,128)(2,1)} %constant_dynamic-update-slice_fusion.rest_0_.kept_ref), channel_id=1, source_target_pairs={{0,480},{4,36},{12,44},{20,52},{28,60},{32,0},{36,68},{40,8},{44,7... | collective-permute-start | bytes 4177928 | tf_op jit(solution)/shard_map/ppermute | solution.py:59
  61.2 1.3 %collective-permute-start.5 = (bf16[1088,640]{1,0:T(8,128)(2,1)}, bf16[1088,640]{1,0:T(8,128)(2,1)S(1)}, u32[]{:S(2)}, u32[]{:S(2)}) collective-permute-start(bf16[1088,640]{1,0:T(8,128)(2,1)} %constant_dynamic-update-slice_fusion.rest_0_.kept_ref), channel_id=1, source_target_pairs={{0,8},{8,16},{12,4},{16,24},{20,12},{24,32},{28,20},{32,40},{36,28... | collective-permute-start | bytes 4177928 | tf_op jit(solution)/shard_map/ppermute | solution.py:59
  62.5 1.1 %shard_map.151 = bf16[528,640]{1,0:T(8,128)(2,1)S(1)} custom-call(s32[1]{0:T(128)} %bitcast.here_ref, bf16[1088,640]{1,0:T(8,128)(2,1)} %constant_dynamic-update-slice_fusion.rest_0_.kept_ref), custom_call_target="tpu_custom_call" | custom-call | flops 1000000 | bytes 4000000 | tf_op jit(solution)/shard_map/pallas_call | solution.py:471
  63.7 2.1 %collective-permute-start.4 = (bf16[528,640]{1,0:T(8,128)(2,1)S(1)}, bf16[528,640]{1,0:T(8,128)(2,1)S(1)}, u32[]{:S(2)}, u32[]{:S(2)}) collective-permute-start(bf16[528,640]{1,0:T(8,128)(2,1)S(1)} %shard_map.151), channel_id=1, source_target_pairs={{0,4},{4,0},{8,12},{12,8},{16,20},{20,16},{24,28},{28,24},{32,36},... | collective-permute-start | bytes 2027528 | tf_op jit(solution)/shard_map/ppermute | solution.py:64
  65.8 2.4 %collective-permute-start.3 = (f32[16,128]{1,0:T(8,128)S(1)}, f32[16,128]{1,0:T(8,128)S(1)}, u32[]{:S(2)}, u32[]{:S(2)}) collective-permute-start(f32[16,128]{1,0:T(8,128)S(1)} %psum.7.sums_ref), channel_id=1, source_target_pairs={{0,4},{4,0},{8,12},{12,8},{16,20},{20,16},{24,28},{28,24},{32,36},... | collective-permute-start | bytes 24584 | tf_op jit(solution)/shard_map/ppermute | solution.py:64
  68.3 1.6 %shard_map.149.text_ref = f32[128,1280]{1,0:T(8,128)S(1)} custom-call(s32[128]{0:T(128)S(1)} %copy-done.7, s32[128]{0:T(128)S(1)} %copy-done.10, s32[1]{0:T(128)} %bitcast.here_ref, f32[16,128]{1,0:T(8,128)S(1)} %psum.7.sums_ref, bf16[128,1280]{1,0:T(8,128)(2,1)S(1)} %copy-done.3, bf16[256,1280]{1,0:T(8,128)(2,1)S(1)} %copy-done, ...), custom_call_target="tpu_custom_call" | custom-call | flops 400000000 | bytes 4000000 | tf_op jit(solution)/shard_map/pallas_call | solution.py:482
  69.9 3.0 %shard_map.152 = (bf16[768,640]{1,0:T(8,128)(2,1)S(1)}, bf16[768,640]{1,0:T(8,128)(2,1)S(1)}, bf16[128,640]{1,0:T(8,128)(2,1)S(1)}, bf16[128,640]{1,0:T(8,128)(2,1)S(1)}) custom-call(s32[128]{0:T(128)S(1)} %copy-done.7, s32[1]{0:T(128)} %bitcast.here_ref, f32[16,128]{1,0:T(8,128)S(1)} %psum.7.sums_ref, f32[16,128]{1,0:T(8,128)S(1)} %collective-permute-done.3.mate_sums_ref, ...), custom_call_target="tpu_custom_call" | custom-call | flops 200000000 | bytes 4000000 | tf_op jit(solution)/shard_map/pallas_call | solution.py:499
  73.0 18.8 %collective-permute-done.6.rest_1_.third_ref = bf16[1088,640]{1,0:T(8,128)(2,1)S(1)} collective-permute-done((bf16[1088,640]{1,0:T(8,128)(2,1)}, bf16[1088,640]{1,0:T(8,128)(2,1)S(1)}, u32[]{:S(2)}, u32[]{:S(2)}) %collective-permute-start.6) | collective-permute-done | bytes 1392672 | tf_op jit(solution)/shard_map/ppermute | solution.py:59
  91.8 0.5 shard_map.153
  92.3 1.9 %collective-permute-start.7 = (bf16[1056,640]{1,0:T(8,128)(2,1)S(1)}, bf16[1056,640]{1,0:T(8,128)(2,1)S(1)}, u32[]{:S(2)}, u32[]{:S(2)}) collective-permute-start(bf16[1056,640]{1,0:T(8,128)(2,1)S(1)} %shard_map.153), channel_id=1, source_target_pairs={{0,4},{4,0},{8,12},{12,8},{16,20},{20,16},{24,28},{28,24},{32,36},... | collective-permute-start | bytes 4055048 | tf_op jit(solution)/shard_map/ppermute | solution.py:64
  94.2 3.1 %collective-permute-done.7.part_ref = bf16[1056,640]{1,0:T(8,128)(2,1)S(1)} collective-permute-done((bf16[1056,640]{1,0:T(8,128)(2,1)S(1)}, bf16[1056,640]{1,0:T(8,128)(2,1)S(1)}, u32[]{:S(2)}, u32[]{:S(2)}) %collective-permute-start.7) | collective-permute-done | bytes 1351712 | tf_op jit(solution)/shard_map/ppermute | solution.py:64
  97.3 3.5 %shard_map.154 = (f32[128,640]{1,0:T(8,128)S(1)}, bf16[1792,640]{1,0:T(8,128)(2,1)S(1)}, bf16[1792,640]{1,0:T(8,128)(2,1)S(1)}) custom-call(s32[128]{0:T(128)S(1)} %copy-done.7, s32[128]{0:T(128)S(1)} %copy-done.9, s32[1]{0:T(128)} %bitcast.here_ref, f32[1,1280]{1,0:T(1,128)S(1)} %broadcast_in_dim.15.k_gain_ref, f32[896,128]{1,0:T(8,128)S(1)} %copy-done.2, ...), custom_call_target="tpu_custom_call" | custom-call | flops 300000000 | bytes 4000000 | tf_op jit(solution)/shard_map/pallas_call | solution.py:512
  100.8 2.0 %collective-permute-start.8 = (f32[128,640]{1,0:T(8,128)S(1)}, f32[128,640]{1,0:T(8,128)S(1)}, u32[]{:S(2)}, u32[]{:S(2)}) collective-permute-start(f32[128,640]{1,0:T(8,128)S(1)} %get-tuple-element.47), channel_id=1, source_target_pairs={{0,4},{4,0},{8,12},{12,8},{16,20},{20,16},{24,28},{28,24},{32,36},... | collective-permute-start | bytes 983048 | tf_op jit(solution)/shard_map/ppermute | solution.py:64
  102.8 2.5 %shard_map.155.own_ref = f32[128,640]{1,0:T(8,128)S(1)} custom-call(s32[128]{0:T(128)S(1)} %copy-done.7, s32[128]{0:T(128)S(1)} %copy-done.9, s32[1]{0:T(128)} %bitcast.here_ref, bf16[128,640]{1,0:T(8,128)(2,1)S(1)} %get-tuple-element.36.q_ref, bf16[1792,640]{1,0:T(8,128)(2,1)S(1)} %get-tuple-element.45.keys_ref, ...), custom_call_target="tpu_custom_call" | custom-call | flops 300000000 | bytes 4000000 | tf_op jit(solution)/shard_map/pallas_call | solution.py:522
  105.3 0.8 shard_map.156
  (42 shorter events, 0.2 us)
Async XLA Ops:
  2.5 17.3 %copy-start.4 = (bf16[672,640]{1,0:T(8,128)(2,1)S(1)}, bf16[672,640]{1,0:T(8,128)(2,1)}, u32[]{:S(2)}) copy-start(bf16[672,640]{1,0:T(8,128)(2,1)} %get-tuple-element.27.own_ref) | copy-start | bytes 2580484
  2.5 11.1 %collective-permute-start = (bf16[672,640]{1,0:T(8,128)(2,1)}, bf16[672,640]{1,0:T(8,128)(2,1)S(1)}, u32[]{:S(2)}, u32[]{:S(2)}) collective-permute-start(bf16[672,640]{1,0:T(8,128)(2,1)} %get-tuple-element.27.own_ref), channel_id=1, source_target_pairs={{0,4},{4,0},{8,12},{12,8},{16,20},{20,16},{24,28},{28,24},{32,36},... | collective-permute-start | bytes 2580488 | tf_op jit(solution)/shard_map/ppermute | solution.py:64
  13.7 0.7 copy-start.8
  14.3 6.3 %collective-permute-start.1 = (f32[8,128]{1,0:T(8,128)S(1)}, f32[8,128]{1,0:T(8,128)S(1)}, u32[]{:S(2)}, u32[]{:S(2)}) collective-permute-start(f32[8,128]{1,0:T(8,128)S(1)} %shard_map.147.own_ref), channel_id=1, source_target_pairs={{0,8},{4,508},{8,16},{12,4},{16,24},{20,12},{24,32},{28,20},{32,40... | collective-permute-start | bytes 12296 | tf_op jit(solution)/shard_map/ppermute | solution.py:59
  20.4 45.3 %copy-start.11 = (f32[1280]{0:T(1024)S(1)}, f32[1280]{0:T(1024)}, u32[]{:S(2)}) copy-start(f32[1280]{0:T(1024)} %param.21) | copy-start | bytes 15364
  20.4 45.3 %copy-start.12 = (f32[1280]{0:T(1024)S(1)}, f32[1280]{0:T(1024)}, u32[]{:S(2)}) copy-start(f32[1280]{0:T(1024)} %param.22) | copy-start | bytes 15364
  20.4 45.3 %copy-start.13 = (f32[1280]{0:T(1024)S(1)}, f32[1280]{0:T(1024)}, u32[]{:S(2)}) copy-start(f32[1280]{0:T(1024)} %param.23) | copy-start | bytes 15364
  20.5 45.3 %copy-start.14 = (f32[1280]{0:T(1024)S(1)}, f32[1280]{0:T(1024)}, u32[]{:S(2)}) copy-start(f32[1280]{0:T(1024)} %param.24) | copy-start | bytes 15364
  20.5 47.8 %copy-start = (bf16[256,1280]{1,0:T(8,128)(2,1)S(1)}, bf16[256,1280]{1,0:T(8,128)(2,1)}, u32[]{:S(2)}) copy-start(bf16[256,1280]{1,0:T(8,128)(2,1)} %k_ref.1) | copy-start | bytes 1966084
  20.5 47.8 %copy-start.3 = (bf16[128,1280]{1,0:T(8,128)(2,1)S(1)}, bf16[128,1280]{1,0:T(8,128)(2,1)}, u32[]{:S(2)}) copy-start(bf16[128,1280]{1,0:T(8,128)(2,1)} %q_ref.1) | copy-start | bytes 983044
  20.5 47.8 %copy-start.7 = (s32[128]{0:T(128)S(1)}, s32[128]{0:T(128)}, u32[]{:S(2)}) copy-start(s32[128]{0:T(128)} %item_ref.7) | copy-start | bytes 1540
  20.5 47.8 %copy-start.10 = (s32[128]{0:T(128)S(1)}, s32[128]{0:T(128)}, u32[]{:S(2)}) copy-start(s32[128]{0:T(128)} %len_ref.1) | copy-start | bytes 1540
  20.6 38.6 %collective-permute-start.2 = (bf16[1088,640]{1,0:T(8,128)(2,1)S(1)}, bf16[1088,640]{1,0:T(8,128)(2,1)}, u32[]{:S(2)}, u32[]{:S(2)}) collective-permute-start(bf16[1088,640]{1,0:T(8,128)(2,1)S(1)} %shard_map.146.block_ref), channel_id=1, source_target_pairs={{0,8},{4,508},{8,16},{12,4},{16,24},{20,12},{24,32},{28,20},{32,40... | collective-permute-start | bytes 4177928 | tf_op jit(solution)/shard_map/ppermute | solution.py:59
  59.2 9.1 %copy-start.5 = (bf16[256,1280]{1,0:T(8,128)(2,1)S(1)}, bf16[256,1280]{1,0:T(8,128)(2,1)}, u32[]{:S(2)}) copy-start(bf16[256,1280]{1,0:T(8,128)(2,1)} %v_ref.1) | copy-start | bytes 1966084
  59.8 31.9 %collective-permute-start.6 = (bf16[1088,640]{1,0:T(8,128)(2,1)}, bf16[1088,640]{1,0:T(8,128)(2,1)S(1)}, u32[]{:S(2)}, u32[]{:S(2)}) collective-permute-start(bf16[1088,640]{1,0:T(8,128)(2,1)} %constant_dynamic-update-slice_fusion.rest_0_.kept_ref), channel_id=1, source_target_pairs={{0,480},{4,36},{12,44},{20,52},{28,60},{32,0},{36,68},{40,8},{44,7... | collective-permute-start | bytes 4177928 | tf_op jit(solution)/shard_map/ppermute | solution.py:59
  61.2 30.6 %collective-permute-start.5 = (bf16[1088,640]{1,0:T(8,128)(2,1)}, bf16[1088,640]{1,0:T(8,128)(2,1)S(1)}, u32[]{:S(2)}, u32[]{:S(2)}) collective-permute-start(bf16[1088,640]{1,0:T(8,128)(2,1)} %constant_dynamic-update-slice_fusion.rest_0_.kept_ref), channel_id=1, source_target_pairs={{0,8},{8,16},{12,4},{16,24},{20,12},{24,32},{28,20},{32,40},{36,28... | collective-permute-start | bytes 4177928 | tf_op jit(solution)/shard_map/ppermute | solution.py:59
  63.6 6.3 %copy-start.1 = (f32[896,128]{1,0:T(8,128)S(1)}, f32[896,128]{1,0:T(8,128)}, u32[]{:S(2)}) copy-start(f32[896,128]{1,0:T(8,128)} %constant.15.clone.sin_ref) | copy-start | bytes 1376260
  63.6 6.3 %copy-start.2 = (f32[896,128]{1,0:T(8,128)S(1)}, f32[896,128]{1,0:T(8,128)}, u32[]{:S(2)}) copy-start(f32[896,128]{1,0:T(8,128)} %constant.14.clone.cos_ref) | copy-start | bytes 1376260
  63.7 6.3 %copy-start.6 = (bf16[128,640]{1,0:T(8,128)(2,1)S(1)}, bf16[128,640]{1,0:T(8,128)(2,1)}, u32[]{:S(2)}) copy-start(bf16[128,640]{1,0:T(8,128)(2,1)} %get-tuple-element.34.q_own_ref) | copy-start | bytes 491524
  63.7 6.2 %collective-permute-start.4 = (bf16[528,640]{1,0:T(8,128)(2,1)S(1)}, bf16[528,640]{1,0:T(8,128)(2,1)S(1)}, u32[]{:S(2)}, u32[]{:S(2)}) collective-permute-start(bf16[528,640]{1,0:T(8,128)(2,1)S(1)} %shard_map.151), channel_id=1, source_target_pairs={{0,4},{4,0},{8,12},{12,8},{16,20},{20,16},{24,28},{28,24},{32,36},... | collective-permute-start | bytes 2027528 | tf_op jit(solution)/shard_map/ppermute | solution.py:64
  65.8 4.1 %collective-permute-start.3 = (f32[16,128]{1,0:T(8,128)S(1)}, f32[16,128]{1,0:T(8,128)S(1)}, u32[]{:S(2)}, u32[]{:S(2)}) collective-permute-start(f32[16,128]{1,0:T(8,128)S(1)} %psum.7.sums_ref), channel_id=1, source_target_pairs={{0,4},{4,0},{8,12},{12,8},{16,20},{20,16},{24,28},{28,24},{32,36},... | collective-permute-start | bytes 24584 | tf_op jit(solution)/shard_map/ppermute | solution.py:64
  91.8 5.5 %copy-start.9 = (s32[128]{0:T(128)S(1)}, s32[128]{0:T(128)}, u32[]{:S(2)}) copy-start(s32[128]{0:T(128)} %count_ref.3) | copy-start | bytes 1540
  92.3 5.0 %collective-permute-start.7 = (bf16[1056,640]{1,0:T(8,128)(2,1)S(1)}, bf16[1056,640]{1,0:T(8,128)(2,1)S(1)}, u32[]{:S(2)}, u32[]{:S(2)}) collective-permute-start(bf16[1056,640]{1,0:T(8,128)(2,1)S(1)} %shard_map.153), channel_id=1, source_target_pairs={{0,4},{4,0},{8,12},{12,8},{16,20},{20,16},{24,28},{28,24},{32,36},... | collective-permute-start | bytes 4055048 | tf_op jit(solution)/shard_map/ppermute | solution.py:64
  100.8 4.5 %collective-permute-start.8 = (f32[128,640]{1,0:T(8,128)S(1)}, f32[128,640]{1,0:T(8,128)S(1)}, u32[]{:S(2)}, u32[]{:S(2)}) collective-permute-start(f32[128,640]{1,0:T(8,128)S(1)} %get-tuple-element.47), channel_id=1, source_target_pairs={{0,4},{4,0},{8,12},{12,8},{16,20},{20,16},{24,28},{28,24},{32,36},... | collective-permute-start | bytes 983048 | tf_op jit(solution)/shard_map/ppermute | solution.py:64

commit v11 on v9

--- a/solution.py
+++ b/solution.py
@@ -16,7 +16,7 @@
 SPAN = 7
 ROWS = 128
 EPSILON = 1e-06
-SCALE = 1.0 / math.sqrt(HD)
+SCALE = math.log2(math.e) / math.sqrt(HD)
 NEG = -1e30
 OWN_LINES, SIDE_LINES, QUERY_LINES = (0, 5), (7, 8), (1, 6)
 SPARE = 16
@@ -49,14 +49,11 @@
     return cosine, sine.reshape(SPAN * ROWS, HD).astype(np.float32)
 
 
-def shifted(value, by, wrapped=()):
+def shifted(value, by, extra=()):
     peers = lax.axis_size("tile")
-    pairs = []
-    for i in range(peers):
-        goal = i - by if i % 2 else i + by
-        if 0 <= goal < peers or i in wrapped:
-            pairs.append((i, goal % peers))
-    return lax.ppermute(value, "tile", pairs)
+    pairs = [(i, i - by if i % 2 else i + by) for i in range(peers)]
+    pairs = [pair for pair in pairs if 0 <= pair[1] < peers]
+    return lax.ppermute(value, "tile", pairs + list(extra))
 
 
 def swapped(value):
@@ -198,8 +195,8 @@
         ]
         k = jnp.concatenate(keys, axis=0)
         s = lax.dot_general(q, k, (((1,), (1,)), ((), ())), preferred_element_type=jnp.float32)
-        s = jnp.where(live, s * SCALE, NEG)
-        w = jnp.exp(s - jnp.max(s, axis=1, keepdims=True))
+        s = jnp.where(live, s, NEG)
+        w = jnp.exp2((s - jnp.max(s, axis=1, keepdims=True)) * SCALE)
         total = jnp.sum(w, axis=1, keepdims=True)
         o = jnp.dot(w.astype(jnp.bfloat16), v_ref[:, cols], preferred_element_type=jnp.float32)
         out_ref[:, cols] = o / total
@@ -246,17 +243,17 @@
             turn(block, key_rows, by_rows(total), gains, *tables, start, keys_ref, goal)
 
 
-def kept_rows(core):
+def kept_rows(core, turned=0):
     def rows_of(parity):
-        slot = jnp.where(core == parity, 0, 1)
+        slot = jnp.where(core == parity, turned, 1 - turned)
         return slot, (2 * slot + core) * HALF_ROWS
 
     return rows_of
 
 
-def part_rows(core, index):
+def part_rows(core, index, turned=0):
     def rows_of(parity):
-        slot = jnp.where(core == parity, 1, 0)
+        slot = jnp.where(core == parity, 1 - turned, turned)
         return slot, index * PART_ROWS + slot * 2 * ROWS
 
     return rows_of
@@ -327,12 +324,12 @@
             preferred_element_type=jnp.float32,
         )
         parts = [
-            jnp.where(live[slot], s[:, slot * ROWS : (slot + 1) * ROWS] * SCALE, NEG)
+            jnp.where(live[slot], s[:, slot * ROWS : (slot + 1) * ROWS], NEG)
             for slot in range(SPAN)
         ]
         top = functools.reduce(jnp.maximum, parts)
         top = jnp.max(top, axis=1, keepdims=True)
-        parts = [jnp.exp(part - top) for part in parts]
+        parts = [jnp.exp2((part - top) * SCALE) for part in parts]
         total = jnp.sum(functools.reduce(jnp.add, parts), axis=1, keepdims=True)
         weights = jnp.concatenate([part.astype(jnp.bfloat16) for part in parts], axis=1)
         mixed = jnp.dot(weights, values_ref[window, cols], preferred_element_type=jnp.float32)
@@ -349,14 +346,16 @@
     half = keys_ref.shape[1]
     bounds = (*extent(item_ref, left), *extent(item_ref, left + 1))
     k_gains = k_gain_ref.at[:, pl.ds(pl.multiple_of(core * half, HD), half)]
+    low_end = jnp.where(left == 6, 1, 0)
+    high_end = jnp.where(left == item_ref.shape[0] - 8, 1, 0)
     near = slice(4 * ROWS, 10 * ROWS)
     keys_ref[near, :] = near_keys_ref[...]
     values_ref[near, :] = near_values_ref[...]
     for chip, rows_of, totals, block in (
         (2 * sign, kept_rows(core), spares(second_ref, 2 * ROWS), second_ref),
-        (-3 * sign, kept_rows(core), spares(third_ref, 2 * ROWS), third_ref),
+        (-3 * sign, kept_rows(core, jnp.where(sign > 0, low_end, high_end)), spares(third_ref, 2 * ROWS), third_ref),
         (-2 * sign, part_rows(core, 0), spares(part_ref, 4 * ROWS), part_ref),
-        (3 * sign, part_rows(core, 1), spares(part_ref, PART_ROWS + 4 * ROWS), part_ref),
+        (3 * sign, part_rows(core, 1, jnp.where(sign > 0, high_end, low_end)), spares(part_ref, PART_ROWS + 4 * ROWS), part_ref),
     ):
         gather(
             chip, rows_of, totals, block, core, left, bounds, k_gains, (cos_ref, sin_ref), keys_ref, values_ref, -3
@@ -429,19 +428,18 @@
     )(where, self_query, self_key, self_value, cross_query, text_key)
     got = swapped(theirs)
     peers = lax.axis_size("tile")
-    ends = (peers - 2, 1)
     sums = call(mate_kernel, jax.ShapeDtypeStruct((8, ROWS), f32), [vmem] * 2)(sums, got)
-    side_sums = shifted(sums, 2, ends)
+    side_sums = shifted(sums, 2)
     block = jnp.concatenate([theirs[: 2 * HALF_ROWS], got[: 2 * HALF_ROWS]], axis=0)
     block, side_sums = lax.optimization_barrier((block, side_sums))
-    side = shifted(block, 2, ends)
+    side = shifted(block, 2)
     sums = call(table_kernel, jax.ShapeDtypeStruct((16, ROWS), f32), [vmem] * 2)(sums, side_sums)
     sums = lax.psum(sums, "head")
     side, sums = lax.optimization_barrier((side, sums))
     marks = call(pieces_kernel, jax.ShapeDtypeStruct((SPARE, half), bf16), [vmem])(sums)
     side = lax.dynamic_update_slice(side, marks, (2 * ROWS, 0))
     second = shifted(side, 2)
-    third = shifted(side, -8, (0, peers - 1))
+    third = shifted(side, -8, ((2, 7), (peers - 3, peers - 8)))
 
     def parts(*blocks):
         return swapped(

time: 105 us -> 101 us (0.962)
  waiting for transfers between devices: 32.6 us -> 25.2 us
  starting transfers between devices: 35.4 us -> 38.7 us
    ppermute x4, waiting for transfers between devices: 28.9 us -> 21.5 us  [shifted(): return lax.ppermute(value, 'tile', pairs + list(extra))]
    ppermute x5, starting transfers between devices: 27.2 us -> 30.5 us  [swapped(): return lax.ppermute(value, 'tile', [(i, i ^ 1) for i in range(peers)])]
  transfers between devices with their start and end apart: 9 -> 9, of which waited for: 5 -> 5; matrix products, arithmetic and copies ran while one was open for 2% -> 2% of each run, Pallas kernels for 7% -> 8%
where the time goes in v11:
time: 101 us
  starting transfers between devices  38.7 us (38%)
  waiting for transfers between devices  25.2 us (25%)
  blocking collectives  19.6 us (19%)
  Pallas kernels  14.7 us (15%)
  local copies, waits for them, and re-layouts  1.33 us (1%)
  other arithmetic  1.22 us (1%)
    ppermute x5, starting transfers between devices, swapped(): return lax.ppermute(value, 'tile', [(i, i ^ 1) for i in range(peers)])  30.5 us
    ppermute x4, waiting for transfers between devices, shifted(): return lax.ppermute(value, 'tile', pairs + list(extra))  21.5 us
    psum x1, blocking collectives, per_device(): sums = lax.psum(sums, 'head')  19.6 us
    ppermute x4, starting transfers between devices, shifted(): return lax.ppermute(value, 'tile', pairs + list(extra))  8.19 us
    ppermute x5, waiting for transfers between devices, swapped(): return lax.ppermute(value, 'tile', [(i, i ^ 1) for i in range(peers)])  3.75 us
    pallas_call x1, Pallas kernels, per_device(): call(near_kernel, (jax.ShapeDtypeStruct((6 * ROWS, half), bf16),) * 2 + (...  3.39 us
    pallas_call x1, Pallas kernels, per_device(): call(far_kernel, (jax.ShapeDtypeStruct((ROWS, half), f32), window, window...  3.16 us
    pallas_call x1, Pallas kernels, per_device(): call(pack_kernel, (jax.ShapeDtypeStruct((2 * HALF_ROWS + ROWS, half), bf1...  2.51 us
  transfers between devices with their start and end apart: 9, of which 5 were waited for; matrix products, arithmetic and copies ran while one was open for 2% of the time, Pallas kernels for 8%

profile of v11, /device:TPU:31, one launch (start us, length us, event | category | flops | bytes accessed | tf_op | source)
XLA Modules:
  0.0 101.2 jit_solution(9653267993855039608)
XLA Ops:
  0.0 2.5 %shard_map.145 = (bf16[672,640]{1,0:T(8,128)(2,1)}, bf16[128,640]{1,0:T(8,128)(2,1)}, f32[8,128]{1,0:T(8,128)}) custom-call(s32[1]{0:T(128)} %bitcast.here_ref, bf16[128,1280]{1,0:T(8,128)(2,1)} %q_hbm.1, bf16[128,1280]{1,0:T(8,128)(2,1)} %k_hbm.1, bf16[128,1280]{1,0:T(8,128)(2,1)} %v_hbm.1, bf16[128,1280]{1,0:T(8,128)(2,1)} %q_ref.1, bf16[256,1280]{1,0:T(8,128)(2,1)} %k_ref.1), custom_call_target="tpu_custom_call" | custom-call | flops 1000000 | bytes 4000000 | tf_op jit(solution)/shard_map/pallas_call | solution.py:417
  2.5 2.6 %collective-permute-start = (bf16[672,640]{1,0:T(8,128)(2,1)}, bf16[672,640]{1,0:T(8,128)(2,1)S(1)}, u32[]{:S(2)}, u32[]{:S(2)}) collective-permute-start(bf16[672,640]{1,0:T(8,128)(2,1)} %get-tuple-element.27), channel_id=1, source_target_pairs={{0,4},{4,0},{8,12},{12,8},{16,20},{20,16},{24,28},{28,24},{32,36},... | collective-permute-start | bytes 2580488 | tf_op jit(solution)/shard_map/ppermute | solution.py:61
  5.1 1.2 %slice.6 = bf16[544,640]{1,0:T(8,128)(2,1)S(1)} slice(bf16[672,640]{1,0:T(8,128)(2,1)} %get-tuple-element.27), slice={[0:544], [0:640]} | slice | bytes 1392640 | tf_op jit(solution)/shard_map/slice | solution.py:433
  6.3 1.0 %collective-permute-done.got_ref = bf16[672,640]{1,0:T(8,128)(2,1)S(1)} collective-permute-done((bf16[672,640]{1,0:T(8,128)(2,1)}, bf16[672,640]{1,0:T(8,128)(2,1)S(1)}, u32[]{:S(2)}, u32[]{:S(2)}) %collective-permute-start) | collective-permute-done | bytes 860192 | tf_op jit(solution)/shard_map/ppermute | solution.py:61
  7.3 2.4 %collective-permute-start.1 = (f32[8,128]{1,0:T(8,128)S(1)}, f32[8,128]{1,0:T(8,128)S(1)}, u32[]{:S(2)}, u32[]{:S(2)}) collective-permute-start(f32[8,128]{1,0:T(8,128)S(1)} %shard_map.146.own_ref), channel_id=1, source_target_pairs={{0,8},{8,16},{12,4},{16,24},{20,12},{24,32},{28,20},{32,40},{36,28... | collective-permute-start | bytes 12296 | tf_op jit(solution)/shard_map/ppermute | solution.py:56
  9.9 1.2 %pad_maximum_fusion.block_ref = bf16[1088,640]{1,0:T(8,128)(2,1)} fusion(bf16[544,640]{1,0:T(8,128)(2,1)S(1)} %slice.8, bf16[544,640]{1,0:T(8,128)(2,1)S(1)} %slice.6), kind=kLoop, calls=%fused_computation | loop fusion | flops 2785280 | bytes 2785280 | tf_op jit(solution)/shard_map/concatenate | solution.py:433
  11.1 4.8 %collective-permute-done.1.side_ref = f32[8,128]{1,0:T(8,128)S(1)} collective-permute-done((f32[8,128]{1,0:T(8,128)S(1)}, f32[8,128]{1,0:T(8,128)S(1)}, u32[]{:S(2)}, u32[]{:S(2)}) %collective-permute-start.1) | collective-permute-done | bytes 4128 | tf_op jit(solution)/shard_map/ppermute | solution.py:56
  15.9 1.9 %collective-permute-start.2 = (bf16[1088,640]{1,0:T(8,128)(2,1)}, bf16[1088,640]{1,0:T(8,128)(2,1)S(1)}, u32[]{:S(2)}, u32[]{:S(2)}) collective-permute-start(bf16[1088,640]{1,0:T(8,128)(2,1)} %pad_maximum_fusion.block_ref), channel_id=1, source_target_pairs={{0,8},{8,16},{12,4},{16,24},{20,12},{24,32},{28,20},{32,40},{36,28... | collective-permute-start | bytes 4177928 | tf_op jit(solution)/shard_map/ppermute | solution.py:56
  17.8 19.6 %psum.7.sums_ref = f32[16,128]{1,0:T(8,128)S(1)} all-reduce(f32[16,128]{1,0:T(8,128)S(1)} %shard_map.147), channel_id=1, replica_groups=mesh['tile'=128,'head'=4] {'head'}, use_global_device_ids=true, to_apply=%region_0.0 | all-reduce | flops 2048 | bytes 16384 | tf_op jit(solution)/shard_map/psum | solution.py:437
  37.4 2.5 %collective-permute-done.2 = bf16[1088,640]{1,0:T(8,128)(2,1)S(1)} collective-permute-done((bf16[1088,640]{1,0:T(8,128)(2,1)}, bf16[1088,640]{1,0:T(8,128)(2,1)S(1)}, u32[]{:S(2)}, u32[]{:S(2)}) %collective-permute-start.2) | collective-permute-done | bytes 1392672 | tf_op jit(solution)/shard_map/ppermute | solution.py:56
  40.0 1.9 %collective-permute-start.6 = (bf16[1088,640]{1,0:T(8,128)(2,1)S(1)}, bf16[1088,640]{1,0:T(8,128)(2,1)S(1)}, u32[]{:S(2)}, u32[]{:S(2)}) collective-permute-start(bf16[1088,640]{1,0:T(8,128)(2,1)S(1)} %constant_dynamic-update-slice_fusion.rest_0_.kept_ref), channel_id=1, source_target_pairs={{4,36},{12,44},{20,52},{28,60},{32,0},{36,68},{40,8},{44,76},{48,1... | collective-permute-start | bytes 4177928 | tf_op jit(solution)/shard_map/ppermute | solution.py:56
  41.9 1.9 %collective-permute-start.5 = (bf16[1088,640]{1,0:T(8,128)(2,1)S(1)}, bf16[1088,640]{1,0:T(8,128)(2,1)S(1)}, u32[]{:S(2)}, u32[]{:S(2)}) collective-permute-start(bf16[1088,640]{1,0:T(8,128)(2,1)S(1)} %constant_dynamic-update-slice_fusion.rest_0_.kept_ref), channel_id=1, source_target_pairs={{0,8},{8,16},{12,4},{16,24},{20,12},{24,32},{28,20},{32,40},{36,28... | collective-permute-start | bytes 4177928 | tf_op jit(solution)/shard_map/ppermute | solution.py:56
  44.2 15.9 %collective-permute-start.4 = (bf16[528,640]{1,0:T(8,128)(2,1)S(1)}, bf16[528,640]{1,0:T(8,128)(2,1)S(1)}, u32[]{:S(2)}, u32[]{:S(2)}) collective-permute-start(bf16[528,640]{1,0:T(8,128)(2,1)S(1)} %shard_map.150), channel_id=1, source_target_pairs={{0,4},{4,0},{8,12},{12,8},{16,20},{20,16},{24,28},{28,24},{32,36},... | collective-permute-start | bytes 2027528 | tf_op jit(solution)/shard_map/ppermute | solution.py:61
  60.2 1.9 %collective-permute-start.3 = (f32[16,128]{1,0:T(8,128)S(1)}, f32[16,128]{1,0:T(8,128)S(1)}, u32[]{:S(2)}, u32[]{:S(2)}) collective-permute-start(f32[16,128]{1,0:T(8,128)S(1)} %psum.7.sums_ref), channel_id=1, source_target_pairs={{0,4},{4,0},{8,12},{12,8},{16,20},{20,16},{24,28},{28,24},{32,36},... | collective-permute-start | bytes 24584 | tf_op jit(solution)/shard_map/ppermute | solution.py:61
  62.2 1.6 %shard_map.148.text_ref = f32[128,1280]{1,0:T(8,128)S(1)} custom-call(s32[128]{0:T(128)S(1)} %copy-done.6, s32[128]{0:T(128)S(1)} %copy-done.9, s32[1]{0:T(128)} %bitcast.here_ref, f32[16,128]{1,0:T(8,128)S(1)} %psum.7.sums_ref, bf16[128,1280]{1,0:T(8,128)(2,1)S(1)} %copy-done.3, bf16[256,1280]{1,0:T(8,128)(2,1)S(1)} %copy-done, ...), custom_call_target="tpu_custom_call" | custom-call | flops 400000000 | bytes 4000000 | tf_op jit(solution)/shard_map/pallas_call | solution.py:457
  63.8 3.4 %shard_map.151 = (bf16[768,640]{1,0:T(8,128)(2,1)S(1)}, bf16[768,640]{1,0:T(8,128)(2,1)S(1)}, bf16[128,640]{1,0:T(8,128)(2,1)S(1)}, bf16[128,640]{1,0:T(8,128)(2,1)S(1)}) custom-call(s32[128]{0:T(128)S(1)} %copy-done.6, s32[1]{0:T(128)} %bitcast.here_ref, f32[16,128]{1,0:T(8,128)S(1)} %psum.7.sums_ref, f32[16,128]{1,0:T(8,128)S(1)} %collective-permute-done.3.mate_sums_ref, ...), custom_call_target="tpu_custom_call" | custom-call | flops 200000000 | bytes 4000000 | tf_op jit(solution)/shard_map/pallas_call | solution.py:474
  67.2 14.2 %collective-permute-done.5.rest_0_.second_ref = bf16[1088,640]{1,0:T(8,128)(2,1)S(1)} collective-permute-done((bf16[1088,640]{1,0:T(8,128)(2,1)S(1)}, bf16[1088,640]{1,0:T(8,128)(2,1)S(1)}, u32[]{:S(2)}, u32[]{:S(2)}) %collective-permute-start.5) | collective-permute-done | bytes 1392672 | tf_op jit(solution)/shard_map/ppermute | solution.py:56
  81.3 0.5 shard_map.152
  81.9 7.9 %collective-permute-start.7 = (bf16[1056,640]{1,0:T(8,128)(2,1)S(1)}, bf16[1056,640]{1,0:T(8,128)(2,1)S(1)}, u32[]{:S(2)}, u32[]{:S(2)}) collective-permute-start(bf16[1056,640]{1,0:T(8,128)(2,1)S(1)} %shard_map.152), channel_id=1, source_target_pairs={{0,4},{4,0},{8,12},{12,8},{16,20},{20,16},{24,28},{28,24},{32,36},... | collective-permute-start | bytes 4055048 | tf_op jit(solution)/shard_map/ppermute | solution.py:61
  89.7 2.7 %collective-permute-done.7.part_ref = bf16[1056,640]{1,0:T(8,128)(2,1)S(1)} collective-permute-done((bf16[1056,640]{1,0:T(8,128)(2,1)S(1)}, bf16[1056,640]{1,0:T(8,128)(2,1)S(1)}, u32[]{:S(2)}, u32[]{:S(2)}) %collective-permute-start.7) | collective-permute-done | bytes 1351712 | tf_op jit(solution)/shard_map/ppermute | solution.py:61
  92.4 3.2 %shard_map.153 = (f32[128,640]{1,0:T(8,128)S(1)}, bf16[1792,640]{1,0:T(8,128)(2,1)S(1)}, bf16[1792,640]{1,0:T(8,128)(2,1)S(1)}) custom-call(s32[128]{0:T(128)S(1)} %copy-done.6, s32[128]{0:T(128)S(1)} %copy-done.8, s32[1]{0:T(128)} %bitcast.here_ref, f32[1,1280]{1,0:T(1,128)S(1)} %broadcast_in_dim.15.k_gain_ref, f32[896,128]{1,0:T(8,128)S(1)} %copy-done.2, ...), custom_call_target="tpu_custom_call" | custom-call | flops 300000000 | bytes 4000000 | tf_op jit(solution)/shard_map/pallas_call | solution.py:487
  95.6 2.3 %collective-permute-start.8 = (f32[128,640]{1,0:T(8,128)S(1)}, f32[128,640]{1,0:T(8,128)S(1)}, u32[]{:S(2)}, u32[]{:S(2)}) collective-permute-start(f32[128,640]{1,0:T(8,128)S(1)} %get-tuple-element.47), channel_id=1, source_target_pairs={{0,4},{4,0},{8,12},{12,8},{16,20},{20,16},{24,28},{28,24},{32,36},... | collective-permute-start | bytes 983048 | tf_op jit(solution)/shard_map/ppermute | solution.py:61
  97.9 2.5 %shard_map.154.own_ref = f32[128,640]{1,0:T(8,128)S(1)} custom-call(s32[128]{0:T(128)S(1)} %copy-done.6, s32[128]{0:T(128)S(1)} %copy-done.8, s32[1]{0:T(128)} %bitcast.here_ref, bf16[128,640]{1,0:T(8,128)(2,1)S(1)} %get-tuple-element.36.q_ref, bf16[1792,640]{1,0:T(8,128)(2,1)S(1)} %get-tuple-element.45.keys_ref, ...), custom_call_target="tpu_custom_call" | custom-call | flops 300000000 | bytes 4000000 | tf_op jit(solution)/shard_map/pallas_call | solution.py:496
  100.4 0.8 shard_map.155
  (42 shorter events, 0.5 us)
Async XLA Ops:
  2.5 4.8 %copy-start.7 = (f32[8,128]{1,0:T(8,128)S(1)}, f32[8,128]{1,0:T(8,128)}, u32[]{:S(2)}) copy-start(f32[8,128]{1,0:T(8,128)} %get-tuple-element.28.own_ref) | copy-start | bytes 12292
  2.5 4.8 %collective-permute-start = (bf16[672,640]{1,0:T(8,128)(2,1)}, bf16[672,640]{1,0:T(8,128)(2,1)S(1)}, u32[]{:S(2)}, u32[]{:S(2)}) collective-permute-start(bf16[672,640]{1,0:T(8,128)(2,1)} %get-tuple-element.27), channel_id=1, source_target_pairs={{0,4},{4,0},{8,12},{12,8},{16,20},{20,16},{24,28},{28,24},{32,36},... | collective-permute-start | bytes 2580488 | tf_op jit(solution)/shard_map/ppermute | solution.py:61
  7.3 8.6 %collective-permute-start.1 = (f32[8,128]{1,0:T(8,128)S(1)}, f32[8,128]{1,0:T(8,128)S(1)}, u32[]{:S(2)}, u32[]{:S(2)}) collective-permute-start(f32[8,128]{1,0:T(8,128)S(1)} %shard_map.146.own_ref), channel_id=1, source_target_pairs={{0,8},{8,16},{12,4},{16,24},{20,12},{24,32},{28,20},{32,40},{36,28... | collective-permute-start | bytes 12296 | tf_op jit(solution)/shard_map/ppermute | solution.py:56
  11.1 49.0 %copy-start.10 = (f32[1280]{0:T(1024)S(1)}, f32[1280]{0:T(1024)}, u32[]{:S(2)}) copy-start(f32[1280]{0:T(1024)} %param.21) | copy-start | bytes 15364
  11.1 49.0 %copy-start.11 = (f32[1280]{0:T(1024)S(1)}, f32[1280]{0:T(1024)}, u32[]{:S(2)}) copy-start(f32[1280]{0:T(1024)} %param.22) | copy-start | bytes 15364
  11.1 49.1 %copy-start.12 = (f32[1280]{0:T(1024)S(1)}, f32[1280]{0:T(1024)}, u32[]{:S(2)}) copy-start(f32[1280]{0:T(1024)} %param.23) | copy-start | bytes 15364
  11.1 49.1 %copy-start.13 = (f32[1280]{0:T(1024)S(1)}, f32[1280]{0:T(1024)}, u32[]{:S(2)}) copy-start(f32[1280]{0:T(1024)} %param.24) | copy-start | bytes 15364
  11.1 51.0 %copy-start = (bf16[256,1280]{1,0:T(8,128)(2,1)S(1)}, bf16[256,1280]{1,0:T(8,128)(2,1)}, u32[]{:S(2)}) copy-start(bf16[256,1280]{1,0:T(8,128)(2,1)} %k_ref.1) | copy-start | bytes 1966084
  11.1 51.0 %copy-start.3 = (bf16[128,1280]{1,0:T(8,128)(2,1)S(1)}, bf16[128,1280]{1,0:T(8,128)(2,1)}, u32[]{:S(2)}) copy-start(bf16[128,1280]{1,0:T(8,128)(2,1)} %q_ref.1) | copy-start | bytes 983044
  11.1 51.0 %copy-start.6 = (s32[128]{0:T(128)S(1)}, s32[128]{0:T(128)}, u32[]{:S(2)}) copy-start(s32[128]{0:T(128)} %item_ref.7) | copy-start | bytes 1540
  11.1 51.0 %copy-start.9 = (s32[128]{0:T(128)S(1)}, s32[128]{0:T(128)}, u32[]{:S(2)}) copy-start(s32[128]{0:T(128)} %len_ref.1) | copy-start | bytes 1540
  15.9 24.1 %collective-permute-start.2 = (bf16[1088,640]{1,0:T(8,128)(2,1)}, bf16[1088,640]{1,0:T(8,128)(2,1)S(1)}, u32[]{:S(2)}, u32[]{:S(2)}) collective-permute-start(bf16[1088,640]{1,0:T(8,128)(2,1)} %pad_maximum_fusion.block_ref), channel_id=1, source_target_pairs={{0,8},{8,16},{12,4},{16,24},{20,12},{24,32},{28,20},{32,40},{36,28... | collective-permute-start | bytes 4177928 | tf_op jit(solution)/shard_map/ppermute | solution.py:56
  37.4 24.7 %copy-start.4 = (bf16[256,1280]{1,0:T(8,128)(2,1)S(1)}, bf16[256,1280]{1,0:T(8,128)(2,1)}, u32[]{:S(2)}) copy-start(bf16[256,1280]{1,0:T(8,128)(2,1)} %v_ref.1) | copy-start | bytes 1966084
  40.0 27.2 %collective-permute-start.6 = (bf16[1088,640]{1,0:T(8,128)(2,1)S(1)}, bf16[1088,640]{1,0:T(8,128)(2,1)S(1)}, u32[]{:S(2)}, u32[]{:S(2)}) collective-permute-start(bf16[1088,640]{1,0:T(8,128)(2,1)S(1)} %constant_dynamic-update-slice_fusion.rest_0_.kept_ref), channel_id=1, source_target_pairs={{4,36},{12,44},{20,52},{28,60},{32,0},{36,68},{40,8},{44,76},{48,1... | collective-permute-start | bytes 4177928 | tf_op jit(solution)/shard_map/ppermute | solution.py:56
  41.9 39.4 %collective-permute-start.5 = (bf16[1088,640]{1,0:T(8,128)(2,1)S(1)}, bf16[1088,640]{1,0:T(8,128)(2,1)S(1)}, u32[]{:S(2)}, u32[]{:S(2)}) collective-permute-start(bf16[1088,640]{1,0:T(8,128)(2,1)S(1)} %constant_dynamic-update-slice_fusion.rest_0_.kept_ref), channel_id=1, source_target_pairs={{0,8},{8,16},{12,4},{16,24},{20,12},{24,32},{28,20},{32,40},{36,28... | collective-permute-start | bytes 4177928 | tf_op jit(solution)/shard_map/ppermute | solution.py:56
  44.2 19.6 %copy-start.1 = (f32[896,128]{1,0:T(8,128)S(1)}, f32[896,128]{1,0:T(8,128)}, u32[]{:S(2)}) copy-start(f32[896,128]{1,0:T(8,128)} %constant.15.clone.sin_ref) | copy-start | bytes 1376260
  44.2 19.6 %copy-start.2 = (f32[896,128]{1,0:T(8,128)S(1)}, f32[896,128]{1,0:T(8,128)}, u32[]{:S(2)}) copy-start(f32[896,128]{1,0:T(8,128)} %constant.14.clone.cos_ref) | copy-start | bytes 1376260
  44.2 19.6 %copy-start.5 = (bf16[128,640]{1,0:T(8,128)(2,1)S(1)}, bf16[128,640]{1,0:T(8,128)(2,1)}, u32[]{:S(2)}) copy-start(bf16[128,640]{1,0:T(8,128)(2,1)} %get-tuple-element.34.q_own_ref) | copy-start | bytes 491524
  44.2 19.6 %collective-permute-start.4 = (bf16[528,640]{1,0:T(8,128)(2,1)S(1)}, bf16[528,640]{1,0:T(8,128)(2,1)S(1)}, u32[]{:S(2)}, u32[]{:S(2)}) collective-permute-start(bf16[528,640]{1,0:T(8,128)(2,1)S(1)} %shard_map.150), channel_id=1, source_target_pairs={{0,4},{4,0},{8,12},{12,8},{16,20},{20,16},{24,28},{28,24},{32,36},... | collective-permute-start | bytes 2027528 | tf_op jit(solution)/shard_map/ppermute | solution.py:61
  60.2 3.5 %collective-permute-start.3 = (f32[16,128]{1,0:T(8,128)S(1)}, f32[16,128]{1,0:T(8,128)S(1)}, u32[]{:S(2)}, u32[]{:S(2)}) collective-permute-start(f32[16,128]{1,0:T(8,128)S(1)} %psum.7.sums_ref), channel_id=1, source_target_pairs={{0,4},{4,0},{8,12},{12,8},{16,20},{20,16},{24,28},{28,24},{32,36},... | collective-permute-start | bytes 24584 | tf_op jit(solution)/shard_map/ppermute | solution.py:61
  81.3 11.1 %copy-start.8 = (s32[128]{0:T(128)S(1)}, s32[128]{0:T(128)}, u32[]{:S(2)}) copy-start(s32[128]{0:T(128)} %count_ref.3) | copy-start | bytes 1540
  81.9 10.6 %collective-permute-start.7 = (bf16[1056,640]{1,0:T(8,128)(2,1)S(1)}, bf16[1056,640]{1,0:T(8,128)(2,1)S(1)}, u32[]{:S(2)}, u32[]{:S(2)}) collective-permute-start(bf16[1056,640]{1,0:T(8,128)(2,1)S(1)} %shard_map.152), channel_id=1, source_target_pairs={{0,4},{4,0},{8,12},{12,8},{16,20},{20,16},{24,28},{28,24},{32,36},... | collective-permute-start | bytes 4055048 | tf_op jit(solution)/shard_map/ppermute | solution.py:61
  95.6 4.8 %collective-permute-start.8 = (f32[128,640]{1,0:T(8,128)S(1)}, f32[128,640]{1,0:T(8,128)S(1)}, u32[]{:S(2)}, u32[]{:S(2)}) collective-permute-start(f32[128,640]{1,0:T(8,128)S(1)} %get-tuple-element.47), channel_id=1, source_target_pairs={{0,4},{4,0},{8,12},{12,8},{16,20},{20,16},{24,28},{28,24},{32,36},... | collective-permute-start | bytes 983048 | tf_op jit(solution)/shard_map/ppermute | solution.py:61

commit v12 on v11

--- a/solution.py
+++ b/solution.py
@@ -89,11 +89,18 @@
     return rows[first : first + 1] + rows[first + 1 : first + 2] + rows[first + 2 : first + 3]
 
 
+def square_sums(ref, first):
+    rows = None
+    for head in range(ref.shape[1] // HD):
+        x = ref[first : first + ROWS, head * HD : (head + 1) * HD].astype(jnp.float32)
+        rows = x * x if rows is None else rows + x * x
+    return jnp.sum(jnp.transpose(rows), axis=0, keepdims=True)
+
+
 def pack_kernel(
-    here_ref, q_hbm, k_hbm, v_hbm, c_hbm, t_hbm, theirs_ref, q_mine_ref, sums_ref,
-    q_ref, k_ref, v_ref, c_ref, t_ref, arrived
+    here_ref, q_hbm, k_hbm, v_hbm, theirs_ref, q_mine_ref, sums_ref, q_ref, k_ref, v_ref, arrived
 ):
-    pairs = ((k_hbm, k_ref), (v_hbm, v_ref), (q_hbm, q_ref), (c_hbm, c_ref), (t_hbm, t_ref))
+    pairs = ((k_hbm, k_ref), (v_hbm, v_ref), (q_hbm, q_ref))
     copies = [
         pltpu.make_async_copy(source, target, arrived.at[index])
         for index, (source, target) in enumerate(pairs)
@@ -103,13 +110,6 @@
     core = lax.rem(here_ref[0], 2)
     half = theirs_ref.shape[1]
 
-    def total(ref, first):
-        rows = None
-        for head in range(ref.shape[1] // HD):
-            x = ref[first : first + ROWS, head * HD : (head + 1) * HD].astype(jnp.float32)
-            rows = x * x if rows is None else rows + x * x
-        return jnp.sum(jnp.transpose(rows), axis=0, keepdims=True)
-
     def split(ref, first):
         for side in range(2):
             row = side * HALF_ROWS + first
@@ -118,25 +118,27 @@
     sums_ref[...] = jnp.zeros((8, ROWS), jnp.float32)
     copies[0].wait()
     split(k_ref, 0)
-    k_total = total(k_ref, 0)
+    k_total = square_sums(k_ref, 0)
     copies[1].wait()
     split(v_ref, ROWS)
     copies[2].wait()
     low, high = q_ref[:, :half], q_ref[:, half:]
     q_mine_ref[...] = jnp.where(core == 0, low, high)
     theirs_ref[2 * HALF_ROWS :, :] = jnp.where(core == 0, high, low)
-    q_total = total(q_ref, 0)
+    q_total = square_sums(q_ref, 0)
     sums_ref[0:1, :] = k_total
     sums_ref[1:2, :] = q_total
     for side in range(2):
         rows = slice(side * HALF_ROWS + 2 * ROWS, (side + 1) * HALF_ROWS)
         theirs_ref[rows, 0:ROWS] = pieces(k_total, q_total)
         theirs_ref[rows, ROWS:] = jnp.zeros((SPARE, half - ROWS), jnp.bfloat16)
-    copies[3].wait()
-    sums_ref[2:3, :] = total(c_ref, 0)
-    copies[4].wait()
-    sums_ref[3:4, :] = total(t_ref, 0)
-    sums_ref[4:5, :] = total(t_ref, ROWS)
+
+
+def text_sums_kernel(c_ref, t_ref, out_ref):
+    out_ref[0:1, :] = square_sums(c_ref, 0)
+    out_ref[1:2, :] = square_sums(t_ref, 0)
+    out_ref[2:3, :] = square_sums(t_ref, ROWS)
+    out_ref[3:8, :] = jnp.zeros((5, ROWS), jnp.float32)
 
 
 def mate_kernel(own_ref, got_ref, out_ref):
@@ -146,8 +148,9 @@
     out_ref[6:7, :] = joined(rows, 3)
 
 
-def table_kernel(own_ref, side_ref, out_ref):
+def table_kernel(own_ref, side_ref, text_ref, out_ref):
     out_ref[0:8, :] = own_ref[...]
+    out_ref[2:5, :] = text_ref[0:3, :]
     out_ref[8:16, :] = jnp.zeros((8, ROWS), jnp.float32)
     out_ref[7:8, :] = side_ref[0:1, :]
     out_ref[8:9, :] = side_ref[5:6, :]
@@ -421,19 +424,21 @@
             jax.ShapeDtypeStruct((ROWS, half), bf16),
             jax.ShapeDtypeStruct((8, ROWS), f32),
         ),
-        [smem] + [hbm] * 5,
-        scratch=[pltpu.VMEM((ROWS, width), bf16)] * 4
-        + [pltpu.VMEM((2 * ROWS, width), bf16), pltpu.SemaphoreType.DMA((5,))],
+        [smem] + [hbm] * 3,
+        scratch=[pltpu.VMEM((ROWS, width), bf16)] * 3 + [pltpu.SemaphoreType.DMA((3,))],
         limit=60,
-    )(where, self_query, self_key, self_value, cross_query, text_key)
+    )(where, self_query, self_key, self_value)
     got = swapped(theirs)
     peers = lax.axis_size("tile")
     sums = call(mate_kernel, jax.ShapeDtypeStruct((8, ROWS), f32), [vmem] * 2)(sums, got)
+    text_sums = call(text_sums_kernel, jax.ShapeDtypeStruct((8, ROWS), f32), [vmem] * 2)(cross_query, text_key)
     side_sums = shifted(sums, 2)
     block = jnp.concatenate([theirs[: 2 * HALF_ROWS], got[: 2 * HALF_ROWS]], axis=0)
-    block, side_sums = lax.optimization_barrier((block, side_sums))
+    block, side_sums, text_sums = lax.optimization_barrier((block, side_sums, text_sums))
     side = shifted(block, 2)
-    sums = call(table_kernel, jax.ShapeDtypeStruct((16, ROWS), f32), [vmem] * 2)(sums, side_sums)
+    sums = call(table_kernel, jax.ShapeDtypeStruct((16, ROWS), f32), [vmem] * 3)(
+        sums, side_sums, text_sums
+    )
     sums = lax.psum(sums, "head")
     side, sums = lax.optimization_barrier((side, sums))
     marks = call(pieces_kernel, jax.ShapeDtypeStruct((SPARE, half), bf16), [vmem])(sums)

time: 101 us -> 101 us (level)
  no operation moved by 1% of the time
where the time goes in v12:
time: 101 us
  starting transfers between devices  38.7 us (38%)
  waiting for transfers between devices  25 us (25%)
  blocking collectives  19.6 us (19%)
  Pallas kernels  14.5 us (14%)
  local copies, waits for them, and re-layouts  1.33 us (1%)
  other arithmetic  1.22 us (1%)
    ppermute x5, starting transfers between devices, swapped(): return lax.ppermute(value, 'tile', [(i, i ^ 1) for i in range(peers)])  30.5 us
    ppermute x4, waiting for transfers between devices, shifted(): return lax.ppermute(value, 'tile', pairs + list(extra))  21.5 us
    psum x1, blocking collectives, per_device(): sums = lax.psum(sums, 'head')  19.6 us
    ppermute x4, starting transfers between devices, shifted(): return lax.ppermute(value, 'tile', pairs + list(extra))  8.19 us
    ppermute x5, waiting for transfers between devices, swapped(): return lax.ppermute(value, 'tile', [(i, i ^ 1) for i in range(peers)])  3.46 us
    pallas_call x1, Pallas kernels, per_device(): call(near_kernel, (jax.ShapeDtypeStruct((6 * ROWS, half), bf16),) * 2 + (...  3.39 us
    pallas_call x1, Pallas kernels, per_device(): call(far_kernel, (jax.ShapeDtypeStruct((ROWS, half), f32), window, window...  2.81 us
    pallas_call x1, Pallas kernels, per_device(): call(functools.partial(attend, False), jax.ShapeDtypeStruct((ROWS, half),...  2.48 us
  transfers between devices with their start and end apart: 9, of which 5 were waited for; matrix products, arithmetic and copies ran while one was open for 2% of the time, Pallas kernels for 8%

profile of v12, /device:TPU:31, one launch (start us, length us, event | category | flops | bytes accessed | tf_op | source)
XLA Modules:
  0.0 100.7 jit_solution(411413253523505426)
XLA Ops:
  0.0 2.4 %shard_map.145 = (bf16[672,640]{1,0:T(8,128)(2,1)}, bf16[128,640]{1,0:T(8,128)(2,1)}, f32[8,128]{1,0:T(8,128)}) custom-call(s32[1]{0:T(128)} %bitcast.here_ref, bf16[128,1280]{1,0:T(8,128)(2,1)} %q_hbm.1, bf16[128,1280]{1,0:T(8,128)(2,1)} %k_hbm.1, bf16[128,1280]{1,0:T(8,128)(2,1)} %v_hbm.1), custom_call_target="tpu_custom_call" | custom-call | flops 1000000 | bytes 4000000 | tf_op jit(solution)/shard_map/pallas_call | solution.py:420
  2.4 2.6 %collective-permute-start = (bf16[672,640]{1,0:T(8,128)(2,1)}, bf16[672,640]{1,0:T(8,128)(2,1)S(1)}, u32[]{:S(2)}, u32[]{:S(2)}) collective-permute-start(bf16[672,640]{1,0:T(8,128)(2,1)} %get-tuple-element.28), channel_id=1, source_target_pairs={{0,4},{4,0},{8,12},{12,8},{16,20},{20,16},{24,28},{28,24},{32,36},... | collective-permute-start | bytes 2580488 | tf_op jit(solution)/shard_map/ppermute | solution.py:61
  5.0 1.2 %slice.6 = bf16[544,640]{1,0:T(8,128)(2,1)S(1)} slice(bf16[672,640]{1,0:T(8,128)(2,1)} %get-tuple-element.28), slice={[0:544], [0:640]} | slice | bytes 1392640 | tf_op jit(solution)/shard_map/slice | solution.py:436
  6.4 0.8 collective-permute-done.got_ref
  7.2 2.4 %collective-permute-start.1 = (f32[8,128]{1,0:T(8,128)S(1)}, f32[8,128]{1,0:T(8,128)S(1)}, u32[]{:S(2)}, u32[]{:S(2)}) collective-permute-start(f32[8,128]{1,0:T(8,128)S(1)} %shard_map.146.own_ref), channel_id=1, source_target_pairs={{0,8},{8,16},{12,4},{16,24},{20,12},{24,32},{28,20},{32,40},{36,28... | collective-permute-start | bytes 12296 | tf_op jit(solution)/shard_map/ppermute | solution.py:56
  9.7 1.2 %pad_maximum_fusion.block_ref = bf16[1088,640]{1,0:T(8,128)(2,1)} fusion(bf16[544,640]{1,0:T(8,128)(2,1)S(1)} %slice.8, bf16[544,640]{1,0:T(8,128)(2,1)S(1)} %slice.6), kind=kLoop, calls=%fused_computation | loop fusion | flops 2785280 | bytes 2785280 | tf_op jit(solution)/shard_map/concatenate | solution.py:436
  11.0 4.8 %collective-permute-done.1.side_ref = f32[8,128]{1,0:T(8,128)S(1)} collective-permute-done((f32[8,128]{1,0:T(8,128)S(1)}, f32[8,128]{1,0:T(8,128)S(1)}, u32[]{:S(2)}, u32[]{:S(2)}) %collective-permute-start.1) | collective-permute-done | bytes 4128 | tf_op jit(solution)/shard_map/ppermute | solution.py:56
  15.7 1.9 %collective-permute-start.2 = (bf16[1088,640]{1,0:T(8,128)(2,1)}, bf16[1088,640]{1,0:T(8,128)(2,1)S(1)}, u32[]{:S(2)}, u32[]{:S(2)}) collective-permute-start(bf16[1088,640]{1,0:T(8,128)(2,1)} %pad_maximum_fusion.block_ref), channel_id=1, source_target_pairs={{0,8},{8,16},{12,4},{16,24},{20,12},{24,32},{28,20},{32,40},{36,28... | collective-permute-start | bytes 4177928 | tf_op jit(solution)/shard_map/ppermute | solution.py:56
  17.7 19.6 %psum.7.sums_ref = f32[16,128]{1,0:T(8,128)S(1)} all-reduce(f32[16,128]{1,0:T(8,128)S(1)} %shard_map.148), channel_id=1, replica_groups=mesh['tile'=128,'head'=4] {'head'}, use_global_device_ids=true, to_apply=%region_0.0 | all-reduce | flops 2048 | bytes 16384 | tf_op jit(solution)/shard_map/psum | solution.py:442
  37.3 2.5 %collective-permute-done.2 = bf16[1088,640]{1,0:T(8,128)(2,1)S(1)} collective-permute-done((bf16[1088,640]{1,0:T(8,128)(2,1)}, bf16[1088,640]{1,0:T(8,128)(2,1)S(1)}, u32[]{:S(2)}, u32[]{:S(2)}) %collective-permute-start.2) | collective-permute-done | bytes 1392672 | tf_op jit(solution)/shard_map/ppermute | solution.py:56
  39.9 1.9 %collective-permute-start.6 = (bf16[1088,640]{1,0:T(8,128)(2,1)S(1)}, bf16[1088,640]{1,0:T(8,128)(2,1)S(1)}, u32[]{:S(2)}, u32[]{:S(2)}) collective-permute-start(bf16[1088,640]{1,0:T(8,128)(2,1)S(1)} %constant_dynamic-update-slice_fusion.rest_0_.kept_ref), channel_id=1, source_target_pairs={{4,36},{12,44},{20,52},{28,60},{32,0},{36,68},{40,8},{44,76},{48,1... | collective-permute-start | bytes 4177928 | tf_op jit(solution)/shard_map/ppermute | solution.py:56
  41.8 1.9 %collective-permute-start.5 = (bf16[1088,640]{1,0:T(8,128)(2,1)S(1)}, bf16[1088,640]{1,0:T(8,128)(2,1)S(1)}, u32[]{:S(2)}, u32[]{:S(2)}) collective-permute-start(bf16[1088,640]{1,0:T(8,128)(2,1)S(1)} %constant_dynamic-update-slice_fusion.rest_0_.kept_ref), channel_id=1, source_target_pairs={{0,8},{8,16},{12,4},{16,24},{20,12},{24,32},{28,20},{32,40},{36,28... | collective-permute-start | bytes 4177928 | tf_op jit(solution)/shard_map/ppermute | solution.py:56
  44.0 15.9 %collective-permute-start.4 = (bf16[528,640]{1,0:T(8,128)(2,1)S(1)}, bf16[528,640]{1,0:T(8,128)(2,1)S(1)}, u32[]{:S(2)}, u32[]{:S(2)}) collective-permute-start(bf16[528,640]{1,0:T(8,128)(2,1)S(1)} %shard_map.151), channel_id=1, source_target_pairs={{0,4},{4,0},{8,12},{12,8},{16,20},{20,16},{24,28},{28,24},{32,36},... | collective-permute-start | bytes 2027528 | tf_op jit(solution)/shard_map/ppermute | solution.py:61
  60.0 1.9 %collective-permute-start.3 = (f32[16,128]{1,0:T(8,128)S(1)}, f32[16,128]{1,0:T(8,128)S(1)}, u32[]{:S(2)}, u32[]{:S(2)}) collective-permute-start(f32[16,128]{1,0:T(8,128)S(1)} %psum.7.sums_ref), channel_id=1, source_target_pairs={{0,4},{4,0},{8,12},{12,8},{16,20},{20,16},{24,28},{28,24},{32,36},... | collective-permute-start | bytes 24584 | tf_op jit(solution)/shard_map/ppermute | solution.py:61
  62.0 1.6 %shard_map.149.text_ref = f32[128,1280]{1,0:T(8,128)S(1)} custom-call(s32[128]{0:T(128)S(1)} %copy-done.6, s32[128]{0:T(128)S(1)} %copy-done.9, s32[1]{0:T(128)} %bitcast.here_ref, f32[16,128]{1,0:T(8,128)S(1)} %psum.7.sums_ref, bf16[128,1280]{1,0:T(8,128)(2,1)S(1)} %copy-done.3, bf16[256,1280]{1,0:T(8,128)(2,1)S(1)} %copy-done, ...), custom_call_target="tpu_custom_call" | custom-call | flops 400000000 | bytes 4000000 | tf_op jit(solution)/shard_map/pallas_call | solution.py:462
  63.6 3.4 %shard_map.152 = (bf16[768,640]{1,0:T(8,128)(2,1)S(1)}, bf16[768,640]{1,0:T(8,128)(2,1)S(1)}, bf16[128,640]{1,0:T(8,128)(2,1)S(1)}, bf16[128,640]{1,0:T(8,128)(2,1)S(1)}) custom-call(s32[128]{0:T(128)S(1)} %copy-done.6, s32[1]{0:T(128)} %bitcast.here_ref, f32[16,128]{1,0:T(8,128)S(1)} %psum.7.sums_ref, f32[16,128]{1,0:T(8,128)S(1)} %collective-permute-done.3.mate_sums_ref, ...), custom_call_target="tpu_custom_call" | custom-call | flops 200000000 | bytes 4000000 | tf_op jit(solution)/shard_map/pallas_call | solution.py:479
  67.0 14.2 %collective-permute-done.5.rest_0_.second_ref = bf16[1088,640]{1,0:T(8,128)(2,1)S(1)} collective-permute-done((bf16[1088,640]{1,0:T(8,128)(2,1)S(1)}, bf16[1088,640]{1,0:T(8,128)(2,1)S(1)}, u32[]{:S(2)}, u32[]{:S(2)}) %collective-permute-start.5) | collective-permute-done | bytes 1392672 | tf_op jit(solution)/shard_map/ppermute | solution.py:56
  81.2 0.5 shard_map.153
  81.7 7.9 %collective-permute-start.7 = (bf16[1056,640]{1,0:T(8,128)(2,1)S(1)}, bf16[1056,640]{1,0:T(8,128)(2,1)S(1)}, u32[]{:S(2)}, u32[]{:S(2)}) collective-permute-start(bf16[1056,640]{1,0:T(8,128)(2,1)S(1)} %shard_map.153), channel_id=1, source_target_pairs={{0,4},{4,0},{8,12},{12,8},{16,20},{20,16},{24,28},{28,24},{32,36},... | collective-permute-start | bytes 4055048 | tf_op jit(solution)/shard_map/ppermute | solution.py:61
  89.6 2.7 %collective-permute-done.7.part_ref = bf16[1056,640]{1,0:T(8,128)(2,1)S(1)} collective-permute-done((bf16[1056,640]{1,0:T(8,128)(2,1)S(1)}, bf16[1056,640]{1,0:T(8,128)(2,1)S(1)}, u32[]{:S(2)}, u32[]{:S(2)}) %collective-permute-start.7) | collective-permute-done | bytes 1351712 | tf_op jit(solution)/shard_map/ppermute | solution.py:61
  92.3 2.8 %shard_map.154 = (f32[128,640]{1,0:T(8,128)S(1)}, bf16[1792,640]{1,0:T(8,128)(2,1)S(1)}, bf16[1792,640]{1,0:T(8,128)(2,1)S(1)}) custom-call(s32[128]{0:T(128)S(1)} %copy-done.6, s32[128]{0:T(128)S(1)} %copy-done.8, s32[1]{0:T(128)} %bitcast.here_ref, f32[1,1280]{1,0:T(1,128)S(1)} %broadcast_in_dim.15.k_gain_ref, f32[896,128]{1,0:T(8,128)S(1)} %copy-done.2, ...), custom_call_target="tpu_custom_call" | custom-call | flops 300000000 | bytes 4000000 | tf_op jit(solution)/shard_map/pallas_call | solution.py:492
  95.1 2.3 %collective-permute-start.8 = (f32[128,640]{1,0:T(8,128)S(1)}, f32[128,640]{1,0:T(8,128)S(1)}, u32[]{:S(2)}, u32[]{:S(2)}) collective-permute-start(f32[128,640]{1,0:T(8,128)S(1)} %get-tuple-element.49), channel_id=1, source_target_pairs={{0,4},{4,0},{8,12},{12,8},{16,20},{20,16},{24,28},{28,24},{32,36},... | collective-permute-start | bytes 983048 | tf_op jit(solution)/shard_map/ppermute | solution.py:61
  97.4 2.5 %shard_map.155.own_ref = f32[128,640]{1,0:T(8,128)S(1)} custom-call(s32[128]{0:T(128)S(1)} %copy-done.6, s32[128]{0:T(128)S(1)} %copy-done.8, s32[1]{0:T(128)} %bitcast.here_ref, bf16[128,640]{1,0:T(8,128)(2,1)S(1)} %get-tuple-element.38.q_ref, bf16[1792,640]{1,0:T(8,128)(2,1)S(1)} %get-tuple-element.47.keys_ref, ...), custom_call_target="tpu_custom_call" | custom-call | flops 300000000 | bytes 4000000 | tf_op jit(solution)/shard_map/pallas_call | solution.py:501
  99.9 0.8 shard_map.156
  (43 shorter events, 0.7 us)
Async XLA Ops:
  0.0 6.1 %copy-start = (bf16[256,1280]{1,0:T(8,128)(2,1)S(1)}, bf16[256,1280]{1,0:T(8,128)(2,1)}, u32[]{:S(2)}) copy-start(bf16[256,1280]{1,0:T(8,128)(2,1)} %k_ref.1) | copy-start | bytes 1966084
  0.0 6.1 %copy-start.3 = (bf16[128,1280]{1,0:T(8,128)(2,1)S(1)}, bf16[128,1280]{1,0:T(8,128)(2,1)}, u32[]{:S(2)}) copy-start(bf16[128,1280]{1,0:T(8,128)(2,1)} %q_ref.1) | copy-start | bytes 983044
  2.4 4.8 %copy-start.7 = (f32[8,128]{1,0:T(8,128)S(1)}, f32[8,128]{1,0:T(8,128)}, u32[]{:S(2)}) copy-start(f32[8,128]{1,0:T(8,128)} %get-tuple-element.29.own_ref) | copy-start | bytes 12292
  2.4 4.8 %collective-permute-start = (bf16[672,640]{1,0:T(8,128)(2,1)}, bf16[672,640]{1,0:T(8,128)(2,1)S(1)}, u32[]{:S(2)}, u32[]{:S(2)}) collective-permute-start(bf16[672,640]{1,0:T(8,128)(2,1)} %get-tuple-element.28), channel_id=1, source_target_pairs={{0,4},{4,0},{8,12},{12,8},{16,20},{20,16},{24,28},{28,24},{32,36},... | collective-permute-start | bytes 2580488 | tf_op jit(solution)/shard_map/ppermute | solution.py:61
  7.2 8.6 %collective-permute-start.1 = (f32[8,128]{1,0:T(8,128)S(1)}, f32[8,128]{1,0:T(8,128)S(1)}, u32[]{:S(2)}, u32[]{:S(2)}) collective-permute-start(f32[8,128]{1,0:T(8,128)S(1)} %shard_map.146.own_ref), channel_id=1, source_target_pairs={{0,8},{8,16},{12,4},{16,24},{20,12},{24,32},{28,20},{32,40},{36,28... | collective-permute-start | bytes 12296 | tf_op jit(solution)/shard_map/ppermute | solution.py:56
  10.9 49.0 %copy-start.10 = (f32[1280]{0:T(1024)S(1)}, f32[1280]{0:T(1024)}, u32[]{:S(2)}) copy-start(f32[1280]{0:T(1024)} %param.21) | copy-start | bytes 15364
  10.9 49.0 %copy-start.11 = (f32[1280]{0:T(1024)S(1)}, f32[1280]{0:T(1024)}, u32[]{:S(2)}) copy-start(f32[1280]{0:T(1024)} %param.22) | copy-start | bytes 15364
  10.9 49.1 %copy-start.12 = (f32[1280]{0:T(1024)S(1)}, f32[1280]{0:T(1024)}, u32[]{:S(2)}) copy-start(f32[1280]{0:T(1024)} %param.23) | copy-start | bytes 15364
  10.9 49.1 %copy-start.13 = (f32[1280]{0:T(1024)S(1)}, f32[1280]{0:T(1024)}, u32[]{:S(2)}) copy-start(f32[1280]{0:T(1024)} %param.24) | copy-start | bytes 15364
  10.9 51.0 %copy-start.6 = (s32[128]{0:T(128)S(1)}, s32[128]{0:T(128)}, u32[]{:S(2)}) copy-start(s32[128]{0:T(128)} %item_ref.7) | copy-start | bytes 1540
  10.9 51.0 %copy-start.9 = (s32[128]{0:T(128)S(1)}, s32[128]{0:T(128)}, u32[]{:S(2)}) copy-start(s32[128]{0:T(128)} %len_ref.1) | copy-start | bytes 1540
  15.7 24.1 %collective-permute-start.2 = (bf16[1088,640]{1,0:T(8,128)(2,1)}, bf16[1088,640]{1,0:T(8,128)(2,1)S(1)}, u32[]{:S(2)}, u32[]{:S(2)}) collective-permute-start(bf16[1088,640]{1,0:T(8,128)(2,1)} %pad_maximum_fusion.block_ref), channel_id=1, source_target_pairs={{0,8},{8,16},{12,4},{16,24},{20,12},{24,32},{28,20},{32,40},{36,28... | collective-permute-start | bytes 4177928 | tf_op jit(solution)/shard_map/ppermute | solution.py:56
  37.3 24.7 %copy-start.4 = (bf16[256,1280]{1,0:T(8,128)(2,1)S(1)}, bf16[256,1280]{1,0:T(8,128)(2,1)}, u32[]{:S(2)}) copy-start(bf16[256,1280]{1,0:T(8,128)(2,1)} %v_ref.1) | copy-start | bytes 1966084
  39.9 27.1 %collective-permute-start.6 = (bf16[1088,640]{1,0:T(8,128)(2,1)S(1)}, bf16[1088,640]{1,0:T(8,128)(2,1)S(1)}, u32[]{:S(2)}, u32[]{:S(2)}) collective-permute-start(bf16[1088,640]{1,0:T(8,128)(2,1)S(1)} %constant_dynamic-update-slice_fusion.rest_0_.kept_ref), channel_id=1, source_target_pairs={{4,36},{12,44},{20,52},{28,60},{32,0},{36,68},{40,8},{44,76},{48,1... | collective-permute-start | bytes 4177928 | tf_op jit(solution)/shard_map/ppermute | solution.py:56
  41.8 39.4 %collective-permute-start.5 = (bf16[1088,640]{1,0:T(8,128)(2,1)S(1)}, bf16[1088,640]{1,0:T(8,128)(2,1)S(1)}, u32[]{:S(2)}, u32[]{:S(2)}) collective-permute-start(bf16[1088,640]{1,0:T(8,128)(2,1)S(1)} %constant_dynamic-update-slice_fusion.rest_0_.kept_ref), channel_id=1, source_target_pairs={{0,8},{8,16},{12,4},{16,24},{20,12},{24,32},{28,20},{32,40},{36,28... | collective-permute-start | bytes 4177928 | tf_op jit(solution)/shard_map/ppermute | solution.py:56
  44.0 19.6 %copy-start.1 = (f32[896,128]{1,0:T(8,128)S(1)}, f32[896,128]{1,0:T(8,128)}, u32[]{:S(2)}) copy-start(f32[896,128]{1,0:T(8,128)} %constant.15.clone.sin_ref) | copy-start | bytes 1376260
  44.0 19.6 %copy-start.2 = (f32[896,128]{1,0:T(8,128)S(1)}, f32[896,128]{1,0:T(8,128)}, u32[]{:S(2)}) copy-start(f32[896,128]{1,0:T(8,128)} %constant.14.clone.cos_ref) | copy-start | bytes 1376260
  44.0 19.6 %copy-start.5 = (bf16[128,640]{1,0:T(8,128)(2,1)S(1)}, bf16[128,640]{1,0:T(8,128)(2,1)}, u32[]{:S(2)}) copy-start(bf16[128,640]{1,0:T(8,128)(2,1)} %get-tuple-element.36.q_own_ref) | copy-start | bytes 491524
  44.0 19.5 %collective-permute-start.4 = (bf16[528,640]{1,0:T(8,128)(2,1)S(1)}, bf16[528,640]{1,0:T(8,128)(2,1)S(1)}, u32[]{:S(2)}, u32[]{:S(2)}) collective-permute-start(bf16[528,640]{1,0:T(8,128)(2,1)S(1)} %shard_map.151), channel_id=1, source_target_pairs={{0,4},{4,0},{8,12},{12,8},{16,20},{20,16},{24,28},{28,24},{32,36},... | collective-permute-start | bytes 2027528 | tf_op jit(solution)/shard_map/ppermute | solution.py:61
  60.0 3.5 %collective-permute-start.3 = (f32[16,128]{1,0:T(8,128)S(1)}, f32[16,128]{1,0:T(8,128)S(1)}, u32[]{:S(2)}, u32[]{:S(2)}) collective-permute-start(f32[16,128]{1,0:T(8,128)S(1)} %psum.7.sums_ref), channel_id=1, source_target_pairs={{0,4},{4,0},{8,12},{12,8},{16,20},{20,16},{24,28},{28,24},{32,36},... | collective-permute-start | bytes 24584 | tf_op jit(solution)/shard_map/ppermute | solution.py:61
  81.2 11.1 %copy-start.8 = (s32[128]{0:T(128)S(1)}, s32[128]{0:T(128)}, u32[]{:S(2)}) copy-start(s32[128]{0:T(128)} %count_ref.3) | copy-start | bytes 1540
  81.7 10.6 %collective-permute-start.7 = (bf16[1056,640]{1,0:T(8,128)(2,1)S(1)}, bf16[1056,640]{1,0:T(8,128)(2,1)S(1)}, u32[]{:S(2)}, u32[]{:S(2)}) collective-permute-start(bf16[1056,640]{1,0:T(8,128)(2,1)S(1)} %shard_map.153), channel_id=1, source_target_pairs={{0,4},{4,0},{8,12},{12,8},{16,20},{20,16},{24,28},{28,24},{32,36},... | collective-permute-start | bytes 4055048 | tf_op jit(solution)/shard_map/ppermute | solution.py:61
  95.1 4.8 %collective-permute-start.8 = (f32[128,640]{1,0:T(8,128)S(1)}, f32[128,640]{1,0:T(8,128)S(1)}, u32[]{:S(2)}, u32[]{:S(2)}) collective-permute-start(f32[128,640]{1,0:T(8,128)S(1)} %get-tuple-element.49), channel_id=1, source_target_pairs={{0,4},{4,0},{8,12},{12,8},{16,20},{20,16},{24,28},{28,24},{32,36},... | collective-permute-start | bytes 983048 | tf_op jit(solution)/shard_map/ppermute | solution.py:61

commit v13 on v11

--- a/solution.py
+++ b/solution.py
@@ -90,7 +90,7 @@
 
 
 def pack_kernel(
-    here_ref, q_hbm, k_hbm, v_hbm, c_hbm, t_hbm, theirs_ref, q_mine_ref, sums_ref,
+    here_ref, q_hbm, k_hbm, v_hbm, c_hbm, t_hbm, theirs_ref, own_ref, q_mine_ref, sums_ref,
     q_ref, k_ref, v_ref, c_ref, t_ref, arrived
 ):
     pairs = ((k_hbm, k_ref), (v_hbm, v_ref), (q_hbm, q_ref), (c_hbm, c_ref), (t_hbm, t_ref))
@@ -113,7 +113,9 @@
     def split(ref, first):
         for side in range(2):
             row = side * HALF_ROWS + first
-            theirs_ref[row : row + ROWS, :] = ref[:, side * half : (side + 1) * half]
+            part = ref[:, side * half : (side + 1) * half]
+            theirs_ref[row : row + ROWS, :] = part
+            own_ref[row : row + ROWS, :] = part
 
     sums_ref[...] = jnp.zeros((8, ROWS), jnp.float32)
     copies[0].wait()
@@ -130,8 +132,9 @@
     sums_ref[1:2, :] = q_total
     for side in range(2):
         rows = slice(side * HALF_ROWS + 2 * ROWS, (side + 1) * HALF_ROWS)
-        theirs_ref[rows, 0:ROWS] = pieces(k_total, q_total)
-        theirs_ref[rows, ROWS:] = jnp.zeros((SPARE, half - ROWS), jnp.bfloat16)
+        for ref in (theirs_ref, own_ref):
+            ref[rows, 0:ROWS] = pieces(k_total, q_total)
+            ref[rows, ROWS:] = jnp.zeros((SPARE, half - ROWS), jnp.bfloat16)
     copies[3].wait()
     sums_ref[2:3, :] = total(c_ref, 0)
     copies[4].wait()
@@ -414,10 +417,11 @@
 
     bf16 = jnp.bfloat16
     hbm = pl.BlockSpec(memory_space=pltpu.HBM)
-    theirs, q_mine, sums = call(
+    theirs, own_tile, q_mine, sums = call(
         pack_kernel,
         (
             jax.ShapeDtypeStruct((2 * HALF_ROWS + ROWS, half), bf16),
+            jax.ShapeDtypeStruct((2 * HALF_ROWS, half), bf16),
             jax.ShapeDtypeStruct((ROWS, half), bf16),
             jax.ShapeDtypeStruct((8, ROWS), f32),
         ),
@@ -430,7 +434,7 @@
     peers = lax.axis_size("tile")
     sums = call(mate_kernel, jax.ShapeDtypeStruct((8, ROWS), f32), [vmem] * 2)(sums, got)
     side_sums = shifted(sums, 2)
-    block = jnp.concatenate([theirs[: 2 * HALF_ROWS], got[: 2 * HALF_ROWS]], axis=0)
+    block = jnp.concatenate([own_tile, got[: 2 * HALF_ROWS]], axis=0)
     block, side_sums = lax.optimization_barrier((block, side_sums))
     side = shifted(block, 2)
     sums = call(table_kernel, jax.ShapeDtypeStruct((16, ROWS), f32), [vmem] * 2)(sums, side_sums)

time: 101 us -> 103 us (1.020)
    ppermute x5, waiting for transfers between devices: 3.75 us -> 4.91 us  [swapped(): return lax.ppermute(value, 'tile', [(i, i ^ 1) for i in range(peers)])]
    slice x2 -> x1, local copies, waits for them, and re-layouts: 1.22 us -> 0.06 us  [per_device(): block = jnp.concatenate([own_tile, got[:2 * HALF_ROWS]], axis=0)]
  transfers between devices with their start and end apart: 9 -> 9, of which waited for: 5 -> 5; matrix products, arithmetic and copies ran while one was open for 2% -> 1% of each run, Pallas kernels for 8% -> 8%
where the time goes in v13:
time: 103 us; the launch traced here: 102 us
  starting transfers between devices  38.9 us (38%)
  waiting for transfers between devices  25.7 us (25%)
  blocking collectives  19.6 us (19%)
  Pallas kernels  15.7 us (15%)
  other arithmetic  1.22 us (1%)
    ppermute x5, starting transfers between devices, swapped(): return lax.ppermute(value, 'tile', [(i, i ^ 1) for i in range(peers)])  30.5 us
    ppermute x4, waiting for transfers between devices, shifted(): return lax.ppermute(value, 'tile', pairs + list(extra))  20.8 us
    psum x1, blocking collectives, per_device(): sums = lax.psum(sums, 'head')  19.6 us
    ppermute x4, starting transfers between devices, shifted(): return lax.ppermute(value, 'tile', pairs + list(extra))  8.32 us
    ppermute x5, waiting for transfers between devices, swapped(): return lax.ppermute(value, 'tile', [(i, i ^ 1) for i in range(peers)])  4.91 us
    pallas_call x1, Pallas kernels, per_device(): call(near_kernel, (jax.ShapeDtypeStruct((6 * ROWS, half), bf16),) * 2 + (...  4.07 us
    pallas_call x1, Pallas kernels, per_device(): call(far_kernel, (jax.ShapeDtypeStruct((ROWS, half), f32), window, window...  3.16 us
    pallas_call x1, Pallas kernels, per_device(): call(pack_kernel, (jax.ShapeDtypeStruct((2 * HALF_ROWS + ROWS, half), bf1...  2.76 us
  transfers between devices with their start and end apart: 9, of which 5 were waited for; matrix products, arithmetic and copies ran while one was open for 1% of the time, Pallas kernels for 8%

profile of v13, /device:TPU:31, one launch (start us, length us, event | category | flops | bytes accessed | tf_op | source)
XLA Modules:
  0.0 102.2 jit_solution(13506480906652164137)
XLA Ops:
  0.0 2.8 %shard_map.145 = (bf16[672,640]{1,0:T(8,128)(2,1)}, bf16[544,640]{1,0:T(8,128)(2,1)}, bf16[128,640]{1,0:T(8,128)(2,1)}, f32[8,128]{1,0:T(8,128)}) custom-call(s32[1]{0:T(128)} %bitcast.here_ref, bf16[128,1280]{1,0:T(8,128)(2,1)} %q_hbm.1, bf16[128,1280]{1,0:T(8,128)(2,1)} %k_hbm.1, bf16[128,1280]{1,0:T(8,128)(2,1)} %v_hbm.1, bf16[128,1280]{1,0:T(8,128)(2,1)} %q_ref.1, ...), custom_call_target="tpu_custom_call" | custom-call | flops 1000000 | bytes 4000000 | tf_op jit(solution)/shard_map/pallas_call | solution.py:420
  2.8 2.6 %collective-permute-start = (bf16[672,640]{1,0:T(8,128)(2,1)}, bf16[672,640]{1,0:T(8,128)(2,1)S(1)}, u32[]{:S(2)}, u32[]{:S(2)}) collective-permute-start(bf16[672,640]{1,0:T(8,128)(2,1)} %get-tuple-element.29), channel_id=1, source_target_pairs={{0,4},{4,0},{8,12},{12,8},{16,20},{20,16},{24,28},{28,24},{32,36},... | collective-permute-start | bytes 2580488 | tf_op jit(solution)/shard_map/ppermute | solution.py:61
  5.4 2.2 %collective-permute-done.got_ref = bf16[672,640]{1,0:T(8,128)(2,1)S(1)} collective-permute-done((bf16[672,640]{1,0:T(8,128)(2,1)}, bf16[672,640]{1,0:T(8,128)(2,1)S(1)}, u32[]{:S(2)}, u32[]{:S(2)}) %collective-permute-start) | collective-permute-done | bytes 860192 | tf_op jit(solution)/shard_map/ppermute | solution.py:61
  7.6 0.7 copy-done.7
  8.2 2.6 %collective-permute-start.1 = (f32[8,128]{1,0:T(8,128)S(1)}, f32[8,128]{1,0:T(8,128)S(1)}, u32[]{:S(2)}, u32[]{:S(2)}) collective-permute-start(f32[8,128]{1,0:T(8,128)S(1)} %shard_map.146.own_ref), channel_id=1, source_target_pairs={{0,8},{8,16},{12,4},{16,24},{20,12},{24,32},{28,20},{32,40},{36,28... | collective-permute-start | bytes 12296 | tf_op jit(solution)/shard_map/ppermute | solution.py:56
  10.9 1.2 %pad_maximum_fusion.block_ref = bf16[1088,640]{1,0:T(8,128)(2,1)} fusion(bf16[544,640]{1,0:T(8,128)(2,1)S(1)} %slice.4, bf16[544,640]{1,0:T(8,128)(2,1)S(1)} %copy-done.10), kind=kLoop, calls=%fused_computation | loop fusion | flops 2785280 | bytes 2785280 | tf_op jit(solution)/shard_map/concatenate | solution.py:437
  12.2 4.7 %collective-permute-done.1.side_ref = f32[8,128]{1,0:T(8,128)S(1)} collective-permute-done((f32[8,128]{1,0:T(8,128)S(1)}, f32[8,128]{1,0:T(8,128)S(1)}, u32[]{:S(2)}, u32[]{:S(2)}) %collective-permute-start.1) | collective-permute-done | bytes 4128 | tf_op jit(solution)/shard_map/ppermute | solution.py:56
  16.9 1.9 %collective-permute-start.2 = (bf16[1088,640]{1,0:T(8,128)(2,1)}, bf16[1088,640]{1,0:T(8,128)(2,1)S(1)}, u32[]{:S(2)}, u32[]{:S(2)}) collective-permute-start(bf16[1088,640]{1,0:T(8,128)(2,1)} %pad_maximum_fusion.block_ref), channel_id=1, source_target_pairs={{0,8},{8,16},{12,4},{16,24},{20,12},{24,32},{28,20},{32,40},{36,28... | collective-permute-start | bytes 4177928 | tf_op jit(solution)/shard_map/ppermute | solution.py:56
  18.9 19.6 %psum.7.sums_ref = f32[16,128]{1,0:T(8,128)S(1)} all-reduce(f32[16,128]{1,0:T(8,128)S(1)} %shard_map.147), channel_id=1, replica_groups=mesh['tile'=128,'head'=4] {'head'}, use_global_device_ids=true, to_apply=%region_0.0 | all-reduce | flops 2048 | bytes 16384 | tf_op jit(solution)/shard_map/psum | solution.py:441
  38.5 2.5 %collective-permute-done.2 = bf16[1088,640]{1,0:T(8,128)(2,1)S(1)} collective-permute-done((bf16[1088,640]{1,0:T(8,128)(2,1)}, bf16[1088,640]{1,0:T(8,128)(2,1)S(1)}, u32[]{:S(2)}, u32[]{:S(2)}) %collective-permute-start.2) | collective-permute-done | bytes 1392672 | tf_op jit(solution)/shard_map/ppermute | solution.py:56
  41.1 1.9 %collective-permute-start.6 = (bf16[1088,640]{1,0:T(8,128)(2,1)S(1)}, bf16[1088,640]{1,0:T(8,128)(2,1)S(1)}, u32[]{:S(2)}, u32[]{:S(2)}) collective-permute-start(bf16[1088,640]{1,0:T(8,128)(2,1)S(1)} %constant_dynamic-update-slice_fusion.rest_0_.kept_ref), channel_id=1, source_target_pairs={{4,36},{12,44},{20,52},{28,60},{32,0},{36,68},{40,8},{44,76},{48,1... | collective-permute-start | bytes 4177928 | tf_op jit(solution)/shard_map/ppermute | solution.py:56
  43.0 1.9 %collective-permute-start.5 = (bf16[1088,640]{1,0:T(8,128)(2,1)S(1)}, bf16[1088,640]{1,0:T(8,128)(2,1)S(1)}, u32[]{:S(2)}, u32[]{:S(2)}) collective-permute-start(bf16[1088,640]{1,0:T(8,128)(2,1)S(1)} %constant_dynamic-update-slice_fusion.rest_0_.kept_ref), channel_id=1, source_target_pairs={{0,8},{8,16},{12,4},{16,24},{20,12},{24,32},{28,20},{32,40},{36,28... | collective-permute-start | bytes 4177928 | tf_op jit(solution)/shard_map/ppermute | solution.py:56
  45.2 15.9 %collective-permute-start.4 = (bf16[528,640]{1,0:T(8,128)(2,1)S(1)}, bf16[528,640]{1,0:T(8,128)(2,1)S(1)}, u32[]{:S(2)}, u32[]{:S(2)}) collective-permute-start(bf16[528,640]{1,0:T(8,128)(2,1)S(1)} %shard_map.150), channel_id=1, source_target_pairs={{0,4},{4,0},{8,12},{12,8},{16,20},{20,16},{24,28},{28,24},{32,36},... | collective-permute-start | bytes 2027528 | tf_op jit(solution)/shard_map/ppermute | solution.py:61
  61.2 1.9 %collective-permute-start.3 = (f32[16,128]{1,0:T(8,128)S(1)}, f32[16,128]{1,0:T(8,128)S(1)}, u32[]{:S(2)}, u32[]{:S(2)}) collective-permute-start(f32[16,128]{1,0:T(8,128)S(1)} %psum.7.sums_ref), channel_id=1, source_target_pairs={{0,4},{4,0},{8,12},{12,8},{16,20},{20,16},{24,28},{28,24},{32,36},... | collective-permute-start | bytes 24584 | tf_op jit(solution)/shard_map/ppermute | solution.py:61
  63.2 1.6 %shard_map.148.text_ref = f32[128,1280]{1,0:T(8,128)S(1)} custom-call(s32[128]{0:T(128)S(1)} %copy-done.6, s32[128]{0:T(128)S(1)} %copy-done.9, s32[1]{0:T(128)} %bitcast.here_ref, f32[16,128]{1,0:T(8,128)S(1)} %psum.7.sums_ref, bf16[128,1280]{1,0:T(8,128)(2,1)S(1)} %copy-done.3, bf16[256,1280]{1,0:T(8,128)(2,1)S(1)} %copy-done, ...), custom_call_target="tpu_custom_call" | custom-call | flops 400000000 | bytes 4000000 | tf_op jit(solution)/shard_map/pallas_call | solution.py:461
  64.8 4.1 %shard_map.151 = (bf16[768,640]{1,0:T(8,128)(2,1)S(1)}, bf16[768,640]{1,0:T(8,128)(2,1)S(1)}, bf16[128,640]{1,0:T(8,128)(2,1)S(1)}, bf16[128,640]{1,0:T(8,128)(2,1)S(1)}) custom-call(s32[128]{0:T(128)S(1)} %copy-done.6, s32[1]{0:T(128)} %bitcast.here_ref, f32[16,128]{1,0:T(8,128)S(1)} %psum.7.sums_ref, f32[16,128]{1,0:T(8,128)S(1)} %collective-permute-done.3.mate_sums_ref, ...), custom_call_target="tpu_custom_call" | custom-call | flops 200000000 | bytes 4000000 | tf_op jit(solution)/shard_map/pallas_call | solution.py:478
  68.9 13.5 %collective-permute-done.5.rest_0_.second_ref = bf16[1088,640]{1,0:T(8,128)(2,1)S(1)} collective-permute-done((bf16[1088,640]{1,0:T(8,128)(2,1)S(1)}, bf16[1088,640]{1,0:T(8,128)(2,1)S(1)}, u32[]{:S(2)}, u32[]{:S(2)}) %collective-permute-start.5) | collective-permute-done | bytes 1392672 | tf_op jit(solution)/shard_map/ppermute | solution.py:56
  82.4 0.5 shard_map.152
  82.9 7.9 %collective-permute-start.7 = (bf16[1056,640]{1,0:T(8,128)(2,1)S(1)}, bf16[1056,640]{1,0:T(8,128)(2,1)S(1)}, u32[]{:S(2)}, u32[]{:S(2)}) collective-permute-start(bf16[1056,640]{1,0:T(8,128)(2,1)S(1)} %shard_map.152), channel_id=1, source_target_pairs={{0,4},{4,0},{8,12},{12,8},{16,20},{20,16},{24,28},{28,24},{32,36},... | collective-permute-start | bytes 4055048 | tf_op jit(solution)/shard_map/ppermute | solution.py:61
  90.8 2.7 %collective-permute-done.7.part_ref = bf16[1056,640]{1,0:T(8,128)(2,1)S(1)} collective-permute-done((bf16[1056,640]{1,0:T(8,128)(2,1)S(1)}, bf16[1056,640]{1,0:T(8,128)(2,1)S(1)}, u32[]{:S(2)}, u32[]{:S(2)}) %collective-permute-start.7) | collective-permute-done | bytes 1351712 | tf_op jit(solution)/shard_map/ppermute | solution.py:61
  93.5 3.2 %shard_map.153 = (f32[128,640]{1,0:T(8,128)S(1)}, bf16[1792,640]{1,0:T(8,128)(2,1)S(1)}, bf16[1792,640]{1,0:T(8,128)(2,1)S(1)}) custom-call(s32[128]{0:T(128)S(1)} %copy-done.6, s32[128]{0:T(128)S(1)} %copy-done.8, s32[1]{0:T(128)} %bitcast.here_ref, f32[1,1280]{1,0:T(1,128)S(1)} %broadcast_in_dim.15.k_gain_ref, f32[896,128]{1,0:T(8,128)S(1)} %copy-done.2, ...), custom_call_target="tpu_custom_call" | custom-call | flops 300000000 | bytes 4000000 | tf_op jit(solution)/shard_map/pallas_call | solution.py:491
  96.7 2.3 %collective-permute-start.8 = (f32[128,640]{1,0:T(8,128)S(1)}, f32[128,640]{1,0:T(8,128)S(1)}, u32[]{:S(2)}, u32[]{:S(2)}) collective-permute-start(f32[128,640]{1,0:T(8,128)S(1)} %get-tuple-element.49), channel_id=1, source_target_pairs={{0,4},{4,0},{8,12},{12,8},{16,20},{20,16},{24,28},{28,24},{32,36},... | collective-permute-start | bytes 983048 | tf_op jit(solution)/shard_map/ppermute | solution.py:61
  98.9 2.5 %shard_map.154.own_ref = f32[128,640]{1,0:T(8,128)S(1)} custom-call(s32[128]{0:T(128)S(1)} %copy-done.6, s32[128]{0:T(128)S(1)} %copy-done.8, s32[1]{0:T(128)} %bitcast.here_ref, bf16[128,640]{1,0:T(8,128)(2,1)S(1)} %get-tuple-element.38.q_ref, bf16[1792,640]{1,0:T(8,128)(2,1)S(1)} %get-tuple-element.47.keys_ref, ...), custom_call_target="tpu_custom_call" | custom-call | flops 300000000 | bytes 4000000 | tf_op jit(solution)/shard_map/pallas_call | solution.py:500
  101.4 0.8 shard_map.155
  (43 shorter events, 0.5 us)
Async XLA Ops:
  2.8 4.8 %collective-permute-start = (bf16[672,640]{1,0:T(8,128)(2,1)}, bf16[672,640]{1,0:T(8,128)(2,1)S(1)}, u32[]{:S(2)}, u32[]{:S(2)}) collective-permute-start(bf16[672,640]{1,0:T(8,128)(2,1)} %get-tuple-element.29), channel_id=1, source_target_pairs={{0,4},{4,0},{8,12},{12,8},{16,20},{20,16},{24,28},{28,24},{32,36},... | collective-permute-start | bytes 2580488 | tf_op jit(solution)/shard_map/ppermute | solution.py:61
  7.6 0.7 copy-start.7
  8.2 2.7 %copy-start.10 = (bf16[544,640]{1,0:T(8,128)(2,1)S(1)}, bf16[544,640]{1,0:T(8,128)(2,1)}, u32[]{:S(2)}) copy-start(bf16[544,640]{1,0:T(8,128)(2,1)} %get-tuple-element.28) | copy-start | bytes 2088964
  8.2 8.7 %collective-permute-start.1 = (f32[8,128]{1,0:T(8,128)S(1)}, f32[8,128]{1,0:T(8,128)S(1)}, u32[]{:S(2)}, u32[]{:S(2)}) collective-permute-start(f32[8,128]{1,0:T(8,128)S(1)} %shard_map.146.own_ref), channel_id=1, source_target_pairs={{0,8},{8,16},{12,4},{16,24},{20,12},{24,32},{28,20},{32,40},{36,28... | collective-permute-start | bytes 12296 | tf_op jit(solution)/shard_map/ppermute | solution.py:56
  12.1 49.0 %copy-start.11 = (f32[1280]{0:T(1024)S(1)}, f32[1280]{0:T(1024)}, u32[]{:S(2)}) copy-start(f32[1280]{0:T(1024)} %param.21) | copy-start | bytes 15364
  12.1 49.0 %copy-start.12 = (f32[1280]{0:T(1024)S(1)}, f32[1280]{0:T(1024)}, u32[]{:S(2)}) copy-start(f32[1280]{0:T(1024)} %param.22) | copy-start | bytes 15364
  12.1 49.0 %copy-start.13 = (f32[1280]{0:T(1024)S(1)}, f32[1280]{0:T(1024)}, u32[]{:S(2)}) copy-start(f32[1280]{0:T(1024)} %param.23) | copy-start | bytes 15364
  12.1 49.1 %copy-start.14 = (f32[1280]{0:T(1024)S(1)}, f32[1280]{0:T(1024)}, u32[]{:S(2)}) copy-start(f32[1280]{0:T(1024)} %param.24) | copy-start | bytes 15364
  12.1 51.0 %copy-start = (bf16[256,1280]{1,0:T(8,128)(2,1)S(1)}, bf16[256,1280]{1,0:T(8,128)(2,1)}, u32[]{:S(2)}) copy-start(bf16[256,1280]{1,0:T(8,128)(2,1)} %k_ref.1) | copy-start | bytes 1966084
  12.2 51.0 %copy-start.3 = (bf16[128,1280]{1,0:T(8,128)(2,1)S(1)}, bf16[128,1280]{1,0:T(8,128)(2,1)}, u32[]{:S(2)}) copy-start(bf16[128,1280]{1,0:T(8,128)(2,1)} %q_ref.1) | copy-start | bytes 983044
  12.2 51.0 %copy-start.6 = (s32[128]{0:T(128)S(1)}, s32[128]{0:T(128)}, u32[]{:S(2)}) copy-start(s32[128]{0:T(128)} %item_ref.7) | copy-start | bytes 1540
  12.2 51.0 %copy-start.9 = (s32[128]{0:T(128)S(1)}, s32[128]{0:T(128)}, u32[]{:S(2)}) copy-start(s32[128]{0:T(128)} %len_ref.1) | copy-start | bytes 1540
  16.9 24.1 %collective-permute-start.2 = (bf16[1088,640]{1,0:T(8,128)(2,1)}, bf16[1088,640]{1,0:T(8,128)(2,1)S(1)}, u32[]{:S(2)}, u32[]{:S(2)}) collective-permute-start(bf16[1088,640]{1,0:T(8,128)(2,1)} %pad_maximum_fusion.block_ref), channel_id=1, source_target_pairs={{0,8},{8,16},{12,4},{16,24},{20,12},{24,32},{28,20},{32,40},{36,28... | collective-permute-start | bytes 4177928 | tf_op jit(solution)/shard_map/ppermute | solution.py:56
  38.5 24.7 %copy-start.4 = (bf16[256,1280]{1,0:T(8,128)(2,1)S(1)}, bf16[256,1280]{1,0:T(8,128)(2,1)}, u32[]{:S(2)}) copy-start(bf16[256,1280]{1,0:T(8,128)(2,1)} %v_ref.1) | copy-start | bytes 1966084
  41.1 27.8 %collective-permute-start.6 = (bf16[1088,640]{1,0:T(8,128)(2,1)S(1)}, bf16[1088,640]{1,0:T(8,128)(2,1)S(1)}, u32[]{:S(2)}, u32[]{:S(2)}) collective-permute-start(bf16[1088,640]{1,0:T(8,128)(2,1)S(1)} %constant_dynamic-update-slice_fusion.rest_0_.kept_ref), channel_id=1, source_target_pairs={{4,36},{12,44},{20,52},{28,60},{32,0},{36,68},{40,8},{44,76},{48,1... | collective-permute-start | bytes 4177928 | tf_op jit(solution)/shard_map/ppermute | solution.py:56
  43.0 39.4 %collective-permute-start.5 = (bf16[1088,640]{1,0:T(8,128)(2,1)S(1)}, bf16[1088,640]{1,0:T(8,128)(2,1)S(1)}, u32[]{:S(2)}, u32[]{:S(2)}) collective-permute-start(bf16[1088,640]{1,0:T(8,128)(2,1)S(1)} %constant_dynamic-update-slice_fusion.rest_0_.kept_ref), channel_id=1, source_target_pairs={{0,8},{8,16},{12,4},{16,24},{20,12},{24,32},{28,20},{32,40},{36,28... | collective-permute-start | bytes 4177928 | tf_op jit(solution)/shard_map/ppermute | solution.py:56
  45.2 19.6 %copy-start.1 = (f32[896,128]{1,0:T(8,128)S(1)}, f32[896,128]{1,0:T(8,128)}, u32[]{:S(2)}) copy-start(f32[896,128]{1,0:T(8,128)} %constant.15.clone.sin_ref) | copy-start | bytes 1376260
  45.2 19.6 %copy-start.2 = (f32[896,128]{1,0:T(8,128)S(1)}, f32[896,128]{1,0:T(8,128)}, u32[]{:S(2)}) copy-start(f32[896,128]{1,0:T(8,128)} %constant.14.clone.cos_ref) | copy-start | bytes 1376260
  45.2 19.6 %copy-start.5 = (bf16[128,640]{1,0:T(8,128)(2,1)S(1)}, bf16[128,640]{1,0:T(8,128)(2,1)}, u32[]{:S(2)}) copy-start(bf16[128,640]{1,0:T(8,128)(2,1)} %get-tuple-element.36.q_own_ref) | copy-start | bytes 491524
  45.2 19.6 %collective-permute-start.4 = (bf16[528,640]{1,0:T(8,128)(2,1)S(1)}, bf16[528,640]{1,0:T(8,128)(2,1)S(1)}, u32[]{:S(2)}, u32[]{:S(2)}) collective-permute-start(bf16[528,640]{1,0:T(8,128)(2,1)S(1)} %shard_map.150), channel_id=1, source_target_pairs={{0,4},{4,0},{8,12},{12,8},{16,20},{20,16},{24,28},{28,24},{32,36},... | collective-permute-start | bytes 2027528 | tf_op jit(solution)/shard_map/ppermute | solution.py:61
  61.2 3.5 %collective-permute-start.3 = (f32[16,128]{1,0:T(8,128)S(1)}, f32[16,128]{1,0:T(8,128)S(1)}, u32[]{:S(2)}, u32[]{:S(2)}) collective-permute-start(f32[16,128]{1,0:T(8,128)S(1)} %psum.7.sums_ref), channel_id=1, source_target_pairs={{0,4},{4,0},{8,12},{12,8},{16,20},{20,16},{24,28},{28,24},{32,36},... | collective-permute-start | bytes 24584 | tf_op jit(solution)/shard_map/ppermute | solution.py:61
  82.4 11.1 %copy-start.8 = (s32[128]{0:T(128)S(1)}, s32[128]{0:T(128)}, u32[]{:S(2)}) copy-start(s32[128]{0:T(128)} %count_ref.3) | copy-start | bytes 1540
  82.9 10.6 %collective-permute-start.7 = (bf16[1056,640]{1,0:T(8,128)(2,1)S(1)}, bf16[1056,640]{1,0:T(8,128)(2,1)S(1)}, u32[]{:S(2)}, u32[]{:S(2)}) collective-permute-start(bf16[1056,640]{1,0:T(8,128)(2,1)S(1)} %shard_map.152), channel_id=1, source_target_pairs={{0,4},{4,0},{8,12},{12,8},{16,20},{20,16},{24,28},{28,24},{32,36},... | collective-permute-start | bytes 4055048 | tf_op jit(solution)/shard_map/ppermute | solution.py:61
  96.7 4.8 %collective-permute-start.8 = (f32[128,640]{1,0:T(8,128)S(1)}, f32[128,640]{1,0:T(8,128)S(1)}, u32[]{:S(2)}, u32[]{:S(2)}) collective-permute-start(f32[128,640]{1,0:T(8,128)S(1)} %get-tuple-element.49), channel_id=1, source_target_pairs={{0,4},{4,0},{8,12},{12,8},{16,20},{20,16},{24,28},{28,24},{32,36},... | collective-permute-start | bytes 983048 | tf_op jit(solution)/shard_map/ppermute | solution.py:61
